TPU v7x, 256 devices: a whole 4x4x8 slice. The times are simulated.
256 devices in a mesh: ha: 16 (over z, core), wa: 4 (over y), col: 4 (over x).
Axes of the slice: x: 4, y: 4, z: 8, core: 2. Of those that a mesh axis runs over, the one named last changes fastest.
Arguments:
- features: bfloat16 [4, 128, 128, 512], P(None, 'ha', 'wa', 'col'), may hold values from -64 to 64
- cache_first: bfloat16 [2, 128, 128, 512], P(None, 'ha', 'wa', 'col'), may hold values from -6 to 6
- cache_second: bfloat16 [2, 128, 128, 512], P(None, 'ha', 'wa', 'col'), may hold values from -6 to 6
- weight_first: bfloat16 [27, 512, 512], P(None, 'col'), may hold values from -0.0546875 to 0.0546875
- weight_second: bfloat16 [27, 512, 512], P(None, 'col'), may hold values from -0.0546875 to 0.0546875
- weight_up: bfloat16 [9, 512, 512], P(None, 'col'), may hold values from -0.09375 to 0.09375
Outputs:
- upsampled: bfloat16 [4, 256, 256, 512], P(None, 'ha', 'wa', 'col')
All inputs are finite; a program needn't handle non-finite values.
Results may differ from a plain program's by a relative error of at most 0.01.
Values may be sent and summed in bfloat16 or wider, within the bound.
No kernel may reach another device: no remote copies, remote signals or barrier semaphores. Data moves between devices by JAX's collectives and lax.ppermute only.
A program may use at most 192 MiB of HBM per device.

v0:
```python
import jax
import jax.numpy as jnp
from jax import lax
from jax.sharding import PartitionSpec as P

C = 512
G = 32


def with_halo(x, sides, width):
    for axis, dim in sides:
        count, length = (lax.axis_size(axis), x.shape[dim])
        up = [(i, (i + 1) % count) for i in range(count - 1)]
        down = [(j, i) for i, j in up]
        last = lax.slice_in_dim(x, length - width, length, axis=dim)
        leading = lax.slice_in_dim(x, 0, width, axis=dim)
        before = lax.ppermute(last, axis, up)
        after = lax.ppermute(leading, axis, down)
        x = jnp.concatenate([before, x, after], axis=dim)
    return x


def norm_act(values):
    group_size = C // G
    local_groups = values.shape[3] // group_size
    shaped = values.astype(jnp.float32).reshape(values.shape[:3] + (local_groups, group_size))
    entries = (
        values.shape[0]
        * values.shape[1]
        * values.shape[2]
        * group_size
        * lax.axis_size("ha")
        * lax.axis_size("wa")
    )
    totals = lax.psum(jnp.sum(shaped, axis=(0, 1, 2, 4)), ("ha", "wa"))
    center = (totals / entries)[:, None]
    deviation = shaped - center
    squares = lax.psum(jnp.sum(deviation * deviation, axis=(0, 1, 2, 4)), ("ha", "wa"))
    spread = (squares / entries)[:, None]
    normed = deviation * lax.rsqrt(spread + 1e-06)
    return jax.nn.silu(normed).reshape(values.shape).astype(jnp.bfloat16)


def conv_block(stack, weight, frame_taps, upsample):
    padded = with_halo(stack, (("ha", 1), ("wa", 2)), 1)
    if upsample:
        padded = jnp.repeat(jnp.repeat(padded, 2, axis=1), 2, axis=2)
        padded = padded[:, 1:-1, 1:-1, :]
    rows_here = padded.shape[1] - 2
    cols_here = padded.shape[2] - 2
    frames_out = padded.shape[0] - frame_taps + 1
    pieces = []
    for step_t in range(frame_taps):
        for row_off in range(3):
            for col_off in range(3):
                pieces.append(
                    padded[
                        step_t : step_t + frames_out,
                        row_off : row_off + rows_here,
                        col_off : col_off + cols_here,
                        :,
                    ]
                )
    patches = jnp.concatenate(pieces, axis=-1).reshape(frames_out * rows_here * cols_here, -1)
    flat = weight.reshape(-1, weight.shape[2])
    result = jnp.dot(patches, flat, preferred_element_type=jnp.float32).reshape(
        frames_out, rows_here, cols_here, -1
    )
    result = lax.psum_scatter(result, "col", scatter_dimension=3, tiled=True)
    return result


def on_device(features, cache_first, cache_second, weight_first, weight_second, weight_up):
    act_first = norm_act(features)
    hidden = conv_block(
        jnp.concatenate([cache_first, act_first], axis=0), weight_first, 3, False
    ).astype(jnp.bfloat16)
    act_second = norm_act(hidden)
    branch = conv_block(
        jnp.concatenate([cache_second, act_second], axis=0), weight_second, 3, False
    )
    resid = (features.astype(jnp.float32) + branch).astype(jnp.bfloat16)
    return conv_block(resid, weight_up, 1, True).astype(jnp.bfloat16)


def solution(mesh):
    placed = (
        P(None, "ha", "wa", "col"),
        P(None, "ha", "wa", "col"),
        P(None, "ha", "wa", "col"),
        P(None, "col", None),
        P(None, "col", None),
        P(None, "col", None),
    )
    return jax.shard_map(
        on_device, mesh=mesh, in_specs=placed, out_specs=P(None, "ha", "wa", "col"), check_vma=False
    )
```

profile of v0, /device:TPU:97, one launch (start us, length us, event | category | flops | bytes accessed | tf_op | source)
XLA Modules:
  0.0 766.7 jit_solution(16732108176582445937)
XLA Ops:
  8.0 119.6 %psum.28 = f32[8]{0:T(128)S(1)} all-reduce(f32[8]{0:T(128)S(1)} %reduce_sum.51), channel_id=1, replica_groups=mesh['ha'=16,'wa'=4,'col'=4] {'ha','wa'}, use_global_device_ids=true, to_apply=%region_2.0 | all-reduce | flops 8 | bytes 64 | tf_op jit(solution)/shard_map/psum | solution.py:35
  129.0 125.6 %psum.29 = f32[8]{0:T(128)S(1)} all-reduce(f32[8]{0:T(128)S(1)} %reduce_sum.54), channel_id=1, replica_groups=mesh['ha'=16,'wa'=4,'col'=4] {'ha','wa'}, use_global_device_ids=true, to_apply=%region_5.6 | all-reduce | flops 8 | bytes 64 | tf_op jit(solution)/shard_map/psum | solution.py:38
  256.7 10.5 %collective-permute-start = (bf16[6,1,32,128]{3,2,1,0:T(8,128)(2,1)S(1)}, bf16[6,1,32,128]{3,2,1,0:T(8,128)(2,1)S(1)}, u32[]{:S(2)}, u32[]{:S(2)}) collective-permute-start(bf16[6,1,32,128]{3,2,1,0:T(8,128)(2,1)S(1)} %get-tuple-element.28), channel_id=1, source_target_pairs={{0,16},{16,32},{32,48},{48,64},{64,80},{80,96},{96,112},{112,128},... | collective-permute-start | bytes 147464 | tf_op jit(solution)/shard_map/ppermute | solution.py:17
  267.3 1.9 collective-permute-start.1
  269.2 4.7 collective-permute-done.1
  276.0 4.2 collective-permute-start.2
  286.2 5.3 fusion.27
  291.6 32.7 %reduce-scatter.4.cloned.1.call-done = f32[4,8,32,128]{3,2,1,0:T(8,128)} async-done(((f32[4,8,32,512]{3,2,1,0:T(8,128)}), f32[4,8,32,128]{3,2,1,0:T(8,128)}) %reduce-scatter.4.cloned.1.call-update) | async-done | bytes 524304 | tf_op jit(solution)/shard_map/reduce_scatter | solution.py:69
  325.7 119.3 %psum.30 = f32[8]{0:T(128)S(1)} all-reduce(f32[8]{0:T(128)S(1)} %reduce_sum.72), channel_id=1, replica_groups=mesh['ha'=16,'wa'=4,'col'=4] {'ha','wa'}, use_global_device_ids=true, to_apply=%region_9.10 | all-reduce | flops 8 | bytes 64 | tf_op jit(solution)/shard_map/psum | solution.py:35
  446.5 125.6 %psum.31 = f32[8]{0:T(128)S(1)} all-reduce(f32[8]{0:T(128)S(1)} %reduce_sum.75), channel_id=1, replica_groups=mesh['ha'=16,'wa'=4,'col'=4] {'ha','wa'}, use_global_device_ids=true, to_apply=%region_12.13 | all-reduce | flops 8 | bytes 64 | tf_op jit(solution)/shard_map/psum | solution.py:38
  574.3 10.4 %collective-permute-start.4 = (bf16[6,1,32,128]{3,2,1,0:T(8,128)(2,1)S(1)}, bf16[6,1,32,128]{3,2,1,0:T(8,128)(2,1)S(1)}, u32[]{:S(2)}, u32[]{:S(2)}) collective-permute-start(bf16[6,1,32,128]{3,2,1,0:T(8,128)(2,1)S(1)} %get-tuple-element.24), channel_id=1, source_target_pairs={{0,16},{16,32},{32,48},{48,64},{64,80},{80,96},{96,112},{112,128},... | collective-permute-start | bytes 147464 | tf_op jit(solution)/shard_map/ppermute | solution.py:17
  586.7 4.7 collective-permute-done.5
  593.5 4.4 collective-permute-start.6
  602.9 5.3 fusion.28
  608.3 31.1 %reduce-scatter.6.cloned.1.call-done = f32[4,8,32,128]{3,2,1,0:T(8,128)} async-done(((f32[4,8,32,512]{3,2,1,0:T(8,128)}), f32[4,8,32,128]{3,2,1,0:T(8,128)}) %reduce-scatter.6.cloned.1.call-update) | async-done | bytes 524304 | tf_op jit(solution)/shard_map/reduce_scatter | solution.py:69
  640.5 4.9 collective-permute-start.8
  645.4 1.9 collective-permute-start.9
  647.4 4.5 collective-permute-done.9
  651.9 3.1 collective-permute-start.10
  656.5 3.0 collective-permute-done.11
  660.5 4.3 fusion.25
  668.4 7.9 %fusion.29 = f32[4,16,64,512]{3,2,1,0:T(8,128)} fusion(bf16[4,16,64,1152]{3,2,1,0:T(8,128)(2,1)S(1)} %copy_dynamic-update-slice_fusion, bf16[1152,512,1,1]{1,0,3,2:T(8,128)(2,1)S(1)} %bitcast.27), kind=kOutput, calls=%fused_computation.127 | convolution fusion | flops 4831838208 | bytes 19005440 | tf_op jit(solution)/shard_map/dot_general | solution.py:66
  676.3 81.1 %reduce-scatter.8.cloned.1.call-done = f32[4,16,64,128]{3,2,1,0:T(8,128)} async-done(((f32[4,16,64,512]{3,2,1,0:T(8,128)}), f32[4,16,64,128]{3,2,1,0:T(8,128)}) %reduce-scatter.8.cloned.1.call-update) | async-done | bytes 2097168 | tf_op jit(solution)/shard_map/reduce_scatter | solution.py:69
  757.4 2.8 convert_element_type.28
  (140 shorter events, 33.9 us)
Async XLA Ops:
  6.5 279.7 %copy-start = (bf16[27,128,512]{2,1,0:T(8,128)(2,1)S(1)}, bf16[27,128,512]{2,1,0:T(8,128)(2,1)}, u32[]{:S(2)}) copy-start(bf16[27,128,512]{2,1,0:T(8,128)(2,1)} %param.9) | copy-start | bytes 10616836
  6.5 317.7 %reduce-scatter.4.cloned.1.call-start = ((), (), s32[]{:S(2)}) async-start(), calls=%async_computation.3 | async-start | bytes 2621440 | tf_op jit(solution)/shard_map/reduce_scatter | solution.py:69
  254.8 30.0 %copy-start.5 = (bf16[2,8,32,128]{3,2,1,0:T(8,128)(2,1)S(1)}, bf16[2,8,32,128]{3,2,1,0:T(8,128)(2,1)}, u32[]{:S(2)}) copy-start(bf16[2,8,32,128]{3,2,1,0:T(8,128)(2,1)} %param.7) | copy-start | bytes 393220
  256.7 12.5 %collective-permute-start = (bf16[6,1,32,128]{3,2,1,0:T(8,128)(2,1)S(1)}, bf16[6,1,32,128]{3,2,1,0:T(8,128)(2,1)S(1)}, u32[]{:S(2)}, u32[]{:S(2)}) collective-permute-start(bf16[6,1,32,128]{3,2,1,0:T(8,128)(2,1)S(1)} %get-tuple-element.28), channel_id=1, source_target_pairs={{0,16},{16,32},{32,48},{48,64},{64,80},{80,96},{96,112},{112,128},... | collective-permute-start | bytes 147464 | tf_op jit(solution)/shard_map/ppermute | solution.py:17
  267.3 6.6 collective-permute-start.1
  274.7 6.6 collective-permute-start.3
  276.0 5.4 collective-permute-start.2
  281.4 4.3 copy-start.3
  291.5 309.2 %copy-start.6 = (bf16[2,8,32,128]{3,2,1,0:T(8,128)(2,1)S(1)}, bf16[2,8,32,128]{3,2,1,0:T(8,128)(2,1)}, u32[]{:S(2)}) copy-start(bf16[2,8,32,128]{3,2,1,0:T(8,128)(2,1)} %param.8) | copy-start | bytes 393220
  291.6 347.8 %reduce-scatter.6.cloned.1.call-start = ((), (), s32[]{:S(2)}) async-start(), calls=%async_computation.4 | async-start | bytes 2621440 | tf_op jit(solution)/shard_map/reduce_scatter | solution.py:69
  574.3 12.4 %collective-permute-start.4 = (bf16[6,1,32,128]{3,2,1,0:T(8,128)(2,1)S(1)}, bf16[6,1,32,128]{3,2,1,0:T(8,128)(2,1)S(1)}, u32[]{:S(2)}, u32[]{:S(2)}) collective-permute-start(bf16[6,1,32,128]{3,2,1,0:T(8,128)(2,1)S(1)} %get-tuple-element.24), channel_id=1, source_target_pairs={{0,16},{16,32},{32,48},{48,64},{64,80},{80,96},{96,112},{112,128},... | collective-permute-start | bytes 147464 | tf_op jit(solution)/shard_map/ppermute | solution.py:17
  584.7 6.6 collective-permute-start.5
  592.2 6.8 collective-permute-start.7
  593.5 5.5 collective-permute-start.6
  598.9 3.4 copy-start.2
  600.4 2.5 copy-start.7
  602.9 36.5 %copy-start.4 = (bf16[4,8,32,128]{3,2,1,0:T(8,128)(2,1)S(1)}, bf16[4,8,32,128]{3,2,1,0:T(8,128)(2,1)}, u32[]{:S(2)}) copy-start(bf16[4,8,32,128]{3,2,1,0:T(8,128)(2,1)} %param.6) | copy-start | bytes 786436
  608.2 149.2 %reduce-scatter.8.cloned.1.call-start = ((), (), s32[]{:S(2)}) async-start(), calls=%async_computation.5 | async-start | bytes 10485760 | tf_op jit(solution)/shard_map/reduce_scatter | solution.py:69
  640.5 6.8 collective-permute-start.8
  645.4 6.4 collective-permute-start.9
  651.9 4.6 collective-permute-start.10
  655.0 4.5 collective-permute-start.11
  665.5 2.9 copy-start.8
  668.4 91.8 %copy-start.1 = (bf16[27,128,512]{2,1,0:T(8,128)(2,1)S(1)}, bf16[27,128,512]{2,1,0:T(8,128)(2,1)}, u32[]{:S(2)}) copy-start(bf16[27,128,512]{2,1,0:T(8,128)(2,1)} %param.9) | copy-start | bytes 10616836
Sparse Core Ops, SparseCore 0:
  291.7 32.5 reduce-scatter.3
  608.3 31.0 reduce-scatter.5
  676.4 80.9 reduce-scatter.7
where the time goes:
time: 770 us; the launch traced here: 767 us
  blocking collectives  490 us (64%)
  waiting for transfers between devices  162 us (21%)
  starting transfers between devices  47.5 us (6%)
  other arithmetic  21.4 us (3%)
  matrix products  18.5 us (2%)
  between operations  13.9 us (2%)
  local copies, waits for them, and re-layouts  13.4 us (2%)
    psum x2, blocking collectives, norm_act(): lax.psum(jnp.sum(deviation * deviation, axis=(0, 1, 2, 4)), ('ha', 'wa'))  251 us
    psum x2, blocking collectives, norm_act(): totals = lax.psum(jnp.sum(shaped, axis=(0, 1, 2, 4)), ('ha', 'wa'))  239 us
    reduce_scatter x3, waiting for transfers between devices, conv_block(): result = lax.psum_scatter(result, 'col', scatter_dimension=3, tiled=True)  145 us
    ppermute x6, starting transfers between devices, with_halo(): before = lax.ppermute(last, axis, up)  37.6 us
    dot_general x3, matrix products, conv_block(): jnp.dot(patches, flat, preferred_element_type=jnp.float32)  18.5 us
    ppermute x6, waiting for transfers between devices, with_halo(): after = lax.ppermute(leading, axis, down)  16.9 us
  transfers between devices with their start and end apart: 15, of which 7 were waited for; matrix products, arithmetic and copies ran while one was open for 0% of the time, Pallas kernels for 0%

commit v1 on v0

v1 whole, which is shorter than its diff:
```python
import functools

import jax
import jax.numpy as jnp
from jax import lax
from jax.experimental import pallas as pl
from jax.experimental.pallas import tpu as pltpu
from jax.sharding import PartitionSpec as P

F32 = jnp.float32
BF16 = jnp.bfloat16
CH = 128
GROUP = 16
ROWS = 8
COLS = 32
MIB = 1 << 20

VMEM = pl.BlockSpec(memory_space=pltpu.VMEM)
SMEM = pl.BlockSpec(memory_space=pltpu.SMEM)


def call(body, outs, scratch=(), flops=0, limit=24, name=None):
    def run(*args):
        nbytes = sum(a.size * a.dtype.itemsize for a in list(args) + list(outs))
        return pl.pallas_call(
            body,
            out_shape=list(outs),
            in_specs=[SMEM if a.dtype == jnp.int32 else VMEM for a in args],
            out_specs=[VMEM] * len(outs),
            scratch_shapes=list(scratch),
            compiler_params=pltpu.CompilerParams(vmem_limit_bytes=limit * MIB),
            cost_estimate=pl.CostEstimate(flops=flops, bytes_accessed=nbytes, transcendentals=0),
            name=name,
        )(*args)

    return run


def sds(shape, dtype=BF16):
    return jax.ShapeDtypeStruct(shape, dtype)


def group_sum(row):
    lane = lax.broadcasted_iota(jnp.int32, row.shape, 1)
    shift = 1
    while shift < GROUP:
        other = jnp.where((lane & shift) != 0, pltpu.roll(row, shift, 1), pltpu.roll(row, CH - shift, 1))
        row = row + other
        shift *= 2
    return row


def local_stats(flat):
    count = flat.shape[0] * GROUP
    mean = group_sum(jnp.sum(flat, axis=0, keepdims=True)) * (1.0 / count)
    dev = flat - mean
    m2 = group_sum(jnp.sum(dev * dev, axis=0, keepdims=True))
    return mean, m2


def combine(st_ref, count):
    devices = st_ref.shape[0]
    means = st_ref[:, 0, :]
    mean = jnp.sum(means, axis=0, keepdims=True) * (1.0 / devices)
    apart = means - mean
    m2 = jnp.sum(st_ref[:, 1, :] + count * (apart * apart), axis=0, keepdims=True)
    return mean, lax.rsqrt(m2 * (1.0 / (count * devices)) + 1e-6)


def spread_stats(stats):
    devices = lax.axis_size("ha") * lax.axis_size("wa")
    slots = jnp.broadcast_to(stats[None], (devices,) + stats.shape)
    return lax.all_to_all(slots, ("ha", "wa"), 0, 0, tiled=True)


def store_edges(ref_slices, top_ref, bot_ref, lef_ref, rig_ref):
    at = 0
    for ref in ref_slices:
        n = ref.shape[0]
        top_ref[at : at + n] = ref[:, 0]
        bot_ref[at : at + n] = ref[:, ROWS - 1]
        v = ref[...].astype(F32)
        pad = jnp.zeros((n, 8, CH), F32)
        lef_ref[at : at + n] = jnp.concatenate([v[:, :, 0, :], pad], axis=1).astype(BF16)
        rig_ref[at : at + n] = jnp.concatenate([v[:, :, COLS - 1, :], pad], axis=1).astype(BF16)
        at += n


def first_body(x_ref, c1_ref, c2_ref, st_ref, top_ref, bot_ref, lef_ref, rig_ref):
    mean, m2 = local_stats(x_ref[...].astype(F32).reshape(-1, CH))
    st_ref[0:1, :] = mean
    st_ref[1:2, :] = m2
    store_edges([c1_ref, x_ref, c2_ref], top_ref, bot_ref, lef_ref, rig_ref)


def corner_body(top_ref, bot_ref, lef_ref, rig_ref, lo_ref, ro_ref):
    row = lax.broadcasted_iota(jnp.int32, lef_ref.shape, 1)
    top = top_ref[...].astype(F32)
    bot = bot_ref[...].astype(F32)
    for src, dst, at in ((lef_ref, lo_ref, 0), (rig_ref, ro_ref, COLS - 1)):
        v = src[...].astype(F32)
        v = jnp.where(row == 8, top[:, at : at + 1, :], v)
        v = jnp.where(row == 9, bot[:, at : at + 1, :], v)
        dst[...] = v.astype(BF16)


def swap_borders(top, bot, lef, rig):
    nh, nw = lax.axis_size("ha"), lax.axis_size("wa")
    above = lax.ppermute(bot, "ha", [(i, i + 1) for i in range(nh - 1)])
    below = lax.ppermute(top, "ha", [(i + 1, i) for i in range(nh - 1)])
    n = top.shape[0]
    lo, ro = call(corner_body, [sds((n, 16, CH))] * 2, name="corners")(above, below, lef, rig)
    left = lax.ppermute(ro, "wa", [(i, i + 1) for i in range(nw - 1)])
    right = lax.ppermute(lo, "wa", [(i + 1, i) for i in range(nw - 1)])
    return above, below, left, right


def shifted(rows, left, right):
    n = rows.shape[0]
    flat = rows.reshape(n * COLS, CH)
    col = lax.broadcasted_iota(jnp.int32, rows.shape, 1)
    before = pltpu.roll(flat, 1, 0).reshape(rows.shape)
    after = pltpu.roll(flat, n * COLS - 1, 0).reshape(rows.shape)
    before = jnp.where(col == 0, left[:, None, :], before)
    after = jnp.where(col == COLS - 1, right[:, None, :], after)
    return before, after


def place(patch_ref, frame, rows, at, left, right, lanes):
    n = rows.shape[0]
    before, after = shifted(rows, left, right)
    for e, v in enumerate((before, rows, after)):
        patch_ref[frame, at * COLS : (at + n) * COLS, lanes[e] : lanes[e] + CH] = v.reshape(n * COLS, CH).astype(BF16)


def place_frame(patch_ref, frame, inner, top, bot, lef, rig, lanes):
    place(patch_ref, frame, inner, 1, lef[0:8], rig[0:8], lanes)
    place(patch_ref, frame, top[None], 0, lef[8:9], rig[8:9], lanes)
    place(patch_ref, frame, bot[None], ROWS + 1, lef[9:10], rig[9:10], lanes)


def conv_body(cache_at, act_at, flag_ref, st_ref, x_ref, c_ref, tc, bc, lc, rc, ta, ba, la, ra, w_ref, *rest):
    outs, patch_ref = rest[:4], rest[4]
    has = [flag_ref[i] > 0 for i in range(4)]
    col = flag_ref[4]
    mean, scale = combine(st_ref, x_ref.shape[0] * ROWS * COLS * GROUP)

    def act(v):
        u = (v - mean) * scale
        return u / (1.0 + jnp.exp(-u))

    lanes = (0, CH, 2 * CH)
    for s in range(2):
        place_frame(
            patch_ref,
            s,
            c_ref[s].astype(F32),
            tc[cache_at + s].astype(F32),
            bc[cache_at + s].astype(F32),
            lc[cache_at + s].astype(F32),
            rc[cache_at + s].astype(F32),
            lanes,
        )
    row = lax.broadcasted_iota(jnp.int32, (16, CH), 0)
    edge = jnp.where(row == 8, flag_ref[0], jnp.where(row == 9, flag_ref[1], 1))
    for s in range(4):
        side = []
        for ref, flag in ((la, flag_ref[2]), (ra, flag_ref[3])):
            side.append(jnp.where(edge * flag > 0, act(ref[act_at + s].astype(F32)), 0.0))
        place_frame(
            patch_ref,
            2 + s,
            act(x_ref[s].astype(F32)),
            jnp.where(has[0], act(ta[act_at + s].astype(F32)), 0.0),
            jnp.where(has[1], act(ba[act_at + s].astype(F32)), 0.0),
            side[0],
            side[1],
            lanes,
        )
    depth = 9 * CH
    size = ROWS * COLS
    for t in range(4):
        acc = None
        for a in range(3):
            lhs = jnp.concatenate([patch_ref[t + a, b * COLS : b * COLS + size, :] for b in range(3)], axis=1)
            part = jnp.dot(lhs, w_ref[a * depth : (a + 1) * depth, :], preferred_element_type=F32)
            acc = part if acc is None else acc + part
        for j in range(4):
            piece = acc[:, j * CH : (j + 1) * CH].astype(BF16)
            slot = (j - col) & 3
            for k in range(4):

                @pl.when(slot == k)
                def _():
                    outs[k][t * size : (t + 1) * size, :] = piece


def conv(flags, stats, x, cache, cache_halo, cache_at, act_halo, act_at, weight, name):
    n = x.shape[0] * ROWS * COLS
    body = functools.partial(conv_body, cache_at, act_at)
    run = call(
        body,
        [sds((n, CH))] * 4,
        scratch=[pltpu.VMEM((6, (ROWS + 2) * COLS, 3 * CH), BF16)],
        flops=2 * n * weight.shape[0] * weight.shape[1],
        limit=32,
        name=name,
    )
    return run(flags, stats, x, cache, *cache_halo, *act_halo, weight)


def to_peers(pieces):
    n = lax.axis_size("col")
    return [lax.ppermute(pieces[k - 1], "col", [(i, (i + k) % n) for i in range(n)]) for k in range(1, n)]


def hidden_body(p0, p1, p2, p3, h_ref, st_ref, top_ref, bot_ref, lef_ref, rig_ref):
    total = p0[...].astype(F32) + p1[...].astype(F32) + p2[...].astype(F32) + p3[...].astype(F32)
    h = total.astype(BF16)
    h_ref[...] = h.reshape(h_ref.shape)
    mean, m2 = local_stats(h.astype(F32))
    st_ref[0:1, :] = mean
    st_ref[1:2, :] = m2
    store_edges([h_ref], top_ref, bot_ref, lef_ref, rig_ref)


def resid_body(x_ref, p0, p1, p2, p3, h_ref, top_ref, bot_ref, lef_ref, rig_ref):
    total = p0[...].astype(F32) + p1[...].astype(F32) + p2[...].astype(F32) + p3[...].astype(F32)
    h_ref[...] = (x_ref[...].astype(F32) + total.reshape(x_ref.shape)).astype(BF16)
    store_edges([h_ref], top_ref, bot_ref, lef_ref, rig_ref)


ROW_TAPS = {(0, 0): (-1, 0), (0, 1): (1,), (1, 0): (-1,), (1, 1): (0, 1)}
COL_TAPS = {(0, 0): (-1,), (0, 1): (0, 1), (1, 0): (-1, 0), (1, 1): (1,)}


def split_body(col_ref, *refs):
    for src, dst in zip(refs[:4], refs[4:]):
        dst[...] = src[...]


def split_weight(weight, col):
    taps = weight.shape[0]
    specs = [
        pl.BlockSpec((taps, CH, CH), lambda i, s, k=k: (0, 0, lax.rem(s[0] + k, 4))) for k in range(4)
    ]
    whole = pl.BlockSpec((taps, CH, CH), lambda i, s: (0, 0, 0))
    return pl.pallas_call(
        split_body,
        out_shape=[sds((taps, CH, CH))] * 4,
        grid_spec=pltpu.PrefetchScalarGridSpec(
            num_scalar_prefetch=1, grid=(1,), in_specs=specs, out_specs=[whole] * 4
        ),
        name="split_weight",
    )(col.reshape(1), *([weight] * 4))


def fold_body(w0, w1, w2, w3, o_ref):
    for k, ref in enumerate((w0, w1, w2, w3)):
        taps = [ref[i].astype(F32) for i in range(9)]
        for q in range(2):
            for r in range(2):
                for s in range(2):
                    for p in range(2):
                        total = None
                        for b in ROW_TAPS[p, r]:
                            for e in COL_TAPS[q, s]:
                                tap = taps[(b + 1) * 3 + (e + 1)]
                                total = tap if total is None else total + tap
                        at = (s * 4 + k) * CH
                        o_ref[q, r, at : at + CH, p * CH : (p + 1) * CH] = total.astype(BF16)


def up_body(*refs):
    parts = [refs[5 * k : 5 * k + 5] for k in range(4)]
    w_ref, o_ref, patch_ref, mix_ref = refs[20:24]
    size = (ROWS + 1) * COLS
    half = 2 * 4 * CH
    for k, (x, top, bot, lef, rig) in enumerate(parts):
        place_frame(
            patch_ref,
            0,
            x[0].astype(F32),
            top[0].astype(F32),
            bot[0].astype(F32),
            lef[0].astype(F32),
            rig[0].astype(F32),
            [(e * 4 + k) * CH for e in range(3)],
        )
    for q in range(2):
        acc = None
        for r in range(2):
            lhs = patch_ref[0, r * COLS : r * COLS + size, q * 4 * CH : q * 4 * CH + half]
            part = jnp.dot(lhs, w_ref[q, r], preferred_element_type=F32)
            acc = part if acc is None else acc + part
        for n in range(ROWS + 1):
            for p in range(2):
                i = 2 * n - 1 + p
                if 0 <= i < 2 * ROWS:
                    mix_ref[i, pl.ds(q, COLS, stride=2), :] = acc[n * COLS : (n + 1) * COLS, p * CH : (p + 1) * CH]
    o_ref[0] = mix_ref[...].astype(BF16)


def up_conv(parts, weight):
    specs = []
    args = []
    for part in parts:
        for a in part:
            rest = a.shape[1:]
            specs.append(pl.BlockSpec((1,) + rest, lambda t, n=len(rest): (t,) + (0,) * n))
            args.append(a)
    specs.append(pl.BlockSpec(weight.shape, lambda t: (0, 0, 0, 0)))
    frames = parts[0][0].shape[0]
    out = (frames, 2 * ROWS, 2 * COLS, CH)
    return pl.pallas_call(
        up_body,
        out_shape=sds(out),
        grid=(frames,),
        in_specs=specs,
        out_specs=pl.BlockSpec((1,) + out[1:], lambda t: (t, 0, 0, 0)),
        scratch_shapes=[
            pltpu.VMEM((1, (ROWS + 2) * COLS, 12 * CH), BF16),
            pltpu.VMEM((2 * ROWS, 2 * COLS, CH), F32),
        ],
        compiler_params=pltpu.CompilerParams(vmem_limit_bytes=24 * MIB),
        name="up_conv",
    )(*args, weight)


def on_device(features, cache_first, cache_second, weight_first, weight_second, weight_up):
    frames = features.shape[0]
    n = frames * ROWS * COLS
    ha, wa, col = lax.axis_index("ha"), lax.axis_index("wa"), lax.axis_index("col")
    nh, nw = lax.axis_size("ha"), lax.axis_size("wa")
    flags = jnp.stack([ha > 0, ha < nh - 1, wa > 0, wa < nw - 1, col]).astype(jnp.int32)

    stats, *edges = call(
        first_body, [sds((2, CH), F32)] + [sds((8, COLS, CH))] * 2 + [sds((8, 16, CH))] * 2, name="first"
    )(features, cache_first, cache_second)
    w_pieces = split_weight(weight_up, col)
    w_got = to_peers(w_pieces[1:])
    halo = swap_borders(*edges)
    stats = spread_stats(stats)
    pieces = conv(
        flags, stats, features, cache_first, halo, 0, halo, 2, weight_first.reshape(-1, 4 * CH), "conv_first"
    )
    got = to_peers(pieces[1:])
    hidden, stats, *edges = call(
        hidden_body,
        [sds(features.shape), sds((2, CH), F32)] + [sds((frames, COLS, CH))] * 2 + [sds((frames, 16, CH))] * 2,
        name="hidden",
    )(pieces[0], *got)
    halo2 = swap_borders(*edges)
    stats = spread_stats(stats)
    (folded,) = call(fold_body, [sds((2, 2, 8 * CH, 2 * CH))], name="fold")(w_pieces[0], *w_got)
    pieces = conv(
        flags, stats, hidden, cache_second, halo, 6, halo2, 0, weight_second.reshape(-1, 4 * CH), "conv_second"
    )
    got = to_peers(pieces[1:])
    resid, *edges = call(
        resid_body,
        [sds(features.shape)] + [sds((frames, COLS, CH))] * 2 + [sds((frames, 16, CH))] * 2,
        name="resid",
    )(features, pieces[0], *got)
    others = to_peers([resid] * 3)
    above, below, left, right = swap_borders(*edges)
    border = jnp.concatenate([above, below, left, right], axis=1)
    borders = to_peers([border] * 3)
    parts = [(resid, above, below, left, right)]
    for x, b in zip(others, borders):
        parts.append(
            (x, b[:, :COLS], b[:, COLS : 2 * COLS], b[:, 2 * COLS : 2 * COLS + 16], b[:, 2 * COLS + 16 :])
        )
    parts = [(x, t.reshape(frames, COLS, CH), b, le, ri) for x, t, b, le, ri in parts]
    return up_conv(parts, folded)


def solution(mesh):
    placed = (
        P(None, "ha", "wa", "col"),
        P(None, "ha", "wa", "col"),
        P(None, "ha", "wa", "col"),
        P(None, "col", None),
        P(None, "col", None),
        P(None, "col", None),
    )
    return jax.shard_map(
        on_device, mesh=mesh, in_specs=placed, out_specs=P(None, "ha", "wa", "col"), check_vma=False
    )
```

time: 770 us -> 164 us (0.21)
  blocking collectives: 490 us -> 0 us
  waiting for transfers between devices: 162 us -> 57.6 us
  starting transfers between devices: 47.5 us -> 72.4 us
  other arithmetic: 21.4 us -> 0 us
  Pallas kernels: 0 us -> 21.3 us
  matrix products: 18.5 us -> 0 us
  between operations: 13.9 us -> 0.28 us
    psum x4 -> x0, blocking collectives: 490 us -> none  [the longest x2 251 us: norm_act(): lax.psum(jnp.sum(deviation * deviation, axis=(0, 1, 2, 4)), ('ha', 'wa'))]
    reduce_scatter x3 -> x0, waiting for transfers between devices: 145 us -> none  [conv_block(): result = lax.psum_scatter(result, 'col', scatter_dimension=3, tiled=True)]
    ppermute x12 -> x27, waiting for transfers between devices: 16.9 us -> 57.6 us  [the longest x15 38.7 us: to_peers(): lax.ppermute(pieces[k - 1], 'col', [(i, (i + k) % n) for i in range(n)])]
    pallas_call x0 -> x11, Pallas kernels: none -> 21.3 us  [the longest x9 14.8 us: run(): pl.pallas_call(body, out_shape=list(outs), in_specs=[SMEM if a.dtype == j...]
    all_to_all x0 -> x2, starting transfers between devices: none -> 19.9 us  [spread_stats(): return lax.all_to_all(slots, ('ha', 'wa'), 0, 0, tiled=True)]
    dot_general x3 -> x0, matrix products: 18.5 us -> none  [conv_block(): jnp.dot(patches, flat, preferred_element_type=jnp.float32)]
    ppermute x12 -> x27, starting transfers between devices: 47.4 us -> 52.4 us  [the longest x15 21.6 us: to_peers(): lax.ppermute(pieces[k - 1], 'col', [(i, (i + k) % n) for i in range(n)])]
  transfers between devices with their start and end apart: 15 -> 29, of which waited for: 7 -> 14; matrix products, arithmetic and copies ran while one was open for 0% -> 0% of each run, Pallas kernels for 0% -> 2%
where the time goes in v1:
time: 164 us; the launch traced here: 163 us
  starting transfers between devices  72.4 us (44%)
  waiting for transfers between devices  57.6 us (35%)
  Pallas kernels  21.3 us (13%)
  local copies, waits for them, and re-layouts  11 us (7%)
    ppermute x15, waiting for transfers between devices, to_peers(): lax.ppermute(pieces[k - 1], 'col', [(i, (i + k) % n) for i in range(n)])  38.7 us
    ppermute x15, starting transfers between devices, to_peers(): lax.ppermute(pieces[k - 1], 'col', [(i, (i + k) % n) for i in range(n)])  21.6 us
    all_to_all x2, starting transfers between devices, spread_stats(): return lax.all_to_all(slots, ('ha', 'wa'), 0, 0, tiled=True)  19.9 us
    pallas_call x9, Pallas kernels, run(): pl.pallas_call(body, out_shape=list(outs), in_specs=[SMEM if a.dtype == j...  14.8 us
    ppermute x3, starting transfers between devices, swap_borders(): above = lax.ppermute(bot, 'ha', [(i, i + 1) for i in range(nh - 1)])  11.9 us
    unnamed x23, local copies, waits for them, and re-layouts  9.6 us
    ppermute x3, waiting for transfers between devices, swap_borders(): right = lax.ppermute(lo, 'wa', [(i + 1, i) for i in range(nw - 1)])  9.56 us
    ppermute x3, waiting for transfers between devices, swap_borders(): below = lax.ppermute(top, 'ha', [(i + 1, i) for i in range(nh - 1)])  9.36 us
  transfers between devices with their start and end apart: 29, of which 14 were waited for; matrix products, arithmetic and copies ran while one was open for 0% of the time, Pallas kernels for 2%

profile of v1, /device:TPU:97, one launch (start us, length us, event | category | flops | bytes accessed | tf_op | source)
XLA Modules:
  0.0 162.6 jit_solution(1209666645954599495)
XLA Ops:
  4.3 11.2 %all-to-all-start = ((f32[64,2,128]{2,1,0:T(2,128)}), f32[64,2,128]{2,1,0:T(2,128)S(1)}, u32[]{:S(2)}, u32[]{:S(2)}) async-start(f32[64,2,128]{2,1,0:T(2,128)} %broadcast_in_dim.4), calls=%async_computation | async-start | bytes 131072 | tf_op jit(solution)/shard_map/all_to_all | solution.py:73
  15.5 4.6 %collective-permute-start = (bf16[8,32,128]{2,1,0:T(8,128)(2,1)S(1)}, bf16[8,32,128]{2,1,0:T(8,128)(2,1)S(1)}, u32[]{:S(2)}, u32[]{:S(2)}) collective-permute-start(bf16[8,32,128]{2,1,0:T(8,128)(2,1)S(1)} %get-tuple-element.40), channel_id=1, source_target_pairs={{0,16},{16,32},{32,48},{48,64},{64,80},{80,96},{96,112},{112,128},... | collective-permute-start | bytes 196616 | tf_op jit(solution)/shard_map/ppermute | solution.py:109
  22.0 4.9 %collective-permute-done.1.bot_ref.bc.ba = bf16[8,32,128]{2,1,0:T(8,128)(2,1)S(1)} collective-permute-done((bf16[8,32,128]{2,1,0:T(8,128)(2,1)S(1)}, bf16[8,32,128]{2,1,0:T(8,128)(2,1)S(1)}, u32[]{:S(2)}, u32[]{:S(2)}) %collective-permute-start.1) | collective-permute-done | bytes 65568 | tf_op jit(solution)/shard_map/ppermute | solution.py:110
  26.9 3.1 %collective-permute-start.2 = (bf16[8,16,128]{2,1,0:T(8,128)(2,1)S(1)}, bf16[8,16,128]{2,1,0:T(8,128)(2,1)S(1)}, u32[]{:S(2)}, u32[]{:S(2)}) collective-permute-start(bf16[8,16,128]{2,1,0:T(8,128)(2,1)S(1)} %get-tuple-element.44), channel_id=1, source_target_pairs={{0,4},{4,8},{8,12},{1,5},{5,9},{9,13},{2,6},{6,10},{10,14},{3,7},{... | collective-permute-start | bytes 98312 | tf_op jit(solution)/shard_map/ppermute | solution.py:113
  31.4 3.3 %collective-permute-done.3.rc.ra = bf16[8,16,128]{2,1,0:T(8,128)(2,1)S(1)} collective-permute-done((bf16[8,16,128]{2,1,0:T(8,128)(2,1)S(1)}, bf16[8,16,128]{2,1,0:T(8,128)(2,1)S(1)}, u32[]{:S(2)}, u32[]{:S(2)}) %collective-permute-start.3) | collective-permute-done | bytes 32800 | tf_op jit(solution)/shard_map/ppermute | solution.py:114
  38.5 6.0 %conv_first.1 = (bf16[1024,128]{1,0:T(8,128)(2,1)S(1)}, bf16[1024,128]{1,0:T(8,128)(2,1)S(1)}, bf16[1024,128]{1,0:T(8,128)(2,1)S(1)}, bf16[1024,128]{1,0:T(8,128)(2,1)S(1)}) custom-call(s32[5]{0:T(128)S(1)} %stack.39.flag_ref, f32[64,2,128]{2,1,0:T(2,128)S(1)} %all-to-all-done.st_ref, bf16[4,8,32,128]{3,2,1,0:T(8,128)(2,1)S(1)} %copy-done.1, ...), custom_call_target="tpu_custom_call" | custom-call | flops 3623878656 | bytes 5439508 | tf_op jit(solution)/shard_map/conv_first/pallas_call | solution.py:25
  49.4 3.8 %collective-permute-done.4.p1 = bf16[1024,128]{1,0:T(8,128)(2,1)S(1)} collective-permute-done((bf16[1024,128]{1,0:T(8,128)(2,1)S(1)}, bf16[1024,128]{1,0:T(8,128)(2,1)S(1)}, u32[]{:S(2)}, u32[]{:S(2)}) %collective-permute-start.4) | collective-permute-done | bytes 262176 | tf_op jit(solution)/shard_map/ppermute | solution.py:214
  53.2 5.5 %collective-permute-done.5.p2 = bf16[1024,128]{1,0:T(8,128)(2,1)S(1)} collective-permute-done((bf16[1024,128]{1,0:T(8,128)(2,1)S(1)}, bf16[1024,128]{1,0:T(8,128)(2,1)S(1)}, u32[]{:S(2)}, u32[]{:S(2)}) %collective-permute-start.5) | collective-permute-done | bytes 262176 | tf_op jit(solution)/shard_map/ppermute | solution.py:214
  60.4 8.7 %all-to-all-start.1 = ((f32[64,2,128]{2,1,0:T(2,128)}), f32[64,2,128]{2,1,0:T(2,128)S(1)}, u32[]{:S(2)}, u32[]{:S(2)}) async-start(f32[64,2,128]{2,1,0:T(2,128)} %broadcast_in_dim.5), calls=%async_computation.1 | async-start | bytes 131072 | tf_op jit(solution)/shard_map/all_to_all | solution.py:73
  69.1 4.6 %collective-permute-start.7 = (bf16[4,32,128]{2,1,0:T(8,128)(2,1)S(1)}, bf16[4,32,128]{2,1,0:T(8,128)(2,1)S(1)}, u32[]{:S(2)}, u32[]{:S(2)}) collective-permute-start(bf16[4,32,128]{2,1,0:T(8,128)(2,1)S(1)} %get-tuple-element.52), channel_id=1, source_target_pairs={{0,16},{16,32},{32,48},{48,64},{64,80},{80,96},{96,112},{112,128},... | collective-permute-start | bytes 98312 | tf_op jit(solution)/shard_map/ppermute | solution.py:109
  75.6 4.5 %collective-permute-done.8.bot_ref.ba = bf16[4,32,128]{2,1,0:T(8,128)(2,1)S(1)} collective-permute-done((bf16[4,32,128]{2,1,0:T(8,128)(2,1)S(1)}, bf16[4,32,128]{2,1,0:T(8,128)(2,1)S(1)}, u32[]{:S(2)}, u32[]{:S(2)}) %collective-permute-start.8) | collective-permute-done | bytes 32800 | tf_op jit(solution)/shard_map/ppermute | solution.py:110
  80.2 3.1 %collective-permute-start.9 = (bf16[4,16,128]{2,1,0:T(8,128)(2,1)S(1)}, bf16[4,16,128]{2,1,0:T(8,128)(2,1)S(1)}, u32[]{:S(2)}, u32[]{:S(2)}) collective-permute-start(bf16[4,16,128]{2,1,0:T(8,128)(2,1)S(1)} %get-tuple-element.56), channel_id=1, source_target_pairs={{0,4},{4,8},{8,12},{1,5},{5,9},{9,13},{2,6},{6,10},{10,14},{3,7},{... | collective-permute-start | bytes 49160 | tf_op jit(solution)/shard_map/ppermute | solution.py:113
  84.6 3.2 %collective-permute-done.10.ra = bf16[4,16,128]{2,1,0:T(8,128)(2,1)S(1)} collective-permute-done((bf16[4,16,128]{2,1,0:T(8,128)(2,1)S(1)}, bf16[4,16,128]{2,1,0:T(8,128)(2,1)S(1)}, u32[]{:S(2)}, u32[]{:S(2)}) %collective-permute-start.10) | collective-permute-done | bytes 16416 | tf_op jit(solution)/shard_map/ppermute | solution.py:114
  89.8 6.1 %conv_second.1 = (bf16[1024,128]{1,0:T(8,128)(2,1)S(1)}, bf16[1024,128]{1,0:T(8,128)(2,1)S(1)}, bf16[1024,128]{1,0:T(8,128)(2,1)S(1)}, bf16[1024,128]{1,0:T(8,128)(2,1)S(1)}) custom-call(s32[5]{0:T(128)S(1)} %stack.39.flag_ref, f32[64,2,128]{2,1,0:T(2,128)S(1)} %all-to-all-done.1.st_ref, bf16[4,8,32,128]{3,2,1,0:T(8,128)(2,1)S(1)} %get-tuple-element.51.x_ref, ...), custom_call_target="tpu_custom_call" | custom-call | flops 3623878656 | bytes 5341204 | tf_op jit(solution)/shard_map/conv_second/pallas_call | solution.py:25
  100.4 4.7 %collective-permute-done.11.p1 = bf16[1024,128]{1,0:T(8,128)(2,1)S(1)} collective-permute-done((bf16[1024,128]{1,0:T(8,128)(2,1)S(1)}, bf16[1024,128]{1,0:T(8,128)(2,1)S(1)}, u32[]{:S(2)}, u32[]{:S(2)}) %collective-permute-start.11) | collective-permute-done | bytes 262176 | tf_op jit(solution)/shard_map/ppermute | solution.py:214
  105.1 4.8 %collective-permute-done.12.p2 = bf16[1024,128]{1,0:T(8,128)(2,1)S(1)} collective-permute-done((bf16[1024,128]{1,0:T(8,128)(2,1)S(1)}, bf16[1024,128]{1,0:T(8,128)(2,1)S(1)}, u32[]{:S(2)}, u32[]{:S(2)}) %collective-permute-start.12) | collective-permute-done | bytes 262176 | tf_op jit(solution)/shard_map/ppermute | solution.py:214
  110.6 2.7 %collective-permute-start.14 = (bf16[4,32,128]{2,1,0:T(8,128)(2,1)S(1)}, bf16[4,32,128]{2,1,0:T(8,128)(2,1)S(1)}, u32[]{:S(2)}, u32[]{:S(2)}) collective-permute-start(bf16[4,32,128]{2,1,0:T(8,128)(2,1)S(1)} %get-tuple-element.63), channel_id=1, source_target_pairs={{0,16},{16,32},{32,48},{48,64},{64,80},{80,96},{96,112},{112,128},... | collective-permute-start | bytes 98312 | tf_op jit(solution)/shard_map/ppermute | solution.py:109
  122.1 3.1 %collective-permute-start.16 = (bf16[4,16,128]{2,1,0:T(8,128)(2,1)S(1)}, bf16[4,16,128]{2,1,0:T(8,128)(2,1)S(1)}, u32[]{:S(2)}, u32[]{:S(2)}) collective-permute-start(bf16[4,16,128]{2,1,0:T(8,128)(2,1)S(1)} %get-tuple-element.67), channel_id=1, source_target_pairs={{0,4},{4,8},{8,12},{1,5},{5,9},{9,13},{2,6},{6,10},{10,14},{3,7},{... | collective-permute-start | bytes 49160 | tf_op jit(solution)/shard_map/ppermute | solution.py:113
  126.5 3.1 %collective-permute-done.17.refs_4_ = bf16[4,16,128]{2,1,0:T(8,128)(2,1)S(1)} collective-permute-done((bf16[4,16,128]{2,1,0:T(8,128)(2,1)S(1)}, bf16[4,16,128]{2,1,0:T(8,128)(2,1)S(1)}, u32[]{:S(2)}, u32[]{:S(2)}) %collective-permute-start.17) | collective-permute-done | bytes 16416 | tf_op jit(solution)/shard_map/ppermute | solution.py:114
  130.3 2.9 %collective-permute-done.25.w2 = bf16[9,128,128]{2,1,0:T(8,128)(2,1)S(1)} collective-permute-done((bf16[9,128,128]{2,1,0:T(8,128)(2,1)}, bf16[9,128,128]{2,1,0:T(8,128)(2,1)S(1)}, u32[]{:S(2)}, u32[]{:S(2)}) %collective-permute-start.25) | collective-permute-done | bytes 294944 | tf_op jit(solution)/shard_map/ppermute | solution.py:214
  135.4 3.4 %collective-permute-start.22 = (bf16[4,8,32,128]{3,2,1,0:T(8,128)(2,1)S(1)}, bf16[4,8,32,128]{3,2,1,0:T(8,128)(2,1)S(1)}, u32[]{:S(2)}, u32[]{:S(2)}) collective-permute-start(bf16[4,8,32,128]{3,2,1,0:T(8,128)(2,1)S(1)} %get-tuple-element.62.refs_0_), channel_id=1, source_target_pairs={{0,3},{1,0},{2,1},{3,2},{4,7},{5,4},{6,5},{7,6},{8,11},{9,8},{10,9... | collective-permute-start | bytes 786440 | tf_op jit(solution)/shard_map/ppermute | solution.py:214
  142.5 12.2 %collective-permute-done.21 = bf16[4,96,128]{2,1,0:T(8,128)(2,1)S(1)} collective-permute-done((bf16[4,96,128]{2,1,0:T(8,128)(2,1)S(1)}, bf16[4,96,128]{2,1,0:T(8,128)(2,1)S(1)}, u32[]{:S(2)}, u32[]{:S(2)}) %collective-permute-start.21) | collective-permute-done | bytes 98336 | tf_op jit(solution)/shard_map/ppermute | solution.py:214
  154.7 3.6 %collective-permute-done.19 = bf16[4,96,128]{2,1,0:T(8,128)(2,1)S(1)} collective-permute-done((bf16[4,96,128]{2,1,0:T(8,128)(2,1)S(1)}, bf16[4,96,128]{2,1,0:T(8,128)(2,1)S(1)}, u32[]{:S(2)}, u32[]{:S(2)}) %collective-permute-start.19) | collective-permute-done | bytes 98336 | tf_op jit(solution)/shard_map/ppermute | solution.py:214
  158.4 4.2 %up_conv.1 = bf16[4,16,64,128]{3,2,1,0:T(8,128)(2,1)} custom-call(bf16[4,8,32,128]{3,2,1,0:T(8,128)(2,1)S(1)} %get-tuple-element.62.refs_0_, bf16[4,32,128]{2,1,0:T(8,128)(2,1)S(1)} %collective-permute-done.14.top_ref.refs_1_, bf16[4,32,128]{2,1,0:T(8,128)(2,1)S(1)} %collective-permute-done.15.bot_ref.refs_2_, ...), custom_call_target="tpu_custom_call" | custom-call | tf_op jit(solution)/shard_map/up_conv/pallas_call | solution.py:315
  (78 shorter events, 45.0 us)
Async XLA Ops:
  4.3 30.4 %all-to-all-start = ((f32[64,2,128]{2,1,0:T(2,128)}), f32[64,2,128]{2,1,0:T(2,128)S(1)}, u32[]{:S(2)}, u32[]{:S(2)}) async-start(f32[64,2,128]{2,1,0:T(2,128)} %broadcast_in_dim.4), calls=%async_computation | async-start | bytes 131072 | tf_op jit(solution)/shard_map/all_to_all | solution.py:73
  15.5 6.5 %collective-permute-start = (bf16[8,32,128]{2,1,0:T(8,128)(2,1)S(1)}, bf16[8,32,128]{2,1,0:T(8,128)(2,1)S(1)}, u32[]{:S(2)}, u32[]{:S(2)}) collective-permute-start(bf16[8,32,128]{2,1,0:T(8,128)(2,1)S(1)} %get-tuple-element.40), channel_id=1, source_target_pairs={{0,16},{16,32},{32,48},{48,64},{64,80},{80,96},{96,112},{112,128},... | collective-permute-start | bytes 196616 | tf_op jit(solution)/shard_map/ppermute | solution.py:109
  20.1 6.8 %collective-permute-start.1 = (bf16[8,32,128]{2,1,0:T(8,128)(2,1)S(1)}, bf16[8,32,128]{2,1,0:T(8,128)(2,1)S(1)}, u32[]{:S(2)}, u32[]{:S(2)}) collective-permute-start(bf16[8,32,128]{2,1,0:T(8,128)(2,1)S(1)} %get-tuple-element.41), channel_id=1, source_target_pairs={{16,0},{32,16},{48,32},{64,48},{80,64},{96,80},{112,96},{128,112},... | collective-permute-start | bytes 196616 | tf_op jit(solution)/shard_map/ppermute | solution.py:110
  30.0 4.7 %collective-permute-start.3 = (bf16[8,16,128]{2,1,0:T(8,128)(2,1)S(1)}, bf16[8,16,128]{2,1,0:T(8,128)(2,1)S(1)}, u32[]{:S(2)}, u32[]{:S(2)}) collective-permute-start(bf16[8,16,128]{2,1,0:T(8,128)(2,1)S(1)} %get-tuple-element.45), channel_id=1, source_target_pairs={{4,0},{8,4},{12,8},{5,1},{9,5},{13,9},{6,2},{10,6},{14,10},{7,3},{... | collective-permute-start | bytes 98312 | tf_op jit(solution)/shard_map/ppermute | solution.py:114
  44.5 8.7 %collective-permute-start.4 = (bf16[1024,128]{1,0:T(8,128)(2,1)S(1)}, bf16[1024,128]{1,0:T(8,128)(2,1)S(1)}, u32[]{:S(2)}, u32[]{:S(2)}) collective-permute-start(bf16[1024,128]{1,0:T(8,128)(2,1)S(1)} %get-tuple-element.47), channel_id=1, source_target_pairs={{0,1},{1,2},{2,3},{3,0},{4,5},{5,6},{6,7},{7,4},{8,9},{9,10},{10,1... | collective-permute-start | bytes 786440 | tf_op jit(solution)/shard_map/ppermute | solution.py:214
  45.8 12.9 %collective-permute-start.5 = (bf16[1024,128]{1,0:T(8,128)(2,1)S(1)}, bf16[1024,128]{1,0:T(8,128)(2,1)S(1)}, u32[]{:S(2)}, u32[]{:S(2)}) collective-permute-start(bf16[1024,128]{1,0:T(8,128)(2,1)S(1)} %get-tuple-element.48), channel_id=1, source_target_pairs={{0,2},{1,3},{2,0},{3,1},{4,6},{5,7},{6,4},{7,5},{8,10},{9,11},{10,... | collective-permute-start | bytes 786440 | tf_op jit(solution)/shard_map/ppermute | solution.py:214
  48.2 10.5 %collective-permute-start.6 = (bf16[1024,128]{1,0:T(8,128)(2,1)S(1)}, bf16[1024,128]{1,0:T(8,128)(2,1)S(1)}, u32[]{:S(2)}, u32[]{:S(2)}) collective-permute-start(bf16[1024,128]{1,0:T(8,128)(2,1)S(1)} %get-tuple-element.49), channel_id=1, source_target_pairs={{0,3},{1,0},{2,1},{3,2},{4,7},{5,4},{6,5},{7,6},{8,11},{9,8},{10,9... | collective-permute-start | bytes 786440 | tf_op jit(solution)/shard_map/ppermute | solution.py:214
  60.4 27.4 %all-to-all-start.1 = ((f32[64,2,128]{2,1,0:T(2,128)}), f32[64,2,128]{2,1,0:T(2,128)S(1)}, u32[]{:S(2)}, u32[]{:S(2)}) async-start(f32[64,2,128]{2,1,0:T(2,128)} %broadcast_in_dim.5), calls=%async_computation.1 | async-start | bytes 131072 | tf_op jit(solution)/shard_map/all_to_all | solution.py:73
  69.1 6.5 %collective-permute-start.7 = (bf16[4,32,128]{2,1,0:T(8,128)(2,1)S(1)}, bf16[4,32,128]{2,1,0:T(8,128)(2,1)S(1)}, u32[]{:S(2)}, u32[]{:S(2)}) collective-permute-start(bf16[4,32,128]{2,1,0:T(8,128)(2,1)S(1)} %get-tuple-element.52), channel_id=1, source_target_pairs={{0,16},{16,32},{32,48},{48,64},{64,80},{80,96},{96,112},{112,128},... | collective-permute-start | bytes 98312 | tf_op jit(solution)/shard_map/ppermute | solution.py:109
  73.7 6.4 %collective-permute-start.8 = (bf16[4,32,128]{2,1,0:T(8,128)(2,1)S(1)}, bf16[4,32,128]{2,1,0:T(8,128)(2,1)S(1)}, u32[]{:S(2)}, u32[]{:S(2)}) collective-permute-start(bf16[4,32,128]{2,1,0:T(8,128)(2,1)S(1)} %get-tuple-element.53), channel_id=1, source_target_pairs={{16,0},{32,16},{48,32},{64,48},{80,64},{96,80},{112,96},{128,112},... | collective-permute-start | bytes 98312 | tf_op jit(solution)/shard_map/ppermute | solution.py:110
  95.9 9.2 %collective-permute-start.11 = (bf16[1024,128]{1,0:T(8,128)(2,1)S(1)}, bf16[1024,128]{1,0:T(8,128)(2,1)S(1)}, u32[]{:S(2)}, u32[]{:S(2)}) collective-permute-start(bf16[1024,128]{1,0:T(8,128)(2,1)S(1)} %get-tuple-element.59), channel_id=1, source_target_pairs={{0,1},{1,2},{2,3},{3,0},{4,5},{5,6},{6,7},{7,4},{8,9},{9,10},{10,1... | collective-permute-start | bytes 786440 | tf_op jit(solution)/shard_map/ppermute | solution.py:214
  97.0 12.9 %collective-permute-start.12 = (bf16[1024,128]{1,0:T(8,128)(2,1)S(1)}, bf16[1024,128]{1,0:T(8,128)(2,1)S(1)}, u32[]{:S(2)}, u32[]{:S(2)}) collective-permute-start(bf16[1024,128]{1,0:T(8,128)(2,1)S(1)} %get-tuple-element.60), channel_id=1, source_target_pairs={{0,2},{1,3},{2,0},{3,1},{4,6},{5,7},{6,4},{7,5},{8,10},{9,11},{10,... | collective-permute-start | bytes 786440 | tf_op jit(solution)/shard_map/ppermute | solution.py:214
  99.2 11.2 %collective-permute-start.13 = (bf16[1024,128]{1,0:T(8,128)(2,1)S(1)}, bf16[1024,128]{1,0:T(8,128)(2,1)S(1)}, u32[]{:S(2)}, u32[]{:S(2)}) collective-permute-start(bf16[1024,128]{1,0:T(8,128)(2,1)S(1)} %get-tuple-element.61), channel_id=1, source_target_pairs={{0,3},{1,0},{2,1},{3,2},{4,7},{5,4},{6,5},{7,6},{8,11},{9,8},{10,9... | collective-permute-start | bytes 786440 | tf_op jit(solution)/shard_map/ppermute | solution.py:214
  110.6 11.4 %collective-permute-start.14 = (bf16[4,32,128]{2,1,0:T(8,128)(2,1)S(1)}, bf16[4,32,128]{2,1,0:T(8,128)(2,1)S(1)}, u32[]{:S(2)}, u32[]{:S(2)}) collective-permute-start(bf16[4,32,128]{2,1,0:T(8,128)(2,1)S(1)} %get-tuple-element.63), channel_id=1, source_target_pairs={{0,16},{16,32},{32,48},{48,64},{64,80},{80,96},{96,112},{112,128},... | collective-permute-start | bytes 98312 | tf_op jit(solution)/shard_map/ppermute | solution.py:109
  113.4 8.7 %collective-permute-start.15 = (bf16[4,32,128]{2,1,0:T(8,128)(2,1)S(1)}, bf16[4,32,128]{2,1,0:T(8,128)(2,1)S(1)}, u32[]{:S(2)}, u32[]{:S(2)}) collective-permute-start(bf16[4,32,128]{2,1,0:T(8,128)(2,1)S(1)} %get-tuple-element.64), channel_id=1, source_target_pairs={{16,0},{32,16},{48,32},{64,48},{80,64},{96,80},{112,96},{128,112},... | collective-permute-start | bytes 98312 | tf_op jit(solution)/shard_map/ppermute | solution.py:110
  117.6 12.7 %collective-permute-start.24 = (bf16[9,128,128]{2,1,0:T(8,128)(2,1)}, bf16[9,128,128]{2,1,0:T(8,128)(2,1)S(1)}, u32[]{:S(2)}, u32[]{:S(2)}) collective-permute-start(bf16[9,128,128]{2,1,0:T(8,128)(2,1)} %get-tuple-element.70), channel_id=1, source_target_pairs={{0,1},{1,2},{2,3},{3,0},{4,5},{5,6},{6,7},{7,4},{8,9},{9,10},{10,1... | collective-permute-start | bytes 884744 | tf_op jit(solution)/shard_map/ppermute | solution.py:214
  119.1 14.1 %collective-permute-start.25 = (bf16[9,128,128]{2,1,0:T(8,128)(2,1)}, bf16[9,128,128]{2,1,0:T(8,128)(2,1)S(1)}, u32[]{:S(2)}, u32[]{:S(2)}) collective-permute-start(bf16[9,128,128]{2,1,0:T(8,128)(2,1)} %get-tuple-element.71), channel_id=1, source_target_pairs={{0,2},{1,3},{2,0},{3,1},{4,6},{5,7},{6,4},{7,5},{8,10},{9,11},{10,... | collective-permute-start | bytes 884744 | tf_op jit(solution)/shard_map/ppermute | solution.py:214
  121.2 12.8 %collective-permute-start.26 = (bf16[9,128,128]{2,1,0:T(8,128)(2,1)}, bf16[9,128,128]{2,1,0:T(8,128)(2,1)S(1)}, u32[]{:S(2)}, u32[]{:S(2)}) collective-permute-start(bf16[9,128,128]{2,1,0:T(8,128)(2,1)} %get-tuple-element.72), channel_id=1, source_target_pairs={{0,3},{1,0},{2,1},{3,2},{4,7},{5,4},{6,5},{7,6},{8,11},{9,8},{10,9... | collective-permute-start | bytes 884744 | tf_op jit(solution)/shard_map/ppermute | solution.py:214
  129.7 12.1 %collective-permute-start.23 = (bf16[4,96,128]{2,1,0:T(8,128)(2,1)S(1)}, bf16[4,96,128]{2,1,0:T(8,128)(2,1)S(1)}, u32[]{:S(2)}, u32[]{:S(2)}) collective-permute-start(bf16[4,96,128]{2,1,0:T(8,128)(2,1)S(1)} %constant_dynamic-update-slice_fusion), channel_id=1, source_target_pairs={{0,3},{1,0},{2,1},{3,2},{4,7},{5,4},{6,5},{7,6},{8,11},{9,8},{10,9... | collective-permute-start | bytes 294920 | tf_op jit(solution)/shard_map/ppermute | solution.py:214
  135.4 23.0 %collective-permute-start.22 = (bf16[4,8,32,128]{3,2,1,0:T(8,128)(2,1)S(1)}, bf16[4,8,32,128]{3,2,1,0:T(8,128)(2,1)S(1)}, u32[]{:S(2)}, u32[]{:S(2)}) collective-permute-start(bf16[4,8,32,128]{3,2,1,0:T(8,128)(2,1)S(1)} %get-tuple-element.62.refs_0_), channel_id=1, source_target_pairs={{0,3},{1,0},{2,1},{3,2},{4,7},{5,4},{6,5},{7,6},{8,11},{9,8},{10,9... | collective-permute-start | bytes 786440 | tf_op jit(solution)/shard_map/ppermute | solution.py:214
  138.8 19.6 %collective-permute-start.20 = (bf16[4,8,32,128]{3,2,1,0:T(8,128)(2,1)S(1)}, bf16[4,8,32,128]{3,2,1,0:T(8,128)(2,1)S(1)}, u32[]{:S(2)}, u32[]{:S(2)}) collective-permute-start(bf16[4,8,32,128]{3,2,1,0:T(8,128)(2,1)S(1)} %get-tuple-element.62.refs_0_), channel_id=1, source_target_pairs={{0,2},{1,3},{2,0},{3,1},{4,6},{5,7},{6,4},{7,5},{8,10},{9,11},{10,... | collective-permute-start | bytes 786440 | tf_op jit(solution)/shard_map/ppermute | solution.py:214
  139.2 19.1 %collective-permute-start.18 = (bf16[4,8,32,128]{3,2,1,0:T(8,128)(2,1)S(1)}, bf16[4,8,32,128]{3,2,1,0:T(8,128)(2,1)S(1)}, u32[]{:S(2)}, u32[]{:S(2)}) collective-permute-start(bf16[4,8,32,128]{3,2,1,0:T(8,128)(2,1)S(1)} %get-tuple-element.62.refs_0_), channel_id=1, source_target_pairs={{0,1},{1,2},{2,3},{3,0},{4,5},{5,6},{6,7},{7,4},{8,9},{9,10},{10,1... | collective-permute-start | bytes 786440 | tf_op jit(solution)/shard_map/ppermute | solution.py:214
  139.5 15.3 %collective-permute-start.21 = (bf16[4,96,128]{2,1,0:T(8,128)(2,1)S(1)}, bf16[4,96,128]{2,1,0:T(8,128)(2,1)S(1)}, u32[]{:S(2)}, u32[]{:S(2)}) collective-permute-start(bf16[4,96,128]{2,1,0:T(8,128)(2,1)S(1)} %constant_dynamic-update-slice_fusion), channel_id=1, source_target_pairs={{0,2},{1,3},{2,0},{3,1},{4,6},{5,7},{6,4},{7,5},{8,10},{9,11},{10,... | collective-permute-start | bytes 294920 | tf_op jit(solution)/shard_map/ppermute | solution.py:214
  141.8 16.6 %collective-permute-start.19 = (bf16[4,96,128]{2,1,0:T(8,128)(2,1)S(1)}, bf16[4,96,128]{2,1,0:T(8,128)(2,1)S(1)}, u32[]{:S(2)}, u32[]{:S(2)}) collective-permute-start(bf16[4,96,128]{2,1,0:T(8,128)(2,1)S(1)} %constant_dynamic-update-slice_fusion), channel_id=1, source_target_pairs={{0,1},{1,2},{2,3},{3,0},{4,5},{5,6},{6,7},{7,4},{8,9},{9,10},{10,1... | collective-permute-start | bytes 294920 | tf_op jit(solution)/shard_map/ppermute | solution.py:214
  (15 other events, 101.7 us)

commit v2 on v1

v2 whole, which is shorter than its diff:
```python
import functools

import jax
import jax.numpy as jnp
from jax import lax
from jax.experimental import pallas as pl
from jax.experimental.pallas import tpu as pltpu
from jax.sharding import PartitionSpec as P

F32 = jnp.float32
BF16 = jnp.bfloat16
CH = 128
GROUP = 16
ROWS = 8
COLS = 32
MIB = 1 << 20

VMEM = pl.BlockSpec(memory_space=pltpu.VMEM)
SMEM = pl.BlockSpec(memory_space=pltpu.SMEM)
ANY = pl.BlockSpec(memory_space=pl.ANY)
HBM = pl.BlockSpec(memory_space=pltpu.HBM)
HA = ("z", "core")


class Left:
    def __init__(self, array, spec=ANY):
        self.array, self.spec = array, spec
        if spec is HBM:
            self.array = pltpu.with_memory_space_constraint(array, pltpu.HBM)


def call(body, outs, scratch=(), flops=0, limit=8, name=None):
    def run(*args):
        specs = [a.spec if isinstance(a, Left) else SMEM if a.dtype == jnp.int32 else VMEM for a in args]
        args = [a.array if isinstance(a, Left) else a for a in args]
        nbytes = sum(a.size * a.dtype.itemsize for a in args + list(outs))
        return pl.pallas_call(
            body,
            out_shape=list(outs),
            in_specs=specs,
            out_specs=[VMEM] * len(outs),
            scratch_shapes=list(scratch),
            compiler_params=pltpu.CompilerParams(vmem_limit_bytes=limit * MIB),
            cost_estimate=pl.CostEstimate(flops=flops, bytes_accessed=nbytes, transcendentals=0),
            name=name,
        )(*args)

    return run


def sds(shape, dtype=BF16):
    return jax.ShapeDtypeStruct(shape, dtype)


def group_sum(row):
    lane = lax.broadcasted_iota(jnp.int32, row.shape, 1)
    shift = 1
    while shift < GROUP:
        other = jnp.where((lane & shift) != 0, pltpu.roll(row, shift, 1), pltpu.roll(row, CH - shift, 1))
        row = row + other
        shift *= 2
    return row


def local_stats(flat):
    count = flat.shape[0] * GROUP
    mean = group_sum(jnp.sum(flat, axis=0, keepdims=True)) * (1.0 / count)
    dev = flat - mean
    m2 = group_sum(jnp.sum(dev * dev, axis=0, keepdims=True))
    return mean, m2


def combine(st_ref, count):
    devices = st_ref.shape[0]
    means = st_ref[:, 0, :]
    mean = jnp.sum(means, axis=0, keepdims=True) * (1.0 / devices)
    apart = means - mean
    m2 = jnp.sum(st_ref[:, 1, :] + count * (apart * apart), axis=0, keepdims=True)
    return mean, lax.rsqrt(m2 * (1.0 / (count * devices)) + 1e-6)


def slot_body(st_ref, *rest):
    o_ref = rest[-1]
    o_ref[...] = jnp.broadcast_to(st_ref[...][None], o_ref.shape)


def spread_stats(stats, after):
    pair = lax.all_gather(stats, "core")
    chips = lax.axis_size("z") * lax.axis_size("wa")
    pair = pair.reshape(2 * pair.shape[0], CH)
    (slots,) = call(slot_body, [sds((chips,) + pair.shape, F32)], name="slots")(pair, *[Left(a) for a in after])
    return lax.all_to_all(slots, ("z", "wa"), 0, 0, tiled=True).reshape(-1, 2, CH)


def store_edges(ref_slices, top_ref, bot_ref, lef_ref, rig_ref):
    at = 0
    for ref in ref_slices:
        n = ref.shape[0]
        top_ref[at : at + n] = ref[:, 0]
        bot_ref[at : at + n] = ref[:, ROWS - 1]
        v = ref[...].astype(F32)
        pad = jnp.zeros((n, 8, CH), F32)
        lef_ref[at : at + n] = jnp.concatenate([v[:, :, 0, :], pad], axis=1).astype(BF16)
        rig_ref[at : at + n] = jnp.concatenate([v[:, :, COLS - 1, :], pad], axis=1).astype(BF16)
        at += n


def first_body(x_hbm, c1_hbm, c2_hbm, x_ref, c1_ref, c2_ref, st_ref, top_ref, bot_ref, lef_ref, rig_ref, sem):
    copies = [
        pltpu.make_async_copy(src, dst, sem.at[i])
        for i, (src, dst) in enumerate(((x_hbm, x_ref), (c1_hbm, c1_ref), (c2_hbm, c2_ref)))
    ]
    for c in copies:
        c.start()
    for c in copies:
        c.wait()
    mean, m2 = local_stats(x_ref[...].astype(F32).reshape(-1, CH))
    st_ref[0:1, :] = mean
    st_ref[1:2, :] = m2
    store_edges([c1_ref, x_ref, c2_ref], top_ref, bot_ref, lef_ref, rig_ref)


def corner_body(top_ref, bot_ref, lef_ref, rig_ref, *rest):
    lo_ref, ro_ref = rest[-2:]
    row = lax.broadcasted_iota(jnp.int32, lef_ref.shape, 1)
    top = top_ref[...].astype(F32)
    bot = bot_ref[...].astype(F32)
    for src, dst, at in ((lef_ref, lo_ref, 0), (rig_ref, ro_ref, COLS - 1)):
        v = src[...].astype(F32)
        v = jnp.where(row == 8, top[:, at : at + 1, :], v)
        v = jnp.where(row == 9, bot[:, at : at + 1, :], v)
        dst[...] = v.astype(BF16)


def swap_rows(top, bot):
    n = lax.axis_size(HA)
    above = lax.ppermute(bot, HA, [(i, i + 1) for i in range(n - 1)])
    below = lax.ppermute(top, HA, [(i + 1, i) for i in range(n - 1)])
    return above, below


def swap_columns(above, below, lef, rig, after=()):
    n = lax.axis_size("wa")
    lo, ro = call(corner_body, [sds(lef.shape)] * 2, name="corners")(
        above, below, lef, rig, *[Left(a) for a in after]
    )
    left = lax.ppermute(ro, "wa", [(i, i + 1) for i in range(n - 1)])
    right = lax.ppermute(lo, "wa", [(i + 1, i) for i in range(n - 1)])
    return (left, right), lo


def shifted(rows, left, right):
    n = rows.shape[0]
    flat = rows.reshape(n * COLS, CH)
    col = lax.broadcasted_iota(jnp.int32, rows.shape, 1)
    before = pltpu.roll(flat, 1, 0).reshape(rows.shape)
    after = pltpu.roll(flat, n * COLS - 1, 0).reshape(rows.shape)
    before = jnp.where(col == 0, left[:, None, :], before)
    after = jnp.where(col == COLS - 1, right[:, None, :], after)
    return before, after


def place(patch_ref, frame, rows, at, left, right, lanes):
    n = rows.shape[0]
    before, after = shifted(rows, left, right)
    for e, v in enumerate((before, rows, after)):
        patch_ref[frame, at * COLS : (at + n) * COLS, lanes[e] : lanes[e] + CH] = v.reshape(n * COLS, CH).astype(BF16)


def place_frame(patch_ref, frame, inner, top, bot, lef, rig, lanes):
    place(patch_ref, frame, inner, 1, lef[0:8], rig[0:8], lanes)
    place(patch_ref, frame, top[None], 0, lef[8:9], rig[8:9], lanes)
    place(patch_ref, frame, bot[None], ROWS + 1, lef[9:10], rig[9:10], lanes)


def multiply(patch_ref, w_ref, outs):
    depth = 9 * CH
    size = ROWS * COLS
    for t in range(4):
        acc = None
        for a in range(3):
            lhs = jnp.concatenate([patch_ref[t + a, b * COLS : b * COLS + size, :] for b in range(3)], axis=1)
            part = jnp.dot(lhs, w_ref[a * depth : (a + 1) * depth, :], preferred_element_type=F32)
            acc = part if acc is None else acc + part
        for i, out in enumerate(outs):
            out[t * size : (t + 1) * size, :] = acc[:, i * CH : (i + 1) * CH].astype(BF16)


def far_body(cache_at, act_at, extra, flag_ref, st_ref, x_ref, c_ref, tc, bc, lc, rc, ta, ba, la, ra, w_hbm, *rest):
    out2, out1, patch_ref, near_ref, w_ref, sem = rest[extra:]
    col = flag_ref[4]
    copies = []
    for i, (k, dst, at) in enumerate(((2, w_ref, 0), (1, w_ref, CH), (3, near_ref, 0), (0, near_ref, CH))):
        block = pl.multiple_of(lax.rem(col + k, 4) * CH, CH)
        copies.append(
            pltpu.make_async_copy(w_hbm.at[:, pl.ds(block, CH)], dst.at[:, at : at + CH], sem.at[i])
        )
        copies[-1].start()
    has = [flag_ref[i] > 0 for i in range(4)]
    mean, scale = combine(st_ref, x_ref.shape[0] * ROWS * COLS * GROUP)

    def act(v):
        u = (v - mean) * scale
        return u / (1.0 + jnp.exp(-u))

    lanes = (0, CH, 2 * CH)
    for s in range(2):
        place_frame(
            patch_ref,
            s,
            c_ref[s].astype(F32),
            tc[cache_at + s].astype(F32),
            bc[cache_at + s].astype(F32),
            lc[cache_at + s].astype(F32),
            rc[cache_at + s].astype(F32),
            lanes,
        )
    row = lax.broadcasted_iota(jnp.int32, (16, CH), 0)
    edge = jnp.where(row == 8, flag_ref[0], jnp.where(row == 9, flag_ref[1], 1))
    for s in range(4):
        side = []
        for ref, flag in ((la, flag_ref[2]), (ra, flag_ref[3])):
            side.append(jnp.where(edge * flag > 0, act(ref[act_at + s].astype(F32)), 0.0))
        place_frame(
            patch_ref,
            2 + s,
            act(x_ref[s].astype(F32)),
            jnp.where(has[0], act(ta[act_at + s].astype(F32)), 0.0),
            jnp.where(has[1], act(ba[act_at + s].astype(F32)), 0.0),
            side[0],
            side[1],
            lanes,
        )
    copies[0].wait()
    copies[1].wait()
    multiply(patch_ref, w_ref, (out2, out1))
    copies[2].wait()
    copies[3].wait()


def near_body(patch_ref, w_ref, out3, out0):
    multiply(patch_ref, w_ref, (out3, out0))


def conv(flags, stats, x, cache, cache_halo, cache_at, act_halo, act_at, weight, name, after=()):
    n = x.shape[0] * ROWS * COLS
    depth, width = weight.shape
    flops = n * depth * width
    piece = sds((n, CH))
    body = functools.partial(far_body, cache_at, act_at, len(after))
    out2, out1, patch, near = call(
        body,
        [piece] * 2 + [sds((6, (ROWS + 2) * COLS, 3 * CH)), sds((depth, 2 * CH))],
        scratch=[pltpu.VMEM((depth, 2 * CH), BF16), pltpu.SemaphoreType.DMA((4,))],
        flops=flops,
        limit=20,
        name=name + "_far",
    )(flags, stats, x, cache, *cache_halo, *act_halo, Left(weight, HBM), *[Left(a) for a in after])
    got2 = to_peer(out2, 2)
    got1 = to_peer(out1, 1)
    out3, own = call(near_body, [piece] * 2, flops=flops, limit=16, name=name + "_near")(patch, near)
    (far,) = call(add_body, [sds((n, CH), F32)], name=name + "_add")(got1, got2)
    return own, far, to_peer(out3, 3)


def add_body(a_ref, b_ref, o_ref):
    o_ref[...] = a_ref[...].astype(F32) + b_ref[...].astype(F32)


def to_peer(piece, k):
    n = lax.axis_size("col")
    return lax.ppermute(piece, "col", [(i, (i + k) % n) for i in range(n)])


def to_peers(pieces):
    got = {k: to_peer(pieces[k - 1], k) for k in (2, 1, 3)}
    return [got[k] for k in (1, 2, 3)]


def hidden_body(p0, far, p3, h_ref, st_ref, top_ref, bot_ref, lef_ref, rig_ref):
    total = p0[...].astype(F32) + p3[...].astype(F32) + far[...]
    h = total.astype(BF16)
    h_ref[...] = h.reshape(h_ref.shape)
    mean, m2 = local_stats(h.astype(F32))
    st_ref[0:1, :] = mean
    st_ref[1:2, :] = m2
    store_edges([h_ref], top_ref, bot_ref, lef_ref, rig_ref)


def resid_body(x_ref, p0, far, p3, h_ref, top_ref, bot_ref, lef_ref, rig_ref):
    total = p0[...].astype(F32) + p3[...].astype(F32) + far[...]
    h_ref[...] = (x_ref[...].astype(F32) + total.reshape(x_ref.shape)).astype(BF16)
    store_edges([h_ref], top_ref, bot_ref, lef_ref, rig_ref)


ROW_TAPS = {(0, 0): (-1, 0), (0, 1): (1,), (1, 0): (-1,), (1, 1): (0, 1)}
COL_TAPS = {(0, 0): (-1,), (0, 1): (0, 1), (1, 0): (-1, 0), (1, 1): (1,)}


def split_body(flag_ref, w_hbm, after_ref, *rest):
    outs, sem = rest[:4], rest[4]
    copies = []
    for k, out in enumerate(outs):
        block = pl.multiple_of(lax.rem(flag_ref[4] + k, 4) * CH, CH)
        copies.append(pltpu.make_async_copy(w_hbm.at[:, :, pl.ds(block, CH)], out, sem.at[k]))
        copies[-1].start()
    for c in copies:
        c.wait()


def split_weight(flags, weight, after):
    return call(
        split_body,
        [sds(weight.shape[:2] + (CH,))] * 4,
        scratch=[pltpu.SemaphoreType.DMA((4,))],
        name="split_weight",
    )(flags, Left(weight, HBM), Left(after))


def fold_body(w0, w1, w2, w3, o_ref):
    for k, ref in enumerate((w0, w1, w2, w3)):
        taps = [ref[i].astype(F32) for i in range(9)]
        for q in range(2):
            for r in range(2):
                for s in range(2):
                    for p in range(2):
                        total = None
                        for b in ROW_TAPS[p, r]:
                            for e in COL_TAPS[q, s]:
                                tap = taps[(b + 1) * 3 + (e + 1)]
                                total = tap if total is None else total + tap
                        at = (s * 4 + k) * CH
                        o_ref[q, r, at : at + CH, p * CH : (p + 1) * CH] = total.astype(BF16)


def up_body(*refs):
    parts = [refs[2 * k : 2 * k + 2] for k in range(4)]
    w_ref, o_ref, patch_ref, mix_ref = refs[8:12]
    size = (ROWS + 1) * COLS
    half = 2 * 4 * CH
    for k, (x, border) in enumerate(parts):
        edge = border[0].astype(F32)
        place_frame(
            patch_ref,
            0,
            x[0].astype(F32),
            edge[:COLS],
            edge[COLS : 2 * COLS],
            edge[2 * COLS : 2 * COLS + 16],
            edge[2 * COLS + 16 :],
            [(e * 4 + k) * CH for e in range(3)],
        )
    for q in range(2):
        acc = None
        for r in range(2):
            lhs = patch_ref[0, r * COLS : r * COLS + size, q * 4 * CH : q * 4 * CH + half]
            part = jnp.dot(lhs, w_ref[q, r], preferred_element_type=F32)
            acc = part if acc is None else acc + part
        for n in range(ROWS + 1):
            for p in range(2):
                i = 2 * n - 1 + p
                if 0 <= i < 2 * ROWS:
                    mix_ref[i, pl.ds(q, COLS, stride=2), :] = acc[n * COLS : (n + 1) * COLS, p * CH : (p + 1) * CH]
    o_ref[0] = mix_ref[...].astype(BF16)


def up_conv(parts, weight):
    specs = []
    args = []
    for part in parts:
        for a in part:
            rest = a.shape[1:]
            specs.append(pl.BlockSpec((1,) + rest, lambda t, n=len(rest): (t,) + (0,) * n))
            args.append(a)
    specs.append(pl.BlockSpec(weight.shape, lambda t: (0, 0, 0, 0)))
    frames = parts[0][0].shape[0]
    out = (frames, 2 * ROWS, 2 * COLS, CH)
    return pl.pallas_call(
        up_body,
        out_shape=sds(out),
        grid=(frames,),
        in_specs=specs,
        out_specs=pl.BlockSpec((1,) + out[1:], lambda t: (t, 0, 0, 0)),
        scratch_shapes=[
            pltpu.VMEM((1, (ROWS + 2) * COLS, 12 * CH), BF16),
            pltpu.VMEM((2 * ROWS, 2 * COLS, CH), F32),
        ],
        compiler_params=pltpu.CompilerParams(vmem_limit_bytes=24 * MIB),
        name="up_conv",
    )(*args, weight)


def on_device(features, cache_first, cache_second, weight_first, weight_second, weight_up):
    frames = features.shape[0]
    ha, wa, col = lax.axis_index(HA), lax.axis_index("wa"), lax.axis_index("col")
    nh, nw = lax.axis_size(HA), lax.axis_size("wa")
    flags = jnp.stack([ha > 0, ha < nh - 1, wa > 0, wa < nw - 1, col]).astype(jnp.int32)

    x, c1, c2, stats, *edges = call(
        first_body,
        [sds(features.shape), sds(cache_first.shape), sds(cache_second.shape), sds((2, CH), F32)]
        + [sds((8, COLS, CH))] * 2
        + [sds((8, 16, CH))] * 2,
        scratch=[pltpu.SemaphoreType.DMA((3,))],
        limit=20,
        name="first",
    )(Left(features, HBM), Left(cache_first, HBM), Left(cache_second, HBM))
    halo = swap_rows(*edges[:2])
    stats = spread_stats(stats, halo)
    columns, carrying = swap_columns(*halo, *edges[2:])
    w_pieces = split_weight(flags, weight_up, carrying)
    w_got = to_peers(w_pieces[1:])
    halo += columns
    pieces = conv(
        flags, stats, x, c1, halo, 0, halo, 2, weight_first.reshape(-1, 4 * CH), "conv_first", after=w_got
    )
    hidden, stats, *edges = call(
        hidden_body,
        [sds(features.shape), sds((2, CH), F32)] + [sds((frames, COLS, CH))] * 2 + [sds((frames, 16, CH))] * 2,
        name="hidden",
    )(*pieces)
    halo2 = swap_rows(*edges[:2])
    stats = spread_stats(stats, halo2)
    halo2 += swap_columns(*halo2, *edges[2:])[0]
    (folded,) = call(fold_body, [sds((2, 2, 8 * CH, 2 * CH))], limit=12, name="fold")(w_pieces[0], *w_got)
    pieces = conv(
        flags, stats, hidden, c2, halo, 6, halo2, 0, weight_second.reshape(-1, 4 * CH), "conv_second"
    )
    resid, *edges = call(
        resid_body,
        [sds(features.shape)] + [sds((frames, COLS, CH))] * 2 + [sds((frames, 16, CH))] * 2,
        name="resid",
    )(features, *pieces)
    others = to_peers([resid] * 3)
    rows = swap_rows(*edges[:2])
    columns, _ = swap_columns(*rows, *edges[2:], after=others[:1])
    (border,) = call(pack_body, [sds((frames, 2 * COLS + 32, CH))], name="pack")(
        *rows, *columns, *[Left(a) for a in others[1:]]
    )
    borders = [border] + to_peers([border] * 3)
    return up_conv(list(zip([resid] + others, borders)), folded)


def pack_body(top_ref, bot_ref, lef_ref, rig_ref, *rest):
    o_ref = rest[-1]
    at = 0
    for ref in (top_ref, bot_ref, lef_ref, rig_ref):
        n = ref.shape[1]
        o_ref[:, at : at + n, :] = ref[...]
        at += n


def solution(mesh):
    shape = mesh.devices.shape
    mesh = jax.sharding.Mesh(
        mesh.devices.reshape((shape[0] // 2, 2) + shape[1:]), HA + tuple(mesh.axis_names[1:])
    )
    block = P(None, HA, "wa", "col")
    weight = P(None, "col", None)
    return jax.shard_map(
        on_device,
        mesh=mesh,
        in_specs=(block, block, block, weight, weight, weight),
        out_specs=block,
        check_vma=False,
    )
```

time: 164 us -> 142 us (0.87)
  waiting for transfers between devices: 57.6 us -> 39.4 us
  local copies, waits for them, and re-layouts: 11 us -> 0.09 us
  blocking collectives: 0 us -> 3.56 us
  Pallas kernels: 21.3 us -> 24 us
    ppermute x27, waiting for transfers between devices: 57.6 us -> 39 us  [the longest x15 19.7 us: to_peer(): return lax.ppermute(piece, 'col', [(i, (i + k) % n) for i in range(n)])]
    unnamed x23 -> x2, local copies, waits for them, and re-layouts: 9.6 us -> 0.01 us
    ppermute x27, starting transfers between devices: 52.4 us -> 57.4 us  [the longest x15 20.4 us: to_peer(): return lax.ppermute(piece, 'col', [(i, (i + k) % n) for i in range(n)])]
    all_to_all x2, starting transfers between devices: 19.9 us -> 15.3 us  [spread_stats(): lax.all_to_all(slots, ('z', 'wa'), 0, 0, tiled=True).reshape(-1, 2, CH)]
    all_gather x0 -> x2, blocking collectives: none -> 3.56 us  [spread_stats(): pair = lax.all_gather(stats, 'core')]
    pallas_call x10 -> x17, Pallas kernels: 17.1 us -> 19.9 us  [run(): pl.pallas_call(body, out_shape=list(outs), in_specs=specs, out_specs=[VME...]
  transfers between devices with their start and end apart: 29 -> 29, of which waited for: 14 -> 15; matrix products, arithmetic and copies ran while one was open for 0% -> 0% of each run, Pallas kernels for 2% -> 4%
where the time goes in v2:
time: 142 us; the launch traced here: 140 us
  starting transfers between devices  72.7 us (51%)
  waiting for transfers between devices  39.4 us (28%)
  Pallas kernels  24 us (17%)
  blocking collectives  3.56 us (3%)
    ppermute x15, starting transfers between devices, to_peer(): return lax.ppermute(piece, 'col', [(i, (i + k) % n) for i in range(n)])  20.4 us
    pallas_call x17, Pallas kernels, run(): pl.pallas_call(body, out_shape=list(outs), in_specs=specs, out_specs=[VME...  19.9 us
    ppermute x15, waiting for transfers between devices, to_peer(): return lax.ppermute(piece, 'col', [(i, (i + k) % n) for i in range(n)])  19.7 us
    ppermute x3, starting transfers between devices, swap_rows(): above = lax.ppermute(bot, HA, [(i, i + 1) for i in range(n - 1)])  17.3 us
    all_to_all x2, starting transfers between devices, spread_stats(): lax.all_to_all(slots, ('z', 'wa'), 0, 0, tiled=True).reshape(-1, 2, CH)  15.3 us
    ppermute x3, waiting for transfers between devices, swap_rows(): below = lax.ppermute(top, HA, [(i + 1, i) for i in range(n - 1)])  12 us
    ppermute x3, starting transfers between devices, swap_columns(): left = lax.ppermute(ro, 'wa', [(i, i + 1) for i in range(n - 1)])  10.2 us
    ppermute x3, waiting for transfers between devices, swap_columns(): right = lax.ppermute(lo, 'wa', [(i + 1, i) for i in range(n - 1)])  6.33 us
  transfers between devices with their start and end apart: 29, of which 15 were waited for; matrix products, arithmetic and copies ran while one was open for 0% of the time, Pallas kernels for 4%

profile of v2, /device:TPU:97, one launch (start us, length us, event | category | flops | bytes accessed | tf_op | source)
XLA Modules:
  0.0 140.0 jit_solution(5397933503270437976)
XLA Ops:
  2.0 5.3 %collective-permute-start = (bf16[8,32,128]{2,1,0:T(8,128)(2,1)S(1)}, bf16[8,32,128]{2,1,0:T(8,128)(2,1)S(1)}, u32[]{:S(2)}, u32[]{:S(2)}) collective-permute-start(bf16[8,32,128]{2,1,0:T(8,128)(2,1)S(1)} %get-tuple-element.47), channel_id=1, source_target_pairs={{0,16},{16,32},{32,48},{48,64},{64,80},{80,96},{96,112},{112,128},... | collective-permute-start | bytes 196616 | tf_op jit(solution)/shard_map/ppermute | solution.py:137
  9.3 4.8 %collective-permute-done.1.rest_1_.bot_ref.bc.ba = bf16[8,32,128]{2,1,0:T(8,128)(2,1)S(1)} collective-permute-done((bf16[8,32,128]{2,1,0:T(8,128)(2,1)S(1)}, bf16[8,32,128]{2,1,0:T(8,128)(2,1)S(1)}, u32[]{:S(2)}, u32[]{:S(2)}) %collective-permute-start.1) | collective-permute-done | bytes 65568 | tf_op jit(solution)/shard_map/ppermute | solution.py:138
  17.3 2.5 %collective-permute-start.5 = (bf16[9,128,128]{2,1,0:T(8,128)(2,1)S(1)}, bf16[9,128,128]{2,1,0:T(8,128)(2,1)S(1)}, u32[]{:S(2)}, u32[]{:S(2)}) collective-permute-start(bf16[9,128,128]{2,1,0:T(8,128)(2,1)S(1)} %get-tuple-element.56), channel_id=1, source_target_pairs={{0,2},{1,3},{2,0},{3,1},{4,6},{5,7},{6,4},{7,5},{8,10},{9,11},{10,... | collective-permute-start | bytes 884744 | tf_op jit(solution)/shard_map/ppermute | solution.py:272
  23.3 7.6 %all-to-all-start = ((f32[32,4,128]{2,1,0:T(4,128)}), f32[32,4,128]{2,1,0:T(4,128)S(1)}, u32[]{:S(2)}, u32[]{:S(2)}) async-start(f32[32,4,128]{2,1,0:T(4,128)} %slots.2), calls=%async_computation | async-start | bytes 131072 | tf_op jit(solution)/shard_map/all_to_all | solution.py:92
  32.2 4.0 %collective-permute-start.2 = (bf16[8,16,128]{2,1,0:T(8,128)(2,1)S(1)}, bf16[8,16,128]{2,1,0:T(8,128)(2,1)S(1)}, u32[]{:S(2)}, u32[]{:S(2)}) collective-permute-start(bf16[8,16,128]{2,1,0:T(8,128)(2,1)S(1)} %get-tuple-element.53), channel_id=1, source_target_pairs={{0,4},{4,8},{8,12},{1,5},{5,9},{9,13},{2,6},{6,10},{10,14},{3,7},{... | collective-permute-start | bytes 98312 | tf_op jit(solution)/shard_map/ppermute | solution.py:147
  37.6 4.2 %conv_first_far.1 = (bf16[1024,128]{1,0:T(8,128)(2,1)S(1)}, bf16[1024,128]{1,0:T(8,128)(2,1)S(1)}, bf16[6,320,384]{2,1,0:T(8,128)(2,1)S(1)}, bf16[3456,256]{1,0:T(8,128)(2,1)S(1)}) custom-call(s32[5]{0:T(128)S(1)} %stack.39.flag_ref, f32[64,2,128]{2,1,0:T(2,128)S(1)} %bitcast.14, bf16[4,8,32,128]{3,2,1,0:T(8,128)(2,1)S(1)} %get-tuple-element.49.x_ref, ...), custom_call_target="tpu_custom_call" | custom-call | flops 1811939328 | bytes 9043988 | tf_op jit(solution)/shard_map/conv_first_far/pallas_call | solution.py:37
  42.9 2.2 %conv_first_near.1 = (bf16[1024,128]{1,0:T(8,128)(2,1)S(1)}, bf16[1024,128]{1,0:T(8,128)(2,1)S(1)}) custom-call(bf16[6,320,384]{2,1,0:T(8,128)(2,1)S(1)} %get-tuple-element.58.patch_ref, bf16[3456,256]{1,0:T(8,128)(2,1)S(1)} %get-tuple-element.59.w_ref), custom_call_target="tpu_custom_call" | custom-call | flops 1811939328 | bytes 3768320 | tf_op jit(solution)/shard_map/conv_first_near/pallas_call | solution.py:37
  47.0 4.5 %collective-permute-done.7.a_ref = bf16[1024,128]{1,0:T(8,128)(2,1)S(1)} collective-permute-done((bf16[1024,128]{1,0:T(8,128)(2,1)S(1)}, bf16[1024,128]{1,0:T(8,128)(2,1)S(1)}, u32[]{:S(2)}, u32[]{:S(2)}) %collective-permute-start.7) | collective-permute-done | bytes 262176 | tf_op jit(solution)/shard_map/ppermute | solution.py:272
  53.3 2.7 %collective-permute-done.9.p3 = bf16[1024,128]{1,0:T(8,128)(2,1)S(1)} collective-permute-done((bf16[1024,128]{1,0:T(8,128)(2,1)S(1)}, bf16[1024,128]{1,0:T(8,128)(2,1)S(1)}, u32[]{:S(2)}, u32[]{:S(2)}) %collective-permute-start.9) | collective-permute-done | bytes 262176 | tf_op jit(solution)/shard_map/ppermute | solution.py:272
  57.0 5.9 %collective-permute-start.10 = (bf16[4,32,128]{2,1,0:T(8,128)(2,1)S(1)}, bf16[4,32,128]{2,1,0:T(8,128)(2,1)S(1)}, u32[]{:S(2)}, u32[]{:S(2)}) collective-permute-start(bf16[4,32,128]{2,1,0:T(8,128)(2,1)S(1)} %get-tuple-element.65), channel_id=1, source_target_pairs={{0,16},{16,32},{32,48},{48,64},{64,80},{80,96},{96,112},{112,128},... | collective-permute-start | bytes 98312 | tf_op jit(solution)/shard_map/ppermute | solution.py:137
  66.6 2.7 %collective-permute-done.11.rest_1_.bot_ref.ba = bf16[4,32,128]{2,1,0:T(8,128)(2,1)S(1)} collective-permute-done((bf16[4,32,128]{2,1,0:T(8,128)(2,1)S(1)}, bf16[4,32,128]{2,1,0:T(8,128)(2,1)S(1)}, u32[]{:S(2)}, u32[]{:S(2)}) %collective-permute-start.11) | collective-permute-done | bytes 32800 | tf_op jit(solution)/shard_map/ppermute | solution.py:138
  70.0 7.7 %all-to-all-start.1 = ((f32[32,4,128]{2,1,0:T(4,128)}), f32[32,4,128]{2,1,0:T(4,128)S(1)}, u32[]{:S(2)}, u32[]{:S(2)}) async-start(f32[32,4,128]{2,1,0:T(4,128)} %slots.3), calls=%async_computation.1 | async-start | bytes 131072 | tf_op jit(solution)/shard_map/all_to_all | solution.py:92
  77.7 3.1 %collective-permute-start.12 = (bf16[4,16,128]{2,1,0:T(8,128)(2,1)S(1)}, bf16[4,16,128]{2,1,0:T(8,128)(2,1)S(1)}, u32[]{:S(2)}, u32[]{:S(2)}) collective-permute-start(bf16[4,16,128]{2,1,0:T(8,128)(2,1)S(1)} %get-tuple-element.71), channel_id=1, source_target_pairs={{0,4},{4,8},{8,12},{1,5},{5,9},{9,13},{2,6},{6,10},{10,14},{3,7},{... | collective-permute-start | bytes 49160 | tf_op jit(solution)/shard_map/ppermute | solution.py:147
  82.1 3.2 %collective-permute-done.13.ra = bf16[4,16,128]{2,1,0:T(8,128)(2,1)S(1)} collective-permute-done((bf16[4,16,128]{2,1,0:T(8,128)(2,1)S(1)}, bf16[4,16,128]{2,1,0:T(8,128)(2,1)S(1)}, u32[]{:S(2)}, u32[]{:S(2)}) %collective-permute-start.13) | collective-permute-done | bytes 16416 | tf_op jit(solution)/shard_map/ppermute | solution.py:148
  85.3 4.2 %conv_second_far.1 = (bf16[1024,128]{1,0:T(8,128)(2,1)S(1)}, bf16[1024,128]{1,0:T(8,128)(2,1)S(1)}, bf16[6,320,384]{2,1,0:T(8,128)(2,1)S(1)}, bf16[3456,256]{1,0:T(8,128)(2,1)S(1)}) custom-call(s32[5]{0:T(128)S(1)} %stack.39.flag_ref, f32[64,2,128]{2,1,0:T(2,128)S(1)} %bitcast.13, bf16[4,8,32,128]{3,2,1,0:T(8,128)(2,1)S(1)} %get-tuple-element.67.x_ref, ...), custom_call_target="tpu_custom_call" | custom-call | flops 1811939328 | bytes 8060948 | tf_op jit(solution)/shard_map/conv_second_far/pallas_call | solution.py:37
  90.2 3.2 %collective-permute-start.15 = (bf16[1024,128]{1,0:T(8,128)(2,1)S(1)}, bf16[1024,128]{1,0:T(8,128)(2,1)S(1)}, u32[]{:S(2)}, u32[]{:S(2)}) collective-permute-start(bf16[1024,128]{1,0:T(8,128)(2,1)S(1)} %get-tuple-element.77), channel_id=1, source_target_pairs={{0,2},{1,3},{2,0},{3,1},{4,6},{5,7},{6,4},{7,5},{8,10},{9,11},{10,... | collective-permute-start | bytes 786440 | tf_op jit(solution)/shard_map/ppermute | solution.py:272
  93.4 2.2 %conv_second_near.1 = (bf16[1024,128]{1,0:T(8,128)(2,1)S(1)}, bf16[1024,128]{1,0:T(8,128)(2,1)S(1)}) custom-call(bf16[6,320,384]{2,1,0:T(8,128)(2,1)S(1)} %get-tuple-element.73.patch_ref, bf16[3456,256]{1,0:T(8,128)(2,1)S(1)} %get-tuple-element.74.w_ref), custom_call_target="tpu_custom_call" | custom-call | flops 1811939328 | bytes 3768320 | tf_op jit(solution)/shard_map/conv_second_near/pallas_call | solution.py:37
  96.7 6.5 %collective-permute-done.15.b_ref = bf16[1024,128]{1,0:T(8,128)(2,1)S(1)} collective-permute-done((bf16[1024,128]{1,0:T(8,128)(2,1)S(1)}, bf16[1024,128]{1,0:T(8,128)(2,1)S(1)}, u32[]{:S(2)}, u32[]{:S(2)}) %collective-permute-start.15) | collective-permute-done | bytes 262176 | tf_op jit(solution)/shard_map/ppermute | solution.py:272
  104.7 3.9 %collective-permute-start.22 = (bf16[4,8,32,128]{3,2,1,0:T(8,128)(2,1)S(1)}, bf16[4,8,32,128]{3,2,1,0:T(8,128)(2,1)S(1)}, u32[]{:S(2)}, u32[]{:S(2)}) collective-permute-start(bf16[4,8,32,128]{3,2,1,0:T(8,128)(2,1)S(1)} %get-tuple-element.79.refs_0_), channel_id=1, source_target_pairs={{0,2},{1,3},{2,0},{3,1},{4,6},{5,7},{6,4},{7,5},{8,10},{9,11},{10,... | collective-permute-start | bytes 786440 | tf_op jit(solution)/shard_map/ppermute | solution.py:272
  108.6 6.0 %collective-permute-start.17 = (bf16[4,32,128]{2,1,0:T(8,128)(2,1)S(1)}, bf16[4,32,128]{2,1,0:T(8,128)(2,1)S(1)}, u32[]{:S(2)}, u32[]{:S(2)}) collective-permute-start(bf16[4,32,128]{2,1,0:T(8,128)(2,1)S(1)} %get-tuple-element.80), channel_id=1, source_target_pairs={{0,16},{16,32},{32,48},{48,64},{64,80},{80,96},{96,112},{112,128},... | collective-permute-start | bytes 98312 | tf_op jit(solution)/shard_map/ppermute | solution.py:137
  116.5 4.5 %collective-permute-done.18.bot_ref = bf16[4,32,128]{2,1,0:T(8,128)(2,1)S(1)} collective-permute-done((bf16[4,32,128]{2,1,0:T(8,128)(2,1)S(1)}, bf16[4,32,128]{2,1,0:T(8,128)(2,1)S(1)}, u32[]{:S(2)}, u32[]{:S(2)}) %collective-permute-start.18) | collective-permute-done | bytes 32800 | tf_op jit(solution)/shard_map/ppermute | solution.py:138
  121.1 3.1 %collective-permute-start.20 = (bf16[4,16,128]{2,1,0:T(8,128)(2,1)S(1)}, bf16[4,16,128]{2,1,0:T(8,128)(2,1)S(1)}, u32[]{:S(2)}, u32[]{:S(2)}) collective-permute-start(bf16[4,16,128]{2,1,0:T(8,128)(2,1)S(1)} %get-tuple-element.84), channel_id=1, source_target_pairs={{0,4},{4,8},{8,12},{1,5},{5,9},{9,13},{2,6},{6,10},{10,14},{3,7},{... | collective-permute-start | bytes 49160 | tf_op jit(solution)/shard_map/ppermute | solution.py:147
  125.5 3.2 %collective-permute-done.21.rig_ref = bf16[4,16,128]{2,1,0:T(8,128)(2,1)S(1)} collective-permute-done((bf16[4,16,128]{2,1,0:T(8,128)(2,1)S(1)}, bf16[4,16,128]{2,1,0:T(8,128)(2,1)S(1)}, u32[]{:S(2)}, u32[]{:S(2)}) %collective-permute-start.21) | collective-permute-done | bytes 16416 | tf_op jit(solution)/shard_map/ppermute | solution.py:148
  136.0 4.1 %up_conv.1 = bf16[4,16,64,128]{3,2,1,0:T(8,128)(2,1)} custom-call(bf16[4,8,32,128]{3,2,1,0:T(8,128)(2,1)S(1)} %get-tuple-element.79.refs_0_, bf16[4,96,128]{2,1,0:T(8,128)(2,1)S(1)} %pack.1.refs_1_, bf16[4,8,32,128]{3,2,1,0:T(8,128)(2,1)S(1)} %collective-permute-done.19.rest_0_.refs_2_, bf16[4,96,128]{2,1,0:T(8,128)(2,1)S(1)} %collective-permute-done.24.refs_3_, ...), custom_call_target="tpu_custom_call" | custom-call | tf_op jit(solution)/shard_map/up_conv/pallas_call | solution.py:378
  (57 shorter events, 38.6 us)
Async XLA Ops:
  2.0 7.4 %collective-permute-start = (bf16[8,32,128]{2,1,0:T(8,128)(2,1)S(1)}, bf16[8,32,128]{2,1,0:T(8,128)(2,1)S(1)}, u32[]{:S(2)}, u32[]{:S(2)}) collective-permute-start(bf16[8,32,128]{2,1,0:T(8,128)(2,1)S(1)} %get-tuple-element.47), channel_id=1, source_target_pairs={{0,16},{16,32},{32,48},{48,64},{64,80},{80,96},{96,112},{112,128},... | collective-permute-start | bytes 196616 | tf_op jit(solution)/shard_map/ppermute | solution.py:137
  7.3 6.8 %collective-permute-start.1 = (bf16[8,32,128]{2,1,0:T(8,128)(2,1)S(1)}, bf16[8,32,128]{2,1,0:T(8,128)(2,1)S(1)}, u32[]{:S(2)}, u32[]{:S(2)}) collective-permute-start(bf16[8,32,128]{2,1,0:T(8,128)(2,1)S(1)} %get-tuple-element.48), channel_id=1, source_target_pairs={{16,0},{32,16},{48,32},{64,48},{80,64},{96,80},{112,96},{128,112},... | collective-permute-start | bytes 196616 | tf_op jit(solution)/shard_map/ppermute | solution.py:138
  16.0 21.6 %collective-permute-start.4 = (bf16[9,128,128]{2,1,0:T(8,128)(2,1)S(1)}, bf16[9,128,128]{2,1,0:T(8,128)(2,1)S(1)}, u32[]{:S(2)}, u32[]{:S(2)}) collective-permute-start(bf16[9,128,128]{2,1,0:T(8,128)(2,1)S(1)} %get-tuple-element.55), channel_id=1, source_target_pairs={{0,1},{1,2},{2,3},{3,0},{4,5},{5,6},{6,7},{7,4},{8,9},{9,10},{10,1... | collective-permute-start | bytes 884744 | tf_op jit(solution)/shard_map/ppermute | solution.py:272
  17.3 20.4 %collective-permute-start.5 = (bf16[9,128,128]{2,1,0:T(8,128)(2,1)S(1)}, bf16[9,128,128]{2,1,0:T(8,128)(2,1)S(1)}, u32[]{:S(2)}, u32[]{:S(2)}) collective-permute-start(bf16[9,128,128]{2,1,0:T(8,128)(2,1)S(1)} %get-tuple-element.56), channel_id=1, source_target_pairs={{0,2},{1,3},{2,0},{3,1},{4,6},{5,7},{6,4},{7,5},{8,10},{9,11},{10,... | collective-permute-start | bytes 884744 | tf_op jit(solution)/shard_map/ppermute | solution.py:272
  19.7 17.9 %collective-permute-start.6 = (bf16[9,128,128]{2,1,0:T(8,128)(2,1)S(1)}, bf16[9,128,128]{2,1,0:T(8,128)(2,1)S(1)}, u32[]{:S(2)}, u32[]{:S(2)}) collective-permute-start(bf16[9,128,128]{2,1,0:T(8,128)(2,1)S(1)} %get-tuple-element.57), channel_id=1, source_target_pairs={{0,3},{1,0},{2,1},{3,2},{4,7},{5,4},{6,5},{7,6},{8,11},{9,8},{10,9... | collective-permute-start | bytes 884744 | tf_op jit(solution)/shard_map/ppermute | solution.py:272
  23.3 14.3 %all-to-all-start = ((f32[32,4,128]{2,1,0:T(4,128)}), f32[32,4,128]{2,1,0:T(4,128)S(1)}, u32[]{:S(2)}, u32[]{:S(2)}) async-start(f32[32,4,128]{2,1,0:T(4,128)} %slots.2), calls=%async_computation | async-start | bytes 131072 | tf_op jit(solution)/shard_map/all_to_all | solution.py:92
  30.9 5.3 %collective-permute-start.3 = (bf16[8,16,128]{2,1,0:T(8,128)(2,1)S(1)}, bf16[8,16,128]{2,1,0:T(8,128)(2,1)S(1)}, u32[]{:S(2)}, u32[]{:S(2)}) collective-permute-start(bf16[8,16,128]{2,1,0:T(8,128)(2,1)S(1)} %get-tuple-element.54.after_ref), channel_id=1, source_target_pairs={{4,0},{8,4},{12,8},{5,1},{9,5},{13,9},{6,2},{10,6},{14,10},{7,3},{... | collective-permute-start | bytes 98312 | tf_op jit(solution)/shard_map/ppermute | solution.py:148
  41.9 9.6 %collective-permute-start.7 = (bf16[1024,128]{1,0:T(8,128)(2,1)S(1)}, bf16[1024,128]{1,0:T(8,128)(2,1)S(1)}, u32[]{:S(2)}, u32[]{:S(2)}) collective-permute-start(bf16[1024,128]{1,0:T(8,128)(2,1)S(1)} %get-tuple-element.61), channel_id=1, source_target_pairs={{0,1},{1,2},{2,3},{3,0},{4,5},{5,6},{6,7},{7,4},{8,9},{9,10},{10,1... | collective-permute-start | bytes 786440 | tf_op jit(solution)/shard_map/ppermute | solution.py:272
  42.3 10.9 %collective-permute-start.8 = (bf16[1024,128]{1,0:T(8,128)(2,1)S(1)}, bf16[1024,128]{1,0:T(8,128)(2,1)S(1)}, u32[]{:S(2)}, u32[]{:S(2)}) collective-permute-start(bf16[1024,128]{1,0:T(8,128)(2,1)S(1)} %get-tuple-element.62), channel_id=1, source_target_pairs={{0,2},{1,3},{2,0},{3,1},{4,6},{5,7},{6,4},{7,5},{8,10},{9,11},{10,... | collective-permute-start | bytes 786440 | tf_op jit(solution)/shard_map/ppermute | solution.py:272
  45.0 10.9 %collective-permute-start.9 = (bf16[1024,128]{1,0:T(8,128)(2,1)S(1)}, bf16[1024,128]{1,0:T(8,128)(2,1)S(1)}, u32[]{:S(2)}, u32[]{:S(2)}) collective-permute-start(bf16[1024,128]{1,0:T(8,128)(2,1)S(1)} %get-tuple-element.63), channel_id=1, source_target_pairs={{0,3},{1,0},{2,1},{3,2},{4,7},{5,4},{6,5},{7,6},{8,11},{9,8},{10,9... | collective-permute-start | bytes 786440 | tf_op jit(solution)/shard_map/ppermute | solution.py:272
  57.0 9.7 %collective-permute-start.10 = (bf16[4,32,128]{2,1,0:T(8,128)(2,1)S(1)}, bf16[4,32,128]{2,1,0:T(8,128)(2,1)S(1)}, u32[]{:S(2)}, u32[]{:S(2)}) collective-permute-start(bf16[4,32,128]{2,1,0:T(8,128)(2,1)S(1)} %get-tuple-element.65), channel_id=1, source_target_pairs={{0,16},{16,32},{32,48},{48,64},{64,80},{80,96},{96,112},{112,128},... | collective-permute-start | bytes 98312 | tf_op jit(solution)/shard_map/ppermute | solution.py:137
  62.9 6.4 %collective-permute-start.11 = (bf16[4,32,128]{2,1,0:T(8,128)(2,1)S(1)}, bf16[4,32,128]{2,1,0:T(8,128)(2,1)S(1)}, u32[]{:S(2)}, u32[]{:S(2)}) collective-permute-start(bf16[4,32,128]{2,1,0:T(8,128)(2,1)S(1)} %get-tuple-element.66), channel_id=1, source_target_pairs={{16,0},{32,16},{48,32},{64,48},{80,64},{96,80},{112,96},{128,112},... | collective-permute-start | bytes 98312 | tf_op jit(solution)/shard_map/ppermute | solution.py:138
  70.0 15.3 %all-to-all-start.1 = ((f32[32,4,128]{2,1,0:T(4,128)}), f32[32,4,128]{2,1,0:T(4,128)S(1)}, u32[]{:S(2)}, u32[]{:S(2)}) async-start(f32[32,4,128]{2,1,0:T(4,128)} %slots.3), calls=%async_computation.1 | async-start | bytes 131072 | tf_op jit(solution)/shard_map/all_to_all | solution.py:92
  89.5 7.2 %collective-permute-start.14 = (bf16[1024,128]{1,0:T(8,128)(2,1)S(1)}, bf16[1024,128]{1,0:T(8,128)(2,1)S(1)}, u32[]{:S(2)}, u32[]{:S(2)}) collective-permute-start(bf16[1024,128]{1,0:T(8,128)(2,1)S(1)} %get-tuple-element.76), channel_id=1, source_target_pairs={{0,1},{1,2},{2,3},{3,0},{4,5},{5,6},{6,7},{7,4},{8,9},{9,10},{10,1... | collective-permute-start | bytes 786440 | tf_op jit(solution)/shard_map/ppermute | solution.py:272
  90.2 13.1 %collective-permute-start.15 = (bf16[1024,128]{1,0:T(8,128)(2,1)S(1)}, bf16[1024,128]{1,0:T(8,128)(2,1)S(1)}, u32[]{:S(2)}, u32[]{:S(2)}) collective-permute-start(bf16[1024,128]{1,0:T(8,128)(2,1)S(1)} %get-tuple-element.77), channel_id=1, source_target_pairs={{0,2},{1,3},{2,0},{3,1},{4,6},{5,7},{6,4},{7,5},{8,10},{9,11},{10,... | collective-permute-start | bytes 786440 | tf_op jit(solution)/shard_map/ppermute | solution.py:272
  95.6 8.4 %collective-permute-start.16 = (bf16[1024,128]{1,0:T(8,128)(2,1)S(1)}, bf16[1024,128]{1,0:T(8,128)(2,1)S(1)}, u32[]{:S(2)}, u32[]{:S(2)}) collective-permute-start(bf16[1024,128]{1,0:T(8,128)(2,1)S(1)} %get-tuple-element.78), channel_id=1, source_target_pairs={{0,3},{1,0},{2,1},{3,2},{4,7},{5,4},{6,5},{7,6},{8,11},{9,8},{10,9... | collective-permute-start | bytes 786440 | tf_op jit(solution)/shard_map/ppermute | solution.py:272
  104.2 16.8 %collective-permute-start.19 = (bf16[4,8,32,128]{3,2,1,0:T(8,128)(2,1)S(1)}, bf16[4,8,32,128]{3,2,1,0:T(8,128)(2,1)S(1)}, u32[]{:S(2)}, u32[]{:S(2)}) collective-permute-start(bf16[4,8,32,128]{3,2,1,0:T(8,128)(2,1)S(1)} %get-tuple-element.79.refs_0_), channel_id=1, source_target_pairs={{0,1},{1,2},{2,3},{3,0},{4,5},{5,6},{6,7},{7,4},{8,9},{9,10},{10,1... | collective-permute-start | bytes 786440 | tf_op jit(solution)/shard_map/ppermute | solution.py:272
  104.7 20.8 %collective-permute-start.22 = (bf16[4,8,32,128]{3,2,1,0:T(8,128)(2,1)S(1)}, bf16[4,8,32,128]{3,2,1,0:T(8,128)(2,1)S(1)}, u32[]{:S(2)}, u32[]{:S(2)}) collective-permute-start(bf16[4,8,32,128]{3,2,1,0:T(8,128)(2,1)S(1)} %get-tuple-element.79.refs_0_), channel_id=1, source_target_pairs={{0,2},{1,3},{2,0},{3,1},{4,6},{5,7},{6,4},{7,5},{8,10},{9,11},{10,... | collective-permute-start | bytes 786440 | tf_op jit(solution)/shard_map/ppermute | solution.py:272
  108.6 16.9 %collective-permute-start.23 = (bf16[4,8,32,128]{3,2,1,0:T(8,128)(2,1)S(1)}, bf16[4,8,32,128]{3,2,1,0:T(8,128)(2,1)S(1)}, u32[]{:S(2)}, u32[]{:S(2)}) collective-permute-start(bf16[4,8,32,128]{3,2,1,0:T(8,128)(2,1)S(1)} %get-tuple-element.79.refs_0_), channel_id=1, source_target_pairs={{0,3},{1,0},{2,1},{3,2},{4,7},{5,4},{6,5},{7,6},{8,11},{9,8},{10,9... | collective-permute-start | bytes 786440 | tf_op jit(solution)/shard_map/ppermute | solution.py:272
  108.6 7.9 %collective-permute-start.17 = (bf16[4,32,128]{2,1,0:T(8,128)(2,1)S(1)}, bf16[4,32,128]{2,1,0:T(8,128)(2,1)S(1)}, u32[]{:S(2)}, u32[]{:S(2)}) collective-permute-start(bf16[4,32,128]{2,1,0:T(8,128)(2,1)S(1)} %get-tuple-element.80), channel_id=1, source_target_pairs={{0,16},{16,32},{32,48},{48,64},{64,80},{80,96},{96,112},{112,128},... | collective-permute-start | bytes 98312 | tf_op jit(solution)/shard_map/ppermute | solution.py:137
  114.6 6.5 %collective-permute-start.18 = (bf16[4,32,128]{2,1,0:T(8,128)(2,1)S(1)}, bf16[4,32,128]{2,1,0:T(8,128)(2,1)S(1)}, u32[]{:S(2)}, u32[]{:S(2)}) collective-permute-start(bf16[4,32,128]{2,1,0:T(8,128)(2,1)S(1)} %get-tuple-element.81), channel_id=1, source_target_pairs={{16,0},{32,16},{48,32},{64,48},{80,64},{96,80},{112,96},{128,112},... | collective-permute-start | bytes 98312 | tf_op jit(solution)/shard_map/ppermute | solution.py:138
  128.7 6.9 %collective-permute-start.24 = (bf16[4,96,128]{2,1,0:T(8,128)(2,1)S(1)}, bf16[4,96,128]{2,1,0:T(8,128)(2,1)S(1)}, u32[]{:S(2)}, u32[]{:S(2)}) collective-permute-start(bf16[4,96,128]{2,1,0:T(8,128)(2,1)S(1)} %pack.1.refs_1_), channel_id=1, source_target_pairs={{0,1},{1,2},{2,3},{3,0},{4,5},{5,6},{6,7},{7,4},{8,9},{9,10},{10,1... | collective-permute-start | bytes 294920 | tf_op jit(solution)/shard_map/ppermute | solution.py:272
  130.4 5.1 %collective-permute-start.25 = (bf16[4,96,128]{2,1,0:T(8,128)(2,1)S(1)}, bf16[4,96,128]{2,1,0:T(8,128)(2,1)S(1)}, u32[]{:S(2)}, u32[]{:S(2)}) collective-permute-start(bf16[4,96,128]{2,1,0:T(8,128)(2,1)S(1)} %pack.1.refs_1_), channel_id=1, source_target_pairs={{0,2},{1,3},{2,0},{3,1},{4,6},{5,7},{6,4},{7,5},{8,10},{9,11},{10,... | collective-permute-start | bytes 294920 | tf_op jit(solution)/shard_map/ppermute | solution.py:272
  131.0 5.0 %collective-permute-start.26 = (bf16[4,96,128]{2,1,0:T(8,128)(2,1)S(1)}, bf16[4,96,128]{2,1,0:T(8,128)(2,1)S(1)}, u32[]{:S(2)}, u32[]{:S(2)}) collective-permute-start(bf16[4,96,128]{2,1,0:T(8,128)(2,1)S(1)} %pack.1.refs_1_), channel_id=1, source_target_pairs={{0,3},{1,0},{2,1},{3,2},{4,7},{5,4},{6,5},{7,6},{8,11},{9,8},{10,9... | collective-permute-start | bytes 294920 | tf_op jit(solution)/shard_map/ppermute | solution.py:272
  (6 other events, 33.4 us)

commit v3 on v2

--- a/solution.py
+++ b/solution.py
@@ -14,6 +14,7 @@
 ROWS = 8
 COLS = 32
 MIB = 1 << 20
+CORNERS = ((0, 0), (0, 1), (1, 0), (1, 1))
 
 VMEM = pl.BlockSpec(memory_space=pltpu.VMEM)
 SMEM = pl.BlockSpec(memory_space=pltpu.SMEM)
@@ -79,45 +80,66 @@
     return mean, lax.rsqrt(m2 * (1.0 / (count * devices)) + 1e-6)
 
 
-def slot_body(st_ref, *rest):
-    o_ref = rest[-1]
-    o_ref[...] = jnp.broadcast_to(st_ref[...][None], o_ref.shape)
-
-
-def spread_stats(stats, after):
-    pair = lax.all_gather(stats, "core")
-    chips = lax.axis_size("z") * lax.axis_size("wa")
-    pair = pair.reshape(2 * pair.shape[0], CH)
-    (slots,) = call(slot_body, [sds((chips,) + pair.shape, F32)], name="slots")(pair, *[Left(a) for a in after])
-    return lax.all_to_all(slots, ("z", "wa"), 0, 0, tiled=True).reshape(-1, 2, CH)
-
-
-def store_edges(ref_slices, top_ref, bot_ref, lef_ref, rig_ref):
+def spread(slots):
+    return lax.all_to_all(slots, HA + ("wa",), 0, 0, tiled=True)
+
+
+def diagonals(flag_ref):
+    wa_size = lax.axis_size("wa")
+    found = []
+    for r, c in CORNERS:
+        valid = flag_ref[r] * flag_ref[2 + c]
+        found.append((valid, flag_ref[5] + valid * ((2 * r - 1) * wa_size + 2 * c - 1)))
+    return found
+
+
+def fill_slots(slot_ref, flag_ref, mean, m2, frames):
+    row = lax.broadcasted_iota(jnp.int32, (8, CH), 0)
+    base = jnp.where(row == 0, mean, jnp.where(row == 1, m2, 0.0))
+    slot_ref[...] = jnp.broadcast_to(base[None], slot_ref.shape)
+    for (r, c), (valid, at) in zip(CORNERS, diagonals(flag_ref)):
+
+        @pl.when(valid > 0)
+        def _():
+            f = 0
+            for v in frames:
+                for i in range(v.shape[0]):
+                    pixel = v[i, r * (ROWS - 1), c * (COLS - 1) : c * (COLS - 1) + 1, :]
+                    slot_ref[pl.ds(at, 1), 2 + f, :] = pixel
+                    f += 1
+
+
+def store_edges(frames, refs, pad=0):
+    top_ref, bot_ref, lef_ref, rig_ref = refs
     at = 0
-    for ref in ref_slices:
-        n = ref.shape[0]
-        top_ref[at : at + n] = ref[:, 0]
-        bot_ref[at : at + n] = ref[:, ROWS - 1]
-        v = ref[...].astype(F32)
-        pad = jnp.zeros((n, 8, CH), F32)
-        lef_ref[at : at + n] = jnp.concatenate([v[:, :, 0, :], pad], axis=1).astype(BF16)
-        rig_ref[at : at + n] = jnp.concatenate([v[:, :, COLS - 1, :], pad], axis=1).astype(BF16)
+    for v in frames:
+        n = v.shape[0]
+        top_ref[at : at + n] = v[:, 0].astype(BF16)
+        bot_ref[at : at + n] = v[:, ROWS - 1].astype(BF16)
+        for ref, column in ((lef_ref, v[:, :, 0, :]), (rig_ref, v[:, :, COLS - 1, :])):
+            if pad:
+                column = jnp.concatenate([column, jnp.zeros((n, pad, CH), F32)], axis=1)
+            ref[at : at + n] = column.astype(BF16)
         at += n
 
 
-def first_body(x_hbm, c1_hbm, c2_hbm, x_ref, c1_ref, c2_ref, st_ref, top_ref, bot_ref, lef_ref, rig_ref, sem):
-    copies = [
-        pltpu.make_async_copy(src, dst, sem.at[i])
-        for i, (src, dst) in enumerate(((x_hbm, x_ref), (c1_hbm, c1_ref), (c2_hbm, c2_ref)))
-    ]
+def first_body(flag_ref, x_hbm, c1_hbm, c2_hbm, w_hbm, x_ref, c1_ref, c2_ref, slot_ref, *rest):
+    edges, pieces, sem = rest[:4], rest[4:8], rest[8]
+    pairs = [(x_hbm, x_ref), (c1_hbm, c1_ref), (c2_hbm, c2_ref)]
+    for k, piece in enumerate(pieces):
+        block = pl.multiple_of(lax.rem(flag_ref[4] + k, 4) * CH, CH)
+        pairs.append((w_hbm.at[:, :, pl.ds(block, CH)], piece))
+    copies = [pltpu.make_async_copy(src, dst, sem.at[i]) for i, (src, dst) in enumerate(pairs)]
     for c in copies:
         c.start()
-    for c in copies:
+    for c in copies[:3]:
         c.wait()
-    mean, m2 = local_stats(x_ref[...].astype(F32).reshape(-1, CH))
-    st_ref[0:1, :] = mean
-    st_ref[1:2, :] = m2
-    store_edges([c1_ref, x_ref, c2_ref], top_ref, bot_ref, lef_ref, rig_ref)
+    x, c1, c2 = x_ref[...].astype(F32), c1_ref[...].astype(F32), c2_ref[...].astype(F32)
+    mean, m2 = local_stats(x.reshape(-1, CH))
+    fill_slots(slot_ref, flag_ref, mean, m2, (c1, x))
+    store_edges((c1, x, c2), edges)
+    for c in copies[3:]:
+        c.wait()
 
 
 def corner_body(top_ref, bot_ref, lef_ref, rig_ref, *rest):
@@ -139,14 +161,11 @@
     return above, below
 
 
-def swap_columns(above, below, lef, rig, after=()):
+def swap_columns(lef, rig):
     n = lax.axis_size("wa")
-    lo, ro = call(corner_body, [sds(lef.shape)] * 2, name="corners")(
-        above, below, lef, rig, *[Left(a) for a in after]
-    )
-    left = lax.ppermute(ro, "wa", [(i, i + 1) for i in range(n - 1)])
-    right = lax.ppermute(lo, "wa", [(i + 1, i) for i in range(n - 1)])
-    return (left, right), lo
+    left = lax.ppermute(rig, "wa", [(i, i + 1) for i in range(n - 1)])
+    right = lax.ppermute(lef, "wa", [(i + 1, i) for i in range(n - 1)])
+    return left, right
 
 
 def shifted(rows, left, right):
@@ -167,10 +186,10 @@
         patch_ref[frame, at * COLS : (at + n) * COLS, lanes[e] : lanes[e] + CH] = v.reshape(n * COLS, CH).astype(BF16)
 
 
-def place_frame(patch_ref, frame, inner, top, bot, lef, rig, lanes):
-    place(patch_ref, frame, inner, 1, lef[0:8], rig[0:8], lanes)
-    place(patch_ref, frame, top[None], 0, lef[8:9], rig[8:9], lanes)
-    place(patch_ref, frame, bot[None], ROWS + 1, lef[9:10], rig[9:10], lanes)
+def place_frame(patch_ref, frame, inner, top, bot, lef, rig, corners, lanes):
+    place(patch_ref, frame, inner, 1, lef, rig, lanes)
+    place(patch_ref, frame, top[None], 0, corners[0], corners[1], lanes)
+    place(patch_ref, frame, bot[None], ROWS + 1, corners[2], corners[3], lanes)
 
 
 def multiply(patch_ref, w_ref, outs):
@@ -204,33 +223,17 @@
         return u / (1.0 + jnp.exp(-u))
 
     lanes = (0, CH, 2 * CH)
-    for s in range(2):
-        place_frame(
-            patch_ref,
-            s,
-            c_ref[s].astype(F32),
-            tc[cache_at + s].astype(F32),
-            bc[cache_at + s].astype(F32),
-            lc[cache_at + s].astype(F32),
-            rc[cache_at + s].astype(F32),
-            lanes,
-        )
-    row = lax.broadcasted_iota(jnp.int32, (16, CH), 0)
-    edge = jnp.where(row == 8, flag_ref[0], jnp.where(row == 9, flag_ref[1], 1))
-    for s in range(4):
-        side = []
-        for ref, flag in ((la, flag_ref[2]), (ra, flag_ref[3])):
-            side.append(jnp.where(edge * flag > 0, act(ref[act_at + s].astype(F32)), 0.0))
-        place_frame(
-            patch_ref,
-            2 + s,
-            act(x_ref[s].astype(F32)),
-            jnp.where(has[0], act(ta[act_at + s].astype(F32)), 0.0),
-            jnp.where(has[1], act(ba[act_at + s].astype(F32)), 0.0),
-            side[0],
-            side[1],
-            lanes,
-        )
+    across = diagonals(flag_ref)
+    for s in range(6):
+        if s < 2:
+            own, at, halo, change = c_ref[s], cache_at + s, (tc, bc, lc, rc), lambda v: v
+        else:
+            own, at, halo, change = x_ref[s - 2], act_at + s - 2, (ta, ba, la, ra), act
+        sides = [jnp.where(has[i], change(ref[at].astype(F32)), 0.0) for i, ref in enumerate(halo)]
+        corners = [
+            jnp.where(valid > 0, change(st_ref[pl.ds(slot, 1), 2 + s, :]), 0.0) for valid, slot in across
+        ]
+        place_frame(patch_ref, s, change(own.astype(F32)), *sides, corners, lanes)
     copies[0].wait()
     copies[1].wait()
     multiply(patch_ref, w_ref, (out2, out1))
@@ -277,44 +280,25 @@
     return [got[k] for k in (1, 2, 3)]
 
 
-def hidden_body(p0, far, p3, h_ref, st_ref, top_ref, bot_ref, lef_ref, rig_ref):
+def hidden_body(flag_ref, p0, far, p3, c2_ref, h_ref, slot_ref, *edges):
+    h = (p0[...].astype(F32) + p3[...].astype(F32) + far[...]).astype(BF16)
+    h_ref[...] = h.reshape(h_ref.shape)
+    h = h.astype(F32)
+    mean, m2 = local_stats(h)
+    h = h.reshape(h_ref.shape)
+    fill_slots(slot_ref, flag_ref, mean, m2, (c2_ref[...].astype(F32), h))
+    store_edges((h,), edges)
+
+
+def resid_body(x_ref, p0, far, p3, h_ref, *edges):
     total = p0[...].astype(F32) + p3[...].astype(F32) + far[...]
-    h = total.astype(BF16)
-    h_ref[...] = h.reshape(h_ref.shape)
-    mean, m2 = local_stats(h.astype(F32))
-    st_ref[0:1, :] = mean
-    st_ref[1:2, :] = m2
-    store_edges([h_ref], top_ref, bot_ref, lef_ref, rig_ref)
-
-
-def resid_body(x_ref, p0, far, p3, h_ref, top_ref, bot_ref, lef_ref, rig_ref):
-    total = p0[...].astype(F32) + p3[...].astype(F32) + far[...]
-    h_ref[...] = (x_ref[...].astype(F32) + total.reshape(x_ref.shape)).astype(BF16)
-    store_edges([h_ref], top_ref, bot_ref, lef_ref, rig_ref)
+    h = (x_ref[...].astype(F32) + total.reshape(x_ref.shape)).astype(BF16)
+    h_ref[...] = h
+    store_edges((h.astype(F32),), edges, pad=8)
 
 
 ROW_TAPS = {(0, 0): (-1, 0), (0, 1): (1,), (1, 0): (-1,), (1, 1): (0, 1)}
 COL_TAPS = {(0, 0): (-1,), (0, 1): (0, 1), (1, 0): (-1, 0), (1, 1): (1,)}
-
-
-def split_body(flag_ref, w_hbm, after_ref, *rest):
-    outs, sem = rest[:4], rest[4]
-    copies = []
-    for k, out in enumerate(outs):
-        block = pl.multiple_of(lax.rem(flag_ref[4] + k, 4) * CH, CH)
-        copies.append(pltpu.make_async_copy(w_hbm.at[:, :, pl.ds(block, CH)], out, sem.at[k]))
-        copies[-1].start()
-    for c in copies:
-        c.wait()
-
-
-def split_weight(flags, weight, after):
-    return call(
-        split_body,
-        [sds(weight.shape[:2] + (CH,))] * 4,
-        scratch=[pltpu.SemaphoreType.DMA((4,))],
-        name="split_weight",
-    )(flags, Left(weight, HBM), Left(after))
 
 
 def fold_body(w0, w1, w2, w3, o_ref):
@@ -346,8 +330,9 @@
             x[0].astype(F32),
             edge[:COLS],
             edge[COLS : 2 * COLS],
-            edge[2 * COLS : 2 * COLS + 16],
-            edge[2 * COLS + 16 :],
+            edge[2 * COLS : 2 * COLS + 8],
+            edge[2 * COLS + 16 : 2 * COLS + 24],
+            [edge[2 * COLS + i : 2 * COLS + i + 1] for i in (8, 24, 9, 25)],
             [(e * 4 + k) * CH for e in range(3)],
         )
     for q in range(2):
@@ -394,34 +379,34 @@
     frames = features.shape[0]
     ha, wa, col = lax.axis_index(HA), lax.axis_index("wa"), lax.axis_index("col")
     nh, nw = lax.axis_size(HA), lax.axis_size("wa")
-    flags = jnp.stack([ha > 0, ha < nh - 1, wa > 0, wa < nw - 1, col]).astype(jnp.int32)
+    flags = jnp.stack([ha > 0, ha < nh - 1, wa > 0, wa < nw - 1, col, ha * nw + wa]).astype(jnp.int32)
+    slots = sds((nh * nw, 8, CH), F32)
 
     x, c1, c2, stats, *edges = call(
         first_body,
-        [sds(features.shape), sds(cache_first.shape), sds(cache_second.shape), sds((2, CH), F32)]
+        [sds(features.shape), sds(cache_first.shape), sds(cache_second.shape), slots]
         + [sds((8, COLS, CH))] * 2
-        + [sds((8, 16, CH))] * 2,
-        scratch=[pltpu.SemaphoreType.DMA((3,))],
+        + [sds((8, ROWS, CH))] * 2
+        + [sds(weight_up.shape[:2] + (CH,))] * 4,
+        scratch=[pltpu.SemaphoreType.DMA((7,))],
         limit=20,
         name="first",
-    )(Left(features, HBM), Left(cache_first, HBM), Left(cache_second, HBM))
-    halo = swap_rows(*edges[:2])
-    stats = spread_stats(stats, halo)
-    columns, carrying = swap_columns(*halo, *edges[2:])
-    w_pieces = split_weight(flags, weight_up, carrying)
+    )(flags, *[Left(a, HBM) for a in (features, cache_first, cache_second, weight_up)])
+    edges, w_pieces = edges[:4], edges[4:]
     w_got = to_peers(w_pieces[1:])
-    halo += columns
+    halo = swap_rows(*edges[:2]) + swap_columns(*edges[2:])
+    stats = spread(stats)
     pieces = conv(
         flags, stats, x, c1, halo, 0, halo, 2, weight_first.reshape(-1, 4 * CH), "conv_first", after=w_got
     )
     hidden, stats, *edges = call(
         hidden_body,
-        [sds(features.shape), sds((2, CH), F32)] + [sds((frames, COLS, CH))] * 2 + [sds((frames, 16, CH))] * 2,
+        [sds(features.shape), slots] + [sds((frames, COLS, CH))] * 2 + [sds((frames, ROWS, CH))] * 2,
+        limit=12,
         name="hidden",
-    )(*pieces)
-    halo2 = swap_rows(*edges[:2])
-    stats = spread_stats(stats, halo2)
-    halo2 += swap_columns(*halo2, *edges[2:])[0]
+    )(flags, *pieces, c2)
+    halo2 = swap_rows(*edges[:2]) + swap_columns(*edges[2:])
+    stats = spread(stats)
     (folded,) = call(fold_body, [sds((2, 2, 8 * CH, 2 * CH))], limit=12, name="fold")(w_pieces[0], *w_got)
     pieces = conv(
         flags, stats, hidden, c2, halo, 6, halo2, 0, weight_second.reshape(-1, 4 * CH), "conv_second"
@@ -433,7 +418,8 @@
     )(features, *pieces)
     others = to_peers([resid] * 3)
     rows = swap_rows(*edges[:2])
-    columns, _ = swap_columns(*rows, *edges[2:], after=others[:1])
+    cornered = call(corner_body, [sds((frames, 16, CH))] * 2, name="corners")(*rows, *edges[2:], Left(others[0]))
+    columns = swap_columns(*cornered)
     (border,) = call(pack_body, [sds((frames, 2 * COLS + 32, CH))], name="pack")(
         *rows, *columns, *[Left(a) for a in others[1:]]
     )

time: 142 us -> 137 us (0.965)
  blocking collectives: 3.56 us -> 0 us
  waiting for transfers between devices: 39.4 us -> 36 us
  starting transfers between devices: 72.7 us -> 75.8 us
    all_to_all x2, starting transfers between devices: 15.3 us -> 21.9 us  [spread(): return lax.all_to_all(slots, HA + ('wa',), 0, 0, tiled=True)]
    all_gather x2 -> x0, blocking collectives: 3.56 us -> none  [spread_stats(): pair = lax.all_gather(stats, 'core')]
    ppermute x3, starting transfers between devices: 17.3 us -> 14.3 us  [swap_rows(): above = lax.ppermute(bot, HA, [(i, i + 1) for i in range(n - 1)])]
    ppermute x3, waiting for transfers between devices: 12 us -> 9.66 us  [swap_rows(): below = lax.ppermute(top, HA, [(i + 1, i) for i in range(n - 1)])]
    pallas_call x17 -> x12, Pallas kernels: 19.9 us -> 19.2 us  [run(): pl.pallas_call(body, out_shape=list(outs), in_specs=specs, out_specs=[VME...]
  transfers between devices with their start and end apart: 29 -> 29, of which waited for: 15 -> 11; matrix products, arithmetic and copies ran while one was open for 0% -> 0% of each run, Pallas kernels for 4% -> 4%
where the time goes in v3:
time: 137 us; the launch traced here: 136 us
  starting transfers between devices  75.8 us (55%)
  waiting for transfers between devices  36 us (26%)
  Pallas kernels  23.3 us (17%)
    all_to_all x2, starting transfers between devices, spread(): return lax.all_to_all(slots, HA + ('wa',), 0, 0, tiled=True)  21.9 us
    ppermute x15, starting transfers between devices, to_peer(): return lax.ppermute(piece, 'col', [(i, (i + k) % n) for i in range(n)])  20.4 us
    ppermute x15, waiting for transfers between devices, to_peer(): return lax.ppermute(piece, 'col', [(i, (i + k) % n) for i in range(n)])  20.3 us
    pallas_call x12, Pallas kernels, run(): pl.pallas_call(body, out_shape=list(outs), in_specs=specs, out_specs=[VME...  19.2 us
    ppermute x3, starting transfers between devices, swap_rows(): above = lax.ppermute(bot, HA, [(i, i + 1) for i in range(n - 1)])  14.3 us
    ppermute x3, waiting for transfers between devices, swap_rows(): below = lax.ppermute(top, HA, [(i + 1, i) for i in range(n - 1)])  9.66 us
    ppermute x3, starting transfers between devices, swap_columns(): left = lax.ppermute(rig, 'wa', [(i, i + 1) for i in range(n - 1)])  9.26 us
    ppermute x3, waiting for transfers between devices, swap_columns(): right = lax.ppermute(lef, 'wa', [(i + 1, i) for i in range(n - 1)])  6.06 us
  transfers between devices with their start and end apart: 29, of which 11 were waited for; matrix products, arithmetic and copies ran while one was open for 0% of the time, Pallas kernels for 4%

profile of v3, /device:TPU:97, one launch (start us, length us, event | category | flops | bytes accessed | tf_op | source)
XLA Modules:
  0.0 135.5 jit_solution(13879261606206268346)
XLA Ops:
  0.1 3.3 %first.1 = (bf16[4,8,32,128]{3,2,1,0:T(8,128)(2,1)S(1)}, bf16[2,8,32,128]{3,2,1,0:T(8,128)(2,1)S(1)}, bf16[2,8,32,128]{3,2,1,0:T(8,128)(2,1)S(1)}, f32[64,8,128]...) custom-call(s32[6]{0:T(128)S(1)} %stack.43.flag_ref, ...), custom_call_target="tpu_custom_call" | custom-call | bytes 3833880 | tf_op jit(solution)/shard_map/first/pallas_call | solution.py:38
  3.4 11.2 %all-to-all-start = ((f32[64,8,128]{2,1,0:T(8,128)}), f32[64,8,128]{2,1,0:T(8,128)S(1)}, u32[]{:S(2)}, u32[]{:S(2)}) async-start(f32[64,8,128]{2,1,0:T(8,128)} %get-tuple-element.42), calls=%async_computation | async-start | bytes 524288 | tf_op jit(solution)/shard_map/all_to_all | solution.py:84
  15.9 2.5 %collective-permute-start.5 = (bf16[9,128,128]{2,1,0:T(8,128)(2,1)S(1)}, bf16[9,128,128]{2,1,0:T(8,128)(2,1)S(1)}, u32[]{:S(2)}, u32[]{:S(2)}) collective-permute-start(bf16[9,128,128]{2,1,0:T(8,128)(2,1)S(1)} %get-tuple-element.50), channel_id=1, source_target_pairs={{0,2},{1,3},{2,0},{3,1},{4,6},{5,7},{6,4},{7,5},{8,10},{9,11},{10,... | collective-permute-start | bytes 884744 | tf_op jit(solution)/shard_map/ppermute | solution.py:275
  19.5 3.1 %collective-permute-start.2 = (bf16[8,8,128]{2,1,0:T(8,128)(2,1)S(1)}, bf16[8,8,128]{2,1,0:T(8,128)(2,1)S(1)}, u32[]{:S(2)}, u32[]{:S(2)}) collective-permute-start(bf16[8,8,128]{2,1,0:T(8,128)(2,1)S(1)} %get-tuple-element.47), channel_id=1, source_target_pairs={{0,4},{4,8},{8,12},{1,5},{5,9},{9,13},{2,6},{6,10},{10,14},{3,7},{... | collective-permute-start | bytes 49160 | tf_op jit(solution)/shard_map/ppermute | solution.py:166
  23.9 5.8 %collective-permute-start = (bf16[8,32,128]{2,1,0:T(8,128)(2,1)S(1)}, bf16[8,32,128]{2,1,0:T(8,128)(2,1)S(1)}, u32[]{:S(2)}, u32[]{:S(2)}) collective-permute-start(bf16[8,32,128]{2,1,0:T(8,128)(2,1)S(1)} %get-tuple-element.45), channel_id=1, source_target_pairs={{0,16},{16,32},{32,48},{48,64},{64,80},{80,96},{96,112},{112,128},... | collective-permute-start | bytes 196616 | tf_op jit(solution)/shard_map/ppermute | solution.py:159
  31.7 4.9 %collective-permute-done.1.bc.ba = bf16[8,32,128]{2,1,0:T(8,128)(2,1)S(1)} collective-permute-done((bf16[8,32,128]{2,1,0:T(8,128)(2,1)S(1)}, bf16[8,32,128]{2,1,0:T(8,128)(2,1)S(1)}, u32[]{:S(2)}, u32[]{:S(2)}) %collective-permute-start.1) | collective-permute-done | bytes 65568 | tf_op jit(solution)/shard_map/ppermute | solution.py:160
  36.6 4.2 %conv_first_far.1 = (bf16[1024,128]{1,0:T(8,128)(2,1)S(1)}, bf16[1024,128]{1,0:T(8,128)(2,1)S(1)}, bf16[6,320,384]{2,1,0:T(8,128)(2,1)S(1)}, bf16[3456,256]{1,0:T(8,128)(2,1)S(1)}) custom-call(s32[6]{0:T(128)S(1)} %stack.43.flag_ref, f32[64,8,128]{2,1,0:T(8,128)S(1)} %all-to-all-done.st_ref, bf16[4,8,32,128]{3,2,1,0:T(8,128)(2,1)S(1)} %get-tuple-element.43.x_ref, ...), custom_call_target="tpu_custom_call" | custom-call | flops 1811939328 | bytes 9175064 | tf_op jit(solution)/shard_map/conv_first_far/pallas_call | solution.py:38
  46.0 7.2 %collective-permute-done.7.a_ref = bf16[1024,128]{1,0:T(8,128)(2,1)S(1)} collective-permute-done((bf16[1024,128]{1,0:T(8,128)(2,1)S(1)}, bf16[1024,128]{1,0:T(8,128)(2,1)S(1)}, u32[]{:S(2)}, u32[]{:S(2)}) %collective-permute-start.7) | collective-permute-done | bytes 262176 | tf_op jit(solution)/shard_map/ppermute | solution.py:275
  54.1 2.3 %hidden.1 = (bf16[4,8,32,128]{3,2,1,0:T(8,128)(2,1)S(1)}, f32[64,8,128]{2,1,0:T(8,128)}, bf16[4,32,128]{2,1,0:T(8,128)(2,1)S(1)}, bf16[4,32,128]{2,1,0:T(8,128)(...) custom-call(s32[6]{0:T(128)S(1)} %stack.43.flag_ref, ...), custom_call_target="tpu_custom_call" | custom-call | bytes 1785880 | tf_op jit(solution)/shard_map/hidden/pallas_call | solution.py:38
  56.4 10.7 %all-to-all-start.1 = ((f32[64,8,128]{2,1,0:T(8,128)}), f32[64,8,128]{2,1,0:T(8,128)S(1)}, u32[]{:S(2)}, u32[]{:S(2)}) async-start(f32[64,8,128]{2,1,0:T(8,128)} %get-tuple-element.59), calls=%async_computation.1 | async-start | bytes 524288 | tf_op jit(solution)/shard_map/all_to_all | solution.py:84
  67.1 4.6 %collective-permute-start.10 = (bf16[4,32,128]{2,1,0:T(8,128)(2,1)S(1)}, bf16[4,32,128]{2,1,0:T(8,128)(2,1)S(1)}, u32[]{:S(2)}, u32[]{:S(2)}) collective-permute-start(bf16[4,32,128]{2,1,0:T(8,128)(2,1)S(1)} %get-tuple-element.61), channel_id=1, source_target_pairs={{0,16},{16,32},{32,48},{48,64},{64,80},{80,96},{96,112},{112,128},... | collective-permute-start | bytes 98312 | tf_op jit(solution)/shard_map/ppermute | solution.py:159
  73.6 3.1 %collective-permute-start.12 = (bf16[4,8,128]{2,1,0:T(8,128)(2,1)S(1)}, bf16[4,8,128]{2,1,0:T(8,128)(2,1)S(1)}, u32[]{:S(2)}, u32[]{:S(2)}) collective-permute-start(bf16[4,8,128]{2,1,0:T(8,128)(2,1)S(1)} %get-tuple-element.63), channel_id=1, source_target_pairs={{0,4},{4,8},{8,12},{1,5},{5,9},{9,13},{2,6},{6,10},{10,14},{3,7},{... | collective-permute-start | bytes 24584 | tf_op jit(solution)/shard_map/ppermute | solution.py:166
  78.2 2.9 %collective-permute-done.13.ra = bf16[4,8,128]{2,1,0:T(8,128)(2,1)S(1)} collective-permute-done((bf16[4,8,128]{2,1,0:T(8,128)(2,1)S(1)}, bf16[4,8,128]{2,1,0:T(8,128)(2,1)S(1)}, u32[]{:S(2)}, u32[]{:S(2)}) %collective-permute-start.13) | collective-permute-done | bytes 8224 | tf_op jit(solution)/shard_map/ppermute | solution.py:167
  81.1 4.2 %conv_second_far.1 = (bf16[1024,128]{1,0:T(8,128)(2,1)S(1)}, bf16[1024,128]{1,0:T(8,128)(2,1)S(1)}, bf16[6,320,384]{2,1,0:T(8,128)(2,1)S(1)}, bf16[3456,256]{1,0:T(8,128)(2,1)S(1)}) custom-call(s32[6]{0:T(128)S(1)} %stack.43.flag_ref, f32[64,8,128]{2,1,0:T(8,128)S(1)} %all-to-all-done.1.st_ref, bf16[4,8,32,128]{3,2,1,0:T(8,128)(2,1)S(1)} %get-tuple-element.60.x_ref, ...), custom_call_target="tpu_custom_call" | custom-call | flops 1811939328 | bytes 8208408 | tf_op jit(solution)/shard_map/conv_second_far/pallas_call | solution.py:38
  85.5 3.4 %collective-permute-start.15 = (bf16[1024,128]{1,0:T(8,128)(2,1)S(1)}, bf16[1024,128]{1,0:T(8,128)(2,1)S(1)}, u32[]{:S(2)}, u32[]{:S(2)}) collective-permute-start(bf16[1024,128]{1,0:T(8,128)(2,1)S(1)} %get-tuple-element.69), channel_id=1, source_target_pairs={{0,2},{1,3},{2,0},{3,1},{4,6},{5,7},{6,4},{7,5},{8,10},{9,11},{10,... | collective-permute-start | bytes 786440 | tf_op jit(solution)/shard_map/ppermute | solution.py:275
  91.3 2.4 %collective-permute-done.14.a_ref = bf16[1024,128]{1,0:T(8,128)(2,1)S(1)} collective-permute-done((bf16[1024,128]{1,0:T(8,128)(2,1)S(1)}, bf16[1024,128]{1,0:T(8,128)(2,1)S(1)}, u32[]{:S(2)}, u32[]{:S(2)}) %collective-permute-start.14) | collective-permute-done | bytes 262176 | tf_op jit(solution)/shard_map/ppermute | solution.py:275
  93.6 6.5 %collective-permute-done.15.b_ref = bf16[1024,128]{1,0:T(8,128)(2,1)S(1)} collective-permute-done((bf16[1024,128]{1,0:T(8,128)(2,1)S(1)}, bf16[1024,128]{1,0:T(8,128)(2,1)S(1)}, u32[]{:S(2)}, u32[]{:S(2)}) %collective-permute-start.15) | collective-permute-done | bytes 262176 | tf_op jit(solution)/shard_map/ppermute | solution.py:275
  100.7 4.1 %collective-permute-start.22 = (bf16[4,8,32,128]{3,2,1,0:T(8,128)(2,1)S(1)}, bf16[4,8,32,128]{3,2,1,0:T(8,128)(2,1)S(1)}, u32[]{:S(2)}, u32[]{:S(2)}) collective-permute-start(bf16[4,8,32,128]{3,2,1,0:T(8,128)(2,1)S(1)} %get-tuple-element.71.refs_0_), channel_id=1, source_target_pairs={{0,2},{1,3},{2,0},{3,1},{4,6},{5,7},{6,4},{7,5},{8,10},{9,11},{10,... | collective-permute-start | bytes 786440 | tf_op jit(solution)/shard_map/ppermute | solution.py:275
  104.8 3.9 %collective-permute-start.17 = (bf16[4,32,128]{2,1,0:T(8,128)(2,1)S(1)}, bf16[4,32,128]{2,1,0:T(8,128)(2,1)S(1)}, u32[]{:S(2)}, u32[]{:S(2)}) collective-permute-start(bf16[4,32,128]{2,1,0:T(8,128)(2,1)S(1)} %get-tuple-element.72), channel_id=1, source_target_pairs={{0,16},{16,32},{32,48},{48,64},{64,80},{80,96},{96,112},{112,128},... | collective-permute-start | bytes 98312 | tf_op jit(solution)/shard_map/ppermute | solution.py:159
  110.7 4.8 %collective-permute-done.18.bot_ref = bf16[4,32,128]{2,1,0:T(8,128)(2,1)S(1)} collective-permute-done((bf16[4,32,128]{2,1,0:T(8,128)(2,1)S(1)}, bf16[4,32,128]{2,1,0:T(8,128)(2,1)S(1)}, u32[]{:S(2)}, u32[]{:S(2)}) %collective-permute-start.18) | collective-permute-done | bytes 32800 | tf_op jit(solution)/shard_map/ppermute | solution.py:160
  115.5 3.1 %collective-permute-start.20 = (bf16[4,16,128]{2,1,0:T(8,128)(2,1)S(1)}, bf16[4,16,128]{2,1,0:T(8,128)(2,1)S(1)}, u32[]{:S(2)}, u32[]{:S(2)}) collective-permute-start(bf16[4,16,128]{2,1,0:T(8,128)(2,1)S(1)} %get-tuple-element.76), channel_id=1, source_target_pairs={{0,4},{4,8},{8,12},{1,5},{5,9},{9,13},{2,6},{6,10},{10,14},{3,7},{... | collective-permute-start | bytes 49160 | tf_op jit(solution)/shard_map/ppermute | solution.py:166
  119.9 3.2 %collective-permute-done.21.rig_ref = bf16[4,16,128]{2,1,0:T(8,128)(2,1)S(1)} collective-permute-done((bf16[4,16,128]{2,1,0:T(8,128)(2,1)S(1)}, bf16[4,16,128]{2,1,0:T(8,128)(2,1)S(1)}, u32[]{:S(2)}, u32[]{:S(2)}) %collective-permute-start.21) | collective-permute-done | bytes 16416 | tf_op jit(solution)/shard_map/ppermute | solution.py:167
  128.4 2.5 %collective-permute-done.25.refs_5_ = bf16[4,96,128]{2,1,0:T(8,128)(2,1)S(1)} collective-permute-done((bf16[4,96,128]{2,1,0:T(8,128)(2,1)S(1)}, bf16[4,96,128]{2,1,0:T(8,128)(2,1)S(1)}, u32[]{:S(2)}, u32[]{:S(2)}) %collective-permute-start.25) | collective-permute-done | bytes 98336 | tf_op jit(solution)/shard_map/ppermute | solution.py:275
  131.4 4.1 %up_conv.1 = bf16[4,16,64,128]{3,2,1,0:T(8,128)(2,1)} custom-call(bf16[4,8,32,128]{3,2,1,0:T(8,128)(2,1)S(1)} %get-tuple-element.71.refs_0_, bf16[4,96,128]{2,1,0:T(8,128)(2,1)S(1)} %pack.1.refs_1_, bf16[4,8,32,128]{3,2,1,0:T(8,128)(2,1)S(1)} %collective-permute-done.19.rest_0_.refs_2_, bf16[4,96,128]{2,1,0:T(8,128)(2,1)S(1)} %collective-permute-done.24.refs_3_, ...), custom_call_target="tpu_custom_call" | custom-call | tf_op jit(solution)/shard_map/up_conv/pallas_call | solution.py:363
  (50 shorter events, 27.2 us)
Async XLA Ops:
  3.4 33.2 %all-to-all-start = ((f32[64,8,128]{2,1,0:T(8,128)}), f32[64,8,128]{2,1,0:T(8,128)S(1)}, u32[]{:S(2)}, u32[]{:S(2)}) async-start(f32[64,8,128]{2,1,0:T(8,128)} %get-tuple-element.42), calls=%async_computation | async-start | bytes 524288 | tf_op jit(solution)/shard_map/all_to_all | solution.py:84
  14.7 21.9 %collective-permute-start.4 = (bf16[9,128,128]{2,1,0:T(8,128)(2,1)S(1)}, bf16[9,128,128]{2,1,0:T(8,128)(2,1)S(1)}, u32[]{:S(2)}, u32[]{:S(2)}) collective-permute-start(bf16[9,128,128]{2,1,0:T(8,128)(2,1)S(1)} %get-tuple-element.49), channel_id=1, source_target_pairs={{0,1},{1,2},{2,3},{3,0},{4,5},{5,6},{6,7},{7,4},{8,9},{9,10},{10,1... | collective-permute-start | bytes 884744 | tf_op jit(solution)/shard_map/ppermute | solution.py:275
  15.9 20.6 %collective-permute-start.5 = (bf16[9,128,128]{2,1,0:T(8,128)(2,1)S(1)}, bf16[9,128,128]{2,1,0:T(8,128)(2,1)S(1)}, u32[]{:S(2)}, u32[]{:S(2)}) collective-permute-start(bf16[9,128,128]{2,1,0:T(8,128)(2,1)S(1)} %get-tuple-element.50), channel_id=1, source_target_pairs={{0,2},{1,3},{2,0},{3,1},{4,6},{5,7},{6,4},{7,5},{8,10},{9,11},{10,... | collective-permute-start | bytes 884744 | tf_op jit(solution)/shard_map/ppermute | solution.py:275
  18.4 18.2 %collective-permute-start.6 = (bf16[9,128,128]{2,1,0:T(8,128)(2,1)S(1)}, bf16[9,128,128]{2,1,0:T(8,128)(2,1)S(1)}, u32[]{:S(2)}, u32[]{:S(2)}) collective-permute-start(bf16[9,128,128]{2,1,0:T(8,128)(2,1)S(1)} %get-tuple-element.51), channel_id=1, source_target_pairs={{0,3},{1,0},{2,1},{3,2},{4,7},{5,4},{6,5},{7,6},{8,11},{9,8},{10,9... | collective-permute-start | bytes 884744 | tf_op jit(solution)/shard_map/ppermute | solution.py:275
  22.6 7.1 %collective-permute-start.3 = (bf16[8,8,128]{2,1,0:T(8,128)(2,1)S(1)}, bf16[8,8,128]{2,1,0:T(8,128)(2,1)S(1)}, u32[]{:S(2)}, u32[]{:S(2)}) collective-permute-start(bf16[8,8,128]{2,1,0:T(8,128)(2,1)S(1)} %get-tuple-element.48), channel_id=1, source_target_pairs={{4,0},{8,4},{12,8},{5,1},{9,5},{13,9},{6,2},{10,6},{14,10},{7,3},{... | collective-permute-start | bytes 49160 | tf_op jit(solution)/shard_map/ppermute | solution.py:167
  23.9 7.8 %collective-permute-start = (bf16[8,32,128]{2,1,0:T(8,128)(2,1)S(1)}, bf16[8,32,128]{2,1,0:T(8,128)(2,1)S(1)}, u32[]{:S(2)}, u32[]{:S(2)}) collective-permute-start(bf16[8,32,128]{2,1,0:T(8,128)(2,1)S(1)} %get-tuple-element.45), channel_id=1, source_target_pairs={{0,16},{16,32},{32,48},{48,64},{64,80},{80,96},{96,112},{112,128},... | collective-permute-start | bytes 196616 | tf_op jit(solution)/shard_map/ppermute | solution.py:159
  29.8 6.8 %collective-permute-start.1 = (bf16[8,32,128]{2,1,0:T(8,128)(2,1)S(1)}, bf16[8,32,128]{2,1,0:T(8,128)(2,1)S(1)}, u32[]{:S(2)}, u32[]{:S(2)}) collective-permute-start(bf16[8,32,128]{2,1,0:T(8,128)(2,1)S(1)} %get-tuple-element.46), channel_id=1, source_target_pairs={{16,0},{32,16},{48,32},{64,48},{80,64},{96,80},{112,96},{128,112},... | collective-permute-start | bytes 196616 | tf_op jit(solution)/shard_map/ppermute | solution.py:160
  40.9 12.4 %collective-permute-start.7 = (bf16[1024,128]{1,0:T(8,128)(2,1)S(1)}, bf16[1024,128]{1,0:T(8,128)(2,1)S(1)}, u32[]{:S(2)}, u32[]{:S(2)}) collective-permute-start(bf16[1024,128]{1,0:T(8,128)(2,1)S(1)} %get-tuple-element.55), channel_id=1, source_target_pairs={{0,1},{1,2},{2,3},{3,0},{4,5},{5,6},{6,7},{7,4},{8,9},{9,10},{10,1... | collective-permute-start | bytes 786440 | tf_op jit(solution)/shard_map/ppermute | solution.py:275
  41.2 12.0 %collective-permute-start.8 = (bf16[1024,128]{1,0:T(8,128)(2,1)S(1)}, bf16[1024,128]{1,0:T(8,128)(2,1)S(1)}, u32[]{:S(2)}, u32[]{:S(2)}) collective-permute-start(bf16[1024,128]{1,0:T(8,128)(2,1)S(1)} %get-tuple-element.56), channel_id=1, source_target_pairs={{0,2},{1,3},{2,0},{3,1},{4,6},{5,7},{6,4},{7,5},{8,10},{9,11},{10,... | collective-permute-start | bytes 786440 | tf_op jit(solution)/shard_map/ppermute | solution.py:275
  44.0 10.0 %collective-permute-start.9 = (bf16[1024,128]{1,0:T(8,128)(2,1)S(1)}, bf16[1024,128]{1,0:T(8,128)(2,1)S(1)}, u32[]{:S(2)}, u32[]{:S(2)}) collective-permute-start(bf16[1024,128]{1,0:T(8,128)(2,1)S(1)} %get-tuple-element.57), channel_id=1, source_target_pairs={{0,3},{1,0},{2,1},{3,2},{4,7},{5,4},{6,5},{7,6},{8,11},{9,8},{10,9... | collective-permute-start | bytes 786440 | tf_op jit(solution)/shard_map/ppermute | solution.py:275
  56.4 24.7 %all-to-all-start.1 = ((f32[64,8,128]{2,1,0:T(8,128)}), f32[64,8,128]{2,1,0:T(8,128)S(1)}, u32[]{:S(2)}, u32[]{:S(2)}) async-start(f32[64,8,128]{2,1,0:T(8,128)} %get-tuple-element.59), calls=%async_computation.1 | async-start | bytes 524288 | tf_op jit(solution)/shard_map/all_to_all | solution.py:84
  67.1 14.0 %collective-permute-start.10 = (bf16[4,32,128]{2,1,0:T(8,128)(2,1)S(1)}, bf16[4,32,128]{2,1,0:T(8,128)(2,1)S(1)}, u32[]{:S(2)}, u32[]{:S(2)}) collective-permute-start(bf16[4,32,128]{2,1,0:T(8,128)(2,1)S(1)} %get-tuple-element.61), channel_id=1, source_target_pairs={{0,16},{16,32},{32,48},{48,64},{64,80},{80,96},{96,112},{112,128},... | collective-permute-start | bytes 98312 | tf_op jit(solution)/shard_map/ppermute | solution.py:159
  71.7 9.4 %collective-permute-start.11 = (bf16[4,32,128]{2,1,0:T(8,128)(2,1)S(1)}, bf16[4,32,128]{2,1,0:T(8,128)(2,1)S(1)}, u32[]{:S(2)}, u32[]{:S(2)}) collective-permute-start(bf16[4,32,128]{2,1,0:T(8,128)(2,1)S(1)} %get-tuple-element.62), channel_id=1, source_target_pairs={{16,0},{32,16},{48,32},{64,48},{80,64},{96,80},{112,96},{128,112},... | collective-permute-start | bytes 98312 | tf_op jit(solution)/shard_map/ppermute | solution.py:160
  85.4 8.3 %collective-permute-start.14 = (bf16[1024,128]{1,0:T(8,128)(2,1)S(1)}, bf16[1024,128]{1,0:T(8,128)(2,1)S(1)}, u32[]{:S(2)}, u32[]{:S(2)}) collective-permute-start(bf16[1024,128]{1,0:T(8,128)(2,1)S(1)} %get-tuple-element.68), channel_id=1, source_target_pairs={{0,1},{1,2},{2,3},{3,0},{4,5},{5,6},{6,7},{7,4},{8,9},{9,10},{10,1... | collective-permute-start | bytes 786440 | tf_op jit(solution)/shard_map/ppermute | solution.py:275
  85.5 14.6 %collective-permute-start.15 = (bf16[1024,128]{1,0:T(8,128)(2,1)S(1)}, bf16[1024,128]{1,0:T(8,128)(2,1)S(1)}, u32[]{:S(2)}, u32[]{:S(2)}) collective-permute-start(bf16[1024,128]{1,0:T(8,128)(2,1)S(1)} %get-tuple-element.69), channel_id=1, source_target_pairs={{0,2},{1,3},{2,0},{3,1},{4,6},{5,7},{6,4},{7,5},{8,10},{9,11},{10,... | collective-permute-start | bytes 786440 | tf_op jit(solution)/shard_map/ppermute | solution.py:275
  91.2 9.0 %collective-permute-start.16 = (bf16[1024,128]{1,0:T(8,128)(2,1)S(1)}, bf16[1024,128]{1,0:T(8,128)(2,1)S(1)}, u32[]{:S(2)}, u32[]{:S(2)}) collective-permute-start(bf16[1024,128]{1,0:T(8,128)(2,1)S(1)} %get-tuple-element.70), channel_id=1, source_target_pairs={{0,3},{1,0},{2,1},{3,2},{4,7},{5,4},{6,5},{7,6},{8,11},{9,8},{10,9... | collective-permute-start | bytes 786440 | tf_op jit(solution)/shard_map/ppermute | solution.py:275
  100.4 15.1 %collective-permute-start.19 = (bf16[4,8,32,128]{3,2,1,0:T(8,128)(2,1)S(1)}, bf16[4,8,32,128]{3,2,1,0:T(8,128)(2,1)S(1)}, u32[]{:S(2)}, u32[]{:S(2)}) collective-permute-start(bf16[4,8,32,128]{3,2,1,0:T(8,128)(2,1)S(1)} %get-tuple-element.71.refs_0_), channel_id=1, source_target_pairs={{0,1},{1,2},{2,3},{3,0},{4,5},{5,6},{6,7},{7,4},{8,9},{9,10},{10,1... | collective-permute-start | bytes 786440 | tf_op jit(solution)/shard_map/ppermute | solution.py:275
  100.7 19.2 %collective-permute-start.22 = (bf16[4,8,32,128]{3,2,1,0:T(8,128)(2,1)S(1)}, bf16[4,8,32,128]{3,2,1,0:T(8,128)(2,1)S(1)}, u32[]{:S(2)}, u32[]{:S(2)}) collective-permute-start(bf16[4,8,32,128]{3,2,1,0:T(8,128)(2,1)S(1)} %get-tuple-element.71.refs_0_), channel_id=1, source_target_pairs={{0,2},{1,3},{2,0},{3,1},{4,6},{5,7},{6,4},{7,5},{8,10},{9,11},{10,... | collective-permute-start | bytes 786440 | tf_op jit(solution)/shard_map/ppermute | solution.py:275
  104.8 15.1 %collective-permute-start.23 = (bf16[4,8,32,128]{3,2,1,0:T(8,128)(2,1)S(1)}, bf16[4,8,32,128]{3,2,1,0:T(8,128)(2,1)S(1)}, u32[]{:S(2)}, u32[]{:S(2)}) collective-permute-start(bf16[4,8,32,128]{3,2,1,0:T(8,128)(2,1)S(1)} %get-tuple-element.71.refs_0_), channel_id=1, source_target_pairs={{0,3},{1,0},{2,1},{3,2},{4,7},{5,4},{6,5},{7,6},{8,11},{9,8},{10,9... | collective-permute-start | bytes 786440 | tf_op jit(solution)/shard_map/ppermute | solution.py:275
  104.8 5.9 %collective-permute-start.17 = (bf16[4,32,128]{2,1,0:T(8,128)(2,1)S(1)}, bf16[4,32,128]{2,1,0:T(8,128)(2,1)S(1)}, u32[]{:S(2)}, u32[]{:S(2)}) collective-permute-start(bf16[4,32,128]{2,1,0:T(8,128)(2,1)S(1)} %get-tuple-element.72), channel_id=1, source_target_pairs={{0,16},{16,32},{32,48},{48,64},{64,80},{80,96},{96,112},{112,128},... | collective-permute-start | bytes 98312 | tf_op jit(solution)/shard_map/ppermute | solution.py:159
  108.7 6.7 %collective-permute-start.18 = (bf16[4,32,128]{2,1,0:T(8,128)(2,1)S(1)}, bf16[4,32,128]{2,1,0:T(8,128)(2,1)S(1)}, u32[]{:S(2)}, u32[]{:S(2)}) collective-permute-start(bf16[4,32,128]{2,1,0:T(8,128)(2,1)S(1)} %get-tuple-element.73), channel_id=1, source_target_pairs={{16,0},{32,16},{48,32},{64,48},{80,64},{96,80},{112,96},{128,112},... | collective-permute-start | bytes 98312 | tf_op jit(solution)/shard_map/ppermute | solution.py:160
  123.1 5.3 %collective-permute-start.24 = (bf16[4,96,128]{2,1,0:T(8,128)(2,1)S(1)}, bf16[4,96,128]{2,1,0:T(8,128)(2,1)S(1)}, u32[]{:S(2)}, u32[]{:S(2)}) collective-permute-start(bf16[4,96,128]{2,1,0:T(8,128)(2,1)S(1)} %pack.1.refs_1_), channel_id=1, source_target_pairs={{0,1},{1,2},{2,3},{3,0},{4,5},{5,6},{6,7},{7,4},{8,9},{9,10},{10,1... | collective-permute-start | bytes 294920 | tf_op jit(solution)/shard_map/ppermute | solution.py:275
  124.6 6.2 %collective-permute-start.25 = (bf16[4,96,128]{2,1,0:T(8,128)(2,1)S(1)}, bf16[4,96,128]{2,1,0:T(8,128)(2,1)S(1)}, u32[]{:S(2)}, u32[]{:S(2)}) collective-permute-start(bf16[4,96,128]{2,1,0:T(8,128)(2,1)S(1)} %pack.1.refs_1_), channel_id=1, source_target_pairs={{0,2},{1,3},{2,0},{3,1},{4,6},{5,7},{6,4},{7,5},{8,10},{9,11},{10,... | collective-permute-start | bytes 294920 | tf_op jit(solution)/shard_map/ppermute | solution.py:275
  125.6 5.9 %collective-permute-start.26 = (bf16[4,96,128]{2,1,0:T(8,128)(2,1)S(1)}, bf16[4,96,128]{2,1,0:T(8,128)(2,1)S(1)}, u32[]{:S(2)}, u32[]{:S(2)}) collective-permute-start(bf16[4,96,128]{2,1,0:T(8,128)(2,1)S(1)} %pack.1.refs_1_), channel_id=1, source_target_pairs={{0,3},{1,0},{2,1},{3,2},{4,7},{5,4},{6,5},{7,6},{8,11},{9,8},{10,9... | collective-permute-start | bytes 294920 | tf_op jit(solution)/shard_map/ppermute | solution.py:275
  (6 other events, 33.5 us)

commit v4 on v3

--- a/solution.py
+++ b/solution.py
@@ -13,6 +13,7 @@
 GROUP = 16
 ROWS = 8
 COLS = 32
+BLOCK = 4 * ROWS * COLS * GROUP
 MIB = 1 << 20
 CORNERS = ((0, 0), (0, 1), (1, 0), (1, 1))
 
@@ -71,42 +72,49 @@
     return mean, m2
 
 
-def combine(st_ref, count):
-    devices = st_ref.shape[0]
+def merge(st_ref, count):
     means = st_ref[:, 0, :]
-    mean = jnp.sum(means, axis=0, keepdims=True) * (1.0 / devices)
+    mean = jnp.sum(means, axis=0, keepdims=True) * (1.0 / st_ref.shape[0])
     apart = means - mean
-    m2 = jnp.sum(st_ref[:, 1, :] + count * (apart * apart), axis=0, keepdims=True)
-    return mean, lax.rsqrt(m2 * (1.0 / (count * devices)) + 1e-6)
-
-
-def spread(slots):
-    return lax.all_to_all(slots, HA + ("wa",), 0, 0, tiled=True)
-
-
-def diagonals(flag_ref):
-    wa_size = lax.axis_size("wa")
+    return mean, jnp.sum(st_ref[:, 1, :] + count * (apart * apart), axis=0, keepdims=True)
+
+
+def store_stats(ref, mean, m2):
+    row = lax.broadcasted_iota(jnp.int32, ref.shape[1:], 0)
+    ref[...] = jnp.broadcast_to(jnp.where(row == 0, mean, jnp.where(row == 1, m2, 0.0))[None], ref.shape)
+
+
+def mix_body(count, flag_ref, st_ref, top_ref, bot_ref, *rest):
+    o_ref = rest[-1]
+    store_stats(o_ref, *merge(st_ref, count))
+    n = top_ref.shape[0]
+    for c in range(2):
+
+        @pl.when(flag_ref[2 + c] > 0)
+        def _():
+            peer = flag_ref[5] + 2 * c - 1
+            for i, ref in enumerate((top_ref, bot_ref)):
+                pixels = ref[...].astype(F32)[:, c * (COLS - 1), :]
+                o_ref[pl.ds(peer, 1), 2 + i * n : 2 + (i + 1) * n, :] = pixels[None]
+
+
+def spread(flags, stats, rows, after):
+    stats = lax.all_to_all(stats, HA, 0, 0, tiled=True)
+    n = rows[0].shape[0]
+    slots = sds((lax.axis_size("wa"), (2 + 2 * n + 7) // 8 * 8, CH), F32)
+    (slots,) = call(functools.partial(mix_body, BLOCK), [slots], name="mix")(
+        flags, stats, *rows, *[Left(a) for a in after]
+    )
+    return lax.all_to_all(slots, "wa", 0, 0, tiled=True)
+
+
+def corner_pixels(flag_ref, ref, frames, frame):
     found = []
     for r, c in CORNERS:
-        valid = flag_ref[r] * flag_ref[2 + c]
-        found.append((valid, flag_ref[5] + valid * ((2 * r - 1) * wa_size + 2 * c - 1)))
+        inside = flag_ref[2 + c]
+        source = flag_ref[5] + inside * (2 * c - 1)
+        found.append((inside * flag_ref[r], ref[pl.ds(source, 1), 2 + r * frames + frame, :]))
     return found
-
-
-def fill_slots(slot_ref, flag_ref, mean, m2, frames):
-    row = lax.broadcasted_iota(jnp.int32, (8, CH), 0)
-    base = jnp.where(row == 0, mean, jnp.where(row == 1, m2, 0.0))
-    slot_ref[...] = jnp.broadcast_to(base[None], slot_ref.shape)
-    for (r, c), (valid, at) in zip(CORNERS, diagonals(flag_ref)):
-
-        @pl.when(valid > 0)
-        def _():
-            f = 0
-            for v in frames:
-                for i in range(v.shape[0]):
-                    pixel = v[i, r * (ROWS - 1), c * (COLS - 1) : c * (COLS - 1) + 1, :]
-                    slot_ref[pl.ds(at, 1), 2 + f, :] = pixel
-                    f += 1
 
 
 def store_edges(frames, refs, pad=0):
@@ -136,7 +144,7 @@
         c.wait()
     x, c1, c2 = x_ref[...].astype(F32), c1_ref[...].astype(F32), c2_ref[...].astype(F32)
     mean, m2 = local_stats(x.reshape(-1, CH))
-    fill_slots(slot_ref, flag_ref, mean, m2, (c1, x))
+    store_stats(slot_ref, mean, m2)
     store_edges((c1, x, c2), edges)
     for c in copies[3:]:
         c.wait()
@@ -205,7 +213,9 @@
             out[t * size : (t + 1) * size, :] = acc[:, i * CH : (i + 1) * CH].astype(BF16)
 
 
-def far_body(cache_at, act_at, extra, flag_ref, st_ref, x_ref, c_ref, tc, bc, lc, rc, ta, ba, la, ra, w_hbm, *rest):
+def far_body(
+    cache_at, act_at, extra, flag_ref, x_ref, c_ref, tc, bc, lc, rc, pc, ta, ba, la, ra, st_ref, w_hbm, *rest
+):
     out2, out1, patch_ref, near_ref, w_ref, sem = rest[extra:]
     col = flag_ref[4]
     copies = []
@@ -216,22 +226,24 @@
         )
         copies[-1].start()
     has = [flag_ref[i] > 0 for i in range(4)]
-    mean, scale = combine(st_ref, x_ref.shape[0] * ROWS * COLS * GROUP)
+    count = BLOCK * lax.axis_size(HA)
+    mean, m2 = merge(st_ref, count)
+    scale = lax.rsqrt(m2 * (1.0 / (count * st_ref.shape[0])) + 1e-6)
 
     def act(v):
         u = (v - mean) * scale
         return u / (1.0 + jnp.exp(-u))
 
     lanes = (0, CH, 2 * CH)
-    across = diagonals(flag_ref)
     for s in range(6):
         if s < 2:
-            own, at, halo, change = c_ref[s], cache_at + s, (tc, bc, lc, rc), lambda v: v
+            own, at, halo, pixels, change = c_ref[s], cache_at + s, (tc, bc, lc, rc), pc, lambda v: v
         else:
-            own, at, halo, change = x_ref[s - 2], act_at + s - 2, (ta, ba, la, ra), act
+            own, at, halo, pixels, change = x_ref[s - 2], act_at + s - 2, (ta, ba, la, ra), st_ref, act
         sides = [jnp.where(has[i], change(ref[at].astype(F32)), 0.0) for i, ref in enumerate(halo)]
         corners = [
-            jnp.where(valid > 0, change(st_ref[pl.ds(slot, 1), 2 + s, :]), 0.0) for valid, slot in across
+            jnp.where(inside > 0, change(v), 0.0)
+            for inside, v in corner_pixels(flag_ref, pixels, halo[0].shape[0], at)
         ]
         place_frame(patch_ref, s, change(own.astype(F32)), *sides, corners, lanes)
     copies[0].wait()
@@ -245,7 +257,7 @@
     multiply(patch_ref, w_ref, (out3, out0))
 
 
-def conv(flags, stats, x, cache, cache_halo, cache_at, act_halo, act_at, weight, name, after=()):
+def conv(flags, x, cache, cache_halo, cache_at, act_halo, act_at, weight, name, after=()):
     n = x.shape[0] * ROWS * COLS
     depth, width = weight.shape
     flops = n * depth * width
@@ -258,7 +270,7 @@
         flops=flops,
         limit=20,
         name=name + "_far",
-    )(flags, stats, x, cache, *cache_halo, *act_halo, Left(weight, HBM), *[Left(a) for a in after])
+    )(flags, x, cache, *cache_halo, *act_halo, Left(weight, HBM), *[Left(a) for a in after])
     got2 = to_peer(out2, 2)
     got1 = to_peer(out1, 1)
     out3, own = call(near_body, [piece] * 2, flops=flops, limit=16, name=name + "_near")(patch, near)
@@ -280,14 +292,13 @@
     return [got[k] for k in (1, 2, 3)]
 
 
-def hidden_body(flag_ref, p0, far, p3, c2_ref, h_ref, slot_ref, *edges):
+def hidden_body(p0, far, p3, h_ref, slot_ref, *edges):
     h = (p0[...].astype(F32) + p3[...].astype(F32) + far[...]).astype(BF16)
     h_ref[...] = h.reshape(h_ref.shape)
     h = h.astype(F32)
     mean, m2 = local_stats(h)
-    h = h.reshape(h_ref.shape)
-    fill_slots(slot_ref, flag_ref, mean, m2, (c2_ref[...].astype(F32), h))
-    store_edges((h,), edges)
+    store_stats(slot_ref, mean, m2)
+    store_edges((h.reshape(h_ref.shape),), edges)
 
 
 def resid_body(x_ref, p0, far, p3, h_ref, *edges):
@@ -379,8 +390,8 @@
     frames = features.shape[0]
     ha, wa, col = lax.axis_index(HA), lax.axis_index("wa"), lax.axis_index("col")
     nh, nw = lax.axis_size(HA), lax.axis_size("wa")
-    flags = jnp.stack([ha > 0, ha < nh - 1, wa > 0, wa < nw - 1, col, ha * nw + wa]).astype(jnp.int32)
-    slots = sds((nh * nw, 8, CH), F32)
+    flags = jnp.stack([ha > 0, ha < nh - 1, wa > 0, wa < nw - 1, col, wa]).astype(jnp.int32)
+    slots = sds((nh, 2, CH), F32)
 
     x, c1, c2, stats, *edges = call(
         first_body,
@@ -394,23 +405,21 @@
     )(flags, *[Left(a, HBM) for a in (features, cache_first, cache_second, weight_up)])
     edges, w_pieces = edges[:4], edges[4:]
     w_got = to_peers(w_pieces[1:])
-    halo = swap_rows(*edges[:2]) + swap_columns(*edges[2:])
-    stats = spread(stats)
-    pieces = conv(
-        flags, stats, x, c1, halo, 0, halo, 2, weight_first.reshape(-1, 4 * CH), "conv_first", after=w_got
-    )
+    rows = swap_rows(*edges[:2])
+    columns = swap_columns(*edges[2:])
+    halo = rows + columns + (spread(flags, stats, rows, ()),)
+    pieces = conv(flags, x, c1, halo, 0, halo, 2, weight_first.reshape(-1, 4 * CH), "conv_first", after=w_got)
     hidden, stats, *edges = call(
         hidden_body,
         [sds(features.shape), slots] + [sds((frames, COLS, CH))] * 2 + [sds((frames, ROWS, CH))] * 2,
         limit=12,
         name="hidden",
-    )(flags, *pieces, c2)
-    halo2 = swap_rows(*edges[:2]) + swap_columns(*edges[2:])
-    stats = spread(stats)
+    )(*pieces)
+    rows = swap_rows(*edges[:2])
+    columns = swap_columns(*edges[2:])
+    halo2 = rows + columns + (spread(flags, stats, rows, columns),)
     (folded,) = call(fold_body, [sds((2, 2, 8 * CH, 2 * CH))], limit=12, name="fold")(w_pieces[0], *w_got)
-    pieces = conv(
-        flags, stats, hidden, c2, halo, 6, halo2, 0, weight_second.reshape(-1, 4 * CH), "conv_second"
-    )
+    pieces = conv(flags, hidden, c2, halo, 6, halo2, 0, weight_second.reshape(-1, 4 * CH), "conv_second")
     resid, *edges = call(
         resid_body,
         [sds(features.shape)] + [sds((frames, COLS, CH))] * 2 + [sds((frames, 16, CH))] * 2,

time: 137 us -> 144 us (1.051)
  blocking collectives: 0 us -> 18.5 us
  starting transfers between devices: 75.8 us -> 68.1 us
  waiting for transfers between devices: 36 us -> 32.2 us
    all_to_all x0 -> x2, blocking collectives: none -> 18.5 us  [the longest x1 11.8 us: spread(): stats = lax.all_to_all(stats, HA, 0, 0, tiled=True)]
    all_to_all x2, starting transfers between devices: 21.9 us -> 11.7 us  [the longest x1 7.54 us: spread(): stats = lax.all_to_all(stats, HA, 0, 0, tiled=True)]
    ppermute x3, waiting for transfers between devices: 9.66 us -> 4.51 us  [swap_rows(): below = lax.ppermute(top, HA, [(i + 1, i) for i in range(n - 1)])]
    ppermute x3, starting transfers between devices: 14.3 us -> 18.6 us  [swap_rows(): above = lax.ppermute(bot, HA, [(i, i + 1) for i in range(n - 1)])]
    ppermute x3, waiting for transfers between devices: 6.06 us -> 9.41 us  [swap_columns(): right = lax.ppermute(lef, 'wa', [(i + 1, i) for i in range(n - 1)])]
    ppermute x15, waiting for transfers between devices: 20.3 us -> 18.3 us  [to_peer(): return lax.ppermute(piece, 'col', [(i, (i + k) % n) for i in range(n)])]
    pallas_call x12 -> x14, Pallas kernels: 19.2 us -> 19.5 us  [run(): pl.pallas_call(body, out_shape=list(outs), in_specs=specs, out_specs=[VME...]
where the time goes in v4:
time: 144 us; the launch traced here: 143 us
  starting transfers between devices  68.1 us (47%)
  waiting for transfers between devices  32.2 us (22%)
  Pallas kernels  23.6 us (16%)
  blocking collectives  18.5 us (13%)
    pallas_call x14, Pallas kernels, run(): pl.pallas_call(body, out_shape=list(outs), in_specs=specs, out_specs=[VME...  19.5 us
    ppermute x15, starting transfers between devices, to_peer(): return lax.ppermute(piece, 'col', [(i, (i + k) % n) for i in range(n)])  19.5 us
    ppermute x3, starting transfers between devices, swap_rows(): above = lax.ppermute(bot, HA, [(i, i + 1) for i in range(n - 1)])  18.6 us
    ppermute x15, waiting for transfers between devices, to_peer(): return lax.ppermute(piece, 'col', [(i, (i + k) % n) for i in range(n)])  18.3 us
    all_to_all x1, blocking collectives, spread(): stats = lax.all_to_all(stats, HA, 0, 0, tiled=True)  11.8 us
    ppermute x3, waiting for transfers between devices, swap_columns(): right = lax.ppermute(lef, 'wa', [(i + 1, i) for i in range(n - 1)])  9.41 us
    ppermute x3, starting transfers between devices, swap_columns(): left = lax.ppermute(rig, 'wa', [(i, i + 1) for i in range(n - 1)])  8.63 us
    all_to_all x1, starting transfers between devices, spread(): stats = lax.all_to_all(stats, HA, 0, 0, tiled=True)  7.54 us
  transfers between devices with their start and end apart: 29, of which 11 were waited for; matrix products, arithmetic and copies ran while one was open for 0% of the time, Pallas kernels for 4%

profile of v4, /device:TPU:97, one launch (start us, length us, event | category | flops | bytes accessed | tf_op | source)
XLA Modules:
  0.0 142.7 jit_solution(4579233372017986466)
XLA Ops:
  0.1 2.5 %first.1 = (bf16[4,8,32,128]{3,2,1,0:T(8,128)(2,1)S(1)}, bf16[2,8,32,128]{3,2,1,0:T(8,128)(2,1)S(1)}, bf16[2,8,32,128]{3,2,1,0:T(8,128)(2,1)S(1)}, f32[16,2,128]...) custom-call(s32[6]{0:T(128)S(1)} %stack.43.flag_ref, ...), custom_call_target="tpu_custom_call" | custom-call | bytes 3588120 | tf_op jit(solution)/shard_map/first/pallas_call | solution.py:39
  3.9 2.5 %collective-permute-start.5 = (bf16[9,128,128]{2,1,0:T(8,128)(2,1)S(1)}, bf16[9,128,128]{2,1,0:T(8,128)(2,1)S(1)}, u32[]{:S(2)}, u32[]{:S(2)}) collective-permute-start(bf16[9,128,128]{2,1,0:T(8,128)(2,1)S(1)} %get-tuple-element.50), channel_id=1, source_target_pairs={{0,2},{1,3},{2,0},{3,1},{4,6},{5,7},{6,4},{7,5},{8,10},{9,11},{10,... | collective-permute-start | bytes 884744 | tf_op jit(solution)/shard_map/ppermute | solution.py:287
  7.5 6.1 %collective-permute-start = (bf16[8,32,128]{2,1,0:T(8,128)(2,1)S(1)}, bf16[8,32,128]{2,1,0:T(8,128)(2,1)S(1)}, u32[]{:S(2)}, u32[]{:S(2)}) collective-permute-start(bf16[8,32,128]{2,1,0:T(8,128)(2,1)S(1)} %get-tuple-element.44), channel_id=1, source_target_pairs={{0,16},{16,32},{32,48},{48,64},{64,80},{80,96},{96,112},{112,128},... | collective-permute-start | bytes 196616 | tf_op jit(solution)/shard_map/ppermute | solution.py:167
  15.6 11.8 %all_to_all.20.st_ref = f32[16,2,128]{2,1,0:T(2,128)S(1)} all-to-all(f32[16,2,128]{2,1,0:T(2,128)S(1)} %get-tuple-element.48), channel_id=1, replica_groups=mesh['z'=8,'core'=2,'wa'=4,'col'=4] {'z','core'}, dimensions={0} | all-to-all | bytes 32768 | tf_op jit(solution)/shard_map/all_to_all | solution.py:102
  28.6 4.2 %all-to-all-start.1 = ((f32[4,24,128]{2,1,0:T(8,128)}), f32[4,24,128]{2,1,0:T(8,128)S(1)}, u32[]{:S(2)}, u32[]{:S(2)}) async-start(f32[4,24,128]{2,1,0:T(8,128)} %mix.2), calls=%async_computation.1 | async-start | bytes 98304 | tf_op jit(solution)/shard_map/all_to_all | solution.py:108
  32.8 3.4 %collective-permute-start.2 = (bf16[8,8,128]{2,1,0:T(8,128)(2,1)S(1)}, bf16[8,8,128]{2,1,0:T(8,128)(2,1)S(1)}, u32[]{:S(2)}, u32[]{:S(2)}) collective-permute-start(bf16[8,8,128]{2,1,0:T(8,128)(2,1)S(1)} %get-tuple-element.46), channel_id=1, source_target_pairs={{0,4},{4,8},{8,12},{1,5},{5,9},{9,13},{2,6},{6,10},{10,14},{3,7},{... | collective-permute-start | bytes 49160 | tf_op jit(solution)/shard_map/ppermute | solution.py:174
  37.5 3.2 %collective-permute-done.3.rc.ra = bf16[8,8,128]{2,1,0:T(8,128)(2,1)S(1)} collective-permute-done((bf16[8,8,128]{2,1,0:T(8,128)(2,1)S(1)}, bf16[8,8,128]{2,1,0:T(8,128)(2,1)S(1)}, u32[]{:S(2)}, u32[]{:S(2)}) %collective-permute-start.3) | collective-permute-done | bytes 16416 | tf_op jit(solution)/shard_map/ppermute | solution.py:175
  40.6 4.2 %conv_first_far.1 = (bf16[1024,128]{1,0:T(8,128)(2,1)S(1)}, bf16[1024,128]{1,0:T(8,128)(2,1)S(1)}, bf16[6,320,384]{2,1,0:T(8,128)(2,1)S(1)}, bf16[3456,256]{1,0:T(8,128)(2,1)S(1)}) custom-call(s32[6]{0:T(128)S(1)} %stack.43.flag_ref, bf16[4,8,32,128]{3,2,1,0:T(8,128)(2,1)S(1)} %get-tuple-element.42.x_ref, ...), custom_call_target="tpu_custom_call" | custom-call | flops 1811939328 | bytes 9011224 | tf_op jit(solution)/shard_map/conv_first_far/pallas_call | solution.py:39
  50.0 5.2 %collective-permute-done.7.a_ref = bf16[1024,128]{1,0:T(8,128)(2,1)S(1)} collective-permute-done((bf16[1024,128]{1,0:T(8,128)(2,1)S(1)}, bf16[1024,128]{1,0:T(8,128)(2,1)S(1)}, u32[]{:S(2)}, u32[]{:S(2)}) %collective-permute-start.7) | collective-permute-done | bytes 262176 | tf_op jit(solution)/shard_map/ppermute | solution.py:287
  55.3 2.7 %collective-permute-done.9.p3 = bf16[1024,128]{1,0:T(8,128)(2,1)S(1)} collective-permute-done((bf16[1024,128]{1,0:T(8,128)(2,1)S(1)}, bf16[1024,128]{1,0:T(8,128)(2,1)S(1)}, u32[]{:S(2)}, u32[]{:S(2)}) %collective-permute-start.9) | collective-permute-done | bytes 262176 | tf_op jit(solution)/shard_map/ppermute | solution.py:287
  59.7 5.1 %collective-permute-start.10 = (bf16[4,32,128]{2,1,0:T(8,128)(2,1)S(1)}, bf16[4,32,128]{2,1,0:T(8,128)(2,1)S(1)}, u32[]{:S(2)}, u32[]{:S(2)}) collective-permute-start(bf16[4,32,128]{2,1,0:T(8,128)(2,1)S(1)} %get-tuple-element.60), channel_id=1, source_target_pairs={{0,16},{16,32},{32,48},{48,64},{64,80},{80,96},{96,112},{112,128},... | collective-permute-start | bytes 98312 | tf_op jit(solution)/shard_map/ppermute | solution.py:167
  66.8 7.5 %all-to-all-start.2 = ((f32[16,2,128]{2,1,0:T(2,128)}), f32[16,2,128]{2,1,0:T(2,128)S(1)}, u32[]{:S(2)}, u32[]{:S(2)}) async-start(f32[16,2,128]{2,1,0:T(2,128)} %get-tuple-element.64), calls=%async_computation.2 | async-start | bytes 32768 | tf_op jit(solution)/shard_map/all_to_all | solution.py:102
  74.3 3.1 %collective-permute-start.12 = (bf16[4,8,128]{2,1,0:T(8,128)(2,1)S(1)}, bf16[4,8,128]{2,1,0:T(8,128)(2,1)S(1)}, u32[]{:S(2)}, u32[]{:S(2)}) collective-permute-start(bf16[4,8,128]{2,1,0:T(8,128)(2,1)S(1)} %get-tuple-element.62), channel_id=1, source_target_pairs={{0,4},{4,8},{8,12},{1,5},{5,9},{9,13},{2,6},{6,10},{10,14},{3,7},{... | collective-permute-start | bytes 24584 | tf_op jit(solution)/shard_map/ppermute | solution.py:174
  78.7 3.1 %collective-permute-done.13.rest_1_.ra = bf16[4,8,128]{2,1,0:T(8,128)(2,1)S(1)} collective-permute-done((bf16[4,8,128]{2,1,0:T(8,128)(2,1)S(1)}, bf16[4,8,128]{2,1,0:T(8,128)(2,1)S(1)}, u32[]{:S(2)}, u32[]{:S(2)}) %collective-permute-start.13) | collective-permute-done | bytes 8224 | tf_op jit(solution)/shard_map/ppermute | solution.py:175
  82.4 6.7 %all_to_all.21.st_ref = f32[4,16,128]{2,1,0:T(8,128)S(1)} all-to-all(f32[4,16,128]{2,1,0:T(8,128)S(1)} %mix.3), channel_id=1, replica_groups=mesh['z'=8,'core'=2,'wa'=4,'col'=4] {'wa'}, dimensions={0} | all-to-all | bytes 65536 | tf_op jit(solution)/shard_map/all_to_all | solution.py:108
  89.1 4.2 %conv_second_far.1 = (bf16[1024,128]{1,0:T(8,128)(2,1)S(1)}, bf16[1024,128]{1,0:T(8,128)(2,1)S(1)}, bf16[6,320,384]{2,1,0:T(8,128)(2,1)S(1)}, bf16[3456,256]{1,0:T(8,128)(2,1)S(1)}) custom-call(s32[6]{0:T(128)S(1)} %stack.43.flag_ref, bf16[4,8,32,128]{3,2,1,0:T(8,128)(2,1)S(1)} %get-tuple-element.58.x_ref, ...), custom_call_target="tpu_custom_call" | custom-call | flops 1811939328 | bytes 8028184 | tf_op jit(solution)/shard_map/conv_second_far/pallas_call | solution.py:39
  93.8 3.1 %collective-permute-start.15 = (bf16[1024,128]{1,0:T(8,128)(2,1)S(1)}, bf16[1024,128]{1,0:T(8,128)(2,1)S(1)}, u32[]{:S(2)}, u32[]{:S(2)}) collective-permute-start(bf16[1024,128]{1,0:T(8,128)(2,1)S(1)} %get-tuple-element.69), channel_id=1, source_target_pairs={{0,2},{1,3},{2,0},{3,1},{4,6},{5,7},{6,4},{7,5},{8,10},{9,11},{10,... | collective-permute-start | bytes 786440 | tf_op jit(solution)/shard_map/ppermute | solution.py:287
  99.8 5.9 %collective-permute-done.15.b_ref = bf16[1024,128]{1,0:T(8,128)(2,1)S(1)} collective-permute-done((bf16[1024,128]{1,0:T(8,128)(2,1)S(1)}, bf16[1024,128]{1,0:T(8,128)(2,1)S(1)}, u32[]{:S(2)}, u32[]{:S(2)}) %collective-permute-start.15) | collective-permute-done | bytes 262176 | tf_op jit(solution)/shard_map/ppermute | solution.py:287
  108.2 2.6 %collective-permute-start.22 = (bf16[4,8,32,128]{3,2,1,0:T(8,128)(2,1)S(1)}, bf16[4,8,32,128]{3,2,1,0:T(8,128)(2,1)S(1)}, u32[]{:S(2)}, u32[]{:S(2)}) collective-permute-start(bf16[4,8,32,128]{3,2,1,0:T(8,128)(2,1)S(1)} %get-tuple-element.71.refs_0_), channel_id=1, source_target_pairs={{0,2},{1,3},{2,0},{3,1},{4,6},{5,7},{6,4},{7,5},{8,10},{9,11},{10,... | collective-permute-start | bytes 786440 | tf_op jit(solution)/shard_map/ppermute | solution.py:287
  110.8 7.3 %collective-permute-start.17 = (bf16[4,32,128]{2,1,0:T(8,128)(2,1)S(1)}, bf16[4,32,128]{2,1,0:T(8,128)(2,1)S(1)}, u32[]{:S(2)}, u32[]{:S(2)}) collective-permute-start(bf16[4,32,128]{2,1,0:T(8,128)(2,1)S(1)} %get-tuple-element.72), channel_id=1, source_target_pairs={{0,16},{16,32},{32,48},{48,64},{64,80},{80,96},{96,112},{112,128},... | collective-permute-start | bytes 98312 | tf_op jit(solution)/shard_map/ppermute | solution.py:167
  120.1 4.5 %collective-permute-done.18.bot_ref = bf16[4,32,128]{2,1,0:T(8,128)(2,1)S(1)} collective-permute-done((bf16[4,32,128]{2,1,0:T(8,128)(2,1)S(1)}, bf16[4,32,128]{2,1,0:T(8,128)(2,1)S(1)}, u32[]{:S(2)}, u32[]{:S(2)}) %collective-permute-start.18) | collective-permute-done | bytes 32800 | tf_op jit(solution)/shard_map/ppermute | solution.py:168
  124.6 2.2 %collective-permute-start.20 = (bf16[4,16,128]{2,1,0:T(8,128)(2,1)S(1)}, bf16[4,16,128]{2,1,0:T(8,128)(2,1)S(1)}, u32[]{:S(2)}, u32[]{:S(2)}) collective-permute-start(bf16[4,16,128]{2,1,0:T(8,128)(2,1)S(1)} %get-tuple-element.76), channel_id=1, source_target_pairs={{0,4},{4,8},{8,12},{1,5},{5,9},{9,13},{2,6},{6,10},{10,14},{3,7},{... | collective-permute-start | bytes 49160 | tf_op jit(solution)/shard_map/ppermute | solution.py:174
  128.1 3.2 %collective-permute-done.21.rig_ref = bf16[4,16,128]{2,1,0:T(8,128)(2,1)S(1)} collective-permute-done((bf16[4,16,128]{2,1,0:T(8,128)(2,1)S(1)}, bf16[4,16,128]{2,1,0:T(8,128)(2,1)S(1)}, u32[]{:S(2)}, u32[]{:S(2)}) %collective-permute-start.21) | collective-permute-done | bytes 16416 | tf_op jit(solution)/shard_map/ppermute | solution.py:175
  138.6 4.1 %up_conv.1 = bf16[4,16,64,128]{3,2,1,0:T(8,128)(2,1)} custom-call(bf16[4,8,32,128]{3,2,1,0:T(8,128)(2,1)S(1)} %get-tuple-element.71.refs_0_, bf16[4,96,128]{2,1,0:T(8,128)(2,1)S(1)} %pack.1.refs_1_, bf16[4,8,32,128]{3,2,1,0:T(8,128)(2,1)S(1)} %collective-permute-done.19.rest_0_.refs_2_, bf16[4,96,128]{2,1,0:T(8,128)(2,1)S(1)} %collective-permute-done.24.refs_3_, ...), custom_call_target="tpu_custom_call" | custom-call | tf_op jit(solution)/shard_map/up_conv/pallas_call | solution.py:374
  (54 shorter events, 34.0 us)
Async XLA Ops:
  2.6 38.0 %collective-permute-start.4 = (bf16[9,128,128]{2,1,0:T(8,128)(2,1)S(1)}, bf16[9,128,128]{2,1,0:T(8,128)(2,1)S(1)}, u32[]{:S(2)}, u32[]{:S(2)}) collective-permute-start(bf16[9,128,128]{2,1,0:T(8,128)(2,1)S(1)} %get-tuple-element.49), channel_id=1, source_target_pairs={{0,1},{1,2},{2,3},{3,0},{4,5},{5,6},{6,7},{7,4},{8,9},{9,10},{10,1... | collective-permute-start | bytes 884744 | tf_op jit(solution)/shard_map/ppermute | solution.py:287
  3.9 36.7 %collective-permute-start.5 = (bf16[9,128,128]{2,1,0:T(8,128)(2,1)S(1)}, bf16[9,128,128]{2,1,0:T(8,128)(2,1)S(1)}, u32[]{:S(2)}, u32[]{:S(2)}) collective-permute-start(bf16[9,128,128]{2,1,0:T(8,128)(2,1)S(1)} %get-tuple-element.50), channel_id=1, source_target_pairs={{0,2},{1,3},{2,0},{3,1},{4,6},{5,7},{6,4},{7,5},{8,10},{9,11},{10,... | collective-permute-start | bytes 884744 | tf_op jit(solution)/shard_map/ppermute | solution.py:287
  6.3 34.3 %collective-permute-start.6 = (bf16[9,128,128]{2,1,0:T(8,128)(2,1)S(1)}, bf16[9,128,128]{2,1,0:T(8,128)(2,1)S(1)}, u32[]{:S(2)}, u32[]{:S(2)}) collective-permute-start(bf16[9,128,128]{2,1,0:T(8,128)(2,1)S(1)} %get-tuple-element.51), channel_id=1, source_target_pairs={{0,3},{1,0},{2,1},{3,2},{4,7},{5,4},{6,5},{7,6},{8,11},{9,8},{10,9... | collective-permute-start | bytes 884744 | tf_op jit(solution)/shard_map/ppermute | solution.py:287
  7.5 19.9 %collective-permute-start = (bf16[8,32,128]{2,1,0:T(8,128)(2,1)S(1)}, bf16[8,32,128]{2,1,0:T(8,128)(2,1)S(1)}, u32[]{:S(2)}, u32[]{:S(2)}) collective-permute-start(bf16[8,32,128]{2,1,0:T(8,128)(2,1)S(1)} %get-tuple-element.44), channel_id=1, source_target_pairs={{0,16},{16,32},{32,48},{48,64},{64,80},{80,96},{96,112},{112,128},... | collective-permute-start | bytes 196616 | tf_op jit(solution)/shard_map/ppermute | solution.py:167
  13.7 13.7 %collective-permute-start.1 = (bf16[8,32,128]{2,1,0:T(8,128)(2,1)S(1)}, bf16[8,32,128]{2,1,0:T(8,128)(2,1)S(1)}, u32[]{:S(2)}, u32[]{:S(2)}) collective-permute-start(bf16[8,32,128]{2,1,0:T(8,128)(2,1)S(1)} %get-tuple-element.45), channel_id=1, source_target_pairs={{16,0},{32,16},{48,32},{64,48},{80,64},{96,80},{112,96},{128,112},... | collective-permute-start | bytes 196616 | tf_op jit(solution)/shard_map/ppermute | solution.py:168
  28.6 12.0 %all-to-all-start.1 = ((f32[4,24,128]{2,1,0:T(8,128)}), f32[4,24,128]{2,1,0:T(8,128)S(1)}, u32[]{:S(2)}, u32[]{:S(2)}) async-start(f32[4,24,128]{2,1,0:T(8,128)} %mix.2), calls=%async_computation.1 | async-start | bytes 98304 | tf_op jit(solution)/shard_map/all_to_all | solution.py:108
  32.8 4.7 %collective-permute-start.2 = (bf16[8,8,128]{2,1,0:T(8,128)(2,1)S(1)}, bf16[8,8,128]{2,1,0:T(8,128)(2,1)S(1)}, u32[]{:S(2)}, u32[]{:S(2)}) collective-permute-start(bf16[8,8,128]{2,1,0:T(8,128)(2,1)S(1)} %get-tuple-element.46), channel_id=1, source_target_pairs={{0,4},{4,8},{8,12},{1,5},{5,9},{9,13},{2,6},{6,10},{10,14},{3,7},{... | collective-permute-start | bytes 49160 | tf_op jit(solution)/shard_map/ppermute | solution.py:174
  44.9 10.4 %collective-permute-start.7 = (bf16[1024,128]{1,0:T(8,128)(2,1)S(1)}, bf16[1024,128]{1,0:T(8,128)(2,1)S(1)}, u32[]{:S(2)}, u32[]{:S(2)}) collective-permute-start(bf16[1024,128]{1,0:T(8,128)(2,1)S(1)} %get-tuple-element.55), channel_id=1, source_target_pairs={{0,1},{1,2},{2,3},{3,0},{4,5},{5,6},{6,7},{7,4},{8,9},{9,10},{10,1... | collective-permute-start | bytes 786440 | tf_op jit(solution)/shard_map/ppermute | solution.py:287
  45.3 10.0 %collective-permute-start.8 = (bf16[1024,128]{1,0:T(8,128)(2,1)S(1)}, bf16[1024,128]{1,0:T(8,128)(2,1)S(1)}, u32[]{:S(2)}, u32[]{:S(2)}) collective-permute-start(bf16[1024,128]{1,0:T(8,128)(2,1)S(1)} %get-tuple-element.56), channel_id=1, source_target_pairs={{0,2},{1,3},{2,0},{3,1},{4,6},{5,7},{6,4},{7,5},{8,10},{9,11},{10,... | collective-permute-start | bytes 786440 | tf_op jit(solution)/shard_map/ppermute | solution.py:287
  48.1 10.0 %collective-permute-start.9 = (bf16[1024,128]{1,0:T(8,128)(2,1)S(1)}, bf16[1024,128]{1,0:T(8,128)(2,1)S(1)}, u32[]{:S(2)}, u32[]{:S(2)}) collective-permute-start(bf16[1024,128]{1,0:T(8,128)(2,1)S(1)} %get-tuple-element.57), channel_id=1, source_target_pairs={{0,3},{1,0},{2,1},{3,2},{4,7},{5,4},{6,5},{7,6},{8,11},{9,8},{10,9... | collective-permute-start | bytes 786440 | tf_op jit(solution)/shard_map/ppermute | solution.py:287
  59.7 22.1 %collective-permute-start.10 = (bf16[4,32,128]{2,1,0:T(8,128)(2,1)S(1)}, bf16[4,32,128]{2,1,0:T(8,128)(2,1)S(1)}, u32[]{:S(2)}, u32[]{:S(2)}) collective-permute-start(bf16[4,32,128]{2,1,0:T(8,128)(2,1)S(1)} %get-tuple-element.60), channel_id=1, source_target_pairs={{0,16},{16,32},{32,48},{48,64},{64,80},{80,96},{96,112},{112,128},... | collective-permute-start | bytes 98312 | tf_op jit(solution)/shard_map/ppermute | solution.py:167
  64.9 17.0 %collective-permute-start.11 = (bf16[4,32,128]{2,1,0:T(8,128)(2,1)S(1)}, bf16[4,32,128]{2,1,0:T(8,128)(2,1)S(1)}, u32[]{:S(2)}, u32[]{:S(2)}) collective-permute-start(bf16[4,32,128]{2,1,0:T(8,128)(2,1)S(1)} %get-tuple-element.61), channel_id=1, source_target_pairs={{16,0},{32,16},{48,32},{64,48},{80,64},{96,80},{112,96},{128,112},... | collective-permute-start | bytes 98312 | tf_op jit(solution)/shard_map/ppermute | solution.py:168
  66.8 15.0 %all-to-all-start.2 = ((f32[16,2,128]{2,1,0:T(2,128)}), f32[16,2,128]{2,1,0:T(2,128)S(1)}, u32[]{:S(2)}, u32[]{:S(2)}) async-start(f32[16,2,128]{2,1,0:T(2,128)} %get-tuple-element.64), calls=%async_computation.2 | async-start | bytes 32768 | tf_op jit(solution)/shard_map/all_to_all | solution.py:102
  93.3 6.5 %collective-permute-start.14 = (bf16[1024,128]{1,0:T(8,128)(2,1)S(1)}, bf16[1024,128]{1,0:T(8,128)(2,1)S(1)}, u32[]{:S(2)}, u32[]{:S(2)}) collective-permute-start(bf16[1024,128]{1,0:T(8,128)(2,1)S(1)} %get-tuple-element.68), channel_id=1, source_target_pairs={{0,1},{1,2},{2,3},{3,0},{4,5},{5,6},{6,7},{7,4},{8,9},{9,10},{10,1... | collective-permute-start | bytes 786440 | tf_op jit(solution)/shard_map/ppermute | solution.py:287
  93.8 11.8 %collective-permute-start.15 = (bf16[1024,128]{1,0:T(8,128)(2,1)S(1)}, bf16[1024,128]{1,0:T(8,128)(2,1)S(1)}, u32[]{:S(2)}, u32[]{:S(2)}) collective-permute-start(bf16[1024,128]{1,0:T(8,128)(2,1)S(1)} %get-tuple-element.69), channel_id=1, source_target_pairs={{0,2},{1,3},{2,0},{3,1},{4,6},{5,7},{6,4},{7,5},{8,10},{9,11},{10,... | collective-permute-start | bytes 786440 | tf_op jit(solution)/shard_map/ppermute | solution.py:287
  99.2 8.3 %collective-permute-start.16 = (bf16[1024,128]{1,0:T(8,128)(2,1)S(1)}, bf16[1024,128]{1,0:T(8,128)(2,1)S(1)}, u32[]{:S(2)}, u32[]{:S(2)}) collective-permute-start(bf16[1024,128]{1,0:T(8,128)(2,1)S(1)} %get-tuple-element.70), channel_id=1, source_target_pairs={{0,3},{1,0},{2,1},{3,2},{4,7},{5,4},{6,5},{7,6},{8,11},{9,8},{10,9... | collective-permute-start | bytes 786440 | tf_op jit(solution)/shard_map/ppermute | solution.py:287
  107.6 17.0 %collective-permute-start.19 = (bf16[4,8,32,128]{3,2,1,0:T(8,128)(2,1)S(1)}, bf16[4,8,32,128]{3,2,1,0:T(8,128)(2,1)S(1)}, u32[]{:S(2)}, u32[]{:S(2)}) collective-permute-start(bf16[4,8,32,128]{3,2,1,0:T(8,128)(2,1)S(1)} %get-tuple-element.71.refs_0_), channel_id=1, source_target_pairs={{0,1},{1,2},{2,3},{3,0},{4,5},{5,6},{6,7},{7,4},{8,9},{9,10},{10,1... | collective-permute-start | bytes 786440 | tf_op jit(solution)/shard_map/ppermute | solution.py:287
  108.2 19.9 %collective-permute-start.22 = (bf16[4,8,32,128]{3,2,1,0:T(8,128)(2,1)S(1)}, bf16[4,8,32,128]{3,2,1,0:T(8,128)(2,1)S(1)}, u32[]{:S(2)}, u32[]{:S(2)}) collective-permute-start(bf16[4,8,32,128]{3,2,1,0:T(8,128)(2,1)S(1)} %get-tuple-element.71.refs_0_), channel_id=1, source_target_pairs={{0,2},{1,3},{2,0},{3,1},{4,6},{5,7},{6,4},{7,5},{8,10},{9,11},{10,... | collective-permute-start | bytes 786440 | tf_op jit(solution)/shard_map/ppermute | solution.py:287
  110.8 17.3 %collective-permute-start.23 = (bf16[4,8,32,128]{3,2,1,0:T(8,128)(2,1)S(1)}, bf16[4,8,32,128]{3,2,1,0:T(8,128)(2,1)S(1)}, u32[]{:S(2)}, u32[]{:S(2)}) collective-permute-start(bf16[4,8,32,128]{3,2,1,0:T(8,128)(2,1)S(1)} %get-tuple-element.71.refs_0_), channel_id=1, source_target_pairs={{0,3},{1,0},{2,1},{3,2},{4,7},{5,4},{6,5},{7,6},{8,11},{9,8},{10,9... | collective-permute-start | bytes 786440 | tf_op jit(solution)/shard_map/ppermute | solution.py:287
  110.8 9.2 %collective-permute-start.17 = (bf16[4,32,128]{2,1,0:T(8,128)(2,1)S(1)}, bf16[4,32,128]{2,1,0:T(8,128)(2,1)S(1)}, u32[]{:S(2)}, u32[]{:S(2)}) collective-permute-start(bf16[4,32,128]{2,1,0:T(8,128)(2,1)S(1)} %get-tuple-element.72), channel_id=1, source_target_pairs={{0,16},{16,32},{32,48},{48,64},{64,80},{80,96},{96,112},{112,128},... | collective-permute-start | bytes 98312 | tf_op jit(solution)/shard_map/ppermute | solution.py:167
  118.1 6.4 %collective-permute-start.18 = (bf16[4,32,128]{2,1,0:T(8,128)(2,1)S(1)}, bf16[4,32,128]{2,1,0:T(8,128)(2,1)S(1)}, u32[]{:S(2)}, u32[]{:S(2)}) collective-permute-start(bf16[4,32,128]{2,1,0:T(8,128)(2,1)S(1)} %get-tuple-element.73), channel_id=1, source_target_pairs={{16,0},{32,16},{48,32},{64,48},{80,64},{96,80},{112,96},{128,112},... | collective-permute-start | bytes 98312 | tf_op jit(solution)/shard_map/ppermute | solution.py:168
  131.3 6.9 %collective-permute-start.24 = (bf16[4,96,128]{2,1,0:T(8,128)(2,1)S(1)}, bf16[4,96,128]{2,1,0:T(8,128)(2,1)S(1)}, u32[]{:S(2)}, u32[]{:S(2)}) collective-permute-start(bf16[4,96,128]{2,1,0:T(8,128)(2,1)S(1)} %pack.1.refs_1_), channel_id=1, source_target_pairs={{0,1},{1,2},{2,3},{3,0},{4,5},{5,6},{6,7},{7,4},{8,9},{9,10},{10,1... | collective-permute-start | bytes 294920 | tf_op jit(solution)/shard_map/ppermute | solution.py:287
  133.1 5.0 %collective-permute-start.25 = (bf16[4,96,128]{2,1,0:T(8,128)(2,1)S(1)}, bf16[4,96,128]{2,1,0:T(8,128)(2,1)S(1)}, u32[]{:S(2)}, u32[]{:S(2)}) collective-permute-start(bf16[4,96,128]{2,1,0:T(8,128)(2,1)S(1)} %pack.1.refs_1_), channel_id=1, source_target_pairs={{0,2},{1,3},{2,0},{3,1},{4,6},{5,7},{6,4},{7,5},{8,10},{9,11},{10,... | collective-permute-start | bytes 294920 | tf_op jit(solution)/shard_map/ppermute | solution.py:287
  134.0 4.6 %collective-permute-start.26 = (bf16[4,96,128]{2,1,0:T(8,128)(2,1)S(1)}, bf16[4,96,128]{2,1,0:T(8,128)(2,1)S(1)}, u32[]{:S(2)}, u32[]{:S(2)}) collective-permute-start(bf16[4,96,128]{2,1,0:T(8,128)(2,1)S(1)} %pack.1.refs_1_), channel_id=1, source_target_pairs={{0,3},{1,0},{2,1},{3,2},{4,7},{5,4},{6,5},{7,6},{8,11},{9,8},{10,9... | collective-permute-start | bytes 294920 | tf_op jit(solution)/shard_map/ppermute | solution.py:287
  (6 other events, 31.8 us)

commit v5 on v3

--- a/solution.py
+++ b/solution.py
@@ -13,8 +13,9 @@
 GROUP = 16
 ROWS = 8
 COLS = 32
+WIDE = 3
+BLOCK = 4 * ROWS * COLS * GROUP
 MIB = 1 << 20
-CORNERS = ((0, 0), (0, 1), (1, 0), (1, 1))
 
 VMEM = pl.BlockSpec(memory_space=pltpu.VMEM)
 SMEM = pl.BlockSpec(memory_space=pltpu.SMEM)
@@ -71,55 +72,34 @@
     return mean, m2
 
 
-def combine(st_ref, count):
-    devices = st_ref.shape[0]
+def merge(st_ref, count):
     means = st_ref[:, 0, :]
-    mean = jnp.sum(means, axis=0, keepdims=True) * (1.0 / devices)
+    mean = jnp.sum(means, axis=0, keepdims=True) * (1.0 / st_ref.shape[0])
     apart = means - mean
     m2 = jnp.sum(st_ref[:, 1, :] + count * (apart * apart), axis=0, keepdims=True)
-    return mean, lax.rsqrt(m2 * (1.0 / (count * devices)) + 1e-6)
+    return mean, lax.rsqrt(m2 * (1.0 / (count * st_ref.shape[0])) + 1e-6)
+
+
+def store_stats(ref, mean, m2):
+    row = lax.broadcasted_iota(jnp.int32, (2, CH), 0)
+    ref[...] = jnp.broadcast_to(jnp.where(row == 0, mean, m2)[None], ref.shape)
 
 
 def spread(slots):
     return lax.all_to_all(slots, HA + ("wa",), 0, 0, tiled=True)
 
 
-def diagonals(flag_ref):
-    wa_size = lax.axis_size("wa")
-    found = []
-    for r, c in CORNERS:
-        valid = flag_ref[r] * flag_ref[2 + c]
-        found.append((valid, flag_ref[5] + valid * ((2 * r - 1) * wa_size + 2 * c - 1)))
-    return found
-
-
-def fill_slots(slot_ref, flag_ref, mean, m2, frames):
-    row = lax.broadcasted_iota(jnp.int32, (8, CH), 0)
-    base = jnp.where(row == 0, mean, jnp.where(row == 1, m2, 0.0))
-    slot_ref[...] = jnp.broadcast_to(base[None], slot_ref.shape)
-    for (r, c), (valid, at) in zip(CORNERS, diagonals(flag_ref)):
-
-        @pl.when(valid > 0)
-        def _():
-            f = 0
-            for v in frames:
-                for i in range(v.shape[0]):
-                    pixel = v[i, r * (ROWS - 1), c * (COLS - 1) : c * (COLS - 1) + 1, :]
-                    slot_ref[pl.ds(at, 1), 2 + f, :] = pixel
-                    f += 1
-
-
-def store_edges(frames, refs, pad=0):
+def store_edges(frames, refs):
     top_ref, bot_ref, lef_ref, rig_ref = refs
     at = 0
     for v in frames:
         n = v.shape[0]
         top_ref[at : at + n] = v[:, 0].astype(BF16)
         bot_ref[at : at + n] = v[:, ROWS - 1].astype(BF16)
-        for ref, column in ((lef_ref, v[:, :, 0, :]), (rig_ref, v[:, :, COLS - 1, :])):
-            if pad:
-                column = jnp.concatenate([column, jnp.zeros((n, pad, CH), F32)], axis=1)
-            ref[at : at + n] = column.astype(BF16)
+        for i in range(WIDE):
+            for ref, j in ((lef_ref, i), (rig_ref, COLS - WIDE + i)):
+                column = jnp.concatenate([v[:, :, j, :], jnp.zeros((n, 8, CH), F32)], axis=1)
+                ref[at : at + n, i] = column.astype(BF16)
         at += n
 
 
@@ -136,22 +116,23 @@
         c.wait()
     x, c1, c2 = x_ref[...].astype(F32), c1_ref[...].astype(F32), c2_ref[...].astype(F32)
     mean, m2 = local_stats(x.reshape(-1, CH))
-    fill_slots(slot_ref, flag_ref, mean, m2, (c1, x))
+    store_stats(slot_ref, mean, m2)
     store_edges((c1, x, c2), edges)
     for c in copies[3:]:
         c.wait()
 
 
-def corner_body(top_ref, bot_ref, lef_ref, rig_ref, *rest):
-    lo_ref, ro_ref = rest[-2:]
-    row = lax.broadcasted_iota(jnp.int32, lef_ref.shape, 1)
+def corner_body(top_ref, bot_ref, lef_ref, rig_ref, lo_ref, ro_ref):
     top = top_ref[...].astype(F32)
     bot = bot_ref[...].astype(F32)
-    for src, dst, at in ((lef_ref, lo_ref, 0), (rig_ref, ro_ref, COLS - 1)):
-        v = src[...].astype(F32)
-        v = jnp.where(row == 8, top[:, at : at + 1, :], v)
-        v = jnp.where(row == 9, bot[:, at : at + 1, :], v)
-        dst[...] = v.astype(BF16)
+    shape = (lef_ref.shape[0],) + lef_ref.shape[2:]
+    row = lax.broadcasted_iota(jnp.int32, shape, 1)
+    for i in range(WIDE):
+        for src, dst, at in ((lef_ref, lo_ref, i), (rig_ref, ro_ref, COLS - WIDE + i)):
+            v = src[:, i].astype(F32)
+            v = jnp.where(row == 8, top[:, at : at + 1, :], v)
+            v = jnp.where(row == 9, bot[:, at : at + 1, :], v)
+            dst[:, i] = v.astype(BF16)
 
 
 def swap_rows(top, bot):
@@ -192,21 +173,59 @@
     place(patch_ref, frame, bot[None], ROWS + 1, corners[2], corners[3], lanes)
 
 
-def multiply(patch_ref, w_ref, outs):
+def multiply(patch_ref, side_ref, w_ref, outs):
     depth = 9 * CH
     size = ROWS * COLS
-    for t in range(4):
+    slot = side_ref.shape[1] // (ROWS + 2)
+    jobs = [(t * size, size, [(patch_ref, t + a, COLS) for a in range(3)]) for t in range(4)]
+    jobs.append((4 * size, ROWS * slot, [(side_ref, a, slot) for a in range(3)]))
+    for at, rows, sources in jobs:
         acc = None
-        for a in range(3):
-            lhs = jnp.concatenate([patch_ref[t + a, b * COLS : b * COLS + size, :] for b in range(3)], axis=1)
+        for a, (ref, i, step) in enumerate(sources):
+            lhs = jnp.concatenate([ref[i, b * step : b * step + rows, :] for b in range(3)], axis=1)
             part = jnp.dot(lhs, w_ref[a * depth : (a + 1) * depth, :], preferred_element_type=F32)
             acc = part if acc is None else acc + part
         for i, out in enumerate(outs):
-            out[t * size : (t + 1) * size, :] = acc[:, i * CH : (i + 1) * CH].astype(BF16)
-
-
-def far_body(cache_at, act_at, extra, flag_ref, st_ref, x_ref, c_ref, tc, bc, lc, rc, ta, ba, la, ra, w_hbm, *rest):
-    out2, out1, patch_ref, near_ref, w_ref, sem = rest[extra:]
+            out[at : at + rows, :] = acc[:, i * CH : (i + 1) * CH].astype(BF16)
+
+
+def halo_frame(refs, at, change, has, reach):
+    top, bot, lef, rig = refs
+    above = jnp.where(has[0], change(top[at].astype(F32)), 0.0)
+    below = jnp.where(has[1], change(bot[at].astype(F32)), 0.0)
+    columns = {}
+    for i in range(reach):
+        for ref, flag, j, x in ((lef, has[2], WIDE - 1 - i, -1 - i), (rig, has[3], i, COLS + i)):
+            v = jnp.where(flag, change(ref[at, j].astype(F32)), 0.0)
+            columns[x] = (v[0:8], jnp.where(has[0], v[8:9], 0.0), jnp.where(has[1], v[9:10], 0.0))
+    return above, below, columns
+
+
+def place_sides(mix_ref, frame, ext, inner, above, below, columns):
+    columns = dict(columns)
+    for x in (0, COLS - 1):
+        columns[x] = (inner[:, x, :], above[x : x + 1], below[x : x + 1])
+    step = 8 * ext
+    for a in range(3):
+        t = frame - a
+        if not 0 <= t < 4:
+            continue
+        for c, x in enumerate(list(range(-ext, 0)) + list(range(COLS, COLS + ext))):
+            w = t * 2 * ext + c
+            for e in range(3):
+                rows, up, down = columns[x + e - 1]
+                mix_ref[a, e, pl.ds(w, 1), :] = up
+                mix_ref[a, e, pl.ds(step + w, ROWS, stride=step), :] = rows
+                mix_ref[a, e, pl.ds((ROWS + 1) * step + w, 1), :] = down
+
+
+def far_body(ext, cache_at, act_at, extra, flag_ref, x_ref, c_ref, st_ref, *rest):
+    halo, rest = rest[:4], rest[4:]
+    if act_at is None:
+        beside_ref, above_ref, below_ref = rest[:3]
+        rest = rest[3:]
+    w_hbm, rest = rest[0], rest[1 + extra :]
+    out2, out1, patch_ref, side_ref, near_ref, w_ref, mix_ref, wide_ref, sem = rest
     col = flag_ref[4]
     copies = []
     for i, (k, dst, at) in enumerate(((2, w_ref, 0), (1, w_ref, CH), (3, near_ref, 0), (0, near_ref, CH))):
@@ -216,52 +235,82 @@
         )
         copies[-1].start()
     has = [flag_ref[i] > 0 for i in range(4)]
-    mean, scale = combine(st_ref, x_ref.shape[0] * ROWS * COLS * GROUP)
+    mean, scale = merge(st_ref, BLOCK)
 
     def act(v):
         u = (v - mean) * scale
         return u / (1.0 + jnp.exp(-u))
 
-    lanes = (0, CH, 2 * CH)
-    across = diagonals(flag_ref)
+    if act_at is None:
+        wide_ref[...] = act(beside_ref[...])
+        outer = [
+            jnp.where(flag, act(ref[...].astype(F32)), 0.0) for ref, flag in ((above_ref, has[0]), (below_ref, has[1]))
+        ]
     for s in range(6):
         if s < 2:
-            own, at, halo, change = c_ref[s], cache_at + s, (tc, bc, lc, rc), lambda v: v
+            inner = c_ref[s].astype(F32)
+            above, below, columns = halo_frame(halo, cache_at + s, lambda v: v, has, ext + 1)
         else:
-            own, at, halo, change = x_ref[s - 2], act_at + s - 2, (ta, ba, la, ra), act
-        sides = [jnp.where(has[i], change(ref[at].astype(F32)), 0.0) for i, ref in enumerate(halo)]
-        corners = [
-            jnp.where(valid > 0, change(st_ref[pl.ds(slot, 1), 2 + s, :]), 0.0) for valid, slot in across
-        ]
-        place_frame(patch_ref, s, change(own.astype(F32)), *sides, corners, lanes)
+            t = s - 2
+            inner = act(x_ref[t].astype(F32))
+            if act_at is not None:
+                above, below, columns = halo_frame(halo, act_at + t, act, has, ext + 1)
+            else:
+                above, below = [v[t * COLS : (t + 1) * COLS] for v in outer]
+                columns = {}
+                for c, x in enumerate((-2, -1, COLS, COLS + 1)):
+                    flag = has[2 + c // 2]
+                    px = 4 * COLS + 4 * t + c
+                    rows = wide_ref[pl.ds(4 * t + c, ROWS, stride=16), :]
+                    columns[x] = tuple(
+                        jnp.where(flag, v, 0.0) for v in (rows, outer[0][px : px + 1], outer[1][px : px + 1])
+                    )
+        corners = [columns[-1][1], columns[COLS][1], columns[-1][2], columns[COLS][2]]
+        place_frame(
+            patch_ref, s, inner, above, below, columns[-1][0], columns[COLS][0], corners, (0, CH, 2 * CH)
+        )
+        place_sides(mix_ref, s, ext, inner, above, below, columns)
+    for a in range(3):
+        for e in range(3):
+            side_ref[a, :, e * CH : (e + 1) * CH] = mix_ref[a, e].astype(BF16)
     copies[0].wait()
     copies[1].wait()
-    multiply(patch_ref, w_ref, (out2, out1))
+    multiply(patch_ref, side_ref, w_ref, (out2, out1))
     copies[2].wait()
     copies[3].wait()
 
 
-def near_body(patch_ref, w_ref, out3, out0):
-    multiply(patch_ref, w_ref, (out3, out0))
-
-
-def conv(flags, stats, x, cache, cache_halo, cache_at, act_halo, act_at, weight, name, after=()):
-    n = x.shape[0] * ROWS * COLS
+def near_body(patch_ref, side_ref, w_ref, out3, out0):
+    multiply(patch_ref, side_ref, w_ref, (out3, out0))
+
+
+def conv(flags, x, cache, stats, halo, cache_at, act_at, around, weight, ext, name, after=()):
+    n = x.shape[0] * ROWS * COLS + ROWS * 8 * ext
     depth, width = weight.shape
     flops = n * depth * width
     piece = sds((n, CH))
-    body = functools.partial(far_body, cache_at, act_at, len(after))
-    out2, out1, patch, near = call(
+    body = functools.partial(far_body, ext, cache_at, act_at, len(after))
+    out2, out1, patch, side, near = call(
         body,
-        [piece] * 2 + [sds((6, (ROWS + 2) * COLS, 3 * CH)), sds((depth, 2 * CH))],
-        scratch=[pltpu.VMEM((depth, 2 * CH), BF16), pltpu.SemaphoreType.DMA((4,))],
+        [piece] * 2
+        + [
+            sds((6, (ROWS + 2) * COLS, 3 * CH)),
+            sds((3, (ROWS + 2) * 8 * ext, 3 * CH)),
+            sds((depth, 2 * CH)),
+        ],
+        scratch=[
+            pltpu.VMEM((depth, 2 * CH), BF16),
+            pltpu.VMEM((3, 3, (ROWS + 2) * 8 * ext, CH), F32),
+            pltpu.VMEM((16 * ROWS, CH), F32),
+            pltpu.SemaphoreType.DMA((4,)),
+        ],
         flops=flops,
         limit=20,
         name=name + "_far",
-    )(flags, stats, x, cache, *cache_halo, *act_halo, Left(weight, HBM), *[Left(a) for a in after])
+    )(flags, x, cache, stats, *halo, *around, Left(weight, HBM), *[Left(a) for a in after])
     got2 = to_peer(out2, 2)
     got1 = to_peer(out1, 1)
-    out3, own = call(near_body, [piece] * 2, flops=flops, limit=16, name=name + "_near")(patch, near)
+    out3, own = call(near_body, [piece] * 2, flops=flops, limit=16, name=name + "_near")(patch, side, near)
     (far,) = call(add_body, [sds((n, CH), F32)], name=name + "_add")(got1, got2)
     return own, far, to_peer(out3, 3)
 
@@ -280,28 +329,44 @@
     return [got[k] for k in (1, 2, 3)]
 
 
-def hidden_body(flag_ref, p0, far, p3, c2_ref, h_ref, slot_ref, *edges):
-    h = (p0[...].astype(F32) + p3[...].astype(F32) + far[...]).astype(BF16)
-    h_ref[...] = h.reshape(h_ref.shape)
-    h = h.astype(F32)
-    mean, m2 = local_stats(h)
-    h = h.reshape(h_ref.shape)
-    fill_slots(slot_ref, flag_ref, mean, m2, (c2_ref[...].astype(F32), h))
-    store_edges((h,), edges)
-
-
-def resid_body(x_ref, p0, far, p3, h_ref, *edges):
+def hidden_body(p0, far, p3, h_ref, side_ref, slot_ref, top_ref, bot_ref):
+    h = (p0[...].astype(F32) + p3[...].astype(F32) + far[...]).astype(BF16).astype(F32)
+    size = 4 * ROWS * COLS
+    mean, m2 = local_stats(h[:size])
+    store_stats(slot_ref, mean, m2)
+    main = h[:size].reshape(h_ref.shape)
+    h_ref[...] = main.astype(BF16)
+    side_ref[...] = h[size:]
+    for ref, r in ((top_ref, 0), (bot_ref, ROWS - 1)):
+        ref[0 : 4 * COLS, :] = main[:, r].reshape(4 * COLS, CH).astype(BF16)
+        ref[4 * COLS :, :] = h[size + 16 * r : size + 16 * (r + 1)].astype(BF16)
+
+
+def resid_body(flag_ref, x_ref, lef_ref, rig_ref, p0, far, p3, o_ref, top_ref, bot_ref, side_ref):
     total = p0[...].astype(F32) + p3[...].astype(F32) + far[...]
-    h = (x_ref[...].astype(F32) + total.reshape(x_ref.shape)).astype(BF16)
-    h_ref[...] = h
-    store_edges((h.astype(F32),), edges, pad=8)
+    size = ROWS * COLS
+    side_ref[...] = total[4 * size :]
+    row = lax.broadcasted_iota(jnp.int32, (8, CH), 0)
+    for t in range(4):
+        main = x_ref[t].astype(F32).reshape(size, CH) + total[t * size : (t + 1) * size]
+        o_ref[t, 0:size, :] = main.astype(BF16)
+        beside = []
+        for c, (ref, i) in enumerate(((lef_ref, WIDE - 1), (rig_ref, 0))):
+            v = ref[2 + t, i].astype(F32)[0:ROWS] + side_ref[pl.ds(2 * t + c, ROWS, stride=8), :]
+            beside.append(jnp.where(flag_ref[2 + c] > 0, v, 0.0))
+            o_ref[t, size + 8 * c : size + 8 * (c + 1), :] = beside[c].astype(BF16)
+        for ref, r in ((top_ref, 0), (bot_ref, ROWS - 1)):
+            ref[t, 0:COLS, :] = main[r * COLS : (r + 1) * COLS].astype(BF16)
+            px = [v[r : r + 1] for v in beside]
+            ref[t, COLS:, :] = jnp.where(row == 0, px[0], jnp.where(row == 1, px[1], 0.0)).astype(BF16)
 
 
 ROW_TAPS = {(0, 0): (-1, 0), (0, 1): (1,), (1, 0): (-1,), (1, 1): (0, 1)}
 COL_TAPS = {(0, 0): (-1,), (0, 1): (0, 1), (1, 0): (-1, 0), (1, 1): (1,)}
 
 
-def fold_body(w0, w1, w2, w3, o_ref):
+def fold_body(w0, w1, w2, w3, *rest):
+    o_ref = rest[-1]
     for k, ref in enumerate((w0, w1, w2, w3)):
         taps = [ref[i].astype(F32) for i in range(9)]
         for q in range(2):
@@ -324,15 +389,17 @@
     half = 2 * 4 * CH
     for k, (x, border) in enumerate(parts):
         edge = border[0].astype(F32)
+        own = x[0].astype(F32)
+        inside = ROWS * COLS
         place_frame(
             patch_ref,
             0,
-            x[0].astype(F32),
+            own[:inside].reshape(ROWS, COLS, CH),
             edge[:COLS],
-            edge[COLS : 2 * COLS],
-            edge[2 * COLS : 2 * COLS + 8],
-            edge[2 * COLS + 16 : 2 * COLS + 24],
-            [edge[2 * COLS + i : 2 * COLS + i + 1] for i in (8, 24, 9, 25)],
+            edge[COLS + 8 : 2 * COLS + 8],
+            own[inside : inside + 8],
+            own[inside + 8 :],
+            [edge[i : i + 1] for i in (COLS, COLS + 1, 2 * COLS + 8, 2 * COLS + 9)],
             [(e * 4 + k) * CH for e in range(3)],
         )
     for q in range(2):
@@ -379,14 +446,14 @@
     frames = features.shape[0]
     ha, wa, col = lax.axis_index(HA), lax.axis_index("wa"), lax.axis_index("col")
     nh, nw = lax.axis_size(HA), lax.axis_size("wa")
-    flags = jnp.stack([ha > 0, ha < nh - 1, wa > 0, wa < nw - 1, col, ha * nw + wa]).astype(jnp.int32)
-    slots = sds((nh * nw, 8, CH), F32)
+    flags = jnp.stack([ha > 0, ha < nh - 1, wa > 0, wa < nw - 1, col]).astype(jnp.int32)
+    slots = sds((nh * nw, 2, CH), F32)
 
     x, c1, c2, stats, *edges = call(
         first_body,
         [sds(features.shape), sds(cache_first.shape), sds(cache_second.shape), slots]
         + [sds((8, COLS, CH))] * 2
-        + [sds((8, ROWS, CH))] * 2
+        + [sds((8, WIDE, 16, CH))] * 2
         + [sds(weight_up.shape[:2] + (CH,))] * 4,
         scratch=[pltpu.SemaphoreType.DMA((7,))],
         limit=20,
@@ -394,46 +461,44 @@
     )(flags, *[Left(a, HBM) for a in (features, cache_first, cache_second, weight_up)])
     edges, w_pieces = edges[:4], edges[4:]
     w_got = to_peers(w_pieces[1:])
-    halo = swap_rows(*edges[:2]) + swap_columns(*edges[2:])
     stats = spread(stats)
+    rows = swap_rows(*edges[:2])
+    cornered = call(corner_body, [sds((8, WIDE, 16, CH))] * 2, name="corners")(*rows, *edges[2:])
+    halo = rows + swap_columns(*cornered)
     pieces = conv(
-        flags, stats, x, c1, halo, 0, halo, 2, weight_first.reshape(-1, 4 * CH), "conv_first", after=w_got
+        flags, x, c1, stats, halo, 0, 2, (), weight_first.reshape(-1, 4 * CH), 2, "conv_first", after=w_got
     )
-    hidden, stats, *edges = call(
+    hidden, side, stats, top, bot = call(
         hidden_body,
-        [sds(features.shape), slots] + [sds((frames, COLS, CH))] * 2 + [sds((frames, ROWS, CH))] * 2,
+        [sds(features.shape), sds((16 * ROWS, CH), F32), slots] + [sds((4 * COLS + 16, CH))] * 2,
         limit=12,
         name="hidden",
-    )(flags, *pieces, c2)
-    halo2 = swap_rows(*edges[:2]) + swap_columns(*edges[2:])
+    )(*pieces)
     stats = spread(stats)
-    (folded,) = call(fold_body, [sds((2, 2, 8 * CH, 2 * CH))], limit=12, name="fold")(w_pieces[0], *w_got)
+    around = (side,) + swap_rows(top, bot)
     pieces = conv(
-        flags, stats, hidden, c2, halo, 6, halo2, 0, weight_second.reshape(-1, 4 * CH), "conv_second"
+        flags, hidden, c2, stats, halo, 6, None, around, weight_second.reshape(-1, 4 * CH), 1, "conv_second"
     )
-    resid, *edges = call(
+    resid, top, bot = call(
         resid_body,
-        [sds(features.shape)] + [sds((frames, COLS, CH))] * 2 + [sds((frames, 16, CH))] * 2,
+        [sds((frames, ROWS * COLS + 16, CH))] + [sds((frames, COLS + 8, CH))] * 2,
+        scratch=[pltpu.VMEM((8 * ROWS, CH), F32)],
         name="resid",
-    )(features, *pieces)
+    )(flags, features, *halo[2:], *pieces)
     others = to_peers([resid] * 3)
-    rows = swap_rows(*edges[:2])
-    cornered = call(corner_body, [sds((frames, 16, CH))] * 2, name="corners")(*rows, *edges[2:], Left(others[0]))
-    columns = swap_columns(*cornered)
-    (border,) = call(pack_body, [sds((frames, 2 * COLS + 32, CH))], name="pack")(
-        *rows, *columns, *[Left(a) for a in others[1:]]
+    (border,) = call(pack_body, [sds((frames, 2 * COLS + 16, CH))], name="pack")(
+        *swap_rows(top, bot), Left(others[0])
     )
     borders = [border] + to_peers([border] * 3)
+    (folded,) = call(fold_body, [sds((2, 2, 8 * CH, 2 * CH))], limit=12, name="fold")(
+        w_pieces[0], *w_got, *[Left(a) for a in others[1:]]
+    )
     return up_conv(list(zip([resid] + others, borders)), folded)
 
 
-def pack_body(top_ref, bot_ref, lef_ref, rig_ref, *rest):
-    o_ref = rest[-1]
-    at = 0
-    for ref in (top_ref, bot_ref, lef_ref, rig_ref):
-        n = ref.shape[1]
-        o_ref[:, at : at + n, :] = ref[...]
-        at += n
+def pack_body(top_ref, bot_ref, after_ref, o_ref):
+    o_ref[:, : COLS + 8, :] = top_ref[...]
+    o_ref[:, COLS + 8 :, :] = bot_ref[...]
 
 
 def solution(mesh):

time: 137 us -> 127 us (0.927)
  starting transfers between devices: 75.8 us -> 66.7 us
  waiting for transfers between devices: 36 us -> 34.4 us
    ppermute x3 -> x1, starting transfers between devices: 9.26 us -> 3.1 us  [swap_columns(): left = lax.ppermute(rig, 'wa', [(i, i + 1) for i in range(n - 1)])]
    ppermute x3 -> x1, waiting for transfers between devices: 6.06 us -> 1.42 us  [swap_columns(): right = lax.ppermute(lef, 'wa', [(i + 1, i) for i in range(n - 1)])]
    ppermute x3 -> x1, starting transfers between devices: 4.06 us -> 1.29 us  [swap_columns(): right = lax.ppermute(lef, 'wa', [(i + 1, i) for i in range(n - 1)])]
    all_to_all x2, waiting for transfers between devices: 0.01 us -> 2.64 us  [spread(): return lax.all_to_all(slots, HA + ('wa',), 0, 0, tiled=True)]
    ppermute x15, starting transfers between devices: 20.4 us -> 18.5 us  [to_peer(): return lax.ppermute(piece, 'col', [(i, (i + k) % n) for i in range(n)])]
  transfers between devices with their start and end apart: 29 -> 25, of which waited for: 11 -> 11; matrix products, arithmetic and copies ran while one was open for 0% -> 0% of each run, Pallas kernels for 4% -> 5%
where the time goes in v5:
time: 127 us; the launch traced here: 126 us
  starting transfers between devices  66.7 us (53%)
  waiting for transfers between devices  34.4 us (27%)
  Pallas kernels  24.5 us (19%)
    all_to_all x2, starting transfers between devices, spread(): return lax.all_to_all(slots, HA + ('wa',), 0, 0, tiled=True)  22.5 us
    ppermute x15, waiting for transfers between devices, to_peer(): return lax.ppermute(piece, 'col', [(i, (i + k) % n) for i in range(n)])  20.8 us
    pallas_call x12, Pallas kernels, run(): pl.pallas_call(body, out_shape=list(outs), in_specs=specs, out_specs=[VME...  20.4 us
    ppermute x15, starting transfers between devices, to_peer(): return lax.ppermute(piece, 'col', [(i, (i + k) % n) for i in range(n)])  18.5 us
    ppermute x3, starting transfers between devices, swap_rows(): above = lax.ppermute(bot, HA, [(i, i + 1) for i in range(n - 1)])  15.5 us
    ppermute x3, waiting for transfers between devices, swap_rows(): below = lax.ppermute(top, HA, [(i + 1, i) for i in range(n - 1)])  9.44 us
    ppermute x3, starting transfers between devices, swap_rows(): below = lax.ppermute(top, HA, [(i + 1, i) for i in range(n - 1)])  5.76 us
    pallas_call x1, Pallas kernels, up_conv(): pl.pallas_call(up_body, out_shape=sds(out), grid=(frames,), in_specs=spec...  4.15 us
  transfers between devices with their start and end apart: 25, of which 11 were waited for; matrix products, arithmetic and copies ran while one was open for 0% of the time, Pallas kernels for 5%

profile of v5, /device:TPU:97, one launch (start us, length us, event | category | flops | bytes accessed | tf_op | source)
XLA Modules:
  0.0 125.8 jit_solution(15575408431569314335)
XLA Ops:
  0.1 3.2 %first.1 = (bf16[4,8,32,128]{3,2,1,0:T(8,128)(2,1)S(1)}, bf16[2,8,32,128]{3,2,1,0:T(8,128)(2,1)S(1)}, bf16[2,8,32,128]{3,2,1,0:T(8,128)(2,1)S(1)}, f32[64,2,128]...) custom-call(s32[5]{0:T(128)S(1)} %stack.39.flag_ref, ...), custom_call_target="tpu_custom_call" | custom-call | bytes 3801108 | tf_op jit(solution)/shard_map/first/pallas_call | solution.py:39
  4.5 2.5 %collective-permute-start.5 = (bf16[9,128,128]{2,1,0:T(8,128)(2,1)S(1)}, bf16[9,128,128]{2,1,0:T(8,128)(2,1)S(1)}, u32[]{:S(2)}, u32[]{:S(2)}) collective-permute-start(bf16[9,128,128]{2,1,0:T(8,128)(2,1)S(1)} %get-tuple-element.51), channel_id=1, source_target_pairs={{0,2},{1,3},{2,0},{3,1},{4,6},{5,7},{6,4},{7,5},{8,10},{9,11},{10,... | collective-permute-start | bytes 884744 | tf_op jit(solution)/shard_map/ppermute | solution.py:324
  8.1 6.1 %collective-permute-start = (bf16[8,32,128]{2,1,0:T(8,128)(2,1)S(1)}, bf16[8,32,128]{2,1,0:T(8,128)(2,1)S(1)}, u32[]{:S(2)}, u32[]{:S(2)}) collective-permute-start(bf16[8,32,128]{2,1,0:T(8,128)(2,1)S(1)} %get-tuple-element.41), channel_id=1, source_target_pairs={{0,16},{16,32},{32,48},{48,64},{64,80},{80,96},{96,112},{112,128},... | collective-permute-start | bytes 196616 | tf_op jit(solution)/shard_map/ppermute | solution.py:140
  16.2 10.8 %all-to-all-start = ((f32[64,2,128]{2,1,0:T(2,128)}), f32[64,2,128]{2,1,0:T(2,128)S(1)}, u32[]{:S(2)}, u32[]{:S(2)}) async-start(f32[64,2,128]{2,1,0:T(2,128)} %get-tuple-element.49), calls=%async_computation | async-start | bytes 131072 | tf_op jit(solution)/shard_map/all_to_all | solution.py:89
  27.1 3.1 %collective-permute-start.2 = (bf16[8,3,16,128]{3,2,1,0:T(8,128)(2,1)S(1)}, bf16[8,3,16,128]{3,2,1,0:T(8,128)(2,1)S(1)}, u32[]{:S(2)}, u32[]{:S(2)}) collective-permute-start(bf16[8,3,16,128]{3,2,1,0:T(8,128)(2,1)S(1)} %get-tuple-element.45), channel_id=1, source_target_pairs={{0,4},{4,8},{8,12},{1,5},{5,9},{9,13},{2,6},{6,10},{10,14},{3,7},{... | collective-permute-start | bytes 294920 | tf_op jit(solution)/shard_map/ppermute | solution.py:147
  31.5 2.6 %all-to-all-done.st_ref = f32[64,2,128]{2,1,0:T(2,128)S(1)} async-done(((f32[64,2,128]{2,1,0:T(2,128)}), f32[64,2,128]{2,1,0:T(2,128)S(1)}, u32[]{:S(2)}, u32[]{:S(2)}) %all-to-all-start) | async-done | bytes 65568 | tf_op jit(solution)/shard_map/all_to_all | solution.py:89
  35.6 4.6 %conv_first_far.1 = (bf16[1152,128]{1,0:T(8,128)(2,1)S(1)}, bf16[1152,128]{1,0:T(8,128)(2,1)S(1)}, bf16[6,320,384]{2,1,0:T(8,128)(2,1)S(1)}, bf16[3,160,384]{2,1,0:T(8,128)(2,1)S(1)}, bf16[3456,256]{1,0:T(8,128)(2,1)S(1)}) custom-call(s32[5]{0:T(128)S(1)} %stack.39.flag_ref, bf16[4,8,32,128]{3,2,1,0:T(8,128)(2,1)S(1)} %get-tuple-element.47.x_ref, ...), custom_call_target="tpu_custom_call" | custom-call | flops 2038431744 | bytes 9412628 | tf_op jit(solution)/shard_map/conv_first_far/pallas_call | solution.py:39
  41.1 2.5 %conv_first_near.1 = (bf16[1152,128]{1,0:T(8,128)(2,1)S(1)}, bf16[1152,128]{1,0:T(8,128)(2,1)S(1)}) custom-call(bf16[6,320,384]{2,1,0:T(8,128)(2,1)S(1)} %get-tuple-element.53.patch_ref, bf16[3,160,384]{2,1,0:T(8,128)(2,1)S(1)} %get-tuple-element.54.side_ref, bf16[3456,256]{1,0:T(8,128)(2,1)S(1)} %get-tuple-element.55.w_ref), custom_call_target="tpu_custom_call" | custom-call | flops 2038431744 | bytes 4202496 | tf_op jit(solution)/shard_map/conv_first_near/pallas_call | solution.py:39
  45.6 4.3 %collective-permute-done.7.a_ref = bf16[1152,128]{1,0:T(8,128)(2,1)S(1)} collective-permute-done((bf16[1152,128]{1,0:T(8,128)(2,1)S(1)}, bf16[1152,128]{1,0:T(8,128)(2,1)S(1)}, u32[]{:S(2)}, u32[]{:S(2)}) %collective-permute-start.7) | collective-permute-done | bytes 294944 | tf_op jit(solution)/shard_map/ppermute | solution.py:324
  49.9 2.8 %collective-permute-done.8.b_ref = bf16[1152,128]{1,0:T(8,128)(2,1)S(1)} collective-permute-done((bf16[1152,128]{1,0:T(8,128)(2,1)S(1)}, bf16[1152,128]{1,0:T(8,128)(2,1)S(1)}, u32[]{:S(2)}, u32[]{:S(2)}) %collective-permute-start.8) | collective-permute-done | bytes 294944 | tf_op jit(solution)/shard_map/ppermute | solution.py:324
  52.8 2.9 %collective-permute-done.9.p3 = bf16[1152,128]{1,0:T(8,128)(2,1)S(1)} collective-permute-done((bf16[1152,128]{1,0:T(8,128)(2,1)S(1)}, bf16[1152,128]{1,0:T(8,128)(2,1)S(1)}, u32[]{:S(2)}, u32[]{:S(2)}) %collective-permute-start.9) | collective-permute-done | bytes 294944 | tf_op jit(solution)/shard_map/ppermute | solution.py:324
  57.3 11.7 %all-to-all-start.1 = ((f32[64,2,128]{2,1,0:T(2,128)}), f32[64,2,128]{2,1,0:T(2,128)S(1)}, u32[]{:S(2)}, u32[]{:S(2)}) async-start(f32[64,2,128]{2,1,0:T(2,128)} %get-tuple-element.62), calls=%async_computation.1 | async-start | bytes 131072 | tf_op jit(solution)/shard_map/all_to_all | solution.py:89
  69.0 4.6 %collective-permute-start.10 = (bf16[144,128]{1,0:T(8,128)(2,1)S(1)}, bf16[144,128]{1,0:T(8,128)(2,1)S(1)}, u32[]{:S(2)}, u32[]{:S(2)}) collective-permute-start(bf16[144,128]{1,0:T(8,128)(2,1)S(1)} %get-tuple-element.64), channel_id=1, source_target_pairs={{0,16},{16,32},{32,48},{48,64},{64,80},{80,96},{96,112},{112,128},... | collective-permute-start | bytes 110600 | tf_op jit(solution)/shard_map/ppermute | solution.py:140
  75.6 4.5 %collective-permute-done.11.rest_6_ = bf16[144,128]{1,0:T(8,128)(2,1)S(1)} collective-permute-done((bf16[144,128]{1,0:T(8,128)(2,1)S(1)}, bf16[144,128]{1,0:T(8,128)(2,1)S(1)}, u32[]{:S(2)}, u32[]{:S(2)}) %collective-permute-start.11) | collective-permute-done | bytes 36896 | tf_op jit(solution)/shard_map/ppermute | solution.py:141
  80.1 4.6 %conv_second_far.1 = (bf16[1088,128]{1,0:T(8,128)(2,1)S(1)}, bf16[1088,128]{1,0:T(8,128)(2,1)S(1)}, bf16[6,320,384]{2,1,0:T(8,128)(2,1)S(1)}, bf16[3,80,384]{2,1,0:T(8,128)(2,1)S(1)}, bf16[3456,256]{1,0:T(8,128)(2,1)S(1)}) custom-call(s32[5]{0:T(128)S(1)} %stack.39.flag_ref, bf16[4,8,32,128]{3,2,1,0:T(8,128)(2,1)S(1)} %get-tuple-element.60.x_ref, ...), custom_call_target="tpu_custom_call" | custom-call | flops 1925185536 | bytes 8450068 | tf_op jit(solution)/shard_map/conv_second_far/pallas_call | solution.py:39
  84.9 3.4 %collective-permute-start.13 = (bf16[1088,128]{1,0:T(8,128)(2,1)S(1)}, bf16[1088,128]{1,0:T(8,128)(2,1)S(1)}, u32[]{:S(2)}, u32[]{:S(2)}) collective-permute-start(bf16[1088,128]{1,0:T(8,128)(2,1)S(1)} %get-tuple-element.71), channel_id=1, source_target_pairs={{0,2},{1,3},{2,0},{3,1},{4,6},{5,7},{6,4},{7,5},{8,10},{9,11},{10,... | collective-permute-start | bytes 835592 | tf_op jit(solution)/shard_map/ppermute | solution.py:324
  88.3 2.5 %conv_second_near.1 = (bf16[1088,128]{1,0:T(8,128)(2,1)S(1)}, bf16[1088,128]{1,0:T(8,128)(2,1)S(1)}) custom-call(bf16[6,320,384]{2,1,0:T(8,128)(2,1)S(1)} %get-tuple-element.66.patch_ref, bf16[3,80,384]{2,1,0:T(8,128)(2,1)S(1)} %get-tuple-element.67.side_ref, bf16[3456,256]{1,0:T(8,128)(2,1)S(1)} %get-tuple-element.68.w_ref), custom_call_target="tpu_custom_call" | custom-call | flops 1925185536 | bytes 3985408 | tf_op jit(solution)/shard_map/conv_second_near/pallas_call | solution.py:39
  90.9 2.9 %collective-permute-done.12.a_ref = bf16[1088,128]{1,0:T(8,128)(2,1)S(1)} collective-permute-done((bf16[1088,128]{1,0:T(8,128)(2,1)S(1)}, bf16[1088,128]{1,0:T(8,128)(2,1)S(1)}, u32[]{:S(2)}, u32[]{:S(2)}) %collective-permute-start.12) | collective-permute-done | bytes 278560 | tf_op jit(solution)/shard_map/ppermute | solution.py:324
  93.8 4.5 %collective-permute-done.13.b_ref = bf16[1088,128]{1,0:T(8,128)(2,1)S(1)} collective-permute-done((bf16[1088,128]{1,0:T(8,128)(2,1)S(1)}, bf16[1088,128]{1,0:T(8,128)(2,1)S(1)}, u32[]{:S(2)}, u32[]{:S(2)}) %collective-permute-start.13) | collective-permute-done | bytes 278560 | tf_op jit(solution)/shard_map/ppermute | solution.py:324
  99.5 2.4 %collective-permute-start.21 = (bf16[4,272,128]{2,1,0:T(8,128)(2,1)S(1)}, bf16[4,272,128]{2,1,0:T(8,128)(2,1)S(1)}, u32[]{:S(2)}, u32[]{:S(2)}) collective-permute-start(bf16[4,272,128]{2,1,0:T(8,128)(2,1)S(1)} %get-tuple-element.73.refs_0_), channel_id=1, source_target_pairs={{0,3},{1,0},{2,1},{3,2},{4,7},{5,4},{6,5},{7,6},{8,11},{9,8},{10,9... | collective-permute-start | bytes 835592 | tf_op jit(solution)/shard_map/ppermute | solution.py:324
  102.7 4.8 %collective-permute-start.15 = (bf16[4,40,128]{2,1,0:T(8,128)(2,1)S(1)}, bf16[4,40,128]{2,1,0:T(8,128)(2,1)S(1)}, u32[]{:S(2)}, u32[]{:S(2)}) collective-permute-start(bf16[4,40,128]{2,1,0:T(8,128)(2,1)S(1)} %get-tuple-element.74), channel_id=1, source_target_pairs={{0,16},{16,32},{32,48},{48,64},{64,80},{80,96},{96,112},{112,128},... | collective-permute-start | bytes 122888 | tf_op jit(solution)/shard_map/ppermute | solution.py:140
  109.4 4.9 %collective-permute-done.16.bot_ref = bf16[4,40,128]{2,1,0:T(8,128)(2,1)S(1)} collective-permute-done((bf16[4,40,128]{2,1,0:T(8,128)(2,1)S(1)}, bf16[4,40,128]{2,1,0:T(8,128)(2,1)S(1)}, u32[]{:S(2)}, u32[]{:S(2)}) %collective-permute-start.16) | collective-permute-done | bytes 40992 | tf_op jit(solution)/shard_map/ppermute | solution.py:141
  115.2 2.0 %collective-permute-start.20 = (bf16[4,80,128]{2,1,0:T(8,128)(2,1)S(1)}, bf16[4,80,128]{2,1,0:T(8,128)(2,1)S(1)}, u32[]{:S(2)}, u32[]{:S(2)}) collective-permute-start(bf16[4,80,128]{2,1,0:T(8,128)(2,1)S(1)} %pack.1.refs_1_), channel_id=1, source_target_pairs={{0,2},{1,3},{2,0},{3,1},{4,6},{5,7},{6,4},{7,5},{8,10},{9,11},{10,... | collective-permute-start | bytes 245768 | tf_op jit(solution)/shard_map/ppermute | solution.py:324
  121.7 4.2 %up_conv.1 = bf16[4,16,64,128]{3,2,1,0:T(8,128)(2,1)} custom-call(bf16[4,272,128]{2,1,0:T(8,128)(2,1)S(1)} %get-tuple-element.73.refs_0_, bf16[4,80,128]{2,1,0:T(8,128)(2,1)S(1)} %pack.1.refs_1_, bf16[4,272,128]{2,1,0:T(8,128)(2,1)S(1)} %collective-permute-done.17.after_ref.refs_2_, bf16[4,80,128]{2,1,0:T(8,128)(2,1)S(1)} %collective-permute-done.18.refs_3_, ...), custom_call_target="tpu_custom_call" | custom-call | tf_op jit(solution)/shard_map/up_conv/pallas_call | solution.py:430
  (42 shorter events, 23.4 us)
Async XLA Ops:
  3.2 32.3 %collective-permute-start.4 = (bf16[9,128,128]{2,1,0:T(8,128)(2,1)S(1)}, bf16[9,128,128]{2,1,0:T(8,128)(2,1)S(1)}, u32[]{:S(2)}, u32[]{:S(2)}) collective-permute-start(bf16[9,128,128]{2,1,0:T(8,128)(2,1)S(1)} %get-tuple-element.50), channel_id=1, source_target_pairs={{0,1},{1,2},{2,3},{3,0},{4,5},{5,6},{6,7},{7,4},{8,9},{9,10},{10,1... | collective-permute-start | bytes 884744 | tf_op jit(solution)/shard_map/ppermute | solution.py:324
  4.5 31.0 %collective-permute-start.5 = (bf16[9,128,128]{2,1,0:T(8,128)(2,1)S(1)}, bf16[9,128,128]{2,1,0:T(8,128)(2,1)S(1)}, u32[]{:S(2)}, u32[]{:S(2)}) collective-permute-start(bf16[9,128,128]{2,1,0:T(8,128)(2,1)S(1)} %get-tuple-element.51), channel_id=1, source_target_pairs={{0,2},{1,3},{2,0},{3,1},{4,6},{5,7},{6,4},{7,5},{8,10},{9,11},{10,... | collective-permute-start | bytes 884744 | tf_op jit(solution)/shard_map/ppermute | solution.py:324
  7.0 28.6 %collective-permute-start.6 = (bf16[9,128,128]{2,1,0:T(8,128)(2,1)S(1)}, bf16[9,128,128]{2,1,0:T(8,128)(2,1)S(1)}, u32[]{:S(2)}, u32[]{:S(2)}) collective-permute-start(bf16[9,128,128]{2,1,0:T(8,128)(2,1)S(1)} %get-tuple-element.52), channel_id=1, source_target_pairs={{0,3},{1,0},{2,1},{3,2},{4,7},{5,4},{6,5},{7,6},{8,11},{9,8},{10,9... | collective-permute-start | bytes 884744 | tf_op jit(solution)/shard_map/ppermute | solution.py:324
  8.1 18.9 %collective-permute-start = (bf16[8,32,128]{2,1,0:T(8,128)(2,1)S(1)}, bf16[8,32,128]{2,1,0:T(8,128)(2,1)S(1)}, u32[]{:S(2)}, u32[]{:S(2)}) collective-permute-start(bf16[8,32,128]{2,1,0:T(8,128)(2,1)S(1)} %get-tuple-element.41), channel_id=1, source_target_pairs={{0,16},{16,32},{32,48},{48,64},{64,80},{80,96},{96,112},{112,128},... | collective-permute-start | bytes 196616 | tf_op jit(solution)/shard_map/ppermute | solution.py:140
  14.3 12.7 %collective-permute-start.1 = (bf16[8,32,128]{2,1,0:T(8,128)(2,1)S(1)}, bf16[8,32,128]{2,1,0:T(8,128)(2,1)S(1)}, u32[]{:S(2)}, u32[]{:S(2)}) collective-permute-start(bf16[8,32,128]{2,1,0:T(8,128)(2,1)S(1)} %get-tuple-element.42), channel_id=1, source_target_pairs={{16,0},{32,16},{48,32},{64,48},{80,64},{96,80},{112,96},{128,112},... | collective-permute-start | bytes 196616 | tf_op jit(solution)/shard_map/ppermute | solution.py:141
  16.2 17.9 %all-to-all-start = ((f32[64,2,128]{2,1,0:T(2,128)}), f32[64,2,128]{2,1,0:T(2,128)S(1)}, u32[]{:S(2)}, u32[]{:S(2)}) async-start(f32[64,2,128]{2,1,0:T(2,128)} %get-tuple-element.49), calls=%async_computation | async-start | bytes 131072 | tf_op jit(solution)/shard_map/all_to_all | solution.py:89
  27.1 7.0 %collective-permute-start.2 = (bf16[8,3,16,128]{3,2,1,0:T(8,128)(2,1)S(1)}, bf16[8,3,16,128]{3,2,1,0:T(8,128)(2,1)S(1)}, u32[]{:S(2)}, u32[]{:S(2)}) collective-permute-start(bf16[8,3,16,128]{3,2,1,0:T(8,128)(2,1)S(1)} %get-tuple-element.45), channel_id=1, source_target_pairs={{0,4},{4,8},{8,12},{1,5},{5,9},{9,13},{2,6},{6,10},{10,14},{3,7},{... | collective-permute-start | bytes 294920 | tf_op jit(solution)/shard_map/ppermute | solution.py:147
  30.2 5.4 %collective-permute-start.3 = (bf16[8,3,16,128]{3,2,1,0:T(8,128)(2,1)S(1)}, bf16[8,3,16,128]{3,2,1,0:T(8,128)(2,1)S(1)}, u32[]{:S(2)}, u32[]{:S(2)}) collective-permute-start(bf16[8,3,16,128]{3,2,1,0:T(8,128)(2,1)S(1)} %get-tuple-element.46), channel_id=1, source_target_pairs={{4,0},{8,4},{12,8},{5,1},{9,5},{13,9},{6,2},{10,6},{14,10},{7,3},{... | collective-permute-start | bytes 294920 | tf_op jit(solution)/shard_map/ppermute | solution.py:148
  40.1 9.8 %collective-permute-start.7 = (bf16[1152,128]{1,0:T(8,128)(2,1)S(1)}, bf16[1152,128]{1,0:T(8,128)(2,1)S(1)}, u32[]{:S(2)}, u32[]{:S(2)}) collective-permute-start(bf16[1152,128]{1,0:T(8,128)(2,1)S(1)} %get-tuple-element.57), channel_id=1, source_target_pairs={{0,1},{1,2},{2,3},{3,0},{4,5},{5,6},{6,7},{7,4},{8,9},{9,10},{10,1... | collective-permute-start | bytes 884744 | tf_op jit(solution)/shard_map/ppermute | solution.py:324
  40.5 12.2 %collective-permute-start.8 = (bf16[1152,128]{1,0:T(8,128)(2,1)S(1)}, bf16[1152,128]{1,0:T(8,128)(2,1)S(1)}, u32[]{:S(2)}, u32[]{:S(2)}) collective-permute-start(bf16[1152,128]{1,0:T(8,128)(2,1)S(1)} %get-tuple-element.58), channel_id=1, source_target_pairs={{0,2},{1,3},{2,0},{3,1},{4,6},{5,7},{6,4},{7,5},{8,10},{9,11},{10,... | collective-permute-start | bytes 884744 | tf_op jit(solution)/shard_map/ppermute | solution.py:324
  43.6 12.1 %collective-permute-start.9 = (bf16[1152,128]{1,0:T(8,128)(2,1)S(1)}, bf16[1152,128]{1,0:T(8,128)(2,1)S(1)}, u32[]{:S(2)}, u32[]{:S(2)}) collective-permute-start(bf16[1152,128]{1,0:T(8,128)(2,1)S(1)} %get-tuple-element.59), channel_id=1, source_target_pairs={{0,3},{1,0},{2,1},{3,2},{4,7},{5,4},{6,5},{7,6},{8,11},{9,8},{10,9... | collective-permute-start | bytes 884744 | tf_op jit(solution)/shard_map/ppermute | solution.py:324
  57.3 22.8 %all-to-all-start.1 = ((f32[64,2,128]{2,1,0:T(2,128)}), f32[64,2,128]{2,1,0:T(2,128)S(1)}, u32[]{:S(2)}, u32[]{:S(2)}) async-start(f32[64,2,128]{2,1,0:T(2,128)} %get-tuple-element.62), calls=%async_computation.1 | async-start | bytes 131072 | tf_op jit(solution)/shard_map/all_to_all | solution.py:89
  69.0 6.5 %collective-permute-start.10 = (bf16[144,128]{1,0:T(8,128)(2,1)S(1)}, bf16[144,128]{1,0:T(8,128)(2,1)S(1)}, u32[]{:S(2)}, u32[]{:S(2)}) collective-permute-start(bf16[144,128]{1,0:T(8,128)(2,1)S(1)} %get-tuple-element.64), channel_id=1, source_target_pairs={{0,16},{16,32},{32,48},{48,64},{64,80},{80,96},{96,112},{112,128},... | collective-permute-start | bytes 110600 | tf_op jit(solution)/shard_map/ppermute | solution.py:140
  73.6 6.5 %collective-permute-start.11 = (bf16[144,128]{1,0:T(8,128)(2,1)S(1)}, bf16[144,128]{1,0:T(8,128)(2,1)S(1)}, u32[]{:S(2)}, u32[]{:S(2)}) collective-permute-start(bf16[144,128]{1,0:T(8,128)(2,1)S(1)} %get-tuple-element.65), channel_id=1, source_target_pairs={{16,0},{32,16},{48,32},{64,48},{80,64},{96,80},{112,96},{128,112},... | collective-permute-start | bytes 110600 | tf_op jit(solution)/shard_map/ppermute | solution.py:141
  84.7 9.1 %collective-permute-start.12 = (bf16[1088,128]{1,0:T(8,128)(2,1)S(1)}, bf16[1088,128]{1,0:T(8,128)(2,1)S(1)}, u32[]{:S(2)}, u32[]{:S(2)}) collective-permute-start(bf16[1088,128]{1,0:T(8,128)(2,1)S(1)} %get-tuple-element.70), channel_id=1, source_target_pairs={{0,1},{1,2},{2,3},{3,0},{4,5},{5,6},{6,7},{7,4},{8,9},{9,10},{10,1... | collective-permute-start | bytes 835592 | tf_op jit(solution)/shard_map/ppermute | solution.py:324
  84.9 13.4 %collective-permute-start.13 = (bf16[1088,128]{1,0:T(8,128)(2,1)S(1)}, bf16[1088,128]{1,0:T(8,128)(2,1)S(1)}, u32[]{:S(2)}, u32[]{:S(2)}) collective-permute-start(bf16[1088,128]{1,0:T(8,128)(2,1)S(1)} %get-tuple-element.71), channel_id=1, source_target_pairs={{0,2},{1,3},{2,0},{3,1},{4,6},{5,7},{6,4},{7,5},{8,10},{9,11},{10,... | collective-permute-start | bytes 835592 | tf_op jit(solution)/shard_map/ppermute | solution.py:324
  90.8 7.5 %collective-permute-start.14 = (bf16[1088,128]{1,0:T(8,128)(2,1)S(1)}, bf16[1088,128]{1,0:T(8,128)(2,1)S(1)}, u32[]{:S(2)}, u32[]{:S(2)}) collective-permute-start(bf16[1088,128]{1,0:T(8,128)(2,1)S(1)} %get-tuple-element.72), channel_id=1, source_target_pairs={{0,3},{1,0},{2,1},{3,2},{4,7},{5,4},{6,5},{7,6},{8,11},{9,8},{10,9... | collective-permute-start | bytes 835592 | tf_op jit(solution)/shard_map/ppermute | solution.py:324
  99.2 15.2 %collective-permute-start.17 = (bf16[4,272,128]{2,1,0:T(8,128)(2,1)S(1)}, bf16[4,272,128]{2,1,0:T(8,128)(2,1)S(1)}, u32[]{:S(2)}, u32[]{:S(2)}) collective-permute-start(bf16[4,272,128]{2,1,0:T(8,128)(2,1)S(1)} %get-tuple-element.73.refs_0_), channel_id=1, source_target_pairs={{0,1},{1,2},{2,3},{3,0},{4,5},{5,6},{6,7},{7,4},{8,9},{9,10},{10,1... | collective-permute-start | bytes 835592 | tf_op jit(solution)/shard_map/ppermute | solution.py:324
  99.5 18.2 %collective-permute-start.21 = (bf16[4,272,128]{2,1,0:T(8,128)(2,1)S(1)}, bf16[4,272,128]{2,1,0:T(8,128)(2,1)S(1)}, u32[]{:S(2)}, u32[]{:S(2)}) collective-permute-start(bf16[4,272,128]{2,1,0:T(8,128)(2,1)S(1)} %get-tuple-element.73.refs_0_), channel_id=1, source_target_pairs={{0,3},{1,0},{2,1},{3,2},{4,7},{5,4},{6,5},{7,6},{8,11},{9,8},{10,9... | collective-permute-start | bytes 835592 | tf_op jit(solution)/shard_map/ppermute | solution.py:324
  101.9 15.8 %collective-permute-start.19 = (bf16[4,272,128]{2,1,0:T(8,128)(2,1)S(1)}, bf16[4,272,128]{2,1,0:T(8,128)(2,1)S(1)}, u32[]{:S(2)}, u32[]{:S(2)}) collective-permute-start(bf16[4,272,128]{2,1,0:T(8,128)(2,1)S(1)} %get-tuple-element.73.refs_0_), channel_id=1, source_target_pairs={{0,2},{1,3},{2,0},{3,1},{4,6},{5,7},{6,4},{7,5},{8,10},{9,11},{10,... | collective-permute-start | bytes 835592 | tf_op jit(solution)/shard_map/ppermute | solution.py:324
  102.7 6.7 %collective-permute-start.15 = (bf16[4,40,128]{2,1,0:T(8,128)(2,1)S(1)}, bf16[4,40,128]{2,1,0:T(8,128)(2,1)S(1)}, u32[]{:S(2)}, u32[]{:S(2)}) collective-permute-start(bf16[4,40,128]{2,1,0:T(8,128)(2,1)S(1)} %get-tuple-element.74), channel_id=1, source_target_pairs={{0,16},{16,32},{32,48},{48,64},{64,80},{80,96},{96,112},{112,128},... | collective-permute-start | bytes 122888 | tf_op jit(solution)/shard_map/ppermute | solution.py:140
  107.5 6.8 %collective-permute-start.16 = (bf16[4,40,128]{2,1,0:T(8,128)(2,1)S(1)}, bf16[4,40,128]{2,1,0:T(8,128)(2,1)S(1)}, u32[]{:S(2)}, u32[]{:S(2)}) collective-permute-start(bf16[4,40,128]{2,1,0:T(8,128)(2,1)S(1)} %get-tuple-element.75), channel_id=1, source_target_pairs={{16,0},{32,16},{48,32},{64,48},{80,64},{96,80},{112,96},{128,112},... | collective-permute-start | bytes 122888 | tf_op jit(solution)/shard_map/ppermute | solution.py:141
  115.2 4.9 %collective-permute-start.20 = (bf16[4,80,128]{2,1,0:T(8,128)(2,1)S(1)}, bf16[4,80,128]{2,1,0:T(8,128)(2,1)S(1)}, u32[]{:S(2)}, u32[]{:S(2)}) collective-permute-start(bf16[4,80,128]{2,1,0:T(8,128)(2,1)S(1)} %pack.1.refs_1_), channel_id=1, source_target_pairs={{0,2},{1,3},{2,0},{3,1},{4,6},{5,7},{6,4},{7,5},{8,10},{9,11},{10,... | collective-permute-start | bytes 245768 | tf_op jit(solution)/shard_map/ppermute | solution.py:324
  117.2 4.5 %collective-permute-start.18 = (bf16[4,80,128]{2,1,0:T(8,128)(2,1)S(1)}, bf16[4,80,128]{2,1,0:T(8,128)(2,1)S(1)}, u32[]{:S(2)}, u32[]{:S(2)}) collective-permute-start(bf16[4,80,128]{2,1,0:T(8,128)(2,1)S(1)} %pack.1.refs_1_), channel_id=1, source_target_pairs={{0,1},{1,2},{2,3},{3,0},{4,5},{5,6},{6,7},{7,4},{8,9},{9,10},{10,1... | collective-permute-start | bytes 245768 | tf_op jit(solution)/shard_map/ppermute | solution.py:324
  (2 other events, 14.0 us)

commit v6 on v5

--- a/solution.py
+++ b/solution.py
@@ -103,23 +103,19 @@
         at += n
 
 
-def first_body(flag_ref, x_hbm, c1_hbm, c2_hbm, w_hbm, x_ref, c1_ref, c2_ref, slot_ref, *rest):
-    edges, pieces, sem = rest[:4], rest[4:8], rest[8]
-    pairs = [(x_hbm, x_ref), (c1_hbm, c1_ref), (c2_hbm, c2_ref)]
-    for k, piece in enumerate(pieces):
-        block = pl.multiple_of(lax.rem(flag_ref[4] + k, 4) * CH, CH)
-        pairs.append((w_hbm.at[:, :, pl.ds(block, CH)], piece))
-    copies = [pltpu.make_async_copy(src, dst, sem.at[i]) for i, (src, dst) in enumerate(pairs)]
+def first_body(x_hbm, c1_hbm, c2_hbm, x_ref, c1_ref, c2_ref, slot_ref, *rest):
+    edges, sem = rest[:4], rest[4]
+    copies = [
+        pltpu.make_async_copy(src, dst, sem.at[i])
+        for i, (src, dst) in enumerate(((x_hbm, x_ref), (c1_hbm, c1_ref), (c2_hbm, c2_ref)))
+    ]
     for c in copies:
         c.start()
-    for c in copies[:3]:
+    for c in copies:
         c.wait()
     x, c1, c2 = x_ref[...].astype(F32), c1_ref[...].astype(F32), c2_ref[...].astype(F32)
-    mean, m2 = local_stats(x.reshape(-1, CH))
-    store_stats(slot_ref, mean, m2)
+    store_stats(slot_ref, *local_stats(x.reshape(-1, CH)))
     store_edges((c1, x, c2), edges)
-    for c in copies[3:]:
-        c.wait()
 
 
 def corner_body(top_ref, bot_ref, lef_ref, rig_ref, lo_ref, ro_ref):
@@ -280,16 +276,16 @@
     copies[3].wait()
 
 
-def near_body(patch_ref, side_ref, w_ref, out3, out0):
-    multiply(patch_ref, side_ref, w_ref, (out3, out0))
-
-
-def conv(flags, x, cache, stats, halo, cache_at, act_at, around, weight, ext, name, after=()):
+def near_body(patch_ref, side_ref, w_ref, *rest):
+    multiply(patch_ref, side_ref, w_ref, rest[-2:])
+
+
+def conv(flags, x, cache, stats, halo, cache_at, act_at, around, weight, ext, name, after=(), cut=None):
     n = x.shape[0] * ROWS * COLS + ROWS * 8 * ext
     depth, width = weight.shape
     flops = n * depth * width
     piece = sds((n, CH))
-    body = functools.partial(far_body, ext, cache_at, act_at, len(after))
+    body = functools.partial(far_body, ext, cache_at, act_at, 0)
     out2, out1, patch, side, near = call(
         body,
         [piece] * 2
@@ -307,16 +303,55 @@
         flops=flops,
         limit=20,
         name=name + "_far",
-    )(flags, x, cache, stats, *halo, *around, Left(weight, HBM), *[Left(a) for a in after])
+    )(flags, x, cache, stats, *halo, *around, Left(weight, HBM))
     got2 = to_peer(out2, 2)
     got1 = to_peer(out1, 1)
-    out3, own = call(near_body, [piece] * 2, flops=flops, limit=16, name=name + "_near")(patch, side, near)
-    (far,) = call(add_body, [sds((n, CH), F32)], name=name + "_add")(got1, got2)
-    return own, far, to_peer(out3, 3)
+    out3, own = call(near_body, [piece] * 2, flops=flops, limit=16, name=name + "_near")(
+        patch, side, near, *[Left(a) for a in after]
+    )
+    total = sds((n, CH), F32)
+    if cut is None:
+        return [own, *call(add_body, [total], name=name + "_add")(got1, got2), to_peer(out3, 3)]
+    far, *cut = call(
+        add_cut_body,
+        [total] + [sds(cut.shape[:2] + (CH,))] * 4,
+        scratch=[pltpu.SemaphoreType.DMA((4,))],
+        name=name + "_add",
+    )(flags, got1, got2, Left(cut, HBM))
+    return [own, far, to_peer(out3, 3)], cut
 
 
 def add_body(a_ref, b_ref, o_ref):
     o_ref[...] = a_ref[...].astype(F32) + b_ref[...].astype(F32)
+
+
+def add_cut_body(flag_ref, a_ref, b_ref, w_hbm, o_ref, *rest):
+    pieces, sem = rest[:4], rest[4]
+    copies = []
+    for k, piece in enumerate(pieces):
+        block = pl.multiple_of(lax.rem(flag_ref[4] + k, 4) * CH, CH)
+        copies.append(pltpu.make_async_copy(w_hbm.at[:, :, pl.ds(block, CH)], piece, sem.at[k]))
+        copies[-1].start()
+    add_body(a_ref, b_ref, o_ref)
+    for c in copies:
+        c.wait()
+
+
+def gate_body(*refs):
+    del refs
+
+
+def gate(arrays, after):
+    n = len(arrays)
+    return pl.pallas_call(
+        gate_body,
+        out_shape=[sds(a.shape) for a in arrays],
+        in_specs=[ANY] * (n + 1),
+        out_specs=[ANY] * n,
+        input_output_aliases={i: i for i in range(n)},
+        compiler_params=pltpu.CompilerParams(vmem_limit_bytes=8 * MIB),
+        name="gate",
+    )(*arrays, after)
 
 
 def to_peer(piece, k):
@@ -453,20 +488,17 @@
         first_body,
         [sds(features.shape), sds(cache_first.shape), sds(cache_second.shape), slots]
         + [sds((8, COLS, CH))] * 2
-        + [sds((8, WIDE, 16, CH))] * 2
-        + [sds(weight_up.shape[:2] + (CH,))] * 4,
-        scratch=[pltpu.SemaphoreType.DMA((7,))],
+        + [sds((8, WIDE, 16, CH))] * 2,
+        scratch=[pltpu.SemaphoreType.DMA((3,))],
         limit=20,
         name="first",
-    )(flags, *[Left(a, HBM) for a in (features, cache_first, cache_second, weight_up)])
-    edges, w_pieces = edges[:4], edges[4:]
-    w_got = to_peers(w_pieces[1:])
+    )(*[Left(a, HBM) for a in (features, cache_first, cache_second)])
     stats = spread(stats)
     rows = swap_rows(*edges[:2])
     cornered = call(corner_body, [sds((8, WIDE, 16, CH))] * 2, name="corners")(*rows, *edges[2:])
     halo = rows + swap_columns(*cornered)
-    pieces = conv(
-        flags, x, c1, stats, halo, 0, 2, (), weight_first.reshape(-1, 4 * CH), 2, "conv_first", after=w_got
+    pieces, w_pieces = conv(
+        flags, x, c1, stats, halo, 0, 2, (), weight_first.reshape(-1, 4 * CH), 2, "conv_first", cut=weight_up
     )
     hidden, side, stats, top, bot = call(
         hidden_body,
@@ -474,10 +506,11 @@
         limit=12,
         name="hidden",
     )(*pieces)
+    w_got = to_peers(gate(w_pieces[1:], stats))
     stats = spread(stats)
     around = (side,) + swap_rows(top, bot)
     pieces = conv(
-        flags, hidden, c2, stats, halo, 6, None, around, weight_second.reshape(-1, 4 * CH), 1, "conv_second"
+        flags, hidden, c2, stats, halo, 6, None, around, weight_second.reshape(-1, 4 * CH), 1, "conv_second", w_got
     )
     resid, top, bot = call(
         resid_body,

time: 127 us -> 127 us (level)
  waiting for transfers between devices: 34.4 us -> 32.4 us
    ppermute x15, waiting for transfers between devices: 20.8 us -> 18.7 us  [to_peer(): return lax.ppermute(piece, 'col', [(i, (i + k) % n) for i in range(n)])]
  transfers between devices with their start and end apart: 25 -> 25, of which waited for: 11 -> 11; matrix products, arithmetic and copies ran while one was open for 0% -> 0% of each run, Pallas kernels for 5% -> 10%
where the time goes in v6:
time: 127 us; the launch traced here: 126 us
  starting transfers between devices  67.9 us (53%)
  waiting for transfers between devices  32.4 us (26%)
  Pallas kernels  25.6 us (20%)
    all_to_all x2, starting transfers between devices, spread(): return lax.all_to_all(slots, HA + ('wa',), 0, 0, tiled=True)  23.1 us
    pallas_call x12, Pallas kernels, run(): pl.pallas_call(body, out_shape=list(outs), in_specs=specs, out_specs=[VME...  21.5 us
    ppermute x15, starting transfers between devices, to_peer(): return lax.ppermute(piece, 'col', [(i, (i + k) % n) for i in range(n)])  18.8 us
    ppermute x15, waiting for transfers between devices, to_peer(): return lax.ppermute(piece, 'col', [(i, (i + k) % n) for i in range(n)])  18.7 us
    ppermute x3, starting transfers between devices, swap_rows(): above = lax.ppermute(bot, HA, [(i, i + 1) for i in range(n - 1)])  15.8 us
    ppermute x3, waiting for transfers between devices, swap_rows(): below = lax.ppermute(top, HA, [(i + 1, i) for i in range(n - 1)])  9.73 us
    ppermute x3, starting transfers between devices, swap_rows(): below = lax.ppermute(top, HA, [(i + 1, i) for i in range(n - 1)])  5.76 us
    pallas_call x1, Pallas kernels, up_conv(): pl.pallas_call(up_body, out_shape=sds(out), grid=(frames,), in_specs=spec...  4.15 us
  transfers between devices with their start and end apart: 25, of which 11 were waited for; matrix products, arithmetic and copies ran while one was open for 0% of the time, Pallas kernels for 10%

profile of v6, /device:TPU:97, one launch (start us, length us, event | category | flops | bytes accessed | tf_op | source)
XLA Modules:
  0.0 126.2 jit_solution(7566127621159225872)
XLA Ops:
  0.0 2.6 %first.1 = (bf16[4,8,32,128]{3,2,1,0:T(8,128)(2,1)S(1)}, bf16[2,8,32,128]{3,2,1,0:T(8,128)(2,1)S(1)}, bf16[2,8,32,128]{3,2,1,0:T(8,128)(2,1)S(1)}, f32[64,2,128]...) custom-call(bf16[4,8,32,128]{3,2,1,0:T(8,128)(2,1)} %x_ref.1, ...), custom_call_target="tpu_custom_call" | custom-call | bytes 1441792 | tf_op jit(solution)/shard_map/first/pallas_call | solution.py:39
  2.6 5.3 %collective-permute-start = (bf16[8,32,128]{2,1,0:T(8,128)(2,1)S(1)}, bf16[8,32,128]{2,1,0:T(8,128)(2,1)S(1)}, u32[]{:S(2)}, u32[]{:S(2)}) collective-permute-start(bf16[8,32,128]{2,1,0:T(8,128)(2,1)S(1)} %get-tuple-element.45), channel_id=1, source_target_pairs={{0,16},{16,32},{32,48},{48,64},{64,80},{80,96},{96,112},{112,128},... | collective-permute-start | bytes 196616 | tf_op jit(solution)/shard_map/ppermute | solution.py:136
  7.9 1.9 %collective-permute-start.1 = (bf16[8,32,128]{2,1,0:T(8,128)(2,1)S(1)}, bf16[8,32,128]{2,1,0:T(8,128)(2,1)S(1)}, u32[]{:S(2)}, u32[]{:S(2)}) collective-permute-start(bf16[8,32,128]{2,1,0:T(8,128)(2,1)S(1)} %get-tuple-element.46), channel_id=1, source_target_pairs={{16,0},{32,16},{48,32},{64,48},{80,64},{96,80},{112,96},{128,112},... | collective-permute-start | bytes 196616 | tf_op jit(solution)/shard_map/ppermute | solution.py:137
  9.8 10.8 %all-to-all-start = ((f32[64,2,128]{2,1,0:T(2,128)}), f32[64,2,128]{2,1,0:T(2,128)S(1)}, u32[]{:S(2)}, u32[]{:S(2)}) async-start(f32[64,2,128]{2,1,0:T(2,128)} %get-tuple-element.53), calls=%async_computation | async-start | bytes 131072 | tf_op jit(solution)/shard_map/all_to_all | solution.py:89
  20.7 3.1 %collective-permute-start.2 = (bf16[8,3,16,128]{3,2,1,0:T(8,128)(2,1)S(1)}, bf16[8,3,16,128]{3,2,1,0:T(8,128)(2,1)S(1)}, u32[]{:S(2)}, u32[]{:S(2)}) collective-permute-start(bf16[8,3,16,128]{3,2,1,0:T(8,128)(2,1)S(1)} %get-tuple-element.49), channel_id=1, source_target_pairs={{0,4},{4,8},{8,12},{1,5},{5,9},{9,13},{2,6},{6,10},{10,14},{3,7},{... | collective-permute-start | bytes 294920 | tf_op jit(solution)/shard_map/ppermute | solution.py:143
  25.2 2.5 %all-to-all-done.st_ref = f32[64,2,128]{2,1,0:T(2,128)S(1)} async-done(((f32[64,2,128]{2,1,0:T(2,128)}), f32[64,2,128]{2,1,0:T(2,128)S(1)}, u32[]{:S(2)}, u32[]{:S(2)}) %all-to-all-start) | async-done | bytes 65568 | tf_op jit(solution)/shard_map/all_to_all | solution.py:89
  29.2 4.5 %conv_first_far.1 = (bf16[1152,128]{1,0:T(8,128)(2,1)S(1)}, bf16[1152,128]{1,0:T(8,128)(2,1)S(1)}, bf16[6,320,384]{2,1,0:T(8,128)(2,1)S(1)}, bf16[3,160,384]{2,1,0:T(8,128)(2,1)S(1)}, bf16[3456,256]{1,0:T(8,128)(2,1)S(1)}) custom-call(s32[5]{0:T(128)S(1)} %stack.39.flag_ref, bf16[4,8,32,128]{3,2,1,0:T(8,128)(2,1)S(1)} %get-tuple-element.51.x_ref, ...), custom_call_target="tpu_custom_call" | custom-call | flops 2038431744 | bytes 8527892 | tf_op jit(solution)/shard_map/conv_first_far/pallas_call | solution.py:39
  34.9 2.4 %collective-permute-start.5 = (bf16[1152,128]{1,0:T(8,128)(2,1)S(1)}, bf16[1152,128]{1,0:T(8,128)(2,1)S(1)}, u32[]{:S(2)}, u32[]{:S(2)}) collective-permute-start(bf16[1152,128]{1,0:T(8,128)(2,1)S(1)} %get-tuple-element.59), channel_id=1, source_target_pairs={{0,2},{1,3},{2,0},{3,1},{4,6},{5,7},{6,4},{7,5},{8,10},{9,11},{10,... | collective-permute-start | bytes 884744 | tf_op jit(solution)/shard_map/ppermute | solution.py:359
  37.4 2.5 %conv_first_near.1 = (bf16[1152,128]{1,0:T(8,128)(2,1)S(1)}, bf16[1152,128]{1,0:T(8,128)(2,1)S(1)}) custom-call(bf16[6,320,384]{2,1,0:T(8,128)(2,1)S(1)} %get-tuple-element.54.patch_ref, bf16[3,160,384]{2,1,0:T(8,128)(2,1)S(1)} %get-tuple-element.55.side_ref, bf16[3456,256]{1,0:T(8,128)(2,1)S(1)} %get-tuple-element.56.w_ref), custom_call_target="tpu_custom_call" | custom-call | flops 2038431744 | bytes 4202496 | tf_op jit(solution)/shard_map/conv_first_near/pallas_call | solution.py:39
  41.7 7.3 %collective-permute-done.5.b_ref = bf16[1152,128]{1,0:T(8,128)(2,1)S(1)} collective-permute-done((bf16[1152,128]{1,0:T(8,128)(2,1)S(1)}, bf16[1152,128]{1,0:T(8,128)(2,1)S(1)}, u32[]{:S(2)}, u32[]{:S(2)}) %collective-permute-start.5) | collective-permute-done | bytes 294944 | tf_op jit(solution)/shard_map/ppermute | solution.py:359
  52.5 12.3 %all-to-all-start.1 = ((f32[64,2,128]{2,1,0:T(2,128)}), f32[64,2,128]{2,1,0:T(2,128)S(1)}, u32[]{:S(2)}, u32[]{:S(2)}) async-start(f32[64,2,128]{2,1,0:T(2,128)} %get-tuple-element.64.refs_3_), calls=%async_computation.1 | async-start | bytes 131072 | tf_op jit(solution)/shard_map/all_to_all | solution.py:89
  67.6 5.4 %collective-permute-start.7 = (bf16[144,128]{1,0:T(8,128)(2,1)S(1)}, bf16[144,128]{1,0:T(8,128)(2,1)S(1)}, u32[]{:S(2)}, u32[]{:S(2)}) collective-permute-start(bf16[144,128]{1,0:T(8,128)(2,1)S(1)} %get-tuple-element.66), channel_id=1, source_target_pairs={{0,16},{16,32},{32,48},{48,64},{64,80},{80,96},{96,112},{112,128},... | collective-permute-start | bytes 110600 | tf_op jit(solution)/shard_map/ppermute | solution.py:136
  73.0 1.9 %collective-permute-start.8 = (bf16[144,128]{1,0:T(8,128)(2,1)S(1)}, bf16[144,128]{1,0:T(8,128)(2,1)S(1)}, u32[]{:S(2)}, u32[]{:S(2)}) collective-permute-start(bf16[144,128]{1,0:T(8,128)(2,1)S(1)} %get-tuple-element.67), channel_id=1, source_target_pairs={{16,0},{32,16},{48,32},{64,48},{80,64},{96,80},{112,96},{128,112},... | collective-permute-start | bytes 110600 | tf_op jit(solution)/shard_map/ppermute | solution.py:137
  74.9 4.8 %collective-permute-done.8.rest_6_ = bf16[144,128]{1,0:T(8,128)(2,1)S(1)} collective-permute-done((bf16[144,128]{1,0:T(8,128)(2,1)S(1)}, bf16[144,128]{1,0:T(8,128)(2,1)S(1)}, u32[]{:S(2)}, u32[]{:S(2)}) %collective-permute-start.8) | collective-permute-done | bytes 36896 | tf_op jit(solution)/shard_map/ppermute | solution.py:137
  79.7 4.5 %conv_second_far.1 = (bf16[1088,128]{1,0:T(8,128)(2,1)S(1)}, bf16[1088,128]{1,0:T(8,128)(2,1)S(1)}, bf16[6,320,384]{2,1,0:T(8,128)(2,1)S(1)}, bf16[3,80,384]{2,1,0:T(8,128)(2,1)S(1)}, bf16[3456,256]{1,0:T(8,128)(2,1)S(1)}) custom-call(s32[5]{0:T(128)S(1)} %stack.39.flag_ref, bf16[4,8,32,128]{3,2,1,0:T(8,128)(2,1)S(1)} %get-tuple-element.62.x_ref, ...), custom_call_target="tpu_custom_call" | custom-call | flops 1925185536 | bytes 8450068 | tf_op jit(solution)/shard_map/conv_second_far/pallas_call | solution.py:39
  84.4 2.2 %collective-permute-start.13 = (bf16[1088,128]{1,0:T(8,128)(2,1)S(1)}, bf16[1088,128]{1,0:T(8,128)(2,1)S(1)}, u32[]{:S(2)}, u32[]{:S(2)}) collective-permute-start(bf16[1088,128]{1,0:T(8,128)(2,1)S(1)} %get-tuple-element.79), channel_id=1, source_target_pairs={{0,2},{1,3},{2,0},{3,1},{4,6},{5,7},{6,4},{7,5},{8,10},{9,11},{10,... | collective-permute-start | bytes 835592 | tf_op jit(solution)/shard_map/ppermute | solution.py:359
  86.6 2.5 %conv_second_near.1 = (bf16[1088,128]{1,0:T(8,128)(2,1)S(1)}, bf16[1088,128]{1,0:T(8,128)(2,1)S(1)}) custom-call(bf16[6,320,384]{2,1,0:T(8,128)(2,1)S(1)} %get-tuple-element.68.patch_ref, bf16[3,80,384]{2,1,0:T(8,128)(2,1)S(1)} %get-tuple-element.69.side_ref, bf16[3456,256]{1,0:T(8,128)(2,1)S(1)} %get-tuple-element.70.w_ref, ...), custom_call_target="tpu_custom_call" | custom-call | flops 1925185536 | bytes 4870144 | tf_op jit(solution)/shard_map/conv_second_near/pallas_call | solution.py:39
  89.1 2.1 %collective-permute-start.14 = (bf16[1088,128]{1,0:T(8,128)(2,1)S(1)}, bf16[1088,128]{1,0:T(8,128)(2,1)S(1)}, u32[]{:S(2)}, u32[]{:S(2)}) collective-permute-start(bf16[1088,128]{1,0:T(8,128)(2,1)S(1)} %get-tuple-element.80), channel_id=1, source_target_pairs={{0,3},{1,0},{2,1},{3,2},{4,7},{5,4},{6,5},{7,6},{8,11},{9,8},{10,9... | collective-permute-start | bytes 835592 | tf_op jit(solution)/shard_map/ppermute | solution.py:359
  91.2 5.5 %collective-permute-done.12.a_ref = bf16[1088,128]{1,0:T(8,128)(2,1)S(1)} collective-permute-done((bf16[1088,128]{1,0:T(8,128)(2,1)S(1)}, bf16[1088,128]{1,0:T(8,128)(2,1)S(1)}, u32[]{:S(2)}, u32[]{:S(2)}) %collective-permute-start.12) | collective-permute-done | bytes 278560 | tf_op jit(solution)/shard_map/ppermute | solution.py:359
  102.6 5.1 %collective-permute-start.15 = (bf16[4,40,128]{2,1,0:T(8,128)(2,1)S(1)}, bf16[4,40,128]{2,1,0:T(8,128)(2,1)S(1)}, u32[]{:S(2)}, u32[]{:S(2)}) collective-permute-start(bf16[4,40,128]{2,1,0:T(8,128)(2,1)S(1)} %get-tuple-element.82), channel_id=1, source_target_pairs={{0,16},{16,32},{32,48},{48,64},{64,80},{80,96},{96,112},{112,128},... | collective-permute-start | bytes 122888 | tf_op jit(solution)/shard_map/ppermute | solution.py:136
  107.8 1.9 %collective-permute-start.16 = (bf16[4,40,128]{2,1,0:T(8,128)(2,1)S(1)}, bf16[4,40,128]{2,1,0:T(8,128)(2,1)S(1)}, u32[]{:S(2)}, u32[]{:S(2)}) collective-permute-start(bf16[4,40,128]{2,1,0:T(8,128)(2,1)S(1)} %get-tuple-element.83), channel_id=1, source_target_pairs={{16,0},{32,16},{48,32},{64,48},{80,64},{96,80},{112,96},{128,112},... | collective-permute-start | bytes 122888 | tf_op jit(solution)/shard_map/ppermute | solution.py:137
  109.7 4.9 %collective-permute-done.16.bot_ref = bf16[4,40,128]{2,1,0:T(8,128)(2,1)S(1)} collective-permute-done((bf16[4,40,128]{2,1,0:T(8,128)(2,1)S(1)}, bf16[4,40,128]{2,1,0:T(8,128)(2,1)S(1)}, u32[]{:S(2)}, u32[]{:S(2)}) %collective-permute-start.16) | collective-permute-done | bytes 40992 | tf_op jit(solution)/shard_map/ppermute | solution.py:137
  118.7 2.6 %collective-permute-done.20.refs_5_ = bf16[4,80,128]{2,1,0:T(8,128)(2,1)S(1)} collective-permute-done((bf16[4,80,128]{2,1,0:T(8,128)(2,1)S(1)}, bf16[4,80,128]{2,1,0:T(8,128)(2,1)S(1)}, u32[]{:S(2)}, u32[]{:S(2)}) %collective-permute-start.20) | collective-permute-done | bytes 81952 | tf_op jit(solution)/shard_map/ppermute | solution.py:359
  122.1 4.2 %up_conv.1 = bf16[4,16,64,128]{3,2,1,0:T(8,128)(2,1)} custom-call(bf16[4,272,128]{2,1,0:T(8,128)(2,1)S(1)} %get-tuple-element.81.refs_0_, bf16[4,80,128]{2,1,0:T(8,128)(2,1)S(1)} %pack.1.refs_1_, bf16[4,272,128]{2,1,0:T(8,128)(2,1)S(1)} %collective-permute-done.17.after_ref.refs_2_, bf16[4,80,128]{2,1,0:T(8,128)(2,1)S(1)} %collective-permute-done.18.refs_3_, ...), custom_call_target="tpu_custom_call" | custom-call | tf_op jit(solution)/shard_map/up_conv/pallas_call | solution.py:465
  (43 shorter events, 23.1 us)
Async XLA Ops:
  2.6 18.0 %collective-permute-start = (bf16[8,32,128]{2,1,0:T(8,128)(2,1)S(1)}, bf16[8,32,128]{2,1,0:T(8,128)(2,1)S(1)}, u32[]{:S(2)}, u32[]{:S(2)}) collective-permute-start(bf16[8,32,128]{2,1,0:T(8,128)(2,1)S(1)} %get-tuple-element.45), channel_id=1, source_target_pairs={{0,16},{16,32},{32,48},{48,64},{64,80},{80,96},{96,112},{112,128},... | collective-permute-start | bytes 196616 | tf_op jit(solution)/shard_map/ppermute | solution.py:136
  7.9 12.7 %collective-permute-start.1 = (bf16[8,32,128]{2,1,0:T(8,128)(2,1)S(1)}, bf16[8,32,128]{2,1,0:T(8,128)(2,1)S(1)}, u32[]{:S(2)}, u32[]{:S(2)}) collective-permute-start(bf16[8,32,128]{2,1,0:T(8,128)(2,1)S(1)} %get-tuple-element.46), channel_id=1, source_target_pairs={{16,0},{32,16},{48,32},{64,48},{80,64},{96,80},{112,96},{128,112},... | collective-permute-start | bytes 196616 | tf_op jit(solution)/shard_map/ppermute | solution.py:137
  9.8 17.9 %all-to-all-start = ((f32[64,2,128]{2,1,0:T(2,128)}), f32[64,2,128]{2,1,0:T(2,128)S(1)}, u32[]{:S(2)}, u32[]{:S(2)}) async-start(f32[64,2,128]{2,1,0:T(2,128)} %get-tuple-element.53), calls=%async_computation | async-start | bytes 131072 | tf_op jit(solution)/shard_map/all_to_all | solution.py:89
  20.7 7.0 %collective-permute-start.2 = (bf16[8,3,16,128]{3,2,1,0:T(8,128)(2,1)S(1)}, bf16[8,3,16,128]{3,2,1,0:T(8,128)(2,1)S(1)}, u32[]{:S(2)}, u32[]{:S(2)}) collective-permute-start(bf16[8,3,16,128]{3,2,1,0:T(8,128)(2,1)S(1)} %get-tuple-element.49), channel_id=1, source_target_pairs={{0,4},{4,8},{8,12},{1,5},{5,9},{9,13},{2,6},{6,10},{10,14},{3,7},{... | collective-permute-start | bytes 294920 | tf_op jit(solution)/shard_map/ppermute | solution.py:143
  23.8 5.4 %collective-permute-start.3 = (bf16[8,3,16,128]{3,2,1,0:T(8,128)(2,1)S(1)}, bf16[8,3,16,128]{3,2,1,0:T(8,128)(2,1)S(1)}, u32[]{:S(2)}, u32[]{:S(2)}) collective-permute-start(bf16[8,3,16,128]{3,2,1,0:T(8,128)(2,1)S(1)} %get-tuple-element.50), channel_id=1, source_target_pairs={{4,0},{8,4},{12,8},{5,1},{9,5},{13,9},{6,2},{10,6},{14,10},{7,3},{... | collective-permute-start | bytes 294920 | tf_op jit(solution)/shard_map/ppermute | solution.py:144
  33.7 8.0 %collective-permute-start.4 = (bf16[1152,128]{1,0:T(8,128)(2,1)S(1)}, bf16[1152,128]{1,0:T(8,128)(2,1)S(1)}, u32[]{:S(2)}, u32[]{:S(2)}) collective-permute-start(bf16[1152,128]{1,0:T(8,128)(2,1)S(1)} %get-tuple-element.58), channel_id=1, source_target_pairs={{0,1},{1,2},{2,3},{3,0},{4,5},{5,6},{6,7},{7,4},{8,9},{9,10},{10,1... | collective-permute-start | bytes 884744 | tf_op jit(solution)/shard_map/ppermute | solution.py:359
  34.9 14.0 %collective-permute-start.5 = (bf16[1152,128]{1,0:T(8,128)(2,1)S(1)}, bf16[1152,128]{1,0:T(8,128)(2,1)S(1)}, u32[]{:S(2)}, u32[]{:S(2)}) collective-permute-start(bf16[1152,128]{1,0:T(8,128)(2,1)S(1)} %get-tuple-element.59), channel_id=1, source_target_pairs={{0,2},{1,3},{2,0},{3,1},{4,6},{5,7},{6,4},{7,5},{8,10},{9,11},{10,... | collective-permute-start | bytes 884744 | tf_op jit(solution)/shard_map/ppermute | solution.py:359
  39.9 10.9 %collective-permute-start.6 = (bf16[1152,128]{1,0:T(8,128)(2,1)S(1)}, bf16[1152,128]{1,0:T(8,128)(2,1)S(1)}, u32[]{:S(2)}, u32[]{:S(2)}) collective-permute-start(bf16[1152,128]{1,0:T(8,128)(2,1)S(1)} %get-tuple-element.61), channel_id=1, source_target_pairs={{0,3},{1,0},{2,1},{3,2},{4,7},{5,4},{6,5},{7,6},{8,11},{9,8},{10,9... | collective-permute-start | bytes 884744 | tf_op jit(solution)/shard_map/ppermute | solution.py:359
  52.5 27.3 %all-to-all-start.1 = ((f32[64,2,128]{2,1,0:T(2,128)}), f32[64,2,128]{2,1,0:T(2,128)S(1)}, u32[]{:S(2)}, u32[]{:S(2)}) async-start(f32[64,2,128]{2,1,0:T(2,128)} %get-tuple-element.64.refs_3_), calls=%async_computation.1 | async-start | bytes 131072 | tf_op jit(solution)/shard_map/all_to_all | solution.py:89
  64.8 21.8 %collective-permute-start.9 = (bf16[9,128,128]{2,1,0:T(8,128)(2,1)S(1)}, bf16[9,128,128]{2,1,0:T(8,128)(2,1)S(1)}, u32[]{:S(2)}, u32[]{:S(2)}) collective-permute-start(bf16[9,128,128]{2,1,0:T(8,128)(2,1)S(1)} %get-tuple-element.74), channel_id=1, source_target_pairs={{0,1},{1,2},{2,3},{3,0},{4,5},{5,6},{6,7},{7,4},{8,9},{9,10},{10,1... | collective-permute-start | bytes 884744 | tf_op jit(solution)/shard_map/ppermute | solution.py:359
  64.9 21.7 %collective-permute-start.10 = (bf16[9,128,128]{2,1,0:T(8,128)(2,1)S(1)}, bf16[9,128,128]{2,1,0:T(8,128)(2,1)S(1)}, u32[]{:S(2)}, u32[]{:S(2)}) collective-permute-start(bf16[9,128,128]{2,1,0:T(8,128)(2,1)S(1)} %get-tuple-element.75), channel_id=1, source_target_pairs={{0,2},{1,3},{2,0},{3,1},{4,6},{5,7},{6,4},{7,5},{8,10},{9,11},{10,... | collective-permute-start | bytes 884744 | tf_op jit(solution)/shard_map/ppermute | solution.py:359
  66.2 20.4 %collective-permute-start.11 = (bf16[9,128,128]{2,1,0:T(8,128)(2,1)S(1)}, bf16[9,128,128]{2,1,0:T(8,128)(2,1)S(1)}, u32[]{:S(2)}, u32[]{:S(2)}) collective-permute-start(bf16[9,128,128]{2,1,0:T(8,128)(2,1)S(1)} %get-tuple-element.76), channel_id=1, source_target_pairs={{0,3},{1,0},{2,1},{3,2},{4,7},{5,4},{6,5},{7,6},{8,11},{9,8},{10,9... | collective-permute-start | bytes 884744 | tf_op jit(solution)/shard_map/ppermute | solution.py:359
  67.6 7.3 %collective-permute-start.7 = (bf16[144,128]{1,0:T(8,128)(2,1)S(1)}, bf16[144,128]{1,0:T(8,128)(2,1)S(1)}, u32[]{:S(2)}, u32[]{:S(2)}) collective-permute-start(bf16[144,128]{1,0:T(8,128)(2,1)S(1)} %get-tuple-element.66), channel_id=1, source_target_pairs={{0,16},{16,32},{32,48},{48,64},{64,80},{80,96},{96,112},{112,128},... | collective-permute-start | bytes 110600 | tf_op jit(solution)/shard_map/ppermute | solution.py:136
  73.0 6.8 %collective-permute-start.8 = (bf16[144,128]{1,0:T(8,128)(2,1)S(1)}, bf16[144,128]{1,0:T(8,128)(2,1)S(1)}, u32[]{:S(2)}, u32[]{:S(2)}) collective-permute-start(bf16[144,128]{1,0:T(8,128)(2,1)S(1)} %get-tuple-element.67), channel_id=1, source_target_pairs={{16,0},{32,16},{48,32},{64,48},{80,64},{96,80},{112,96},{128,112},... | collective-permute-start | bytes 110600 | tf_op jit(solution)/shard_map/ppermute | solution.py:137
  84.3 12.4 %collective-permute-start.12 = (bf16[1088,128]{1,0:T(8,128)(2,1)S(1)}, bf16[1088,128]{1,0:T(8,128)(2,1)S(1)}, u32[]{:S(2)}, u32[]{:S(2)}) collective-permute-start(bf16[1088,128]{1,0:T(8,128)(2,1)S(1)} %get-tuple-element.78), channel_id=1, source_target_pairs={{0,1},{1,2},{2,3},{3,0},{4,5},{5,6},{6,7},{7,4},{8,9},{9,10},{10,1... | collective-permute-start | bytes 835592 | tf_op jit(solution)/shard_map/ppermute | solution.py:359
  84.4 12.3 %collective-permute-start.13 = (bf16[1088,128]{1,0:T(8,128)(2,1)S(1)}, bf16[1088,128]{1,0:T(8,128)(2,1)S(1)}, u32[]{:S(2)}, u32[]{:S(2)}) collective-permute-start(bf16[1088,128]{1,0:T(8,128)(2,1)S(1)} %get-tuple-element.79), channel_id=1, source_target_pairs={{0,2},{1,3},{2,0},{3,1},{4,6},{5,7},{6,4},{7,5},{8,10},{9,11},{10,... | collective-permute-start | bytes 835592 | tf_op jit(solution)/shard_map/ppermute | solution.py:359
  89.1 8.5 %collective-permute-start.14 = (bf16[1088,128]{1,0:T(8,128)(2,1)S(1)}, bf16[1088,128]{1,0:T(8,128)(2,1)S(1)}, u32[]{:S(2)}, u32[]{:S(2)}) collective-permute-start(bf16[1088,128]{1,0:T(8,128)(2,1)S(1)} %get-tuple-element.80), channel_id=1, source_target_pairs={{0,3},{1,0},{2,1},{3,2},{4,7},{5,4},{6,5},{7,6},{8,11},{9,8},{10,9... | collective-permute-start | bytes 835592 | tf_op jit(solution)/shard_map/ppermute | solution.py:359
  98.4 16.2 %collective-permute-start.17 = (bf16[4,272,128]{2,1,0:T(8,128)(2,1)S(1)}, bf16[4,272,128]{2,1,0:T(8,128)(2,1)S(1)}, u32[]{:S(2)}, u32[]{:S(2)}) collective-permute-start(bf16[4,272,128]{2,1,0:T(8,128)(2,1)S(1)} %get-tuple-element.81.refs_0_), channel_id=1, source_target_pairs={{0,1},{1,2},{2,3},{3,0},{4,5},{5,6},{6,7},{7,4},{8,9},{9,10},{10,1... | collective-permute-start | bytes 835592 | tf_op jit(solution)/shard_map/ppermute | solution.py:359
  100.3 16.8 %collective-permute-start.21 = (bf16[4,272,128]{2,1,0:T(8,128)(2,1)S(1)}, bf16[4,272,128]{2,1,0:T(8,128)(2,1)S(1)}, u32[]{:S(2)}, u32[]{:S(2)}) collective-permute-start(bf16[4,272,128]{2,1,0:T(8,128)(2,1)S(1)} %get-tuple-element.81.refs_0_), channel_id=1, source_target_pairs={{0,3},{1,0},{2,1},{3,2},{4,7},{5,4},{6,5},{7,6},{8,11},{9,8},{10,9... | collective-permute-start | bytes 835592 | tf_op jit(solution)/shard_map/ppermute | solution.py:359
  101.5 15.6 %collective-permute-start.19 = (bf16[4,272,128]{2,1,0:T(8,128)(2,1)S(1)}, bf16[4,272,128]{2,1,0:T(8,128)(2,1)S(1)}, u32[]{:S(2)}, u32[]{:S(2)}) collective-permute-start(bf16[4,272,128]{2,1,0:T(8,128)(2,1)S(1)} %get-tuple-element.81.refs_0_), channel_id=1, source_target_pairs={{0,2},{1,3},{2,0},{3,1},{4,6},{5,7},{6,4},{7,5},{8,10},{9,11},{10,... | collective-permute-start | bytes 835592 | tf_op jit(solution)/shard_map/ppermute | solution.py:359
  102.6 7.1 %collective-permute-start.15 = (bf16[4,40,128]{2,1,0:T(8,128)(2,1)S(1)}, bf16[4,40,128]{2,1,0:T(8,128)(2,1)S(1)}, u32[]{:S(2)}, u32[]{:S(2)}) collective-permute-start(bf16[4,40,128]{2,1,0:T(8,128)(2,1)S(1)} %get-tuple-element.82), channel_id=1, source_target_pairs={{0,16},{16,32},{32,48},{48,64},{64,80},{80,96},{96,112},{112,128},... | collective-permute-start | bytes 122888 | tf_op jit(solution)/shard_map/ppermute | solution.py:136
  107.8 6.8 %collective-permute-start.16 = (bf16[4,40,128]{2,1,0:T(8,128)(2,1)S(1)}, bf16[4,40,128]{2,1,0:T(8,128)(2,1)S(1)}, u32[]{:S(2)}, u32[]{:S(2)}) collective-permute-start(bf16[4,40,128]{2,1,0:T(8,128)(2,1)S(1)} %get-tuple-element.83), channel_id=1, source_target_pairs={{16,0},{32,16},{48,32},{64,48},{80,64},{96,80},{112,96},{128,112},... | collective-permute-start | bytes 122888 | tf_op jit(solution)/shard_map/ppermute | solution.py:137
  116.4 4.9 %collective-permute-start.20 = (bf16[4,80,128]{2,1,0:T(8,128)(2,1)S(1)}, bf16[4,80,128]{2,1,0:T(8,128)(2,1)S(1)}, u32[]{:S(2)}, u32[]{:S(2)}) collective-permute-start(bf16[4,80,128]{2,1,0:T(8,128)(2,1)S(1)} %pack.1.refs_1_), channel_id=1, source_target_pairs={{0,2},{1,3},{2,0},{3,1},{4,6},{5,7},{6,4},{7,5},{8,10},{9,11},{10,... | collective-permute-start | bytes 245768 | tf_op jit(solution)/shard_map/ppermute | solution.py:359
  116.8 5.3 %collective-permute-start.18 = (bf16[4,80,128]{2,1,0:T(8,128)(2,1)S(1)}, bf16[4,80,128]{2,1,0:T(8,128)(2,1)S(1)}, u32[]{:S(2)}, u32[]{:S(2)}) collective-permute-start(bf16[4,80,128]{2,1,0:T(8,128)(2,1)S(1)} %pack.1.refs_1_), channel_id=1, source_target_pairs={{0,1},{1,2},{2,3},{3,0},{4,5},{5,6},{6,7},{7,4},{8,9},{9,10},{10,1... | collective-permute-start | bytes 245768 | tf_op jit(solution)/shard_map/ppermute | solution.py:359
  (2 other events, 15.1 us)

commit v7 on v6

--- a/solution.py
+++ b/solution.py
@@ -280,6 +280,18 @@
     multiply(patch_ref, side_ref, w_ref, rest[-2:])
 
 
+def near_cut_body(flag_ref, patch_ref, side_ref, w_ref, cut_hbm, out3, out0, *rest):
+    pieces, sem = rest[:4], rest[4]
+    copies = []
+    for k, piece in enumerate(pieces):
+        block = pl.multiple_of(lax.rem(flag_ref[4] + k, 4) * CH, CH)
+        copies.append(pltpu.make_async_copy(cut_hbm.at[:, :, pl.ds(block, CH)], piece, sem.at[k]))
+        copies[-1].start()
+    multiply(patch_ref, side_ref, w_ref, (out3, out0))
+    for c in copies:
+        c.wait()
+
+
 def conv(flags, x, cache, stats, halo, cache_at, act_at, around, weight, ext, name, after=(), cut=None):
     n = x.shape[0] * ROWS * COLS + ROWS * 8 * ext
     depth, width = weight.shape
@@ -306,42 +318,33 @@
     )(flags, x, cache, stats, *halo, *around, Left(weight, HBM))
     got2 = to_peer(out2, 2)
     got1 = to_peer(out1, 1)
-    out3, own = call(near_body, [piece] * 2, flops=flops, limit=16, name=name + "_near")(
-        patch, side, near, *[Left(a) for a in after]
-    )
-    total = sds((n, CH), F32)
+    pieces = []
     if cut is None:
-        return [own, *call(add_body, [total], name=name + "_add")(got1, got2), to_peer(out3, 3)]
-    far, *cut = call(
-        add_cut_body,
-        [total] + [sds(cut.shape[:2] + (CH,))] * 4,
-        scratch=[pltpu.SemaphoreType.DMA((4,))],
-        name=name + "_add",
-    )(flags, got1, got2, Left(cut, HBM))
-    return [own, far, to_peer(out3, 3)], cut
+        out3, own = call(near_body, [piece] * 2, flops=flops, limit=16, name=name + "_near")(
+            patch, side, near, *[Left(a) for a in after]
+        )
+    else:
+        out3, own, *pieces = call(
+            near_cut_body,
+            [piece] * 2 + [sds(cut.shape[:2] + (CH,))] * 4,
+            scratch=[pltpu.SemaphoreType.DMA((4,))],
+            flops=flops,
+            limit=20,
+            name=name + "_near",
+        )(flags, patch, side, near, Left(cut, HBM))
+    (far,) = call(add_body, [sds((n, CH), F32)], name=name + "_add")(got1, got2)
+    return (own, far, to_peer(out3, 3)), pieces
 
 
 def add_body(a_ref, b_ref, o_ref):
     o_ref[...] = a_ref[...].astype(F32) + b_ref[...].astype(F32)
 
 
-def add_cut_body(flag_ref, a_ref, b_ref, w_hbm, o_ref, *rest):
-    pieces, sem = rest[:4], rest[4]
-    copies = []
-    for k, piece in enumerate(pieces):
-        block = pl.multiple_of(lax.rem(flag_ref[4] + k, 4) * CH, CH)
-        copies.append(pltpu.make_async_copy(w_hbm.at[:, :, pl.ds(block, CH)], piece, sem.at[k]))
-        copies[-1].start()
-    add_body(a_ref, b_ref, o_ref)
-    for c in copies:
-        c.wait()
-
-
 def gate_body(*refs):
     del refs
 
 
-def gate(arrays, after):
+def gate(arrays, after, flops=0):
     n = len(arrays)
     return pl.pallas_call(
         gate_body,
@@ -350,6 +353,7 @@
         out_specs=[ANY] * n,
         input_output_aliases={i: i for i in range(n)},
         compiler_params=pltpu.CompilerParams(vmem_limit_bytes=8 * MIB),
+        cost_estimate=pl.CostEstimate(flops=flops, bytes_accessed=0, transcendentals=0),
         name="gate",
     )(*arrays, after)
 
@@ -508,8 +512,9 @@
     )(*pieces)
     w_got = to_peers(gate(w_pieces[1:], stats))
     stats = spread(stats)
-    around = (side,) + swap_rows(top, bot)
-    pieces = conv(
+    top, bot = swap_rows(top, bot)
+    around = (side, *gate([top, bot], side, 5000000000))
+    pieces, _ = conv(
         flags, hidden, c2, stats, halo, 6, None, around, weight_second.reshape(-1, 4 * CH), 1, "conv_second", w_got
     )
     resid, top, bot = call(
@@ -520,7 +525,7 @@
     )(flags, features, *halo[2:], *pieces)
     others = to_peers([resid] * 3)
     (border,) = call(pack_body, [sds((frames, 2 * COLS + 16, CH))], name="pack")(
-        *swap_rows(top, bot), Left(others[0])
+        *gate(swap_rows(top, bot), resid, 2000000000), Left(others[0])
     )
     borders = [border] + to_peers([border] * 3)
     (folded,) = call(fold_body, [sds((2, 2, 8 * CH, 2 * CH))], limit=12, name="fold")(

time: 127 us -> 132 us (1.039)
  starting transfers between devices: 67.9 us -> 75.3 us
  waiting for transfers between devices: 32.4 us -> 29 us
    ppermute x3, waiting for transfers between devices: 9.73 us -> 1.15 us  [swap_rows(): below = lax.ppermute(top, HA, [(i + 1, i) for i in range(n - 1)])]
    ppermute x15, starting transfers between devices: 18.8 us -> 26.2 us  [to_peer(): return lax.ppermute(piece, 'col', [(i, (i + k) % n) for i in range(n)])]
    all_to_all x2, waiting for transfers between devices: 2.54 us -> 5.23 us  [spread(): return lax.all_to_all(slots, HA + ('wa',), 0, 0, tiled=True)]
    ppermute x15, waiting for transfers between devices: 18.7 us -> 21.2 us  [to_peer(): return lax.ppermute(piece, 'col', [(i, (i + k) % n) for i in range(n)])]
    all_to_all x2, starting transfers between devices: 23.1 us -> 21 us  [spread(): return lax.all_to_all(slots, HA + ('wa',), 0, 0, tiled=True)]
    ppermute x3, starting transfers between devices: 15.8 us -> 17.9 us  [swap_rows(): above = lax.ppermute(bot, HA, [(i, i + 1) for i in range(n - 1)])]
  transfers between devices with their start and end apart: 25 -> 25, of which waited for: 11 -> 12; matrix products, arithmetic and copies ran while one was open for 0% -> 0% of each run, Pallas kernels for 10% -> 9%
where the time goes in v7:
time: 132 us; the launch traced here: 130 us
  starting transfers between devices  75.3 us (57%)
  waiting for transfers between devices  29 us (22%)
  Pallas kernels  25.5 us (19%)
    ppermute x15, starting transfers between devices, to_peer(): return lax.ppermute(piece, 'col', [(i, (i + k) % n) for i in range(n)])  26.2 us
    pallas_call x12, Pallas kernels, run(): pl.pallas_call(body, out_shape=list(outs), in_specs=specs, out_specs=[VME...  21.3 us
    ppermute x15, waiting for transfers between devices, to_peer(): return lax.ppermute(piece, 'col', [(i, (i + k) % n) for i in range(n)])  21.2 us
    all_to_all x2, starting transfers between devices, spread(): return lax.all_to_all(slots, HA + ('wa',), 0, 0, tiled=True)  21 us
    ppermute x3, starting transfers between devices, swap_rows(): above = lax.ppermute(bot, HA, [(i, i + 1) for i in range(n - 1)])  17.9 us
    ppermute x3, starting transfers between devices, swap_rows(): below = lax.ppermute(top, HA, [(i + 1, i) for i in range(n - 1)])  5.76 us
    all_to_all x2, waiting for transfers between devices, spread(): return lax.all_to_all(slots, HA + ('wa',), 0, 0, tiled=True)  5.23 us
    pallas_call x1, Pallas kernels, up_conv(): pl.pallas_call(up_body, out_shape=sds(out), grid=(frames,), in_specs=spec...  4.15 us
  transfers between devices with their start and end apart: 25, of which 12 were waited for; matrix products, arithmetic and copies ran while one was open for 0% of the time, Pallas kernels for 9%

profile of v7, /device:TPU:97, one launch (start us, length us, event | category | flops | bytes accessed | tf_op | source)
XLA Modules:
  0.0 130.1 jit_solution(17159340642703494199)
XLA Ops:
  0.0 2.6 %first.1 = (bf16[4,8,32,128]{3,2,1,0:T(8,128)(2,1)S(1)}, bf16[2,8,32,128]{3,2,1,0:T(8,128)(2,1)S(1)}, bf16[2,8,32,128]{3,2,1,0:T(8,128)(2,1)S(1)}, f32[64,2,128]...) custom-call(bf16[4,8,32,128]{3,2,1,0:T(8,128)(2,1)} %x_ref.1, ...), custom_call_target="tpu_custom_call" | custom-call | bytes 1441792 | tf_op jit(solution)/shard_map/first/pallas_call | solution.py:39
  2.6 5.3 %collective-permute-start = (bf16[8,32,128]{2,1,0:T(8,128)(2,1)S(1)}, bf16[8,32,128]{2,1,0:T(8,128)(2,1)S(1)}, u32[]{:S(2)}, u32[]{:S(2)}) collective-permute-start(bf16[8,32,128]{2,1,0:T(8,128)(2,1)S(1)} %get-tuple-element.48), channel_id=1, source_target_pairs={{0,16},{16,32},{32,48},{48,64},{64,80},{80,96},{96,112},{112,128},... | collective-permute-start | bytes 196616 | tf_op jit(solution)/shard_map/ppermute | solution.py:136
  7.9 1.9 %collective-permute-start.1 = (bf16[8,32,128]{2,1,0:T(8,128)(2,1)S(1)}, bf16[8,32,128]{2,1,0:T(8,128)(2,1)S(1)}, u32[]{:S(2)}, u32[]{:S(2)}) collective-permute-start(bf16[8,32,128]{2,1,0:T(8,128)(2,1)S(1)} %get-tuple-element.49), channel_id=1, source_target_pairs={{16,0},{32,16},{48,32},{64,48},{80,64},{96,80},{112,96},{128,112},... | collective-permute-start | bytes 196616 | tf_op jit(solution)/shard_map/ppermute | solution.py:137
  9.8 10.8 %all-to-all-start = ((f32[64,2,128]{2,1,0:T(2,128)}), f32[64,2,128]{2,1,0:T(2,128)S(1)}, u32[]{:S(2)}, u32[]{:S(2)}) async-start(f32[64,2,128]{2,1,0:T(2,128)} %get-tuple-element.56), calls=%async_computation | async-start | bytes 131072 | tf_op jit(solution)/shard_map/all_to_all | solution.py:89
  20.7 3.1 %collective-permute-start.2 = (bf16[8,3,16,128]{3,2,1,0:T(8,128)(2,1)S(1)}, bf16[8,3,16,128]{3,2,1,0:T(8,128)(2,1)S(1)}, u32[]{:S(2)}, u32[]{:S(2)}) collective-permute-start(bf16[8,3,16,128]{3,2,1,0:T(8,128)(2,1)S(1)} %get-tuple-element.52), channel_id=1, source_target_pairs={{0,4},{4,8},{8,12},{1,5},{5,9},{9,13},{2,6},{6,10},{10,14},{3,7},{... | collective-permute-start | bytes 294920 | tf_op jit(solution)/shard_map/ppermute | solution.py:143
  25.2 2.5 %all-to-all-done.st_ref = f32[64,2,128]{2,1,0:T(2,128)S(1)} async-done(((f32[64,2,128]{2,1,0:T(2,128)}), f32[64,2,128]{2,1,0:T(2,128)S(1)}, u32[]{:S(2)}, u32[]{:S(2)}) %all-to-all-start) | async-done | bytes 65568 | tf_op jit(solution)/shard_map/all_to_all | solution.py:89
  29.2 4.5 %conv_first_far.1 = (bf16[1152,128]{1,0:T(8,128)(2,1)S(1)}, bf16[1152,128]{1,0:T(8,128)(2,1)S(1)}, bf16[6,320,384]{2,1,0:T(8,128)(2,1)S(1)}, bf16[3,160,384]{2,1,0:T(8,128)(2,1)S(1)}, bf16[3456,256]{1,0:T(8,128)(2,1)S(1)}) custom-call(s32[5]{0:T(128)S(1)} %stack.39.flag_ref, bf16[4,8,32,128]{3,2,1,0:T(8,128)(2,1)S(1)} %get-tuple-element.54.x_ref, ...), custom_call_target="tpu_custom_call" | custom-call | flops 2038431744 | bytes 8527892 | tf_op jit(solution)/shard_map/conv_first_far/pallas_call | solution.py:39
  34.9 2.4 %collective-permute-start.5 = (bf16[1152,128]{1,0:T(8,128)(2,1)S(1)}, bf16[1152,128]{1,0:T(8,128)(2,1)S(1)}, u32[]{:S(2)}, u32[]{:S(2)}) collective-permute-start(bf16[1152,128]{1,0:T(8,128)(2,1)S(1)} %get-tuple-element.62), channel_id=1, source_target_pairs={{0,2},{1,3},{2,0},{3,1},{4,6},{5,7},{6,4},{7,5},{8,10},{9,11},{10,... | collective-permute-start | bytes 884744 | tf_op jit(solution)/shard_map/ppermute | solution.py:363
  37.4 4.1 %conv_first_near.1 = (bf16[1152,128]{1,0:T(8,128)(2,1)S(1)}, bf16[1152,128]{1,0:T(8,128)(2,1)S(1)}, bf16[9,128,128]{2,1,0:T(8,128)(2,1)S(1)}, bf16[9,128,128]{2,...) custom-call(s32[5]{0:T(128)S(1)} %stack.39.flag_ref, ...), custom_call_target="tpu_custom_call" | custom-call | flops 2038431744 | bytes 6561812 | tf_op jit(solution)/shard_map/conv_first_near/pallas_call | solution.py:39
  42.8 6.2 %collective-permute-done.5.b_ref = bf16[1152,128]{1,0:T(8,128)(2,1)S(1)} collective-permute-done((bf16[1152,128]{1,0:T(8,128)(2,1)S(1)}, bf16[1152,128]{1,0:T(8,128)(2,1)S(1)}, u32[]{:S(2)}, u32[]{:S(2)}) %collective-permute-start.5) | collective-permute-done | bytes 294944 | tf_op jit(solution)/shard_map/ppermute | solution.py:363
  50.7 6.9 %collective-permute-start.7 = (bf16[144,128]{1,0:T(8,128)(2,1)S(1)}, bf16[144,128]{1,0:T(8,128)(2,1)S(1)}, u32[]{:S(2)}, u32[]{:S(2)}) collective-permute-start(bf16[144,128]{1,0:T(8,128)(2,1)S(1)} %get-tuple-element.68), channel_id=1, source_target_pairs={{0,16},{16,32},{32,48},{48,64},{64,80},{80,96},{96,112},{112,128},... | collective-permute-start | bytes 110600 | tf_op jit(solution)/shard_map/ppermute | solution.py:136
  57.6 1.9 %collective-permute-start.8 = (bf16[144,128]{1,0:T(8,128)(2,1)S(1)}, bf16[144,128]{1,0:T(8,128)(2,1)S(1)}, u32[]{:S(2)}, u32[]{:S(2)}) collective-permute-start(bf16[144,128]{1,0:T(8,128)(2,1)S(1)} %get-tuple-element.69), channel_id=1, source_target_pairs={{16,0},{32,16},{48,32},{64,48},{80,64},{96,80},{112,96},{128,112},... | collective-permute-start | bytes 110600 | tf_op jit(solution)/shard_map/ppermute | solution.py:137
  59.6 10.3 %all-to-all-start.1 = ((f32[64,2,128]{2,1,0:T(2,128)}), f32[64,2,128]{2,1,0:T(2,128)S(1)}, u32[]{:S(2)}, u32[]{:S(2)}) async-start(f32[64,2,128]{2,1,0:T(2,128)} %get-tuple-element.66.refs_3_), calls=%async_computation.1 | async-start | bytes 131072 | tf_op jit(solution)/shard_map/all_to_all | solution.py:89
  74.3 2.7 %all-to-all-done.1.st_ref = f32[64,2,128]{2,1,0:T(2,128)S(1)} async-done(((f32[64,2,128]{2,1,0:T(2,128)}), f32[64,2,128]{2,1,0:T(2,128)S(1)}, u32[]{:S(2)}, u32[]{:S(2)}) %all-to-all-start.1) | async-done | bytes 65568 | tf_op jit(solution)/shard_map/all_to_all | solution.py:89
  76.9 4.5 %conv_second_far.1 = (bf16[1088,128]{1,0:T(8,128)(2,1)S(1)}, bf16[1088,128]{1,0:T(8,128)(2,1)S(1)}, bf16[6,320,384]{2,1,0:T(8,128)(2,1)S(1)}, bf16[3,80,384]{2,1,0:T(8,128)(2,1)S(1)}, bf16[3456,256]{1,0:T(8,128)(2,1)S(1)}) custom-call(s32[5]{0:T(128)S(1)} %stack.39.flag_ref, bf16[4,8,32,128]{3,2,1,0:T(8,128)(2,1)S(1)} %get-tuple-element.64.x_ref, ...), custom_call_target="tpu_custom_call" | custom-call | flops 1925185536 | bytes 8450068 | tf_op jit(solution)/shard_map/conv_second_far/pallas_call | solution.py:39
  86.2 2.5 %conv_second_near.1 = (bf16[1088,128]{1,0:T(8,128)(2,1)S(1)}, bf16[1088,128]{1,0:T(8,128)(2,1)S(1)}) custom-call(bf16[6,320,384]{2,1,0:T(8,128)(2,1)S(1)} %get-tuple-element.72.patch_ref, bf16[3,80,384]{2,1,0:T(8,128)(2,1)S(1)} %get-tuple-element.73.side_ref, bf16[3456,256]{1,0:T(8,128)(2,1)S(1)} %get-tuple-element.74.w_ref, ...), custom_call_target="tpu_custom_call" | custom-call | flops 1925185536 | bytes 4870144 | tf_op jit(solution)/shard_map/conv_second_near/pallas_call | solution.py:39
  88.8 4.0 %collective-permute-start.14 = (bf16[1088,128]{1,0:T(8,128)(2,1)S(1)}, bf16[1088,128]{1,0:T(8,128)(2,1)S(1)}, u32[]{:S(2)}, u32[]{:S(2)}) collective-permute-start(bf16[1088,128]{1,0:T(8,128)(2,1)S(1)} %get-tuple-element.84), channel_id=1, source_target_pairs={{0,3},{1,0},{2,1},{3,2},{4,7},{5,4},{6,5},{7,6},{8,11},{9,8},{10,9... | collective-permute-start | bytes 835592 | tf_op jit(solution)/shard_map/ppermute | solution.py:363
  93.4 4.7 %collective-permute-done.13.b_ref = bf16[1088,128]{1,0:T(8,128)(2,1)S(1)} collective-permute-done((bf16[1088,128]{1,0:T(8,128)(2,1)S(1)}, bf16[1088,128]{1,0:T(8,128)(2,1)S(1)}, u32[]{:S(2)}, u32[]{:S(2)}) %collective-permute-start.13) | collective-permute-done | bytes 278560 | tf_op jit(solution)/shard_map/ppermute | solution.py:363
  100.8 5.6 %collective-permute-start.15 = (bf16[4,40,128]{2,1,0:T(8,128)(2,1)S(1)}, bf16[4,40,128]{2,1,0:T(8,128)(2,1)S(1)}, u32[]{:S(2)}, u32[]{:S(2)}) collective-permute-start(bf16[4,40,128]{2,1,0:T(8,128)(2,1)S(1)} %get-tuple-element.86), channel_id=1, source_target_pairs={{0,16},{16,32},{32,48},{48,64},{64,80},{80,96},{96,112},{112,128},... | collective-permute-start | bytes 122888 | tf_op jit(solution)/shard_map/ppermute | solution.py:136
  108.4 1.9 %collective-permute-start.21 = (bf16[4,272,128]{2,1,0:T(8,128)(2,1)S(1)}, bf16[4,272,128]{2,1,0:T(8,128)(2,1)S(1)}, u32[]{:S(2)}, u32[]{:S(2)}) collective-permute-start(bf16[4,272,128]{2,1,0:T(8,128)(2,1)S(1)} %get-tuple-element.85.refs_2_.refs_0_), channel_id=1, source_target_pairs={{0,3},{1,0},{2,1},{3,2},{4,7},{5,4},{6,5},{7,6},{8,11},{9,8},{10,9... | collective-permute-start | bytes 835592 | tf_op jit(solution)/shard_map/ppermute | solution.py:363
  113.0 2.2 %collective-permute-start.22 = (bf16[4,80,128]{2,1,0:T(8,128)(2,1)S(1)}, bf16[4,80,128]{2,1,0:T(8,128)(2,1)S(1)}, u32[]{:S(2)}, u32[]{:S(2)}) collective-permute-start(bf16[4,80,128]{2,1,0:T(8,128)(2,1)S(1)} %pack.1.refs_1_), channel_id=1, source_target_pairs={{0,3},{1,0},{2,1},{3,2},{4,7},{5,4},{6,5},{7,6},{8,11},{9,8},{10,9... | collective-permute-start | bytes 245768 | tf_op jit(solution)/shard_map/ppermute | solution.py:363
  117.4 5.2 %collective-permute-done.21.rest_1_.refs_6_ = bf16[4,272,128]{2,1,0:T(8,128)(2,1)S(1)} collective-permute-done((bf16[4,272,128]{2,1,0:T(8,128)(2,1)S(1)}, bf16[4,272,128]{2,1,0:T(8,128)(2,1)S(1)}, u32[]{:S(2)}, u32[]{:S(2)}) %collective-permute-start.21) | collective-permute-done | bytes 278560 | tf_op jit(solution)/shard_map/ppermute | solution.py:363
  123.1 2.8 %collective-permute-done.22.refs_7_ = bf16[4,80,128]{2,1,0:T(8,128)(2,1)S(1)} collective-permute-done((bf16[4,80,128]{2,1,0:T(8,128)(2,1)S(1)}, bf16[4,80,128]{2,1,0:T(8,128)(2,1)S(1)}, u32[]{:S(2)}, u32[]{:S(2)}) %collective-permute-start.22) | collective-permute-done | bytes 81952 | tf_op jit(solution)/shard_map/ppermute | solution.py:363
  126.0 4.2 %up_conv.1 = bf16[4,16,64,128]{3,2,1,0:T(8,128)(2,1)} custom-call(bf16[4,272,128]{2,1,0:T(8,128)(2,1)S(1)} %get-tuple-element.85.refs_2_.refs_0_, bf16[4,80,128]{2,1,0:T(8,128)(2,1)S(1)} %pack.1.refs_1_, bf16[4,272,128]{2,1,0:T(8,128)(2,1)S(1)} %collective-permute-done.17.after_ref.refs_2_, bf16[4,80,128]{2,1,0:T(8,128)(2,1)S(1)} %collective-permute-done.18.refs_3_, ...), custom_call_target="tpu_custom_call" | custom-call | tf_op jit(solution)/shard_map/up_conv/pallas_call | solution.py:469
  (45 shorter events, 26.9 us)
Async XLA Ops:
  2.6 18.0 %collective-permute-start = (bf16[8,32,128]{2,1,0:T(8,128)(2,1)S(1)}, bf16[8,32,128]{2,1,0:T(8,128)(2,1)S(1)}, u32[]{:S(2)}, u32[]{:S(2)}) collective-permute-start(bf16[8,32,128]{2,1,0:T(8,128)(2,1)S(1)} %get-tuple-element.48), channel_id=1, source_target_pairs={{0,16},{16,32},{32,48},{48,64},{64,80},{80,96},{96,112},{112,128},... | collective-permute-start | bytes 196616 | tf_op jit(solution)/shard_map/ppermute | solution.py:136
  7.9 12.7 %collective-permute-start.1 = (bf16[8,32,128]{2,1,0:T(8,128)(2,1)S(1)}, bf16[8,32,128]{2,1,0:T(8,128)(2,1)S(1)}, u32[]{:S(2)}, u32[]{:S(2)}) collective-permute-start(bf16[8,32,128]{2,1,0:T(8,128)(2,1)S(1)} %get-tuple-element.49), channel_id=1, source_target_pairs={{16,0},{32,16},{48,32},{64,48},{80,64},{96,80},{112,96},{128,112},... | collective-permute-start | bytes 196616 | tf_op jit(solution)/shard_map/ppermute | solution.py:137
  9.8 17.9 %all-to-all-start = ((f32[64,2,128]{2,1,0:T(2,128)}), f32[64,2,128]{2,1,0:T(2,128)S(1)}, u32[]{:S(2)}, u32[]{:S(2)}) async-start(f32[64,2,128]{2,1,0:T(2,128)} %get-tuple-element.56), calls=%async_computation | async-start | bytes 131072 | tf_op jit(solution)/shard_map/all_to_all | solution.py:89
  20.7 7.0 %collective-permute-start.2 = (bf16[8,3,16,128]{3,2,1,0:T(8,128)(2,1)S(1)}, bf16[8,3,16,128]{3,2,1,0:T(8,128)(2,1)S(1)}, u32[]{:S(2)}, u32[]{:S(2)}) collective-permute-start(bf16[8,3,16,128]{3,2,1,0:T(8,128)(2,1)S(1)} %get-tuple-element.52), channel_id=1, source_target_pairs={{0,4},{4,8},{8,12},{1,5},{5,9},{9,13},{2,6},{6,10},{10,14},{3,7},{... | collective-permute-start | bytes 294920 | tf_op jit(solution)/shard_map/ppermute | solution.py:143
  33.7 9.1 %collective-permute-start.4 = (bf16[1152,128]{1,0:T(8,128)(2,1)S(1)}, bf16[1152,128]{1,0:T(8,128)(2,1)S(1)}, u32[]{:S(2)}, u32[]{:S(2)}) collective-permute-start(bf16[1152,128]{1,0:T(8,128)(2,1)S(1)} %get-tuple-element.61), channel_id=1, source_target_pairs={{0,1},{1,2},{2,3},{3,0},{4,5},{5,6},{6,7},{7,4},{8,9},{9,10},{10,1... | collective-permute-start | bytes 884744 | tf_op jit(solution)/shard_map/ppermute | solution.py:363
  34.9 14.0 %collective-permute-start.5 = (bf16[1152,128]{1,0:T(8,128)(2,1)S(1)}, bf16[1152,128]{1,0:T(8,128)(2,1)S(1)}, u32[]{:S(2)}, u32[]{:S(2)}) collective-permute-start(bf16[1152,128]{1,0:T(8,128)(2,1)S(1)} %get-tuple-element.62), channel_id=1, source_target_pairs={{0,2},{1,3},{2,0},{3,1},{4,6},{5,7},{6,4},{7,5},{8,10},{9,11},{10,... | collective-permute-start | bytes 884744 | tf_op jit(solution)/shard_map/ppermute | solution.py:363
  41.5 7.5 %collective-permute-start.6 = (bf16[1152,128]{1,0:T(8,128)(2,1)S(1)}, bf16[1152,128]{1,0:T(8,128)(2,1)S(1)}, u32[]{:S(2)}, u32[]{:S(2)}) collective-permute-start(bf16[1152,128]{1,0:T(8,128)(2,1)S(1)} %get-tuple-element.63), channel_id=1, source_target_pairs={{0,3},{1,0},{2,1},{3,2},{4,7},{5,4},{6,5},{7,6},{8,11},{9,8},{10,9... | collective-permute-start | bytes 884744 | tf_op jit(solution)/shard_map/ppermute | solution.py:363
  50.7 23.6 %collective-permute-start.7 = (bf16[144,128]{1,0:T(8,128)(2,1)S(1)}, bf16[144,128]{1,0:T(8,128)(2,1)S(1)}, u32[]{:S(2)}, u32[]{:S(2)}) collective-permute-start(bf16[144,128]{1,0:T(8,128)(2,1)S(1)} %get-tuple-element.68), channel_id=1, source_target_pairs={{0,16},{16,32},{32,48},{48,64},{64,80},{80,96},{96,112},{112,128},... | collective-permute-start | bytes 110600 | tf_op jit(solution)/shard_map/ppermute | solution.py:136
  57.6 16.6 %collective-permute-start.8 = (bf16[144,128]{1,0:T(8,128)(2,1)S(1)}, bf16[144,128]{1,0:T(8,128)(2,1)S(1)}, u32[]{:S(2)}, u32[]{:S(2)}) collective-permute-start(bf16[144,128]{1,0:T(8,128)(2,1)S(1)} %get-tuple-element.69), channel_id=1, source_target_pairs={{16,0},{32,16},{48,32},{64,48},{80,64},{96,80},{112,96},{128,112},... | collective-permute-start | bytes 110600 | tf_op jit(solution)/shard_map/ppermute | solution.py:137
  59.6 17.4 %all-to-all-start.1 = ((f32[64,2,128]{2,1,0:T(2,128)}), f32[64,2,128]{2,1,0:T(2,128)S(1)}, u32[]{:S(2)}, u32[]{:S(2)}) async-start(f32[64,2,128]{2,1,0:T(2,128)} %get-tuple-element.66.refs_3_), calls=%async_computation.1 | async-start | bytes 131072 | tf_op jit(solution)/shard_map/all_to_all | solution.py:89
  69.8 14.8 %collective-permute-start.9 = (bf16[9,128,128]{2,1,0:T(8,128)(2,1)S(1)}, bf16[9,128,128]{2,1,0:T(8,128)(2,1)S(1)}, u32[]{:S(2)}, u32[]{:S(2)}) collective-permute-start(bf16[9,128,128]{2,1,0:T(8,128)(2,1)S(1)} %get-tuple-element.78), channel_id=1, source_target_pairs={{0,1},{1,2},{2,3},{3,0},{4,5},{5,6},{6,7},{7,4},{8,9},{9,10},{10,1... | collective-permute-start | bytes 884744 | tf_op jit(solution)/shard_map/ppermute | solution.py:363
  71.6 14.5 %collective-permute-start.10 = (bf16[9,128,128]{2,1,0:T(8,128)(2,1)S(1)}, bf16[9,128,128]{2,1,0:T(8,128)(2,1)S(1)}, u32[]{:S(2)}, u32[]{:S(2)}) collective-permute-start(bf16[9,128,128]{2,1,0:T(8,128)(2,1)S(1)} %get-tuple-element.79), channel_id=1, source_target_pairs={{0,2},{1,3},{2,0},{3,1},{4,6},{5,7},{6,4},{7,5},{8,10},{9,11},{10,... | collective-permute-start | bytes 884744 | tf_op jit(solution)/shard_map/ppermute | solution.py:363
  73.0 13.2 %collective-permute-start.11 = (bf16[9,128,128]{2,1,0:T(8,128)(2,1)S(1)}, bf16[9,128,128]{2,1,0:T(8,128)(2,1)S(1)}, u32[]{:S(2)}, u32[]{:S(2)}) collective-permute-start(bf16[9,128,128]{2,1,0:T(8,128)(2,1)S(1)} %get-tuple-element.80), channel_id=1, source_target_pairs={{0,3},{1,0},{2,1},{3,2},{4,7},{5,4},{6,5},{7,6},{8,11},{9,8},{10,9... | collective-permute-start | bytes 884744 | tf_op jit(solution)/shard_map/ppermute | solution.py:363
  81.5 11.9 %collective-permute-start.12 = (bf16[1088,128]{1,0:T(8,128)(2,1)S(1)}, bf16[1088,128]{1,0:T(8,128)(2,1)S(1)}, u32[]{:S(2)}, u32[]{:S(2)}) collective-permute-start(bf16[1088,128]{1,0:T(8,128)(2,1)S(1)} %get-tuple-element.82), channel_id=1, source_target_pairs={{0,1},{1,2},{2,3},{3,0},{4,5},{5,6},{6,7},{7,4},{8,9},{9,10},{10,1... | collective-permute-start | bytes 835592 | tf_op jit(solution)/shard_map/ppermute | solution.py:363
  83.2 14.8 %collective-permute-start.13 = (bf16[1088,128]{1,0:T(8,128)(2,1)S(1)}, bf16[1088,128]{1,0:T(8,128)(2,1)S(1)}, u32[]{:S(2)}, u32[]{:S(2)}) collective-permute-start(bf16[1088,128]{1,0:T(8,128)(2,1)S(1)} %get-tuple-element.83), channel_id=1, source_target_pairs={{0,2},{1,3},{2,0},{3,1},{4,6},{5,7},{6,4},{7,5},{8,10},{9,11},{10,... | collective-permute-start | bytes 835592 | tf_op jit(solution)/shard_map/ppermute | solution.py:363
  88.8 9.4 %collective-permute-start.14 = (bf16[1088,128]{1,0:T(8,128)(2,1)S(1)}, bf16[1088,128]{1,0:T(8,128)(2,1)S(1)}, u32[]{:S(2)}, u32[]{:S(2)}) collective-permute-start(bf16[1088,128]{1,0:T(8,128)(2,1)S(1)} %get-tuple-element.84), channel_id=1, source_target_pairs={{0,3},{1,0},{2,1},{3,2},{4,7},{5,4},{6,5},{7,6},{8,11},{9,8},{10,9... | collective-permute-start | bytes 835592 | tf_op jit(solution)/shard_map/ppermute | solution.py:363
  98.9 14.1 %collective-permute-start.17 = (bf16[4,272,128]{2,1,0:T(8,128)(2,1)S(1)}, bf16[4,272,128]{2,1,0:T(8,128)(2,1)S(1)}, u32[]{:S(2)}, u32[]{:S(2)}) collective-permute-start(bf16[4,272,128]{2,1,0:T(8,128)(2,1)S(1)} %get-tuple-element.85.refs_2_.refs_0_), channel_id=1, source_target_pairs={{0,1},{1,2},{2,3},{3,0},{4,5},{5,6},{6,7},{7,4},{8,9},{9,10},{10,1... | collective-permute-start | bytes 835592 | tf_op jit(solution)/shard_map/ppermute | solution.py:363
  100.8 11.0 %collective-permute-start.15 = (bf16[4,40,128]{2,1,0:T(8,128)(2,1)S(1)}, bf16[4,40,128]{2,1,0:T(8,128)(2,1)S(1)}, u32[]{:S(2)}, u32[]{:S(2)}) collective-permute-start(bf16[4,40,128]{2,1,0:T(8,128)(2,1)S(1)} %get-tuple-element.86), channel_id=1, source_target_pairs={{0,16},{16,32},{32,48},{48,64},{64,80},{80,96},{96,112},{112,128},... | collective-permute-start | bytes 122888 | tf_op jit(solution)/shard_map/ppermute | solution.py:136
  106.5 6.5 %collective-permute-start.16 = (bf16[4,40,128]{2,1,0:T(8,128)(2,1)S(1)}, bf16[4,40,128]{2,1,0:T(8,128)(2,1)S(1)}, u32[]{:S(2)}, u32[]{:S(2)}) collective-permute-start(bf16[4,40,128]{2,1,0:T(8,128)(2,1)S(1)} %get-tuple-element.87), channel_id=1, source_target_pairs={{16,0},{32,16},{48,32},{64,48},{80,64},{96,80},{112,96},{128,112},... | collective-permute-start | bytes 122888 | tf_op jit(solution)/shard_map/ppermute | solution.py:137
  108.4 14.2 %collective-permute-start.21 = (bf16[4,272,128]{2,1,0:T(8,128)(2,1)S(1)}, bf16[4,272,128]{2,1,0:T(8,128)(2,1)S(1)}, u32[]{:S(2)}, u32[]{:S(2)}) collective-permute-start(bf16[4,272,128]{2,1,0:T(8,128)(2,1)S(1)} %get-tuple-element.85.refs_2_.refs_0_), channel_id=1, source_target_pairs={{0,3},{1,0},{2,1},{3,2},{4,7},{5,4},{6,5},{7,6},{8,11},{9,8},{10,9... | collective-permute-start | bytes 835592 | tf_op jit(solution)/shard_map/ppermute | solution.py:363
  110.3 12.3 %collective-permute-start.19 = (bf16[4,272,128]{2,1,0:T(8,128)(2,1)S(1)}, bf16[4,272,128]{2,1,0:T(8,128)(2,1)S(1)}, u32[]{:S(2)}, u32[]{:S(2)}) collective-permute-start(bf16[4,272,128]{2,1,0:T(8,128)(2,1)S(1)} %get-tuple-element.85.refs_2_.refs_0_), channel_id=1, source_target_pairs={{0,2},{1,3},{2,0},{3,1},{4,6},{5,7},{6,4},{7,5},{8,10},{9,11},{10,... | collective-permute-start | bytes 835592 | tf_op jit(solution)/shard_map/ppermute | solution.py:363
  113.0 13.0 %collective-permute-start.22 = (bf16[4,80,128]{2,1,0:T(8,128)(2,1)S(1)}, bf16[4,80,128]{2,1,0:T(8,128)(2,1)S(1)}, u32[]{:S(2)}, u32[]{:S(2)}) collective-permute-start(bf16[4,80,128]{2,1,0:T(8,128)(2,1)S(1)} %pack.1.refs_1_), channel_id=1, source_target_pairs={{0,3},{1,0},{2,1},{3,2},{4,7},{5,4},{6,5},{7,6},{8,11},{9,8},{10,9... | collective-permute-start | bytes 245768 | tf_op jit(solution)/shard_map/ppermute | solution.py:363
  115.2 10.7 %collective-permute-start.20 = (bf16[4,80,128]{2,1,0:T(8,128)(2,1)S(1)}, bf16[4,80,128]{2,1,0:T(8,128)(2,1)S(1)}, u32[]{:S(2)}, u32[]{:S(2)}) collective-permute-start(bf16[4,80,128]{2,1,0:T(8,128)(2,1)S(1)} %pack.1.refs_1_), channel_id=1, source_target_pairs={{0,2},{1,3},{2,0},{3,1},{4,6},{5,7},{6,4},{7,5},{8,10},{9,11},{10,... | collective-permute-start | bytes 245768 | tf_op jit(solution)/shard_map/ppermute | solution.py:363
  116.6 9.4 %collective-permute-start.18 = (bf16[4,80,128]{2,1,0:T(8,128)(2,1)S(1)}, bf16[4,80,128]{2,1,0:T(8,128)(2,1)S(1)}, u32[]{:S(2)}, u32[]{:S(2)}) collective-permute-start(bf16[4,80,128]{2,1,0:T(8,128)(2,1)S(1)} %pack.1.refs_1_), channel_id=1, source_target_pairs={{0,1},{1,2},{2,3},{3,0},{4,5},{5,6},{6,7},{7,4},{8,9},{9,10},{10,1... | collective-permute-start | bytes 245768 | tf_op jit(solution)/shard_map/ppermute | solution.py:363
  (2 other events, 17.3 us)

commit v8 on v5

--- a/solution.py
+++ b/solution.py
@@ -115,8 +115,7 @@
     for c in copies[:3]:
         c.wait()
     x, c1, c2 = x_ref[...].astype(F32), c1_ref[...].astype(F32), c2_ref[...].astype(F32)
-    mean, m2 = local_stats(x.reshape(-1, CH))
-    store_stats(slot_ref, mean, m2)
+    store_stats(slot_ref, *local_stats(x.reshape(-1, CH)))
     store_edges((c1, x, c2), edges)
     for c in copies[3:]:
         c.wait()
@@ -280,8 +279,8 @@
     copies[3].wait()
 
 
-def near_body(patch_ref, side_ref, w_ref, out3, out0):
-    multiply(patch_ref, side_ref, w_ref, (out3, out0))
+def near_body(patch_ref, side_ref, w_ref, *rest):
+    multiply(patch_ref, side_ref, w_ref, rest[-2:])
 
 
 def conv(flags, x, cache, stats, halo, cache_at, act_at, around, weight, ext, name, after=()):
@@ -289,7 +288,7 @@
     depth, width = weight.shape
     flops = n * depth * width
     piece = sds((n, CH))
-    body = functools.partial(far_body, ext, cache_at, act_at, len(after))
+    body = functools.partial(far_body, ext, cache_at, act_at, 0)
     out2, out1, patch, side, near = call(
         body,
         [piece] * 2
@@ -307,16 +306,35 @@
         flops=flops,
         limit=20,
         name=name + "_far",
-    )(flags, x, cache, stats, *halo, *around, Left(weight, HBM), *[Left(a) for a in after])
+    )(flags, x, cache, stats, *halo, *around, Left(weight, HBM))
     got2 = to_peer(out2, 2)
     got1 = to_peer(out1, 1)
-    out3, own = call(near_body, [piece] * 2, flops=flops, limit=16, name=name + "_near")(patch, side, near)
+    out3, own = call(near_body, [piece] * 2, flops=flops, limit=16, name=name + "_near")(
+        patch, side, near, *[Left(a) for a in after]
+    )
     (far,) = call(add_body, [sds((n, CH), F32)], name=name + "_add")(got1, got2)
     return own, far, to_peer(out3, 3)
 
 
 def add_body(a_ref, b_ref, o_ref):
     o_ref[...] = a_ref[...].astype(F32) + b_ref[...].astype(F32)
+
+
+def gate_body(*refs):
+    del refs
+
+
+def gate(arrays, after):
+    n = len(arrays)
+    return pl.pallas_call(
+        gate_body,
+        out_shape=[sds(a.shape) for a in arrays],
+        in_specs=[ANY] * (n + 1),
+        out_specs=[ANY] * n,
+        input_output_aliases={i: i for i in range(n)},
+        compiler_params=pltpu.CompilerParams(vmem_limit_bytes=8 * MIB),
+        name="gate",
+    )(*arrays, after)
 
 
 def to_peer(piece, k):
@@ -382,32 +400,31 @@
                         o_ref[q, r, at : at + CH, p * CH : (p + 1) * CH] = total.astype(BF16)
 
 
+def inner_body(*refs):
+    o_ref = refs[-1]
+    size = ROWS * COLS
+    for k, ref in enumerate(refs[:4]):
+        for t in range(4):
+            v = ref[t].astype(F32)
+            rows = v[:size].reshape(ROWS, COLS, CH)
+            place(o_ref, t, rows, 0, v[size : size + 8], v[size + 8 :], [(e * 4 + k) * CH for e in range(3)])
+
+
 def up_body(*refs):
-    parts = [refs[2 * k : 2 * k + 2] for k in range(4)]
-    w_ref, o_ref, patch_ref, mix_ref = refs[8:12]
-    size = (ROWS + 1) * COLS
+    borders = refs[:4]
+    patch_ref, w_ref, o_ref, edge_ref, mix_ref = refs[4:]
     half = 2 * 4 * CH
-    for k, (x, border) in enumerate(parts):
+    for k, border in enumerate(borders):
         edge = border[0].astype(F32)
-        own = x[0].astype(F32)
-        inside = ROWS * COLS
-        place_frame(
-            patch_ref,
-            0,
-            own[:inside].reshape(ROWS, COLS, CH),
-            edge[:COLS],
-            edge[COLS + 8 : 2 * COLS + 8],
-            own[inside : inside + 8],
-            own[inside + 8 :],
-            [edge[i : i + 1] for i in (COLS, COLS + 1, 2 * COLS + 8, 2 * COLS + 9)],
-            [(e * 4 + k) * CH for e in range(3)],
-        )
+        for i in range(2):
+            v = edge[i * (COLS + 8) : (i + 1) * (COLS + 8)]
+            lanes = [(e * 4 + k) * CH for e in range(3)]
+            place(edge_ref, i, v[:COLS][None], 0, v[COLS : COLS + 1], v[COLS + 1 : COLS + 2], lanes)
     for q in range(2):
-        acc = None
-        for r in range(2):
-            lhs = patch_ref[0, r * COLS : r * COLS + size, q * 4 * CH : q * 4 * CH + half]
-            part = jnp.dot(lhs, w_ref[q, r], preferred_element_type=F32)
-            acc = part if acc is None else acc + part
+        lanes = pl.ds(q * 4 * CH, half)
+        inner = patch_ref[0, :, lanes]
+        acc = jnp.dot(jnp.concatenate([edge_ref[0, :, lanes], inner], axis=0), w_ref[q, 0], preferred_element_type=F32)
+        acc += jnp.dot(jnp.concatenate([inner, edge_ref[1, :, lanes]], axis=0), w_ref[q, 1], preferred_element_type=F32)
         for n in range(ROWS + 1):
             for p in range(2):
                 i = 2 * n - 1 + p
@@ -416,30 +433,26 @@
     o_ref[0] = mix_ref[...].astype(BF16)
 
 
-def up_conv(parts, weight):
-    specs = []
-    args = []
-    for part in parts:
-        for a in part:
-            rest = a.shape[1:]
-            specs.append(pl.BlockSpec((1,) + rest, lambda t, n=len(rest): (t,) + (0,) * n))
-            args.append(a)
-    specs.append(pl.BlockSpec(weight.shape, lambda t: (0, 0, 0, 0)))
-    frames = parts[0][0].shape[0]
+def up_conv(inner, borders, weight):
+    def by_frame(a):
+        return pl.BlockSpec((1,) + a.shape[1:], lambda t: (t, 0, 0))
+
+    frames = inner.shape[0]
     out = (frames, 2 * ROWS, 2 * COLS, CH)
     return pl.pallas_call(
         up_body,
         out_shape=sds(out),
         grid=(frames,),
-        in_specs=specs,
+        in_specs=[by_frame(a) for a in borders]
+        + [by_frame(inner), pl.BlockSpec(weight.shape, lambda t: (0, 0, 0, 0))],
         out_specs=pl.BlockSpec((1,) + out[1:], lambda t: (t, 0, 0, 0)),
         scratch_shapes=[
-            pltpu.VMEM((1, (ROWS + 2) * COLS, 12 * CH), BF16),
+            pltpu.VMEM((2, COLS, 12 * CH), BF16),
             pltpu.VMEM((2 * ROWS, 2 * COLS, CH), F32),
         ],
         compiler_params=pltpu.CompilerParams(vmem_limit_bytes=24 * MIB),
         name="up_conv",
-    )(*args, weight)
+    )(*borders, inner, weight)
 
 
 def on_device(features, cache_first, cache_second, weight_first, weight_second, weight_up):
@@ -460,13 +473,12 @@
         name="first",
     )(flags, *[Left(a, HBM) for a in (features, cache_first, cache_second, weight_up)])
     edges, w_pieces = edges[:4], edges[4:]
-    w_got = to_peers(w_pieces[1:])
     stats = spread(stats)
     rows = swap_rows(*edges[:2])
     cornered = call(corner_body, [sds((8, WIDE, 16, CH))] * 2, name="corners")(*rows, *edges[2:])
     halo = rows + swap_columns(*cornered)
     pieces = conv(
-        flags, x, c1, stats, halo, 0, 2, (), weight_first.reshape(-1, 4 * CH), 2, "conv_first", after=w_got
+        flags, x, c1, stats, halo, 0, 2, (), weight_first.reshape(-1, 4 * CH), 2, "conv_first"
     )
     hidden, side, stats, top, bot = call(
         hidden_body,
@@ -474,10 +486,11 @@
         limit=12,
         name="hidden",
     )(*pieces)
+    w_got = to_peers(gate(w_pieces[1:], stats))
     stats = spread(stats)
     around = (side,) + swap_rows(top, bot)
     pieces = conv(
-        flags, hidden, c2, stats, halo, 6, None, around, weight_second.reshape(-1, 4 * CH), 1, "conv_second"
+        flags, hidden, c2, stats, halo, 6, None, around, weight_second.reshape(-1, 4 * CH), 1, "conv_second", w_got
     )
     resid, top, bot = call(
         resid_body,
@@ -493,7 +506,8 @@
     (folded,) = call(fold_body, [sds((2, 2, 8 * CH, 2 * CH))], limit=12, name="fold")(
         w_pieces[0], *w_got, *[Left(a) for a in others[1:]]
     )
-    return up_conv(list(zip([resid] + others, borders)), folded)
+    (inner,) = call(inner_body, [sds((frames, ROWS * COLS, 12 * CH))], limit=16, name="inner")(resid, *others)
+    return up_conv(inner, borders, folded)
 
 
 def pack_body(top_ref, bot_ref, after_ref, o_ref):

time: 127 us -> 125 us (0.984)
  waiting for transfers between devices: 34.4 us -> 29.8 us
  starting transfers between devices: 66.7 us -> 69.5 us
    ppermute x15, waiting for transfers between devices: 20.8 us -> 16 us  [to_peer(): return lax.ppermute(piece, 'col', [(i, (i + k) % n) for i in range(n)])]
    ppermute x15, starting transfers between devices: 18.5 us -> 20.5 us  [to_peer(): return lax.ppermute(piece, 'col', [(i, (i + k) % n) for i in range(n)])]
    pallas_call x12 -> x13, Pallas kernels: 20.4 us -> 21.1 us  [run(): pl.pallas_call(body, out_shape=list(outs), in_specs=specs, out_specs=[VME...]
    pallas_call x1 -> x2, Pallas kernels: 4.15 us -> 3.97 us  [the longest x1 3.97 us: up_conv(): pl.pallas_call(up_body, out_shape=sds(out), grid=(frames,), in_specs=[by_...]
  transfers between devices with their start and end apart: 25 -> 25, of which waited for: 11 -> 9; matrix products, arithmetic and copies ran while one was open for 0% -> 0% of each run, Pallas kernels for 5% -> 9%
where the time goes in v8:
time: 125 us
  starting transfers between devices  69.5 us (56%)
  waiting for transfers between devices  29.8 us (24%)
  Pallas kernels  25.1 us (20%)
    all_to_all x2, starting transfers between devices, spread(): return lax.all_to_all(slots, HA + ('wa',), 0, 0, tiled=True)  23.1 us
    pallas_call x13, Pallas kernels, run(): pl.pallas_call(body, out_shape=list(outs), in_specs=specs, out_specs=[VME...  21.1 us
    ppermute x15, starting transfers between devices, to_peer(): return lax.ppermute(piece, 'col', [(i, (i + k) % n) for i in range(n)])  20.5 us
    ppermute x15, waiting for transfers between devices, to_peer(): return lax.ppermute(piece, 'col', [(i, (i + k) % n) for i in range(n)])  16 us
    ppermute x3, starting transfers between devices, swap_rows(): above = lax.ppermute(bot, HA, [(i, i + 1) for i in range(n - 1)])  15.8 us
    ppermute x3, waiting for transfers between devices, swap_rows(): below = lax.ppermute(top, HA, [(i + 1, i) for i in range(n - 1)])  9.73 us
    ppermute x3, starting transfers between devices, swap_rows(): below = lax.ppermute(top, HA, [(i + 1, i) for i in range(n - 1)])  5.76 us
    pallas_call x1, Pallas kernels, up_conv(): pl.pallas_call(up_body, out_shape=sds(out), grid=(frames,), in_specs=[by_...  3.97 us
  transfers between devices with their start and end apart: 25, of which 9 were waited for; matrix products, arithmetic and copies ran while one was open for 0% of the time, Pallas kernels for 9%

profile of v8, /device:TPU:97, one launch (start us, length us, event | category | flops | bytes accessed | tf_op | source)
XLA Modules:
  0.0 124.7 jit_solution(5128754498542631479)
XLA Ops:
  0.1 3.2 %first.1 = (bf16[4,8,32,128]{3,2,1,0:T(8,128)(2,1)S(1)}, bf16[2,8,32,128]{3,2,1,0:T(8,128)(2,1)S(1)}, bf16[2,8,32,128]{3,2,1,0:T(8,128)(2,1)S(1)}, f32[64,2,128]...) custom-call(s32[5]{0:T(128)S(1)} %stack.39.flag_ref, ...), custom_call_target="tpu_custom_call" | custom-call | bytes 3801108 | tf_op jit(solution)/shard_map/first/pallas_call | solution.py:39
  3.2 5.3 %collective-permute-start = (bf16[8,32,128]{2,1,0:T(8,128)(2,1)S(1)}, bf16[8,32,128]{2,1,0:T(8,128)(2,1)S(1)}, u32[]{:S(2)}, u32[]{:S(2)}) collective-permute-start(bf16[8,32,128]{2,1,0:T(8,128)(2,1)S(1)} %get-tuple-element.44), channel_id=1, source_target_pairs={{0,16},{16,32},{32,48},{48,64},{64,80},{80,96},{96,112},{112,128},... | collective-permute-start | bytes 196616 | tf_op jit(solution)/shard_map/ppermute | solution.py:139
  8.6 1.9 %collective-permute-start.1 = (bf16[8,32,128]{2,1,0:T(8,128)(2,1)S(1)}, bf16[8,32,128]{2,1,0:T(8,128)(2,1)S(1)}, u32[]{:S(2)}, u32[]{:S(2)}) collective-permute-start(bf16[8,32,128]{2,1,0:T(8,128)(2,1)S(1)} %get-tuple-element.45), channel_id=1, source_target_pairs={{16,0},{32,16},{48,32},{64,48},{80,64},{96,80},{112,96},{128,112},... | collective-permute-start | bytes 196616 | tf_op jit(solution)/shard_map/ppermute | solution.py:140
  10.5 10.8 %all-to-all-start = ((f32[64,2,128]{2,1,0:T(2,128)}), f32[64,2,128]{2,1,0:T(2,128)S(1)}, u32[]{:S(2)}, u32[]{:S(2)}) async-start(f32[64,2,128]{2,1,0:T(2,128)} %get-tuple-element.52), calls=%async_computation | async-start | bytes 131072 | tf_op jit(solution)/shard_map/all_to_all | solution.py:89
  21.4 3.1 %collective-permute-start.2 = (bf16[8,3,16,128]{3,2,1,0:T(8,128)(2,1)S(1)}, bf16[8,3,16,128]{3,2,1,0:T(8,128)(2,1)S(1)}, u32[]{:S(2)}, u32[]{:S(2)}) collective-permute-start(bf16[8,3,16,128]{3,2,1,0:T(8,128)(2,1)S(1)} %get-tuple-element.48), channel_id=1, source_target_pairs={{0,4},{4,8},{8,12},{1,5},{5,9},{9,13},{2,6},{6,10},{10,14},{3,7},{... | collective-permute-start | bytes 294920 | tf_op jit(solution)/shard_map/ppermute | solution.py:146
  25.8 2.6 %all-to-all-done.st_ref = f32[64,2,128]{2,1,0:T(2,128)S(1)} async-done(((f32[64,2,128]{2,1,0:T(2,128)}), f32[64,2,128]{2,1,0:T(2,128)S(1)}, u32[]{:S(2)}, u32[]{:S(2)}) %all-to-all-start) | async-done | bytes 65568 | tf_op jit(solution)/shard_map/all_to_all | solution.py:89
  29.8 4.5 %conv_first_far.1 = (bf16[1152,128]{1,0:T(8,128)(2,1)S(1)}, bf16[1152,128]{1,0:T(8,128)(2,1)S(1)}, bf16[6,320,384]{2,1,0:T(8,128)(2,1)S(1)}, bf16[3,160,384]{2,1,0:T(8,128)(2,1)S(1)}, bf16[3456,256]{1,0:T(8,128)(2,1)S(1)}) custom-call(s32[5]{0:T(128)S(1)} %stack.39.flag_ref, bf16[4,8,32,128]{3,2,1,0:T(8,128)(2,1)S(1)} %get-tuple-element.50.x_ref, ...), custom_call_target="tpu_custom_call" | custom-call | flops 2038431744 | bytes 8527892 | tf_op jit(solution)/shard_map/conv_first_far/pallas_call | solution.py:39
  35.7 2.5 %collective-permute-start.5 = (bf16[1152,128]{1,0:T(8,128)(2,1)S(1)}, bf16[1152,128]{1,0:T(8,128)(2,1)S(1)}, u32[]{:S(2)}, u32[]{:S(2)}) collective-permute-start(bf16[1152,128]{1,0:T(8,128)(2,1)S(1)} %get-tuple-element.58), channel_id=1, source_target_pairs={{0,2},{1,3},{2,0},{3,1},{4,6},{5,7},{6,4},{7,5},{8,10},{9,11},{10,... | collective-permute-start | bytes 884744 | tf_op jit(solution)/shard_map/ppermute | solution.py:342
  38.1 2.5 %conv_first_near.1 = (bf16[1152,128]{1,0:T(8,128)(2,1)S(1)}, bf16[1152,128]{1,0:T(8,128)(2,1)S(1)}) custom-call(bf16[6,320,384]{2,1,0:T(8,128)(2,1)S(1)} %get-tuple-element.53.patch_ref, bf16[3,160,384]{2,1,0:T(8,128)(2,1)S(1)} %get-tuple-element.54.side_ref, bf16[3456,256]{1,0:T(8,128)(2,1)S(1)} %get-tuple-element.55.w_ref), custom_call_target="tpu_custom_call" | custom-call | flops 2038431744 | bytes 4202496 | tf_op jit(solution)/shard_map/conv_first_near/pallas_call | solution.py:39
  42.4 7.3 %collective-permute-done.5.b_ref = bf16[1152,128]{1,0:T(8,128)(2,1)S(1)} collective-permute-done((bf16[1152,128]{1,0:T(8,128)(2,1)S(1)}, bf16[1152,128]{1,0:T(8,128)(2,1)S(1)}, u32[]{:S(2)}, u32[]{:S(2)}) %collective-permute-start.5) | collective-permute-done | bytes 294944 | tf_op jit(solution)/shard_map/ppermute | solution.py:342
  51.4 12.3 %all-to-all-start.1 = ((f32[64,2,128]{2,1,0:T(2,128)}), f32[64,2,128]{2,1,0:T(2,128)S(1)}, u32[]{:S(2)}, u32[]{:S(2)}) async-start(f32[64,2,128]{2,1,0:T(2,128)} %get-tuple-element.62.refs_3_), calls=%async_computation.1 | async-start | bytes 131072 | tf_op jit(solution)/shard_map/all_to_all | solution.py:89
  63.8 2.4 %collective-permute-start.10 = (bf16[9,128,128]{2,1,0:T(8,128)(2,1)S(1)}, bf16[9,128,128]{2,1,0:T(8,128)(2,1)S(1)}, u32[]{:S(2)}, u32[]{:S(2)}) collective-permute-start(bf16[9,128,128]{2,1,0:T(8,128)(2,1)S(1)} %get-tuple-element.73), channel_id=1, source_target_pairs={{0,2},{1,3},{2,0},{3,1},{4,6},{5,7},{6,4},{7,5},{8,10},{9,11},{10,... | collective-permute-start | bytes 884744 | tf_op jit(solution)/shard_map/ppermute | solution.py:342
  67.9 5.1 %collective-permute-start.7 = (bf16[144,128]{1,0:T(8,128)(2,1)S(1)}, bf16[144,128]{1,0:T(8,128)(2,1)S(1)}, u32[]{:S(2)}, u32[]{:S(2)}) collective-permute-start(bf16[144,128]{1,0:T(8,128)(2,1)S(1)} %get-tuple-element.64), channel_id=1, source_target_pairs={{0,16},{16,32},{32,48},{48,64},{64,80},{80,96},{96,112},{112,128},... | collective-permute-start | bytes 110600 | tf_op jit(solution)/shard_map/ppermute | solution.py:139
  75.0 4.8 %collective-permute-done.8.rest_6_ = bf16[144,128]{1,0:T(8,128)(2,1)S(1)} collective-permute-done((bf16[144,128]{1,0:T(8,128)(2,1)S(1)}, bf16[144,128]{1,0:T(8,128)(2,1)S(1)}, u32[]{:S(2)}, u32[]{:S(2)}) %collective-permute-start.8) | collective-permute-done | bytes 36896 | tf_op jit(solution)/shard_map/ppermute | solution.py:140
  79.8 4.5 %conv_second_far.1 = (bf16[1088,128]{1,0:T(8,128)(2,1)S(1)}, bf16[1088,128]{1,0:T(8,128)(2,1)S(1)}, bf16[6,320,384]{2,1,0:T(8,128)(2,1)S(1)}, bf16[3,80,384]{2,1,0:T(8,128)(2,1)S(1)}, bf16[3456,256]{1,0:T(8,128)(2,1)S(1)}) custom-call(s32[5]{0:T(128)S(1)} %stack.39.flag_ref, bf16[4,8,32,128]{3,2,1,0:T(8,128)(2,1)S(1)} %get-tuple-element.60.x_ref, ...), custom_call_target="tpu_custom_call" | custom-call | flops 1925185536 | bytes 8450068 | tf_op jit(solution)/shard_map/conv_second_far/pallas_call | solution.py:39
  84.5 3.9 %collective-permute-start.13 = (bf16[1088,128]{1,0:T(8,128)(2,1)S(1)}, bf16[1088,128]{1,0:T(8,128)(2,1)S(1)}, u32[]{:S(2)}, u32[]{:S(2)}) collective-permute-start(bf16[1088,128]{1,0:T(8,128)(2,1)S(1)} %get-tuple-element.77), channel_id=1, source_target_pairs={{0,2},{1,3},{2,0},{3,1},{4,6},{5,7},{6,4},{7,5},{8,10},{9,11},{10,... | collective-permute-start | bytes 835592 | tf_op jit(solution)/shard_map/ppermute | solution.py:342
  88.5 2.5 %conv_second_near.1 = (bf16[1088,128]{1,0:T(8,128)(2,1)S(1)}, bf16[1088,128]{1,0:T(8,128)(2,1)S(1)}) custom-call(bf16[6,320,384]{2,1,0:T(8,128)(2,1)S(1)} %get-tuple-element.66.patch_ref, bf16[3,80,384]{2,1,0:T(8,128)(2,1)S(1)} %get-tuple-element.67.side_ref, bf16[3456,256]{1,0:T(8,128)(2,1)S(1)} %get-tuple-element.68.w_ref, ...), custom_call_target="tpu_custom_call" | custom-call | flops 1925185536 | bytes 4870144 | tf_op jit(solution)/shard_map/conv_second_near/pallas_call | solution.py:39
  91.1 2.4 %collective-permute-done.12.a_ref = bf16[1088,128]{1,0:T(8,128)(2,1)S(1)} collective-permute-done((bf16[1088,128]{1,0:T(8,128)(2,1)S(1)}, bf16[1088,128]{1,0:T(8,128)(2,1)S(1)}, u32[]{:S(2)}, u32[]{:S(2)}) %collective-permute-start.12) | collective-permute-done | bytes 278560 | tf_op jit(solution)/shard_map/ppermute | solution.py:342
  93.4 4.9 %collective-permute-done.13.b_ref = bf16[1088,128]{1,0:T(8,128)(2,1)S(1)} collective-permute-done((bf16[1088,128]{1,0:T(8,128)(2,1)S(1)}, bf16[1088,128]{1,0:T(8,128)(2,1)S(1)}, u32[]{:S(2)}, u32[]{:S(2)}) %collective-permute-start.13) | collective-permute-done | bytes 278560 | tf_op jit(solution)/shard_map/ppermute | solution.py:342
  99.2 3.0 %collective-permute-start.21 = (bf16[4,272,128]{2,1,0:T(8,128)(2,1)S(1)}, bf16[4,272,128]{2,1,0:T(8,128)(2,1)S(1)}, u32[]{:S(2)}, u32[]{:S(2)}) collective-permute-start(bf16[4,272,128]{2,1,0:T(8,128)(2,1)S(1)} %get-tuple-element.81.refs_0_), channel_id=1, source_target_pairs={{0,2},{1,3},{2,0},{3,1},{4,6},{5,7},{6,4},{7,5},{8,10},{9,11},{10,... | collective-permute-start | bytes 835592 | tf_op jit(solution)/shard_map/ppermute | solution.py:342
  102.3 5.3 %collective-permute-start.15 = (bf16[4,40,128]{2,1,0:T(8,128)(2,1)S(1)}, bf16[4,40,128]{2,1,0:T(8,128)(2,1)S(1)}, u32[]{:S(2)}, u32[]{:S(2)}) collective-permute-start(bf16[4,40,128]{2,1,0:T(8,128)(2,1)S(1)} %get-tuple-element.79), channel_id=1, source_target_pairs={{0,16},{16,32},{32,48},{48,64},{64,80},{80,96},{96,112},{112,128},... | collective-permute-start | bytes 122888 | tf_op jit(solution)/shard_map/ppermute | solution.py:139
  109.5 4.9 %collective-permute-done.16.bot_ref = bf16[4,40,128]{2,1,0:T(8,128)(2,1)S(1)} collective-permute-done((bf16[4,40,128]{2,1,0:T(8,128)(2,1)S(1)}, bf16[4,40,128]{2,1,0:T(8,128)(2,1)S(1)}, u32[]{:S(2)}, u32[]{:S(2)}) %collective-permute-start.16) | collective-permute-done | bytes 40992 | tf_op jit(solution)/shard_map/ppermute | solution.py:140
  116.7 2.0 %collective-permute-start.20 = (bf16[4,80,128]{2,1,0:T(8,128)(2,1)S(1)}, bf16[4,80,128]{2,1,0:T(8,128)(2,1)S(1)}, u32[]{:S(2)}, u32[]{:S(2)}) collective-permute-start(bf16[4,80,128]{2,1,0:T(8,128)(2,1)S(1)} %pack.1.refs_0_), channel_id=1, source_target_pairs={{0,3},{1,0},{2,1},{3,2},{4,7},{5,4},{6,5},{7,6},{8,11},{9,8},{10,9... | collective-permute-start | bytes 245768 | tf_op jit(solution)/shard_map/ppermute | solution.py:342
  120.8 4.0 %up_conv.1 = bf16[4,16,64,128]{3,2,1,0:T(8,128)(2,1)} custom-call(bf16[4,80,128]{2,1,0:T(8,128)(2,1)S(1)} %pack.1.refs_0_, bf16[4,80,128]{2,1,0:T(8,128)(2,1)S(1)} %collective-permute-done.18.refs_1_, bf16[4,80,128]{2,1,0:T(8,128)(2,1)S(1)} %collective-permute-done.19.refs_2_, bf16[4,80,128]{2,1,0:T(8,128)(2,1)S(1)} %collective-permute-done.20.refs_3_, ...), custom_call_target="tpu_custom_call" | custom-call | tf_op jit(solution)/shard_map/up_conv/pallas_call | solution.py:442
  (44 shorter events, 18.7 us)
Async XLA Ops:
  3.2 18.0 %collective-permute-start = (bf16[8,32,128]{2,1,0:T(8,128)(2,1)S(1)}, bf16[8,32,128]{2,1,0:T(8,128)(2,1)S(1)}, u32[]{:S(2)}, u32[]{:S(2)}) collective-permute-start(bf16[8,32,128]{2,1,0:T(8,128)(2,1)S(1)} %get-tuple-element.44), channel_id=1, source_target_pairs={{0,16},{16,32},{32,48},{48,64},{64,80},{80,96},{96,112},{112,128},... | collective-permute-start | bytes 196616 | tf_op jit(solution)/shard_map/ppermute | solution.py:139
  8.6 12.7 %collective-permute-start.1 = (bf16[8,32,128]{2,1,0:T(8,128)(2,1)S(1)}, bf16[8,32,128]{2,1,0:T(8,128)(2,1)S(1)}, u32[]{:S(2)}, u32[]{:S(2)}) collective-permute-start(bf16[8,32,128]{2,1,0:T(8,128)(2,1)S(1)} %get-tuple-element.45), channel_id=1, source_target_pairs={{16,0},{32,16},{48,32},{64,48},{80,64},{96,80},{112,96},{128,112},... | collective-permute-start | bytes 196616 | tf_op jit(solution)/shard_map/ppermute | solution.py:140
  10.5 17.9 %all-to-all-start = ((f32[64,2,128]{2,1,0:T(2,128)}), f32[64,2,128]{2,1,0:T(2,128)S(1)}, u32[]{:S(2)}, u32[]{:S(2)}) async-start(f32[64,2,128]{2,1,0:T(2,128)} %get-tuple-element.52), calls=%async_computation | async-start | bytes 131072 | tf_op jit(solution)/shard_map/all_to_all | solution.py:89
  21.4 7.0 %collective-permute-start.2 = (bf16[8,3,16,128]{3,2,1,0:T(8,128)(2,1)S(1)}, bf16[8,3,16,128]{3,2,1,0:T(8,128)(2,1)S(1)}, u32[]{:S(2)}, u32[]{:S(2)}) collective-permute-start(bf16[8,3,16,128]{3,2,1,0:T(8,128)(2,1)S(1)} %get-tuple-element.48), channel_id=1, source_target_pairs={{0,4},{4,8},{8,12},{1,5},{5,9},{9,13},{2,6},{6,10},{10,14},{3,7},{... | collective-permute-start | bytes 294920 | tf_op jit(solution)/shard_map/ppermute | solution.py:146
  24.5 5.4 %collective-permute-start.3 = (bf16[8,3,16,128]{3,2,1,0:T(8,128)(2,1)S(1)}, bf16[8,3,16,128]{3,2,1,0:T(8,128)(2,1)S(1)}, u32[]{:S(2)}, u32[]{:S(2)}) collective-permute-start(bf16[8,3,16,128]{3,2,1,0:T(8,128)(2,1)S(1)} %get-tuple-element.49), channel_id=1, source_target_pairs={{4,0},{8,4},{12,8},{5,1},{9,5},{13,9},{6,2},{10,6},{14,10},{7,3},{... | collective-permute-start | bytes 294920 | tf_op jit(solution)/shard_map/ppermute | solution.py:147
  34.4 8.0 %collective-permute-start.4 = (bf16[1152,128]{1,0:T(8,128)(2,1)S(1)}, bf16[1152,128]{1,0:T(8,128)(2,1)S(1)}, u32[]{:S(2)}, u32[]{:S(2)}) collective-permute-start(bf16[1152,128]{1,0:T(8,128)(2,1)S(1)} %get-tuple-element.57), channel_id=1, source_target_pairs={{0,1},{1,2},{2,3},{3,0},{4,5},{5,6},{6,7},{7,4},{8,9},{9,10},{10,1... | collective-permute-start | bytes 884744 | tf_op jit(solution)/shard_map/ppermute | solution.py:342
  35.7 14.0 %collective-permute-start.5 = (bf16[1152,128]{1,0:T(8,128)(2,1)S(1)}, bf16[1152,128]{1,0:T(8,128)(2,1)S(1)}, u32[]{:S(2)}, u32[]{:S(2)}) collective-permute-start(bf16[1152,128]{1,0:T(8,128)(2,1)S(1)} %get-tuple-element.58), channel_id=1, source_target_pairs={{0,2},{1,3},{2,0},{3,1},{4,6},{5,7},{6,4},{7,5},{8,10},{9,11},{10,... | collective-permute-start | bytes 884744 | tf_op jit(solution)/shard_map/ppermute | solution.py:342
  40.6 9.2 %collective-permute-start.6 = (bf16[1152,128]{1,0:T(8,128)(2,1)S(1)}, bf16[1152,128]{1,0:T(8,128)(2,1)S(1)}, u32[]{:S(2)}, u32[]{:S(2)}) collective-permute-start(bf16[1152,128]{1,0:T(8,128)(2,1)S(1)} %get-tuple-element.59), channel_id=1, source_target_pairs={{0,3},{1,0},{2,1},{3,2},{4,7},{5,4},{6,5},{7,6},{8,11},{9,8},{10,9... | collective-permute-start | bytes 884744 | tf_op jit(solution)/shard_map/ppermute | solution.py:342
  51.4 28.4 %all-to-all-start.1 = ((f32[64,2,128]{2,1,0:T(2,128)}), f32[64,2,128]{2,1,0:T(2,128)S(1)}, u32[]{:S(2)}, u32[]{:S(2)}) async-start(f32[64,2,128]{2,1,0:T(2,128)} %get-tuple-element.62.refs_3_), calls=%async_computation.1 | async-start | bytes 131072 | tf_op jit(solution)/shard_map/all_to_all | solution.py:89
  63.8 24.7 %collective-permute-start.10 = (bf16[9,128,128]{2,1,0:T(8,128)(2,1)S(1)}, bf16[9,128,128]{2,1,0:T(8,128)(2,1)S(1)}, u32[]{:S(2)}, u32[]{:S(2)}) collective-permute-start(bf16[9,128,128]{2,1,0:T(8,128)(2,1)S(1)} %get-tuple-element.73), channel_id=1, source_target_pairs={{0,2},{1,3},{2,0},{3,1},{4,6},{5,7},{6,4},{7,5},{8,10},{9,11},{10,... | collective-permute-start | bytes 884744 | tf_op jit(solution)/shard_map/ppermute | solution.py:342
  66.2 22.3 %collective-permute-start.11 = (bf16[9,128,128]{2,1,0:T(8,128)(2,1)S(1)}, bf16[9,128,128]{2,1,0:T(8,128)(2,1)S(1)}, u32[]{:S(2)}, u32[]{:S(2)}) collective-permute-start(bf16[9,128,128]{2,1,0:T(8,128)(2,1)S(1)} %get-tuple-element.74), channel_id=1, source_target_pairs={{0,3},{1,0},{2,1},{3,2},{4,7},{5,4},{6,5},{7,6},{8,11},{9,8},{10,9... | collective-permute-start | bytes 884744 | tf_op jit(solution)/shard_map/ppermute | solution.py:342
  67.9 20.5 %collective-permute-start.9 = (bf16[9,128,128]{2,1,0:T(8,128)(2,1)S(1)}, bf16[9,128,128]{2,1,0:T(8,128)(2,1)S(1)}, u32[]{:S(2)}, u32[]{:S(2)}) collective-permute-start(bf16[9,128,128]{2,1,0:T(8,128)(2,1)S(1)} %get-tuple-element.72), channel_id=1, source_target_pairs={{0,1},{1,2},{2,3},{3,0},{4,5},{5,6},{6,7},{7,4},{8,9},{9,10},{10,1... | collective-permute-start | bytes 884744 | tf_op jit(solution)/shard_map/ppermute | solution.py:342
  67.9 7.1 %collective-permute-start.7 = (bf16[144,128]{1,0:T(8,128)(2,1)S(1)}, bf16[144,128]{1,0:T(8,128)(2,1)S(1)}, u32[]{:S(2)}, u32[]{:S(2)}) collective-permute-start(bf16[144,128]{1,0:T(8,128)(2,1)S(1)} %get-tuple-element.64), channel_id=1, source_target_pairs={{0,16},{16,32},{32,48},{48,64},{64,80},{80,96},{96,112},{112,128},... | collective-permute-start | bytes 110600 | tf_op jit(solution)/shard_map/ppermute | solution.py:139
  73.1 6.8 %collective-permute-start.8 = (bf16[144,128]{1,0:T(8,128)(2,1)S(1)}, bf16[144,128]{1,0:T(8,128)(2,1)S(1)}, u32[]{:S(2)}, u32[]{:S(2)}) collective-permute-start(bf16[144,128]{1,0:T(8,128)(2,1)S(1)} %get-tuple-element.65), channel_id=1, source_target_pairs={{16,0},{32,16},{48,32},{64,48},{80,64},{96,80},{112,96},{128,112},... | collective-permute-start | bytes 110600 | tf_op jit(solution)/shard_map/ppermute | solution.py:140
  84.4 9.0 %collective-permute-start.12 = (bf16[1088,128]{1,0:T(8,128)(2,1)S(1)}, bf16[1088,128]{1,0:T(8,128)(2,1)S(1)}, u32[]{:S(2)}, u32[]{:S(2)}) collective-permute-start(bf16[1088,128]{1,0:T(8,128)(2,1)S(1)} %get-tuple-element.76), channel_id=1, source_target_pairs={{0,1},{1,2},{2,3},{3,0},{4,5},{5,6},{6,7},{7,4},{8,9},{9,10},{10,1... | collective-permute-start | bytes 835592 | tf_op jit(solution)/shard_map/ppermute | solution.py:342
  84.5 13.8 %collective-permute-start.13 = (bf16[1088,128]{1,0:T(8,128)(2,1)S(1)}, bf16[1088,128]{1,0:T(8,128)(2,1)S(1)}, u32[]{:S(2)}, u32[]{:S(2)}) collective-permute-start(bf16[1088,128]{1,0:T(8,128)(2,1)S(1)} %get-tuple-element.77), channel_id=1, source_target_pairs={{0,2},{1,3},{2,0},{3,1},{4,6},{5,7},{6,4},{7,5},{8,10},{9,11},{10,... | collective-permute-start | bytes 835592 | tf_op jit(solution)/shard_map/ppermute | solution.py:342
  91.0 7.4 %collective-permute-start.14 = (bf16[1088,128]{1,0:T(8,128)(2,1)S(1)}, bf16[1088,128]{1,0:T(8,128)(2,1)S(1)}, u32[]{:S(2)}, u32[]{:S(2)}) collective-permute-start(bf16[1088,128]{1,0:T(8,128)(2,1)S(1)} %get-tuple-element.78), channel_id=1, source_target_pairs={{0,3},{1,0},{2,1},{3,2},{4,7},{5,4},{6,5},{7,6},{8,11},{9,8},{10,9... | collective-permute-start | bytes 835592 | tf_op jit(solution)/shard_map/ppermute | solution.py:342
  99.2 15.3 %collective-permute-start.17 = (bf16[4,272,128]{2,1,0:T(8,128)(2,1)S(1)}, bf16[4,272,128]{2,1,0:T(8,128)(2,1)S(1)}, u32[]{:S(2)}, u32[]{:S(2)}) collective-permute-start(bf16[4,272,128]{2,1,0:T(8,128)(2,1)S(1)} %get-tuple-element.81.refs_0_), channel_id=1, source_target_pairs={{0,1},{1,2},{2,3},{3,0},{4,5},{5,6},{6,7},{7,4},{8,9},{9,10},{10,1... | collective-permute-start | bytes 835592 | tf_op jit(solution)/shard_map/ppermute | solution.py:342
  99.2 19.4 %collective-permute-start.21 = (bf16[4,272,128]{2,1,0:T(8,128)(2,1)S(1)}, bf16[4,272,128]{2,1,0:T(8,128)(2,1)S(1)}, u32[]{:S(2)}, u32[]{:S(2)}) collective-permute-start(bf16[4,272,128]{2,1,0:T(8,128)(2,1)S(1)} %get-tuple-element.81.refs_0_), channel_id=1, source_target_pairs={{0,2},{1,3},{2,0},{3,1},{4,6},{5,7},{6,4},{7,5},{8,10},{9,11},{10,... | collective-permute-start | bytes 835592 | tf_op jit(solution)/shard_map/ppermute | solution.py:342
  102.3 16.4 %collective-permute-start.22 = (bf16[4,272,128]{2,1,0:T(8,128)(2,1)S(1)}, bf16[4,272,128]{2,1,0:T(8,128)(2,1)S(1)}, u32[]{:S(2)}, u32[]{:S(2)}) collective-permute-start(bf16[4,272,128]{2,1,0:T(8,128)(2,1)S(1)} %get-tuple-element.81.refs_0_), channel_id=1, source_target_pairs={{0,3},{1,0},{2,1},{3,2},{4,7},{5,4},{6,5},{7,6},{8,11},{9,8},{10,9... | collective-permute-start | bytes 835592 | tf_op jit(solution)/shard_map/ppermute | solution.py:342
  102.3 7.3 %collective-permute-start.15 = (bf16[4,40,128]{2,1,0:T(8,128)(2,1)S(1)}, bf16[4,40,128]{2,1,0:T(8,128)(2,1)S(1)}, u32[]{:S(2)}, u32[]{:S(2)}) collective-permute-start(bf16[4,40,128]{2,1,0:T(8,128)(2,1)S(1)} %get-tuple-element.79), channel_id=1, source_target_pairs={{0,16},{16,32},{32,48},{48,64},{64,80},{80,96},{96,112},{112,128},... | collective-permute-start | bytes 122888 | tf_op jit(solution)/shard_map/ppermute | solution.py:139
  107.6 6.8 %collective-permute-start.16 = (bf16[4,40,128]{2,1,0:T(8,128)(2,1)S(1)}, bf16[4,40,128]{2,1,0:T(8,128)(2,1)S(1)}, u32[]{:S(2)}, u32[]{:S(2)}) collective-permute-start(bf16[4,40,128]{2,1,0:T(8,128)(2,1)S(1)} %get-tuple-element.80), channel_id=1, source_target_pairs={{16,0},{32,16},{48,32},{64,48},{80,64},{96,80},{112,96},{128,112},... | collective-permute-start | bytes 122888 | tf_op jit(solution)/shard_map/ppermute | solution.py:140
  114.4 5.5 %collective-permute-start.18 = (bf16[4,80,128]{2,1,0:T(8,128)(2,1)S(1)}, bf16[4,80,128]{2,1,0:T(8,128)(2,1)S(1)}, u32[]{:S(2)}, u32[]{:S(2)}) collective-permute-start(bf16[4,80,128]{2,1,0:T(8,128)(2,1)S(1)} %pack.1.refs_0_), channel_id=1, source_target_pairs={{0,1},{1,2},{2,3},{3,0},{4,5},{5,6},{6,7},{7,4},{8,9},{9,10},{10,1... | collective-permute-start | bytes 245768 | tf_op jit(solution)/shard_map/ppermute | solution.py:342
  116.0 4.8 %collective-permute-start.19 = (bf16[4,80,128]{2,1,0:T(8,128)(2,1)S(1)}, bf16[4,80,128]{2,1,0:T(8,128)(2,1)S(1)}, u32[]{:S(2)}, u32[]{:S(2)}) collective-permute-start(bf16[4,80,128]{2,1,0:T(8,128)(2,1)S(1)} %pack.1.refs_0_), channel_id=1, source_target_pairs={{0,2},{1,3},{2,0},{3,1},{4,6},{5,7},{6,4},{7,5},{8,10},{9,11},{10,... | collective-permute-start | bytes 245768 | tf_op jit(solution)/shard_map/ppermute | solution.py:342
  (2 other events, 14.0 us)

commit v9 on v8

--- a/solution.py
+++ b/solution.py
@@ -110,10 +110,12 @@
         block = pl.multiple_of(lax.rem(flag_ref[4] + k, 4) * CH, CH)
         pairs.append((w_hbm.at[:, :, pl.ds(block, CH)], piece))
     copies = [pltpu.make_async_copy(src, dst, sem.at[i]) for i, (src, dst) in enumerate(pairs)]
-    for c in copies:
+    for c in copies[:3]:
         c.start()
     for c in copies[:3]:
         c.wait()
+    for c in copies[3:]:
+        c.start()
     x, c1, c2 = x_ref[...].astype(F32), c1_ref[...].astype(F32), c2_ref[...].astype(F32)
     store_stats(slot_ref, *local_stats(x.reshape(-1, CH)))
     store_edges((c1, x, c2), edges)
@@ -232,7 +234,8 @@
         copies.append(
             pltpu.make_async_copy(w_hbm.at[:, pl.ds(block, CH)], dst.at[:, at : at + CH], sem.at[i])
         )
-        copies[-1].start()
+    for c in copies[:2]:
+        c.start()
     has = [flag_ref[i] > 0 for i in range(4)]
     mean, scale = merge(st_ref, BLOCK)
 
@@ -274,6 +277,8 @@
             side_ref[a, :, e * CH : (e + 1) * CH] = mix_ref[a, e].astype(BF16)
     copies[0].wait()
     copies[1].wait()
+    copies[2].start()
+    copies[3].start()
     multiply(patch_ref, side_ref, w_ref, (out2, out1))
     copies[2].wait()
     copies[3].wait()

time: 125 us -> 126 us (level)
  no operation moved by 1% of the time
where the time goes in v9:
time: 126 us
  starting transfers between devices  69.5 us (55%)
  waiting for transfers between devices  29.8 us (24%)
  Pallas kernels  26.1 us (21%)
    all_to_all x2, starting transfers between devices, spread(): return lax.all_to_all(slots, HA + ('wa',), 0, 0, tiled=True)  23.1 us
    pallas_call x13, Pallas kernels, run(): pl.pallas_call(body, out_shape=list(outs), in_specs=specs, out_specs=[VME...  22.2 us
    ppermute x15, starting transfers between devices, to_peer(): return lax.ppermute(piece, 'col', [(i, (i + k) % n) for i in range(n)])  20.5 us
    ppermute x15, waiting for transfers between devices, to_peer(): return lax.ppermute(piece, 'col', [(i, (i + k) % n) for i in range(n)])  16 us
    ppermute x3, starting transfers between devices, swap_rows(): above = lax.ppermute(bot, HA, [(i, i + 1) for i in range(n - 1)])  15.8 us
    ppermute x3, waiting for transfers between devices, swap_rows(): below = lax.ppermute(top, HA, [(i + 1, i) for i in range(n - 1)])  9.73 us
    ppermute x3, starting transfers between devices, swap_rows(): below = lax.ppermute(top, HA, [(i + 1, i) for i in range(n - 1)])  5.76 us
    pallas_call x1, Pallas kernels, up_conv(): pl.pallas_call(up_body, out_shape=sds(out), grid=(frames,), in_specs=[by_...  3.97 us
  transfers between devices with their start and end apart: 25, of which 9 were waited for; matrix products, arithmetic and copies ran while one was open for 0% of the time, Pallas kernels for 9%

profile of v9, /device:TPU:97, one launch (start us, length us, event | category | flops | bytes accessed | tf_op | source)
XLA Modules:
  0.0 125.8 jit_solution(2876509753337239456)
XLA Ops:
  0.1 4.2 %first.1 = (bf16[4,8,32,128]{3,2,1,0:T(8,128)(2,1)S(1)}, bf16[2,8,32,128]{3,2,1,0:T(8,128)(2,1)S(1)}, bf16[2,8,32,128]{3,2,1,0:T(8,128)(2,1)S(1)}, f32[64,2,128]...) custom-call(s32[5]{0:T(128)S(1)} %stack.39.flag_ref, ...), custom_call_target="tpu_custom_call" | custom-call | bytes 3801108 | tf_op jit(solution)/shard_map/first/pallas_call | solution.py:39
  4.3 5.3 %collective-permute-start = (bf16[8,32,128]{2,1,0:T(8,128)(2,1)S(1)}, bf16[8,32,128]{2,1,0:T(8,128)(2,1)S(1)}, u32[]{:S(2)}, u32[]{:S(2)}) collective-permute-start(bf16[8,32,128]{2,1,0:T(8,128)(2,1)S(1)} %get-tuple-element.44), channel_id=1, source_target_pairs={{0,16},{16,32},{32,48},{48,64},{64,80},{80,96},{96,112},{112,128},... | collective-permute-start | bytes 196616 | tf_op jit(solution)/shard_map/ppermute | solution.py:141
  9.7 1.9 %collective-permute-start.1 = (bf16[8,32,128]{2,1,0:T(8,128)(2,1)S(1)}, bf16[8,32,128]{2,1,0:T(8,128)(2,1)S(1)}, u32[]{:S(2)}, u32[]{:S(2)}) collective-permute-start(bf16[8,32,128]{2,1,0:T(8,128)(2,1)S(1)} %get-tuple-element.45), channel_id=1, source_target_pairs={{16,0},{32,16},{48,32},{64,48},{80,64},{96,80},{112,96},{128,112},... | collective-permute-start | bytes 196616 | tf_op jit(solution)/shard_map/ppermute | solution.py:142
  11.6 10.8 %all-to-all-start = ((f32[64,2,128]{2,1,0:T(2,128)}), f32[64,2,128]{2,1,0:T(2,128)S(1)}, u32[]{:S(2)}, u32[]{:S(2)}) async-start(f32[64,2,128]{2,1,0:T(2,128)} %get-tuple-element.52), calls=%async_computation | async-start | bytes 131072 | tf_op jit(solution)/shard_map/all_to_all | solution.py:89
  22.4 3.1 %collective-permute-start.2 = (bf16[8,3,16,128]{3,2,1,0:T(8,128)(2,1)S(1)}, bf16[8,3,16,128]{3,2,1,0:T(8,128)(2,1)S(1)}, u32[]{:S(2)}, u32[]{:S(2)}) collective-permute-start(bf16[8,3,16,128]{3,2,1,0:T(8,128)(2,1)S(1)} %get-tuple-element.48), channel_id=1, source_target_pairs={{0,4},{4,8},{8,12},{1,5},{5,9},{9,13},{2,6},{6,10},{10,14},{3,7},{... | collective-permute-start | bytes 294920 | tf_op jit(solution)/shard_map/ppermute | solution.py:148
  26.8 2.6 %all-to-all-done.st_ref = f32[64,2,128]{2,1,0:T(2,128)S(1)} async-done(((f32[64,2,128]{2,1,0:T(2,128)}), f32[64,2,128]{2,1,0:T(2,128)S(1)}, u32[]{:S(2)}, u32[]{:S(2)}) %all-to-all-start) | async-done | bytes 65568 | tf_op jit(solution)/shard_map/all_to_all | solution.py:89
  30.9 4.6 %conv_first_far.1 = (bf16[1152,128]{1,0:T(8,128)(2,1)S(1)}, bf16[1152,128]{1,0:T(8,128)(2,1)S(1)}, bf16[6,320,384]{2,1,0:T(8,128)(2,1)S(1)}, bf16[3,160,384]{2,1,0:T(8,128)(2,1)S(1)}, bf16[3456,256]{1,0:T(8,128)(2,1)S(1)}) custom-call(s32[5]{0:T(128)S(1)} %stack.39.flag_ref, bf16[4,8,32,128]{3,2,1,0:T(8,128)(2,1)S(1)} %get-tuple-element.50.x_ref, ...), custom_call_target="tpu_custom_call" | custom-call | flops 2038431744 | bytes 8527892 | tf_op jit(solution)/shard_map/conv_first_far/pallas_call | solution.py:39
  36.8 2.4 %collective-permute-start.5 = (bf16[1152,128]{1,0:T(8,128)(2,1)S(1)}, bf16[1152,128]{1,0:T(8,128)(2,1)S(1)}, u32[]{:S(2)}, u32[]{:S(2)}) collective-permute-start(bf16[1152,128]{1,0:T(8,128)(2,1)S(1)} %get-tuple-element.58), channel_id=1, source_target_pairs={{0,2},{1,3},{2,0},{3,1},{4,6},{5,7},{6,4},{7,5},{8,10},{9,11},{10,... | collective-permute-start | bytes 884744 | tf_op jit(solution)/shard_map/ppermute | solution.py:347
  39.2 2.5 %conv_first_near.1 = (bf16[1152,128]{1,0:T(8,128)(2,1)S(1)}, bf16[1152,128]{1,0:T(8,128)(2,1)S(1)}) custom-call(bf16[6,320,384]{2,1,0:T(8,128)(2,1)S(1)} %get-tuple-element.53.patch_ref, bf16[3,160,384]{2,1,0:T(8,128)(2,1)S(1)} %get-tuple-element.54.side_ref, bf16[3456,256]{1,0:T(8,128)(2,1)S(1)} %get-tuple-element.55.w_ref), custom_call_target="tpu_custom_call" | custom-call | flops 2038431744 | bytes 4202496 | tf_op jit(solution)/shard_map/conv_first_near/pallas_call | solution.py:39
  43.5 7.3 %collective-permute-done.5.b_ref = bf16[1152,128]{1,0:T(8,128)(2,1)S(1)} collective-permute-done((bf16[1152,128]{1,0:T(8,128)(2,1)S(1)}, bf16[1152,128]{1,0:T(8,128)(2,1)S(1)}, u32[]{:S(2)}, u32[]{:S(2)}) %collective-permute-start.5) | collective-permute-done | bytes 294944 | tf_op jit(solution)/shard_map/ppermute | solution.py:347
  52.5 12.3 %all-to-all-start.1 = ((f32[64,2,128]{2,1,0:T(2,128)}), f32[64,2,128]{2,1,0:T(2,128)S(1)}, u32[]{:S(2)}, u32[]{:S(2)}) async-start(f32[64,2,128]{2,1,0:T(2,128)} %get-tuple-element.62.refs_3_), calls=%async_computation.1 | async-start | bytes 131072 | tf_op jit(solution)/shard_map/all_to_all | solution.py:89
  64.9 2.4 %collective-permute-start.10 = (bf16[9,128,128]{2,1,0:T(8,128)(2,1)S(1)}, bf16[9,128,128]{2,1,0:T(8,128)(2,1)S(1)}, u32[]{:S(2)}, u32[]{:S(2)}) collective-permute-start(bf16[9,128,128]{2,1,0:T(8,128)(2,1)S(1)} %get-tuple-element.73), channel_id=1, source_target_pairs={{0,2},{1,3},{2,0},{3,1},{4,6},{5,7},{6,4},{7,5},{8,10},{9,11},{10,... | collective-permute-start | bytes 884744 | tf_op jit(solution)/shard_map/ppermute | solution.py:347
  69.0 5.1 %collective-permute-start.7 = (bf16[144,128]{1,0:T(8,128)(2,1)S(1)}, bf16[144,128]{1,0:T(8,128)(2,1)S(1)}, u32[]{:S(2)}, u32[]{:S(2)}) collective-permute-start(bf16[144,128]{1,0:T(8,128)(2,1)S(1)} %get-tuple-element.64), channel_id=1, source_target_pairs={{0,16},{16,32},{32,48},{48,64},{64,80},{80,96},{96,112},{112,128},... | collective-permute-start | bytes 110600 | tf_op jit(solution)/shard_map/ppermute | solution.py:141
  76.1 4.8 %collective-permute-done.8.rest_6_ = bf16[144,128]{1,0:T(8,128)(2,1)S(1)} collective-permute-done((bf16[144,128]{1,0:T(8,128)(2,1)S(1)}, bf16[144,128]{1,0:T(8,128)(2,1)S(1)}, u32[]{:S(2)}, u32[]{:S(2)}) %collective-permute-start.8) | collective-permute-done | bytes 36896 | tf_op jit(solution)/shard_map/ppermute | solution.py:142
  80.9 4.6 %conv_second_far.1 = (bf16[1088,128]{1,0:T(8,128)(2,1)S(1)}, bf16[1088,128]{1,0:T(8,128)(2,1)S(1)}, bf16[6,320,384]{2,1,0:T(8,128)(2,1)S(1)}, bf16[3,80,384]{2,1,0:T(8,128)(2,1)S(1)}, bf16[3456,256]{1,0:T(8,128)(2,1)S(1)}) custom-call(s32[5]{0:T(128)S(1)} %stack.39.flag_ref, bf16[4,8,32,128]{3,2,1,0:T(8,128)(2,1)S(1)} %get-tuple-element.60.x_ref, ...), custom_call_target="tpu_custom_call" | custom-call | flops 1925185536 | bytes 8450068 | tf_op jit(solution)/shard_map/conv_second_far/pallas_call | solution.py:39
  85.6 3.9 %collective-permute-start.13 = (bf16[1088,128]{1,0:T(8,128)(2,1)S(1)}, bf16[1088,128]{1,0:T(8,128)(2,1)S(1)}, u32[]{:S(2)}, u32[]{:S(2)}) collective-permute-start(bf16[1088,128]{1,0:T(8,128)(2,1)S(1)} %get-tuple-element.77), channel_id=1, source_target_pairs={{0,2},{1,3},{2,0},{3,1},{4,6},{5,7},{6,4},{7,5},{8,10},{9,11},{10,... | collective-permute-start | bytes 835592 | tf_op jit(solution)/shard_map/ppermute | solution.py:347
  89.6 2.5 %conv_second_near.1 = (bf16[1088,128]{1,0:T(8,128)(2,1)S(1)}, bf16[1088,128]{1,0:T(8,128)(2,1)S(1)}) custom-call(bf16[6,320,384]{2,1,0:T(8,128)(2,1)S(1)} %get-tuple-element.66.patch_ref, bf16[3,80,384]{2,1,0:T(8,128)(2,1)S(1)} %get-tuple-element.67.side_ref, bf16[3456,256]{1,0:T(8,128)(2,1)S(1)} %get-tuple-element.68.w_ref, ...), custom_call_target="tpu_custom_call" | custom-call | flops 1925185536 | bytes 4870144 | tf_op jit(solution)/shard_map/conv_second_near/pallas_call | solution.py:39
  92.2 2.4 %collective-permute-done.12.a_ref = bf16[1088,128]{1,0:T(8,128)(2,1)S(1)} collective-permute-done((bf16[1088,128]{1,0:T(8,128)(2,1)S(1)}, bf16[1088,128]{1,0:T(8,128)(2,1)S(1)}, u32[]{:S(2)}, u32[]{:S(2)}) %collective-permute-start.12) | collective-permute-done | bytes 278560 | tf_op jit(solution)/shard_map/ppermute | solution.py:347
  94.5 4.9 %collective-permute-done.13.b_ref = bf16[1088,128]{1,0:T(8,128)(2,1)S(1)} collective-permute-done((bf16[1088,128]{1,0:T(8,128)(2,1)S(1)}, bf16[1088,128]{1,0:T(8,128)(2,1)S(1)}, u32[]{:S(2)}, u32[]{:S(2)}) %collective-permute-start.13) | collective-permute-done | bytes 278560 | tf_op jit(solution)/shard_map/ppermute | solution.py:347
  100.3 3.0 %collective-permute-start.21 = (bf16[4,272,128]{2,1,0:T(8,128)(2,1)S(1)}, bf16[4,272,128]{2,1,0:T(8,128)(2,1)S(1)}, u32[]{:S(2)}, u32[]{:S(2)}) collective-permute-start(bf16[4,272,128]{2,1,0:T(8,128)(2,1)S(1)} %get-tuple-element.81.refs_0_), channel_id=1, source_target_pairs={{0,2},{1,3},{2,0},{3,1},{4,6},{5,7},{6,4},{7,5},{8,10},{9,11},{10,... | collective-permute-start | bytes 835592 | tf_op jit(solution)/shard_map/ppermute | solution.py:347
  103.4 5.3 %collective-permute-start.15 = (bf16[4,40,128]{2,1,0:T(8,128)(2,1)S(1)}, bf16[4,40,128]{2,1,0:T(8,128)(2,1)S(1)}, u32[]{:S(2)}, u32[]{:S(2)}) collective-permute-start(bf16[4,40,128]{2,1,0:T(8,128)(2,1)S(1)} %get-tuple-element.79), channel_id=1, source_target_pairs={{0,16},{16,32},{32,48},{48,64},{64,80},{80,96},{96,112},{112,128},... | collective-permute-start | bytes 122888 | tf_op jit(solution)/shard_map/ppermute | solution.py:141
  110.6 4.9 %collective-permute-done.16.bot_ref = bf16[4,40,128]{2,1,0:T(8,128)(2,1)S(1)} collective-permute-done((bf16[4,40,128]{2,1,0:T(8,128)(2,1)S(1)}, bf16[4,40,128]{2,1,0:T(8,128)(2,1)S(1)}, u32[]{:S(2)}, u32[]{:S(2)}) %collective-permute-start.16) | collective-permute-done | bytes 40992 | tf_op jit(solution)/shard_map/ppermute | solution.py:142
  117.8 2.0 %collective-permute-start.20 = (bf16[4,80,128]{2,1,0:T(8,128)(2,1)S(1)}, bf16[4,80,128]{2,1,0:T(8,128)(2,1)S(1)}, u32[]{:S(2)}, u32[]{:S(2)}) collective-permute-start(bf16[4,80,128]{2,1,0:T(8,128)(2,1)S(1)} %pack.1.refs_0_), channel_id=1, source_target_pairs={{0,3},{1,0},{2,1},{3,2},{4,7},{5,4},{6,5},{7,6},{8,11},{9,8},{10,9... | collective-permute-start | bytes 245768 | tf_op jit(solution)/shard_map/ppermute | solution.py:347
  121.9 4.0 %up_conv.1 = bf16[4,16,64,128]{3,2,1,0:T(8,128)(2,1)} custom-call(bf16[4,80,128]{2,1,0:T(8,128)(2,1)S(1)} %pack.1.refs_0_, bf16[4,80,128]{2,1,0:T(8,128)(2,1)S(1)} %collective-permute-done.18.refs_1_, bf16[4,80,128]{2,1,0:T(8,128)(2,1)S(1)} %collective-permute-done.19.refs_2_, bf16[4,80,128]{2,1,0:T(8,128)(2,1)S(1)} %collective-permute-done.20.refs_3_, ...), custom_call_target="tpu_custom_call" | custom-call | tf_op jit(solution)/shard_map/up_conv/pallas_call | solution.py:447
  (44 shorter events, 18.7 us)
Async XLA Ops:
  4.3 18.0 %collective-permute-start = (bf16[8,32,128]{2,1,0:T(8,128)(2,1)S(1)}, bf16[8,32,128]{2,1,0:T(8,128)(2,1)S(1)}, u32[]{:S(2)}, u32[]{:S(2)}) collective-permute-start(bf16[8,32,128]{2,1,0:T(8,128)(2,1)S(1)} %get-tuple-element.44), channel_id=1, source_target_pairs={{0,16},{16,32},{32,48},{48,64},{64,80},{80,96},{96,112},{112,128},... | collective-permute-start | bytes 196616 | tf_op jit(solution)/shard_map/ppermute | solution.py:141
  9.7 12.7 %collective-permute-start.1 = (bf16[8,32,128]{2,1,0:T(8,128)(2,1)S(1)}, bf16[8,32,128]{2,1,0:T(8,128)(2,1)S(1)}, u32[]{:S(2)}, u32[]{:S(2)}) collective-permute-start(bf16[8,32,128]{2,1,0:T(8,128)(2,1)S(1)} %get-tuple-element.45), channel_id=1, source_target_pairs={{16,0},{32,16},{48,32},{64,48},{80,64},{96,80},{112,96},{128,112},... | collective-permute-start | bytes 196616 | tf_op jit(solution)/shard_map/ppermute | solution.py:142
  11.6 17.9 %all-to-all-start = ((f32[64,2,128]{2,1,0:T(2,128)}), f32[64,2,128]{2,1,0:T(2,128)S(1)}, u32[]{:S(2)}, u32[]{:S(2)}) async-start(f32[64,2,128]{2,1,0:T(2,128)} %get-tuple-element.52), calls=%async_computation | async-start | bytes 131072 | tf_op jit(solution)/shard_map/all_to_all | solution.py:89
  22.4 7.0 %collective-permute-start.2 = (bf16[8,3,16,128]{3,2,1,0:T(8,128)(2,1)S(1)}, bf16[8,3,16,128]{3,2,1,0:T(8,128)(2,1)S(1)}, u32[]{:S(2)}, u32[]{:S(2)}) collective-permute-start(bf16[8,3,16,128]{3,2,1,0:T(8,128)(2,1)S(1)} %get-tuple-element.48), channel_id=1, source_target_pairs={{0,4},{4,8},{8,12},{1,5},{5,9},{9,13},{2,6},{6,10},{10,14},{3,7},{... | collective-permute-start | bytes 294920 | tf_op jit(solution)/shard_map/ppermute | solution.py:148
  25.5 5.4 %collective-permute-start.3 = (bf16[8,3,16,128]{3,2,1,0:T(8,128)(2,1)S(1)}, bf16[8,3,16,128]{3,2,1,0:T(8,128)(2,1)S(1)}, u32[]{:S(2)}, u32[]{:S(2)}) collective-permute-start(bf16[8,3,16,128]{3,2,1,0:T(8,128)(2,1)S(1)} %get-tuple-element.49), channel_id=1, source_target_pairs={{4,0},{8,4},{12,8},{5,1},{9,5},{13,9},{6,2},{10,6},{14,10},{7,3},{... | collective-permute-start | bytes 294920 | tf_op jit(solution)/shard_map/ppermute | solution.py:149
  35.5 8.0 %collective-permute-start.4 = (bf16[1152,128]{1,0:T(8,128)(2,1)S(1)}, bf16[1152,128]{1,0:T(8,128)(2,1)S(1)}, u32[]{:S(2)}, u32[]{:S(2)}) collective-permute-start(bf16[1152,128]{1,0:T(8,128)(2,1)S(1)} %get-tuple-element.57), channel_id=1, source_target_pairs={{0,1},{1,2},{2,3},{3,0},{4,5},{5,6},{6,7},{7,4},{8,9},{9,10},{10,1... | collective-permute-start | bytes 884744 | tf_op jit(solution)/shard_map/ppermute | solution.py:347
  36.8 14.0 %collective-permute-start.5 = (bf16[1152,128]{1,0:T(8,128)(2,1)S(1)}, bf16[1152,128]{1,0:T(8,128)(2,1)S(1)}, u32[]{:S(2)}, u32[]{:S(2)}) collective-permute-start(bf16[1152,128]{1,0:T(8,128)(2,1)S(1)} %get-tuple-element.58), channel_id=1, source_target_pairs={{0,2},{1,3},{2,0},{3,1},{4,6},{5,7},{6,4},{7,5},{8,10},{9,11},{10,... | collective-permute-start | bytes 884744 | tf_op jit(solution)/shard_map/ppermute | solution.py:347
  41.7 9.2 %collective-permute-start.6 = (bf16[1152,128]{1,0:T(8,128)(2,1)S(1)}, bf16[1152,128]{1,0:T(8,128)(2,1)S(1)}, u32[]{:S(2)}, u32[]{:S(2)}) collective-permute-start(bf16[1152,128]{1,0:T(8,128)(2,1)S(1)} %get-tuple-element.59), channel_id=1, source_target_pairs={{0,3},{1,0},{2,1},{3,2},{4,7},{5,4},{6,5},{7,6},{8,11},{9,8},{10,9... | collective-permute-start | bytes 884744 | tf_op jit(solution)/shard_map/ppermute | solution.py:347
  52.5 28.4 %all-to-all-start.1 = ((f32[64,2,128]{2,1,0:T(2,128)}), f32[64,2,128]{2,1,0:T(2,128)S(1)}, u32[]{:S(2)}, u32[]{:S(2)}) async-start(f32[64,2,128]{2,1,0:T(2,128)} %get-tuple-element.62.refs_3_), calls=%async_computation.1 | async-start | bytes 131072 | tf_op jit(solution)/shard_map/all_to_all | solution.py:89
  64.9 24.7 %collective-permute-start.10 = (bf16[9,128,128]{2,1,0:T(8,128)(2,1)S(1)}, bf16[9,128,128]{2,1,0:T(8,128)(2,1)S(1)}, u32[]{:S(2)}, u32[]{:S(2)}) collective-permute-start(bf16[9,128,128]{2,1,0:T(8,128)(2,1)S(1)} %get-tuple-element.73), channel_id=1, source_target_pairs={{0,2},{1,3},{2,0},{3,1},{4,6},{5,7},{6,4},{7,5},{8,10},{9,11},{10,... | collective-permute-start | bytes 884744 | tf_op jit(solution)/shard_map/ppermute | solution.py:347
  67.2 22.3 %collective-permute-start.11 = (bf16[9,128,128]{2,1,0:T(8,128)(2,1)S(1)}, bf16[9,128,128]{2,1,0:T(8,128)(2,1)S(1)}, u32[]{:S(2)}, u32[]{:S(2)}) collective-permute-start(bf16[9,128,128]{2,1,0:T(8,128)(2,1)S(1)} %get-tuple-element.74), channel_id=1, source_target_pairs={{0,3},{1,0},{2,1},{3,2},{4,7},{5,4},{6,5},{7,6},{8,11},{9,8},{10,9... | collective-permute-start | bytes 884744 | tf_op jit(solution)/shard_map/ppermute | solution.py:347
  69.0 20.5 %collective-permute-start.9 = (bf16[9,128,128]{2,1,0:T(8,128)(2,1)S(1)}, bf16[9,128,128]{2,1,0:T(8,128)(2,1)S(1)}, u32[]{:S(2)}, u32[]{:S(2)}) collective-permute-start(bf16[9,128,128]{2,1,0:T(8,128)(2,1)S(1)} %get-tuple-element.72), channel_id=1, source_target_pairs={{0,1},{1,2},{2,3},{3,0},{4,5},{5,6},{6,7},{7,4},{8,9},{9,10},{10,1... | collective-permute-start | bytes 884744 | tf_op jit(solution)/shard_map/ppermute | solution.py:347
  69.0 7.1 %collective-permute-start.7 = (bf16[144,128]{1,0:T(8,128)(2,1)S(1)}, bf16[144,128]{1,0:T(8,128)(2,1)S(1)}, u32[]{:S(2)}, u32[]{:S(2)}) collective-permute-start(bf16[144,128]{1,0:T(8,128)(2,1)S(1)} %get-tuple-element.64), channel_id=1, source_target_pairs={{0,16},{16,32},{32,48},{48,64},{64,80},{80,96},{96,112},{112,128},... | collective-permute-start | bytes 110600 | tf_op jit(solution)/shard_map/ppermute | solution.py:141
  74.2 6.8 %collective-permute-start.8 = (bf16[144,128]{1,0:T(8,128)(2,1)S(1)}, bf16[144,128]{1,0:T(8,128)(2,1)S(1)}, u32[]{:S(2)}, u32[]{:S(2)}) collective-permute-start(bf16[144,128]{1,0:T(8,128)(2,1)S(1)} %get-tuple-element.65), channel_id=1, source_target_pairs={{16,0},{32,16},{48,32},{64,48},{80,64},{96,80},{112,96},{128,112},... | collective-permute-start | bytes 110600 | tf_op jit(solution)/shard_map/ppermute | solution.py:142
  85.5 9.0 %collective-permute-start.12 = (bf16[1088,128]{1,0:T(8,128)(2,1)S(1)}, bf16[1088,128]{1,0:T(8,128)(2,1)S(1)}, u32[]{:S(2)}, u32[]{:S(2)}) collective-permute-start(bf16[1088,128]{1,0:T(8,128)(2,1)S(1)} %get-tuple-element.76), channel_id=1, source_target_pairs={{0,1},{1,2},{2,3},{3,0},{4,5},{5,6},{6,7},{7,4},{8,9},{9,10},{10,1... | collective-permute-start | bytes 835592 | tf_op jit(solution)/shard_map/ppermute | solution.py:347
  85.6 13.8 %collective-permute-start.13 = (bf16[1088,128]{1,0:T(8,128)(2,1)S(1)}, bf16[1088,128]{1,0:T(8,128)(2,1)S(1)}, u32[]{:S(2)}, u32[]{:S(2)}) collective-permute-start(bf16[1088,128]{1,0:T(8,128)(2,1)S(1)} %get-tuple-element.77), channel_id=1, source_target_pairs={{0,2},{1,3},{2,0},{3,1},{4,6},{5,7},{6,4},{7,5},{8,10},{9,11},{10,... | collective-permute-start | bytes 835592 | tf_op jit(solution)/shard_map/ppermute | solution.py:347
  92.1 7.4 %collective-permute-start.14 = (bf16[1088,128]{1,0:T(8,128)(2,1)S(1)}, bf16[1088,128]{1,0:T(8,128)(2,1)S(1)}, u32[]{:S(2)}, u32[]{:S(2)}) collective-permute-start(bf16[1088,128]{1,0:T(8,128)(2,1)S(1)} %get-tuple-element.78), channel_id=1, source_target_pairs={{0,3},{1,0},{2,1},{3,2},{4,7},{5,4},{6,5},{7,6},{8,11},{9,8},{10,9... | collective-permute-start | bytes 835592 | tf_op jit(solution)/shard_map/ppermute | solution.py:347
  100.3 15.3 %collective-permute-start.17 = (bf16[4,272,128]{2,1,0:T(8,128)(2,1)S(1)}, bf16[4,272,128]{2,1,0:T(8,128)(2,1)S(1)}, u32[]{:S(2)}, u32[]{:S(2)}) collective-permute-start(bf16[4,272,128]{2,1,0:T(8,128)(2,1)S(1)} %get-tuple-element.81.refs_0_), channel_id=1, source_target_pairs={{0,1},{1,2},{2,3},{3,0},{4,5},{5,6},{6,7},{7,4},{8,9},{9,10},{10,1... | collective-permute-start | bytes 835592 | tf_op jit(solution)/shard_map/ppermute | solution.py:347
  100.3 19.4 %collective-permute-start.21 = (bf16[4,272,128]{2,1,0:T(8,128)(2,1)S(1)}, bf16[4,272,128]{2,1,0:T(8,128)(2,1)S(1)}, u32[]{:S(2)}, u32[]{:S(2)}) collective-permute-start(bf16[4,272,128]{2,1,0:T(8,128)(2,1)S(1)} %get-tuple-element.81.refs_0_), channel_id=1, source_target_pairs={{0,2},{1,3},{2,0},{3,1},{4,6},{5,7},{6,4},{7,5},{8,10},{9,11},{10,... | collective-permute-start | bytes 835592 | tf_op jit(solution)/shard_map/ppermute | solution.py:347
  103.4 16.4 %collective-permute-start.22 = (bf16[4,272,128]{2,1,0:T(8,128)(2,1)S(1)}, bf16[4,272,128]{2,1,0:T(8,128)(2,1)S(1)}, u32[]{:S(2)}, u32[]{:S(2)}) collective-permute-start(bf16[4,272,128]{2,1,0:T(8,128)(2,1)S(1)} %get-tuple-element.81.refs_0_), channel_id=1, source_target_pairs={{0,3},{1,0},{2,1},{3,2},{4,7},{5,4},{6,5},{7,6},{8,11},{9,8},{10,9... | collective-permute-start | bytes 835592 | tf_op jit(solution)/shard_map/ppermute | solution.py:347
  103.4 7.3 %collective-permute-start.15 = (bf16[4,40,128]{2,1,0:T(8,128)(2,1)S(1)}, bf16[4,40,128]{2,1,0:T(8,128)(2,1)S(1)}, u32[]{:S(2)}, u32[]{:S(2)}) collective-permute-start(bf16[4,40,128]{2,1,0:T(8,128)(2,1)S(1)} %get-tuple-element.79), channel_id=1, source_target_pairs={{0,16},{16,32},{32,48},{48,64},{64,80},{80,96},{96,112},{112,128},... | collective-permute-start | bytes 122888 | tf_op jit(solution)/shard_map/ppermute | solution.py:141
  108.7 6.8 %collective-permute-start.16 = (bf16[4,40,128]{2,1,0:T(8,128)(2,1)S(1)}, bf16[4,40,128]{2,1,0:T(8,128)(2,1)S(1)}, u32[]{:S(2)}, u32[]{:S(2)}) collective-permute-start(bf16[4,40,128]{2,1,0:T(8,128)(2,1)S(1)} %get-tuple-element.80), channel_id=1, source_target_pairs={{16,0},{32,16},{48,32},{64,48},{80,64},{96,80},{112,96},{128,112},... | collective-permute-start | bytes 122888 | tf_op jit(solution)/shard_map/ppermute | solution.py:142
  115.5 5.5 %collective-permute-start.18 = (bf16[4,80,128]{2,1,0:T(8,128)(2,1)S(1)}, bf16[4,80,128]{2,1,0:T(8,128)(2,1)S(1)}, u32[]{:S(2)}, u32[]{:S(2)}) collective-permute-start(bf16[4,80,128]{2,1,0:T(8,128)(2,1)S(1)} %pack.1.refs_0_), channel_id=1, source_target_pairs={{0,1},{1,2},{2,3},{3,0},{4,5},{5,6},{6,7},{7,4},{8,9},{9,10},{10,1... | collective-permute-start | bytes 245768 | tf_op jit(solution)/shard_map/ppermute | solution.py:347
  117.1 4.8 %collective-permute-start.19 = (bf16[4,80,128]{2,1,0:T(8,128)(2,1)S(1)}, bf16[4,80,128]{2,1,0:T(8,128)(2,1)S(1)}, u32[]{:S(2)}, u32[]{:S(2)}) collective-permute-start(bf16[4,80,128]{2,1,0:T(8,128)(2,1)S(1)} %pack.1.refs_0_), channel_id=1, source_target_pairs={{0,2},{1,3},{2,0},{3,1},{4,6},{5,7},{6,4},{7,5},{8,10},{9,11},{10,... | collective-permute-start | bytes 245768 | tf_op jit(solution)/shard_map/ppermute | solution.py:347
  (2 other events, 14.0 us)

commit v10 on v8

--- a/solution.py
+++ b/solution.py
@@ -312,7 +312,7 @@
     out3, own = call(near_body, [piece] * 2, flops=flops, limit=16, name=name + "_near")(
         patch, side, near, *[Left(a) for a in after]
     )
-    (far,) = call(add_body, [sds((n, CH), F32)], name=name + "_add")(got1, got2)
+    (far,) = call(add_body, [sds((n, CH), F32)], name=name + "_add")(got2, got1)
     return own, far, to_peer(out3, 3)
 
 

time: 125 us -> 124 us (level)
    all_to_all x2, starting transfers between devices: 23.1 us -> 21.4 us  [spread(): return lax.all_to_all(slots, HA + ('wa',), 0, 0, tiled=True)]
  transfers between devices with their start and end apart: 25 -> 25, of which waited for: 9 -> 11; matrix products, arithmetic and copies ran while one was open for 0% -> 0% of each run, Pallas kernels for 9% -> 9%
where the time goes in v10:
time: 124 us
  starting transfers between devices  68.3 us (55%)
  waiting for transfers between devices  30 us (24%)
  Pallas kernels  25.1 us (20%)
    all_to_all x2, starting transfers between devices, spread(): return lax.all_to_all(slots, HA + ('wa',), 0, 0, tiled=True)  21.4 us
    pallas_call x13, Pallas kernels, run(): pl.pallas_call(body, out_shape=list(outs), in_specs=specs, out_specs=[VME...  21.1 us
    ppermute x15, starting transfers between devices, to_peer(): return lax.ppermute(piece, 'col', [(i, (i + k) % n) for i in range(n)])  20.8 us
    ppermute x15, waiting for transfers between devices, to_peer(): return lax.ppermute(piece, 'col', [(i, (i + k) % n) for i in range(n)])  16.2 us
    ppermute x3, starting transfers between devices, swap_rows(): above = lax.ppermute(bot, HA, [(i, i + 1) for i in range(n - 1)])  16.1 us
    ppermute x3, waiting for transfers between devices, swap_rows(): below = lax.ppermute(top, HA, [(i + 1, i) for i in range(n - 1)])  9.73 us
    ppermute x3, starting transfers between devices, swap_rows(): below = lax.ppermute(top, HA, [(i + 1, i) for i in range(n - 1)])  5.76 us
    pallas_call x1, Pallas kernels, up_conv(): pl.pallas_call(up_body, out_shape=sds(out), grid=(frames,), in_specs=[by_...  3.97 us
  transfers between devices with their start and end apart: 25, of which 11 were waited for; matrix products, arithmetic and copies ran while one was open for 0% of the time, Pallas kernels for 9%

profile of v10, /device:TPU:97, one launch (start us, length us, event | category | flops | bytes accessed | tf_op | source)
XLA Modules:
  0.0 123.7 jit_solution(13356975449416991127)
XLA Ops:
  0.1 3.2 %first.1 = (bf16[4,8,32,128]{3,2,1,0:T(8,128)(2,1)S(1)}, bf16[2,8,32,128]{3,2,1,0:T(8,128)(2,1)S(1)}, bf16[2,8,32,128]{3,2,1,0:T(8,128)(2,1)S(1)}, f32[64,2,128]...) custom-call(s32[5]{0:T(128)S(1)} %stack.39.flag_ref, ...), custom_call_target="tpu_custom_call" | custom-call | bytes 3801108 | tf_op jit(solution)/shard_map/first/pallas_call | solution.py:39
  3.2 5.3 %collective-permute-start = (bf16[8,32,128]{2,1,0:T(8,128)(2,1)S(1)}, bf16[8,32,128]{2,1,0:T(8,128)(2,1)S(1)}, u32[]{:S(2)}, u32[]{:S(2)}) collective-permute-start(bf16[8,32,128]{2,1,0:T(8,128)(2,1)S(1)} %get-tuple-element.44), channel_id=1, source_target_pairs={{0,16},{16,32},{32,48},{48,64},{64,80},{80,96},{96,112},{112,128},... | collective-permute-start | bytes 196616 | tf_op jit(solution)/shard_map/ppermute | solution.py:139
  10.5 10.8 %all-to-all-start = ((f32[64,2,128]{2,1,0:T(2,128)}), f32[64,2,128]{2,1,0:T(2,128)S(1)}, u32[]{:S(2)}, u32[]{:S(2)}) async-start(f32[64,2,128]{2,1,0:T(2,128)} %get-tuple-element.52), calls=%async_computation | async-start | bytes 131072 | tf_op jit(solution)/shard_map/all_to_all | solution.py:89
  21.4 3.1 %collective-permute-start.2 = (bf16[8,3,16,128]{3,2,1,0:T(8,128)(2,1)S(1)}, bf16[8,3,16,128]{3,2,1,0:T(8,128)(2,1)S(1)}, u32[]{:S(2)}, u32[]{:S(2)}) collective-permute-start(bf16[8,3,16,128]{3,2,1,0:T(8,128)(2,1)S(1)} %get-tuple-element.48), channel_id=1, source_target_pairs={{0,4},{4,8},{8,12},{1,5},{5,9},{9,13},{2,6},{6,10},{10,14},{3,7},{... | collective-permute-start | bytes 294920 | tf_op jit(solution)/shard_map/ppermute | solution.py:146
  25.8 2.6 %all-to-all-done.st_ref = f32[64,2,128]{2,1,0:T(2,128)S(1)} async-done(((f32[64,2,128]{2,1,0:T(2,128)}), f32[64,2,128]{2,1,0:T(2,128)S(1)}, u32[]{:S(2)}, u32[]{:S(2)}) %all-to-all-start) | async-done | bytes 65568 | tf_op jit(solution)/shard_map/all_to_all | solution.py:89
  29.8 4.5 %conv_first_far.1 = (bf16[1152,128]{1,0:T(8,128)(2,1)S(1)}, bf16[1152,128]{1,0:T(8,128)(2,1)S(1)}, bf16[6,320,384]{2,1,0:T(8,128)(2,1)S(1)}, bf16[3,160,384]{2,1,0:T(8,128)(2,1)S(1)}, bf16[3456,256]{1,0:T(8,128)(2,1)S(1)}) custom-call(s32[5]{0:T(128)S(1)} %stack.39.flag_ref, bf16[4,8,32,128]{3,2,1,0:T(8,128)(2,1)S(1)} %get-tuple-element.50.x_ref, ...), custom_call_target="tpu_custom_call" | custom-call | flops 2038431744 | bytes 8527892 | tf_op jit(solution)/shard_map/conv_first_far/pallas_call | solution.py:39
  34.4 2.8 %collective-permute-start.4 = (bf16[1152,128]{1,0:T(8,128)(2,1)S(1)}, bf16[1152,128]{1,0:T(8,128)(2,1)S(1)}, u32[]{:S(2)}, u32[]{:S(2)}) collective-permute-start(bf16[1152,128]{1,0:T(8,128)(2,1)S(1)} %get-tuple-element.57), channel_id=1, source_target_pairs={{0,2},{1,3},{2,0},{3,1},{4,6},{5,7},{6,4},{7,5},{8,10},{9,11},{10,... | collective-permute-start | bytes 884744 | tf_op jit(solution)/shard_map/ppermute | solution.py:342
  37.5 2.5 %conv_first_near.1 = (bf16[1152,128]{1,0:T(8,128)(2,1)S(1)}, bf16[1152,128]{1,0:T(8,128)(2,1)S(1)}) custom-call(bf16[6,320,384]{2,1,0:T(8,128)(2,1)S(1)} %get-tuple-element.53.patch_ref, bf16[3,160,384]{2,1,0:T(8,128)(2,1)S(1)} %get-tuple-element.54.side_ref, bf16[3456,256]{1,0:T(8,128)(2,1)S(1)} %get-tuple-element.55.w_ref), custom_call_target="tpu_custom_call" | custom-call | flops 2038431744 | bytes 4202496 | tf_op jit(solution)/shard_map/conv_first_near/pallas_call | solution.py:39
  40.0 2.4 %collective-permute-start.6 = (bf16[1152,128]{1,0:T(8,128)(2,1)S(1)}, bf16[1152,128]{1,0:T(8,128)(2,1)S(1)}, u32[]{:S(2)}, u32[]{:S(2)}) collective-permute-start(bf16[1152,128]{1,0:T(8,128)(2,1)S(1)} %get-tuple-element.59), channel_id=1, source_target_pairs={{0,3},{1,0},{2,1},{3,2},{4,7},{5,4},{6,5},{7,6},{8,11},{9,8},{10,9... | collective-permute-start | bytes 884744 | tf_op jit(solution)/shard_map/ppermute | solution.py:342
  42.7 8.1 %collective-permute-done.5.b_ref = bf16[1152,128]{1,0:T(8,128)(2,1)S(1)} collective-permute-done((bf16[1152,128]{1,0:T(8,128)(2,1)S(1)}, bf16[1152,128]{1,0:T(8,128)(2,1)S(1)}, u32[]{:S(2)}, u32[]{:S(2)}) %collective-permute-start.5) | collective-permute-done | bytes 294944 | tf_op jit(solution)/shard_map/ppermute | solution.py:342
  52.5 10.6 %all-to-all-start.1 = ((f32[64,2,128]{2,1,0:T(2,128)}), f32[64,2,128]{2,1,0:T(2,128)S(1)}, u32[]{:S(2)}, u32[]{:S(2)}) async-start(f32[64,2,128]{2,1,0:T(2,128)} %get-tuple-element.62.refs_3_), calls=%async_computation.1 | async-start | bytes 131072 | tf_op jit(solution)/shard_map/all_to_all | solution.py:89
  63.1 2.0 %collective-permute-start.10 = (bf16[9,128,128]{2,1,0:T(8,128)(2,1)S(1)}, bf16[9,128,128]{2,1,0:T(8,128)(2,1)S(1)}, u32[]{:S(2)}, u32[]{:S(2)}) collective-permute-start(bf16[9,128,128]{2,1,0:T(8,128)(2,1)S(1)} %get-tuple-element.73), channel_id=1, source_target_pairs={{0,2},{1,3},{2,0},{3,1},{4,6},{5,7},{6,4},{7,5},{8,10},{9,11},{10,... | collective-permute-start | bytes 884744 | tf_op jit(solution)/shard_map/ppermute | solution.py:342
  66.8 5.1 %collective-permute-start.7 = (bf16[144,128]{1,0:T(8,128)(2,1)S(1)}, bf16[144,128]{1,0:T(8,128)(2,1)S(1)}, u32[]{:S(2)}, u32[]{:S(2)}) collective-permute-start(bf16[144,128]{1,0:T(8,128)(2,1)S(1)} %get-tuple-element.64), channel_id=1, source_target_pairs={{0,16},{16,32},{32,48},{48,64},{64,80},{80,96},{96,112},{112,128},... | collective-permute-start | bytes 110600 | tf_op jit(solution)/shard_map/ppermute | solution.py:139
  73.9 4.8 %collective-permute-done.8.rest_6_ = bf16[144,128]{1,0:T(8,128)(2,1)S(1)} collective-permute-done((bf16[144,128]{1,0:T(8,128)(2,1)S(1)}, bf16[144,128]{1,0:T(8,128)(2,1)S(1)}, u32[]{:S(2)}, u32[]{:S(2)}) %collective-permute-start.8) | collective-permute-done | bytes 36896 | tf_op jit(solution)/shard_map/ppermute | solution.py:140
  78.8 4.6 %conv_second_far.1 = (bf16[1088,128]{1,0:T(8,128)(2,1)S(1)}, bf16[1088,128]{1,0:T(8,128)(2,1)S(1)}, bf16[6,320,384]{2,1,0:T(8,128)(2,1)S(1)}, bf16[3,80,384]{2,1,0:T(8,128)(2,1)S(1)}, bf16[3456,256]{1,0:T(8,128)(2,1)S(1)}) custom-call(s32[5]{0:T(128)S(1)} %stack.39.flag_ref, bf16[4,8,32,128]{3,2,1,0:T(8,128)(2,1)S(1)} %get-tuple-element.60.x_ref, ...), custom_call_target="tpu_custom_call" | custom-call | flops 1925185536 | bytes 8450068 | tf_op jit(solution)/shard_map/conv_second_far/pallas_call | solution.py:39
  84.8 2.2 %collective-permute-start.13 = (bf16[1088,128]{1,0:T(8,128)(2,1)S(1)}, bf16[1088,128]{1,0:T(8,128)(2,1)S(1)}, u32[]{:S(2)}, u32[]{:S(2)}) collective-permute-start(bf16[1088,128]{1,0:T(8,128)(2,1)S(1)} %get-tuple-element.77), channel_id=1, source_target_pairs={{0,1},{1,2},{2,3},{3,0},{4,5},{5,6},{6,7},{7,4},{8,9},{9,10},{10,1... | collective-permute-start | bytes 835592 | tf_op jit(solution)/shard_map/ppermute | solution.py:342
  87.0 2.5 %conv_second_near.1 = (bf16[1088,128]{1,0:T(8,128)(2,1)S(1)}, bf16[1088,128]{1,0:T(8,128)(2,1)S(1)}) custom-call(bf16[6,320,384]{2,1,0:T(8,128)(2,1)S(1)} %get-tuple-element.66.patch_ref, bf16[3,80,384]{2,1,0:T(8,128)(2,1)S(1)} %get-tuple-element.67.side_ref, bf16[3456,256]{1,0:T(8,128)(2,1)S(1)} %get-tuple-element.68.w_ref, ...), custom_call_target="tpu_custom_call" | custom-call | flops 1925185536 | bytes 4870144 | tf_op jit(solution)/shard_map/conv_second_near/pallas_call | solution.py:39
  90.1 3.0 %collective-permute-done.12.a_ref = bf16[1088,128]{1,0:T(8,128)(2,1)S(1)} collective-permute-done((bf16[1088,128]{1,0:T(8,128)(2,1)S(1)}, bf16[1088,128]{1,0:T(8,128)(2,1)S(1)}, u32[]{:S(2)}, u32[]{:S(2)}) %collective-permute-start.12) | collective-permute-done | bytes 278560 | tf_op jit(solution)/shard_map/ppermute | solution.py:342
  93.1 3.0 %collective-permute-done.13.b_ref = bf16[1088,128]{1,0:T(8,128)(2,1)S(1)} collective-permute-done((bf16[1088,128]{1,0:T(8,128)(2,1)S(1)}, bf16[1088,128]{1,0:T(8,128)(2,1)S(1)}, u32[]{:S(2)}, u32[]{:S(2)}) %collective-permute-start.13) | collective-permute-done | bytes 278560 | tf_op jit(solution)/shard_map/ppermute | solution.py:342
  98.5 2.8 %collective-permute-start.21 = (bf16[4,272,128]{2,1,0:T(8,128)(2,1)S(1)}, bf16[4,272,128]{2,1,0:T(8,128)(2,1)S(1)}, u32[]{:S(2)}, u32[]{:S(2)}) collective-permute-start(bf16[4,272,128]{2,1,0:T(8,128)(2,1)S(1)} %get-tuple-element.81.refs_0_), channel_id=1, source_target_pairs={{0,2},{1,3},{2,0},{3,1},{4,6},{5,7},{6,4},{7,5},{8,10},{9,11},{10,... | collective-permute-start | bytes 835592 | tf_op jit(solution)/shard_map/ppermute | solution.py:342
  101.3 5.6 %collective-permute-start.15 = (bf16[4,40,128]{2,1,0:T(8,128)(2,1)S(1)}, bf16[4,40,128]{2,1,0:T(8,128)(2,1)S(1)}, u32[]{:S(2)}, u32[]{:S(2)}) collective-permute-start(bf16[4,40,128]{2,1,0:T(8,128)(2,1)S(1)} %get-tuple-element.79), channel_id=1, source_target_pairs={{0,16},{16,32},{32,48},{48,64},{64,80},{80,96},{96,112},{112,128},... | collective-permute-start | bytes 122888 | tf_op jit(solution)/shard_map/ppermute | solution.py:139
  106.9 1.9 %collective-permute-start.16 = (bf16[4,40,128]{2,1,0:T(8,128)(2,1)S(1)}, bf16[4,40,128]{2,1,0:T(8,128)(2,1)S(1)}, u32[]{:S(2)}, u32[]{:S(2)}) collective-permute-start(bf16[4,40,128]{2,1,0:T(8,128)(2,1)S(1)} %get-tuple-element.80), channel_id=1, source_target_pairs={{16,0},{32,16},{48,32},{64,48},{80,64},{96,80},{112,96},{128,112},... | collective-permute-start | bytes 122888 | tf_op jit(solution)/shard_map/ppermute | solution.py:140
  108.8 4.9 %collective-permute-done.16.bot_ref = bf16[4,40,128]{2,1,0:T(8,128)(2,1)S(1)} collective-permute-done((bf16[4,40,128]{2,1,0:T(8,128)(2,1)S(1)}, bf16[4,40,128]{2,1,0:T(8,128)(2,1)S(1)}, u32[]{:S(2)}, u32[]{:S(2)}) %collective-permute-start.16) | collective-permute-done | bytes 40992 | tf_op jit(solution)/shard_map/ppermute | solution.py:140
  119.8 4.0 %up_conv.1 = bf16[4,16,64,128]{3,2,1,0:T(8,128)(2,1)} custom-call(bf16[4,80,128]{2,1,0:T(8,128)(2,1)S(1)} %pack.1.refs_0_, bf16[4,80,128]{2,1,0:T(8,128)(2,1)S(1)} %collective-permute-done.18.refs_1_, bf16[4,80,128]{2,1,0:T(8,128)(2,1)S(1)} %collective-permute-done.19.refs_2_, bf16[4,80,128]{2,1,0:T(8,128)(2,1)S(1)} %collective-permute-done.20.refs_3_, ...), custom_call_target="tpu_custom_call" | custom-call | tf_op jit(solution)/shard_map/up_conv/pallas_call | solution.py:442
  (44 shorter events, 21.2 us)
Async XLA Ops:
  3.2 18.0 %collective-permute-start = (bf16[8,32,128]{2,1,0:T(8,128)(2,1)S(1)}, bf16[8,32,128]{2,1,0:T(8,128)(2,1)S(1)}, u32[]{:S(2)}, u32[]{:S(2)}) collective-permute-start(bf16[8,32,128]{2,1,0:T(8,128)(2,1)S(1)} %get-tuple-element.44), channel_id=1, source_target_pairs={{0,16},{16,32},{32,48},{48,64},{64,80},{80,96},{96,112},{112,128},... | collective-permute-start | bytes 196616 | tf_op jit(solution)/shard_map/ppermute | solution.py:139
  8.6 12.7 %collective-permute-start.1 = (bf16[8,32,128]{2,1,0:T(8,128)(2,1)S(1)}, bf16[8,32,128]{2,1,0:T(8,128)(2,1)S(1)}, u32[]{:S(2)}, u32[]{:S(2)}) collective-permute-start(bf16[8,32,128]{2,1,0:T(8,128)(2,1)S(1)} %get-tuple-element.45), channel_id=1, source_target_pairs={{16,0},{32,16},{48,32},{64,48},{80,64},{96,80},{112,96},{128,112},... | collective-permute-start | bytes 196616 | tf_op jit(solution)/shard_map/ppermute | solution.py:140
  10.5 17.9 %all-to-all-start = ((f32[64,2,128]{2,1,0:T(2,128)}), f32[64,2,128]{2,1,0:T(2,128)S(1)}, u32[]{:S(2)}, u32[]{:S(2)}) async-start(f32[64,2,128]{2,1,0:T(2,128)} %get-tuple-element.52), calls=%async_computation | async-start | bytes 131072 | tf_op jit(solution)/shard_map/all_to_all | solution.py:89
  21.4 7.0 %collective-permute-start.2 = (bf16[8,3,16,128]{3,2,1,0:T(8,128)(2,1)S(1)}, bf16[8,3,16,128]{3,2,1,0:T(8,128)(2,1)S(1)}, u32[]{:S(2)}, u32[]{:S(2)}) collective-permute-start(bf16[8,3,16,128]{3,2,1,0:T(8,128)(2,1)S(1)} %get-tuple-element.48), channel_id=1, source_target_pairs={{0,4},{4,8},{8,12},{1,5},{5,9},{9,13},{2,6},{6,10},{10,14},{3,7},{... | collective-permute-start | bytes 294920 | tf_op jit(solution)/shard_map/ppermute | solution.py:146
  24.5 5.4 %collective-permute-start.3 = (bf16[8,3,16,128]{3,2,1,0:T(8,128)(2,1)S(1)}, bf16[8,3,16,128]{3,2,1,0:T(8,128)(2,1)S(1)}, u32[]{:S(2)}, u32[]{:S(2)}) collective-permute-start(bf16[8,3,16,128]{3,2,1,0:T(8,128)(2,1)S(1)} %get-tuple-element.49), channel_id=1, source_target_pairs={{4,0},{8,4},{12,8},{5,1},{9,5},{13,9},{6,2},{10,6},{14,10},{7,3},{... | collective-permute-start | bytes 294920 | tf_op jit(solution)/shard_map/ppermute | solution.py:147
  34.4 8.3 %collective-permute-start.4 = (bf16[1152,128]{1,0:T(8,128)(2,1)S(1)}, bf16[1152,128]{1,0:T(8,128)(2,1)S(1)}, u32[]{:S(2)}, u32[]{:S(2)}) collective-permute-start(bf16[1152,128]{1,0:T(8,128)(2,1)S(1)} %get-tuple-element.57), channel_id=1, source_target_pairs={{0,2},{1,3},{2,0},{3,1},{4,6},{5,7},{6,4},{7,5},{8,10},{9,11},{10,... | collective-permute-start | bytes 884744 | tf_op jit(solution)/shard_map/ppermute | solution.py:342
  37.2 13.6 %collective-permute-start.5 = (bf16[1152,128]{1,0:T(8,128)(2,1)S(1)}, bf16[1152,128]{1,0:T(8,128)(2,1)S(1)}, u32[]{:S(2)}, u32[]{:S(2)}) collective-permute-start(bf16[1152,128]{1,0:T(8,128)(2,1)S(1)} %get-tuple-element.58), channel_id=1, source_target_pairs={{0,1},{1,2},{2,3},{3,0},{4,5},{5,6},{6,7},{7,4},{8,9},{9,10},{10,1... | collective-permute-start | bytes 884744 | tf_op jit(solution)/shard_map/ppermute | solution.py:342
  40.0 10.8 %collective-permute-start.6 = (bf16[1152,128]{1,0:T(8,128)(2,1)S(1)}, bf16[1152,128]{1,0:T(8,128)(2,1)S(1)}, u32[]{:S(2)}, u32[]{:S(2)}) collective-permute-start(bf16[1152,128]{1,0:T(8,128)(2,1)S(1)} %get-tuple-element.59), channel_id=1, source_target_pairs={{0,3},{1,0},{2,1},{3,2},{4,7},{5,4},{6,5},{7,6},{8,11},{9,8},{10,9... | collective-permute-start | bytes 884744 | tf_op jit(solution)/shard_map/ppermute | solution.py:342
  52.5 26.3 %all-to-all-start.1 = ((f32[64,2,128]{2,1,0:T(2,128)}), f32[64,2,128]{2,1,0:T(2,128)S(1)}, u32[]{:S(2)}, u32[]{:S(2)}) async-start(f32[64,2,128]{2,1,0:T(2,128)} %get-tuple-element.62.refs_3_), calls=%async_computation.1 | async-start | bytes 131072 | tf_op jit(solution)/shard_map/all_to_all | solution.py:89
  63.1 23.9 %collective-permute-start.10 = (bf16[9,128,128]{2,1,0:T(8,128)(2,1)S(1)}, bf16[9,128,128]{2,1,0:T(8,128)(2,1)S(1)}, u32[]{:S(2)}, u32[]{:S(2)}) collective-permute-start(bf16[9,128,128]{2,1,0:T(8,128)(2,1)S(1)} %get-tuple-element.73), channel_id=1, source_target_pairs={{0,2},{1,3},{2,0},{3,1},{4,6},{5,7},{6,4},{7,5},{8,10},{9,11},{10,... | collective-permute-start | bytes 884744 | tf_op jit(solution)/shard_map/ppermute | solution.py:342
  65.0 21.9 %collective-permute-start.11 = (bf16[9,128,128]{2,1,0:T(8,128)(2,1)S(1)}, bf16[9,128,128]{2,1,0:T(8,128)(2,1)S(1)}, u32[]{:S(2)}, u32[]{:S(2)}) collective-permute-start(bf16[9,128,128]{2,1,0:T(8,128)(2,1)S(1)} %get-tuple-element.74), channel_id=1, source_target_pairs={{0,3},{1,0},{2,1},{3,2},{4,7},{5,4},{6,5},{7,6},{8,11},{9,8},{10,9... | collective-permute-start | bytes 884744 | tf_op jit(solution)/shard_map/ppermute | solution.py:342
  66.8 20.1 %collective-permute-start.9 = (bf16[9,128,128]{2,1,0:T(8,128)(2,1)S(1)}, bf16[9,128,128]{2,1,0:T(8,128)(2,1)S(1)}, u32[]{:S(2)}, u32[]{:S(2)}) collective-permute-start(bf16[9,128,128]{2,1,0:T(8,128)(2,1)S(1)} %get-tuple-element.72), channel_id=1, source_target_pairs={{0,1},{1,2},{2,3},{3,0},{4,5},{5,6},{6,7},{7,4},{8,9},{9,10},{10,1... | collective-permute-start | bytes 884744 | tf_op jit(solution)/shard_map/ppermute | solution.py:342
  66.8 7.1 %collective-permute-start.7 = (bf16[144,128]{1,0:T(8,128)(2,1)S(1)}, bf16[144,128]{1,0:T(8,128)(2,1)S(1)}, u32[]{:S(2)}, u32[]{:S(2)}) collective-permute-start(bf16[144,128]{1,0:T(8,128)(2,1)S(1)} %get-tuple-element.64), channel_id=1, source_target_pairs={{0,16},{16,32},{32,48},{48,64},{64,80},{80,96},{96,112},{112,128},... | collective-permute-start | bytes 110600 | tf_op jit(solution)/shard_map/ppermute | solution.py:139
  72.0 6.8 %collective-permute-start.8 = (bf16[144,128]{1,0:T(8,128)(2,1)S(1)}, bf16[144,128]{1,0:T(8,128)(2,1)S(1)}, u32[]{:S(2)}, u32[]{:S(2)}) collective-permute-start(bf16[144,128]{1,0:T(8,128)(2,1)S(1)} %get-tuple-element.65), channel_id=1, source_target_pairs={{16,0},{32,16},{48,32},{64,48},{80,64},{96,80},{112,96},{128,112},... | collective-permute-start | bytes 110600 | tf_op jit(solution)/shard_map/ppermute | solution.py:140
  83.3 9.8 %collective-permute-start.12 = (bf16[1088,128]{1,0:T(8,128)(2,1)S(1)}, bf16[1088,128]{1,0:T(8,128)(2,1)S(1)}, u32[]{:S(2)}, u32[]{:S(2)}) collective-permute-start(bf16[1088,128]{1,0:T(8,128)(2,1)S(1)} %get-tuple-element.76), channel_id=1, source_target_pairs={{0,2},{1,3},{2,0},{3,1},{4,6},{5,7},{6,4},{7,5},{8,10},{9,11},{10,... | collective-permute-start | bytes 835592 | tf_op jit(solution)/shard_map/ppermute | solution.py:342
  84.8 11.3 %collective-permute-start.13 = (bf16[1088,128]{1,0:T(8,128)(2,1)S(1)}, bf16[1088,128]{1,0:T(8,128)(2,1)S(1)}, u32[]{:S(2)}, u32[]{:S(2)}) collective-permute-start(bf16[1088,128]{1,0:T(8,128)(2,1)S(1)} %get-tuple-element.77), channel_id=1, source_target_pairs={{0,1},{1,2},{2,3},{3,0},{4,5},{5,6},{6,7},{7,4},{8,9},{9,10},{10,1... | collective-permute-start | bytes 835592 | tf_op jit(solution)/shard_map/ppermute | solution.py:342
  89.5 7.4 %collective-permute-start.14 = (bf16[1088,128]{1,0:T(8,128)(2,1)S(1)}, bf16[1088,128]{1,0:T(8,128)(2,1)S(1)}, u32[]{:S(2)}, u32[]{:S(2)}) collective-permute-start(bf16[1088,128]{1,0:T(8,128)(2,1)S(1)} %get-tuple-element.78), channel_id=1, source_target_pairs={{0,3},{1,0},{2,1},{3,2},{4,7},{5,4},{6,5},{7,6},{8,11},{9,8},{10,9... | collective-permute-start | bytes 835592 | tf_op jit(solution)/shard_map/ppermute | solution.py:342
  97.6 16.1 %collective-permute-start.17 = (bf16[4,272,128]{2,1,0:T(8,128)(2,1)S(1)}, bf16[4,272,128]{2,1,0:T(8,128)(2,1)S(1)}, u32[]{:S(2)}, u32[]{:S(2)}) collective-permute-start(bf16[4,272,128]{2,1,0:T(8,128)(2,1)S(1)} %get-tuple-element.81.refs_0_), channel_id=1, source_target_pairs={{0,1},{1,2},{2,3},{3,0},{4,5},{5,6},{6,7},{7,4},{8,9},{9,10},{10,1... | collective-permute-start | bytes 835592 | tf_op jit(solution)/shard_map/ppermute | solution.py:342
  98.5 18.8 %collective-permute-start.21 = (bf16[4,272,128]{2,1,0:T(8,128)(2,1)S(1)}, bf16[4,272,128]{2,1,0:T(8,128)(2,1)S(1)}, u32[]{:S(2)}, u32[]{:S(2)}) collective-permute-start(bf16[4,272,128]{2,1,0:T(8,128)(2,1)S(1)} %get-tuple-element.81.refs_0_), channel_id=1, source_target_pairs={{0,2},{1,3},{2,0},{3,1},{4,6},{5,7},{6,4},{7,5},{8,10},{9,11},{10,... | collective-permute-start | bytes 835592 | tf_op jit(solution)/shard_map/ppermute | solution.py:342
  101.3 16.0 %collective-permute-start.22 = (bf16[4,272,128]{2,1,0:T(8,128)(2,1)S(1)}, bf16[4,272,128]{2,1,0:T(8,128)(2,1)S(1)}, u32[]{:S(2)}, u32[]{:S(2)}) collective-permute-start(bf16[4,272,128]{2,1,0:T(8,128)(2,1)S(1)} %get-tuple-element.81.refs_0_), channel_id=1, source_target_pairs={{0,3},{1,0},{2,1},{3,2},{4,7},{5,4},{6,5},{7,6},{8,11},{9,8},{10,9... | collective-permute-start | bytes 835592 | tf_op jit(solution)/shard_map/ppermute | solution.py:342
  101.3 7.5 %collective-permute-start.15 = (bf16[4,40,128]{2,1,0:T(8,128)(2,1)S(1)}, bf16[4,40,128]{2,1,0:T(8,128)(2,1)S(1)}, u32[]{:S(2)}, u32[]{:S(2)}) collective-permute-start(bf16[4,40,128]{2,1,0:T(8,128)(2,1)S(1)} %get-tuple-element.79), channel_id=1, source_target_pairs={{0,16},{16,32},{32,48},{48,64},{64,80},{80,96},{96,112},{112,128},... | collective-permute-start | bytes 122888 | tf_op jit(solution)/shard_map/ppermute | solution.py:139
  106.9 6.8 %collective-permute-start.16 = (bf16[4,40,128]{2,1,0:T(8,128)(2,1)S(1)}, bf16[4,40,128]{2,1,0:T(8,128)(2,1)S(1)}, u32[]{:S(2)}, u32[]{:S(2)}) collective-permute-start(bf16[4,40,128]{2,1,0:T(8,128)(2,1)S(1)} %get-tuple-element.80), channel_id=1, source_target_pairs={{16,0},{32,16},{48,32},{64,48},{80,64},{96,80},{112,96},{128,112},... | collective-permute-start | bytes 122888 | tf_op jit(solution)/shard_map/ppermute | solution.py:140
  113.7 4.8 %collective-permute-start.18 = (bf16[4,80,128]{2,1,0:T(8,128)(2,1)S(1)}, bf16[4,80,128]{2,1,0:T(8,128)(2,1)S(1)}, u32[]{:S(2)}, u32[]{:S(2)}) collective-permute-start(bf16[4,80,128]{2,1,0:T(8,128)(2,1)S(1)} %pack.1.refs_0_), channel_id=1, source_target_pairs={{0,1},{1,2},{2,3},{3,0},{4,5},{5,6},{6,7},{7,4},{8,9},{9,10},{10,1... | collective-permute-start | bytes 245768 | tf_op jit(solution)/shard_map/ppermute | solution.py:342
  114.8 4.8 %collective-permute-start.19 = (bf16[4,80,128]{2,1,0:T(8,128)(2,1)S(1)}, bf16[4,80,128]{2,1,0:T(8,128)(2,1)S(1)}, u32[]{:S(2)}, u32[]{:S(2)}) collective-permute-start(bf16[4,80,128]{2,1,0:T(8,128)(2,1)S(1)} %pack.1.refs_0_), channel_id=1, source_target_pairs={{0,2},{1,3},{2,0},{3,1},{4,6},{5,7},{6,4},{7,5},{8,10},{9,11},{10,... | collective-permute-start | bytes 245768 | tf_op jit(solution)/shard_map/ppermute | solution.py:342
  (2 other events, 14.1 us)

commit v11 on v10

--- a/solution.py
+++ b/solution.py
@@ -500,7 +500,7 @@
     )(flags, features, *halo[2:], *pieces)
     others = to_peers([resid] * 3)
     (border,) = call(pack_body, [sds((frames, 2 * COLS + 16, CH))], name="pack")(
-        *swap_rows(top, bot), Left(others[0])
+        *swap_rows(top, bot), Left(others[1])
     )
     borders = [border] + to_peers([border] * 3)
     (folded,) = call(fold_body, [sds((2, 2, 8 * CH, 2 * CH))], limit=12, name="fold")(

time: 124 us -> 125 us (level)
  no operation moved by 1% of the time
where the time goes in v11:
time: 125 us
  starting transfers between devices  68.4 us (55%)
  waiting for transfers between devices  30.8 us (25%)
  Pallas kernels  25.1 us (20%)
    all_to_all x2, starting transfers between devices, spread(): return lax.all_to_all(slots, HA + ('wa',), 0, 0, tiled=True)  21.4 us
    pallas_call x13, Pallas kernels, run(): pl.pallas_call(body, out_shape=list(outs), in_specs=specs, out_specs=[VME...  21.1 us
    ppermute x15, starting transfers between devices, to_peer(): return lax.ppermute(piece, 'col', [(i, (i + k) % n) for i in range(n)])  21 us
    ppermute x15, waiting for transfers between devices, to_peer(): return lax.ppermute(piece, 'col', [(i, (i + k) % n) for i in range(n)])  17 us
    ppermute x3, starting transfers between devices, swap_rows(): above = lax.ppermute(bot, HA, [(i, i + 1) for i in range(n - 1)])  15.8 us
    ppermute x3, waiting for transfers between devices, swap_rows(): below = lax.ppermute(top, HA, [(i + 1, i) for i in range(n - 1)])  9.73 us
    ppermute x3, starting transfers between devices, swap_rows(): below = lax.ppermute(top, HA, [(i + 1, i) for i in range(n - 1)])  5.76 us
    pallas_call x1, Pallas kernels, up_conv(): pl.pallas_call(up_body, out_shape=sds(out), grid=(frames,), in_specs=[by_...  3.97 us
  transfers between devices with their start and end apart: 25, of which 11 were waited for; matrix products, arithmetic and copies ran while one was open for 0% of the time, Pallas kernels for 9%

profile of v11, /device:TPU:97, one launch (start us, length us, event | category | flops | bytes accessed | tf_op | source)
XLA Modules:
  0.0 124.6 jit_solution(17610325909012117104)
XLA Ops:
  0.1 3.2 %first.1 = (bf16[4,8,32,128]{3,2,1,0:T(8,128)(2,1)S(1)}, bf16[2,8,32,128]{3,2,1,0:T(8,128)(2,1)S(1)}, bf16[2,8,32,128]{3,2,1,0:T(8,128)(2,1)S(1)}, f32[64,2,128]...) custom-call(s32[5]{0:T(128)S(1)} %stack.39.flag_ref, ...), custom_call_target="tpu_custom_call" | custom-call | bytes 3801108 | tf_op jit(solution)/shard_map/first/pallas_call | solution.py:39
  3.2 5.3 %collective-permute-start = (bf16[8,32,128]{2,1,0:T(8,128)(2,1)S(1)}, bf16[8,32,128]{2,1,0:T(8,128)(2,1)S(1)}, u32[]{:S(2)}, u32[]{:S(2)}) collective-permute-start(bf16[8,32,128]{2,1,0:T(8,128)(2,1)S(1)} %get-tuple-element.44), channel_id=1, source_target_pairs={{0,16},{16,32},{32,48},{48,64},{64,80},{80,96},{96,112},{112,128},... | collective-permute-start | bytes 196616 | tf_op jit(solution)/shard_map/ppermute | solution.py:139
  8.6 1.9 %collective-permute-start.1 = (bf16[8,32,128]{2,1,0:T(8,128)(2,1)S(1)}, bf16[8,32,128]{2,1,0:T(8,128)(2,1)S(1)}, u32[]{:S(2)}, u32[]{:S(2)}) collective-permute-start(bf16[8,32,128]{2,1,0:T(8,128)(2,1)S(1)} %get-tuple-element.45), channel_id=1, source_target_pairs={{16,0},{32,16},{48,32},{64,48},{80,64},{96,80},{112,96},{128,112},... | collective-permute-start | bytes 196616 | tf_op jit(solution)/shard_map/ppermute | solution.py:140
  10.5 10.8 %all-to-all-start = ((f32[64,2,128]{2,1,0:T(2,128)}), f32[64,2,128]{2,1,0:T(2,128)S(1)}, u32[]{:S(2)}, u32[]{:S(2)}) async-start(f32[64,2,128]{2,1,0:T(2,128)} %get-tuple-element.52), calls=%async_computation | async-start | bytes 131072 | tf_op jit(solution)/shard_map/all_to_all | solution.py:89
  21.4 3.1 %collective-permute-start.2 = (bf16[8,3,16,128]{3,2,1,0:T(8,128)(2,1)S(1)}, bf16[8,3,16,128]{3,2,1,0:T(8,128)(2,1)S(1)}, u32[]{:S(2)}, u32[]{:S(2)}) collective-permute-start(bf16[8,3,16,128]{3,2,1,0:T(8,128)(2,1)S(1)} %get-tuple-element.48), channel_id=1, source_target_pairs={{0,4},{4,8},{8,12},{1,5},{5,9},{9,13},{2,6},{6,10},{10,14},{3,7},{... | collective-permute-start | bytes 294920 | tf_op jit(solution)/shard_map/ppermute | solution.py:146
  25.8 2.6 %all-to-all-done.st_ref = f32[64,2,128]{2,1,0:T(2,128)S(1)} async-done(((f32[64,2,128]{2,1,0:T(2,128)}), f32[64,2,128]{2,1,0:T(2,128)S(1)}, u32[]{:S(2)}, u32[]{:S(2)}) %all-to-all-start) | async-done | bytes 65568 | tf_op jit(solution)/shard_map/all_to_all | solution.py:89
  29.8 4.5 %conv_first_far.1 = (bf16[1152,128]{1,0:T(8,128)(2,1)S(1)}, bf16[1152,128]{1,0:T(8,128)(2,1)S(1)}, bf16[6,320,384]{2,1,0:T(8,128)(2,1)S(1)}, bf16[3,160,384]{2,1,0:T(8,128)(2,1)S(1)}, bf16[3456,256]{1,0:T(8,128)(2,1)S(1)}) custom-call(s32[5]{0:T(128)S(1)} %stack.39.flag_ref, bf16[4,8,32,128]{3,2,1,0:T(8,128)(2,1)S(1)} %get-tuple-element.50.x_ref, ...), custom_call_target="tpu_custom_call" | custom-call | flops 2038431744 | bytes 8527892 | tf_op jit(solution)/shard_map/conv_first_far/pallas_call | solution.py:39
  34.4 2.8 %collective-permute-start.4 = (bf16[1152,128]{1,0:T(8,128)(2,1)S(1)}, bf16[1152,128]{1,0:T(8,128)(2,1)S(1)}, u32[]{:S(2)}, u32[]{:S(2)}) collective-permute-start(bf16[1152,128]{1,0:T(8,128)(2,1)S(1)} %get-tuple-element.57), channel_id=1, source_target_pairs={{0,2},{1,3},{2,0},{3,1},{4,6},{5,7},{6,4},{7,5},{8,10},{9,11},{10,... | collective-permute-start | bytes 884744 | tf_op jit(solution)/shard_map/ppermute | solution.py:342
  37.5 2.5 %conv_first_near.1 = (bf16[1152,128]{1,0:T(8,128)(2,1)S(1)}, bf16[1152,128]{1,0:T(8,128)(2,1)S(1)}) custom-call(bf16[6,320,384]{2,1,0:T(8,128)(2,1)S(1)} %get-tuple-element.53.patch_ref, bf16[3,160,384]{2,1,0:T(8,128)(2,1)S(1)} %get-tuple-element.54.side_ref, bf16[3456,256]{1,0:T(8,128)(2,1)S(1)} %get-tuple-element.55.w_ref), custom_call_target="tpu_custom_call" | custom-call | flops 2038431744 | bytes 4202496 | tf_op jit(solution)/shard_map/conv_first_near/pallas_call | solution.py:39
  40.0 2.4 %collective-permute-start.6 = (bf16[1152,128]{1,0:T(8,128)(2,1)S(1)}, bf16[1152,128]{1,0:T(8,128)(2,1)S(1)}, u32[]{:S(2)}, u32[]{:S(2)}) collective-permute-start(bf16[1152,128]{1,0:T(8,128)(2,1)S(1)} %get-tuple-element.59), channel_id=1, source_target_pairs={{0,3},{1,0},{2,1},{3,2},{4,7},{5,4},{6,5},{7,6},{8,11},{9,8},{10,9... | collective-permute-start | bytes 884744 | tf_op jit(solution)/shard_map/ppermute | solution.py:342
  42.7 8.1 %collective-permute-done.5.b_ref = bf16[1152,128]{1,0:T(8,128)(2,1)S(1)} collective-permute-done((bf16[1152,128]{1,0:T(8,128)(2,1)S(1)}, bf16[1152,128]{1,0:T(8,128)(2,1)S(1)}, u32[]{:S(2)}, u32[]{:S(2)}) %collective-permute-start.5) | collective-permute-done | bytes 294944 | tf_op jit(solution)/shard_map/ppermute | solution.py:342
  52.5 10.6 %all-to-all-start.1 = ((f32[64,2,128]{2,1,0:T(2,128)}), f32[64,2,128]{2,1,0:T(2,128)S(1)}, u32[]{:S(2)}, u32[]{:S(2)}) async-start(f32[64,2,128]{2,1,0:T(2,128)} %get-tuple-element.62.refs_3_), calls=%async_computation.1 | async-start | bytes 131072 | tf_op jit(solution)/shard_map/all_to_all | solution.py:89
  63.1 2.0 %collective-permute-start.10 = (bf16[9,128,128]{2,1,0:T(8,128)(2,1)S(1)}, bf16[9,128,128]{2,1,0:T(8,128)(2,1)S(1)}, u32[]{:S(2)}, u32[]{:S(2)}) collective-permute-start(bf16[9,128,128]{2,1,0:T(8,128)(2,1)S(1)} %get-tuple-element.73), channel_id=1, source_target_pairs={{0,2},{1,3},{2,0},{3,1},{4,6},{5,7},{6,4},{7,5},{8,10},{9,11},{10,... | collective-permute-start | bytes 884744 | tf_op jit(solution)/shard_map/ppermute | solution.py:342
  66.8 5.1 %collective-permute-start.7 = (bf16[144,128]{1,0:T(8,128)(2,1)S(1)}, bf16[144,128]{1,0:T(8,128)(2,1)S(1)}, u32[]{:S(2)}, u32[]{:S(2)}) collective-permute-start(bf16[144,128]{1,0:T(8,128)(2,1)S(1)} %get-tuple-element.64), channel_id=1, source_target_pairs={{0,16},{16,32},{32,48},{48,64},{64,80},{80,96},{96,112},{112,128},... | collective-permute-start | bytes 110600 | tf_op jit(solution)/shard_map/ppermute | solution.py:139
  73.9 4.8 %collective-permute-done.8.rest_6_ = bf16[144,128]{1,0:T(8,128)(2,1)S(1)} collective-permute-done((bf16[144,128]{1,0:T(8,128)(2,1)S(1)}, bf16[144,128]{1,0:T(8,128)(2,1)S(1)}, u32[]{:S(2)}, u32[]{:S(2)}) %collective-permute-start.8) | collective-permute-done | bytes 36896 | tf_op jit(solution)/shard_map/ppermute | solution.py:140
  78.8 4.6 %conv_second_far.1 = (bf16[1088,128]{1,0:T(8,128)(2,1)S(1)}, bf16[1088,128]{1,0:T(8,128)(2,1)S(1)}, bf16[6,320,384]{2,1,0:T(8,128)(2,1)S(1)}, bf16[3,80,384]{2,1,0:T(8,128)(2,1)S(1)}, bf16[3456,256]{1,0:T(8,128)(2,1)S(1)}) custom-call(s32[5]{0:T(128)S(1)} %stack.39.flag_ref, bf16[4,8,32,128]{3,2,1,0:T(8,128)(2,1)S(1)} %get-tuple-element.60.x_ref, ...), custom_call_target="tpu_custom_call" | custom-call | flops 1925185536 | bytes 8450068 | tf_op jit(solution)/shard_map/conv_second_far/pallas_call | solution.py:39
  84.8 2.2 %collective-permute-start.13 = (bf16[1088,128]{1,0:T(8,128)(2,1)S(1)}, bf16[1088,128]{1,0:T(8,128)(2,1)S(1)}, u32[]{:S(2)}, u32[]{:S(2)}) collective-permute-start(bf16[1088,128]{1,0:T(8,128)(2,1)S(1)} %get-tuple-element.77), channel_id=1, source_target_pairs={{0,1},{1,2},{2,3},{3,0},{4,5},{5,6},{6,7},{7,4},{8,9},{9,10},{10,1... | collective-permute-start | bytes 835592 | tf_op jit(solution)/shard_map/ppermute | solution.py:342
  87.0 2.5 %conv_second_near.1 = (bf16[1088,128]{1,0:T(8,128)(2,1)S(1)}, bf16[1088,128]{1,0:T(8,128)(2,1)S(1)}) custom-call(bf16[6,320,384]{2,1,0:T(8,128)(2,1)S(1)} %get-tuple-element.66.patch_ref, bf16[3,80,384]{2,1,0:T(8,128)(2,1)S(1)} %get-tuple-element.67.side_ref, bf16[3456,256]{1,0:T(8,128)(2,1)S(1)} %get-tuple-element.68.w_ref, ...), custom_call_target="tpu_custom_call" | custom-call | flops 1925185536 | bytes 4870144 | tf_op jit(solution)/shard_map/conv_second_near/pallas_call | solution.py:39
  90.1 3.0 %collective-permute-done.12.a_ref = bf16[1088,128]{1,0:T(8,128)(2,1)S(1)} collective-permute-done((bf16[1088,128]{1,0:T(8,128)(2,1)S(1)}, bf16[1088,128]{1,0:T(8,128)(2,1)S(1)}, u32[]{:S(2)}, u32[]{:S(2)}) %collective-permute-start.12) | collective-permute-done | bytes 278560 | tf_op jit(solution)/shard_map/ppermute | solution.py:342
  93.1 3.0 %collective-permute-done.13.b_ref = bf16[1088,128]{1,0:T(8,128)(2,1)S(1)} collective-permute-done((bf16[1088,128]{1,0:T(8,128)(2,1)S(1)}, bf16[1088,128]{1,0:T(8,128)(2,1)S(1)}, u32[]{:S(2)}, u32[]{:S(2)}) %collective-permute-start.13) | collective-permute-done | bytes 278560 | tf_op jit(solution)/shard_map/ppermute | solution.py:342
  100.9 5.4 %collective-permute-start.15 = (bf16[4,40,128]{2,1,0:T(8,128)(2,1)S(1)}, bf16[4,40,128]{2,1,0:T(8,128)(2,1)S(1)}, u32[]{:S(2)}, u32[]{:S(2)}) collective-permute-start(bf16[4,40,128]{2,1,0:T(8,128)(2,1)S(1)} %get-tuple-element.79), channel_id=1, source_target_pairs={{0,16},{16,32},{32,48},{48,64},{64,80},{80,96},{96,112},{112,128},... | collective-permute-start | bytes 122888 | tf_op jit(solution)/shard_map/ppermute | solution.py:139
  108.2 4.9 %collective-permute-done.16.bot_ref = bf16[4,40,128]{2,1,0:T(8,128)(2,1)S(1)} collective-permute-done((bf16[4,40,128]{2,1,0:T(8,128)(2,1)S(1)}, bf16[4,40,128]{2,1,0:T(8,128)(2,1)S(1)}, u32[]{:S(2)}, u32[]{:S(2)}) %collective-permute-start.16) | collective-permute-done | bytes 40992 | tf_op jit(solution)/shard_map/ppermute | solution.py:140
  114.2 3.2 %collective-permute-start.19 = (bf16[4,80,128]{2,1,0:T(8,128)(2,1)S(1)}, bf16[4,80,128]{2,1,0:T(8,128)(2,1)S(1)}, u32[]{:S(2)}, u32[]{:S(2)}) collective-permute-start(bf16[4,80,128]{2,1,0:T(8,128)(2,1)S(1)} %pack.1.refs_0_), channel_id=1, source_target_pairs={{0,2},{1,3},{2,0},{3,1},{4,6},{5,7},{6,4},{7,5},{8,10},{9,11},{10,... | collective-permute-start | bytes 245768 | tf_op jit(solution)/shard_map/ppermute | solution.py:342
  120.7 4.0 %up_conv.1 = bf16[4,16,64,128]{3,2,1,0:T(8,128)(2,1)} custom-call(bf16[4,80,128]{2,1,0:T(8,128)(2,1)S(1)} %pack.1.refs_0_, bf16[4,80,128]{2,1,0:T(8,128)(2,1)S(1)} %collective-permute-done.18.refs_1_, bf16[4,80,128]{2,1,0:T(8,128)(2,1)S(1)} %collective-permute-done.19.refs_2_, bf16[4,80,128]{2,1,0:T(8,128)(2,1)S(1)} %collective-permute-done.20.refs_3_, ...), custom_call_target="tpu_custom_call" | custom-call | tf_op jit(solution)/shard_map/up_conv/pallas_call | solution.py:442
  (44 shorter events, 21.9 us)
Async XLA Ops:
  3.2 18.0 %collective-permute-start = (bf16[8,32,128]{2,1,0:T(8,128)(2,1)S(1)}, bf16[8,32,128]{2,1,0:T(8,128)(2,1)S(1)}, u32[]{:S(2)}, u32[]{:S(2)}) collective-permute-start(bf16[8,32,128]{2,1,0:T(8,128)(2,1)S(1)} %get-tuple-element.44), channel_id=1, source_target_pairs={{0,16},{16,32},{32,48},{48,64},{64,80},{80,96},{96,112},{112,128},... | collective-permute-start | bytes 196616 | tf_op jit(solution)/shard_map/ppermute | solution.py:139
  8.6 12.7 %collective-permute-start.1 = (bf16[8,32,128]{2,1,0:T(8,128)(2,1)S(1)}, bf16[8,32,128]{2,1,0:T(8,128)(2,1)S(1)}, u32[]{:S(2)}, u32[]{:S(2)}) collective-permute-start(bf16[8,32,128]{2,1,0:T(8,128)(2,1)S(1)} %get-tuple-element.45), channel_id=1, source_target_pairs={{16,0},{32,16},{48,32},{64,48},{80,64},{96,80},{112,96},{128,112},... | collective-permute-start | bytes 196616 | tf_op jit(solution)/shard_map/ppermute | solution.py:140
  10.5 17.9 %all-to-all-start = ((f32[64,2,128]{2,1,0:T(2,128)}), f32[64,2,128]{2,1,0:T(2,128)S(1)}, u32[]{:S(2)}, u32[]{:S(2)}) async-start(f32[64,2,128]{2,1,0:T(2,128)} %get-tuple-element.52), calls=%async_computation | async-start | bytes 131072 | tf_op jit(solution)/shard_map/all_to_all | solution.py:89
  21.4 7.0 %collective-permute-start.2 = (bf16[8,3,16,128]{3,2,1,0:T(8,128)(2,1)S(1)}, bf16[8,3,16,128]{3,2,1,0:T(8,128)(2,1)S(1)}, u32[]{:S(2)}, u32[]{:S(2)}) collective-permute-start(bf16[8,3,16,128]{3,2,1,0:T(8,128)(2,1)S(1)} %get-tuple-element.48), channel_id=1, source_target_pairs={{0,4},{4,8},{8,12},{1,5},{5,9},{9,13},{2,6},{6,10},{10,14},{3,7},{... | collective-permute-start | bytes 294920 | tf_op jit(solution)/shard_map/ppermute | solution.py:146
  24.5 5.4 %collective-permute-start.3 = (bf16[8,3,16,128]{3,2,1,0:T(8,128)(2,1)S(1)}, bf16[8,3,16,128]{3,2,1,0:T(8,128)(2,1)S(1)}, u32[]{:S(2)}, u32[]{:S(2)}) collective-permute-start(bf16[8,3,16,128]{3,2,1,0:T(8,128)(2,1)S(1)} %get-tuple-element.49), channel_id=1, source_target_pairs={{4,0},{8,4},{12,8},{5,1},{9,5},{13,9},{6,2},{10,6},{14,10},{7,3},{... | collective-permute-start | bytes 294920 | tf_op jit(solution)/shard_map/ppermute | solution.py:147
  34.4 8.3 %collective-permute-start.4 = (bf16[1152,128]{1,0:T(8,128)(2,1)S(1)}, bf16[1152,128]{1,0:T(8,128)(2,1)S(1)}, u32[]{:S(2)}, u32[]{:S(2)}) collective-permute-start(bf16[1152,128]{1,0:T(8,128)(2,1)S(1)} %get-tuple-element.57), channel_id=1, source_target_pairs={{0,2},{1,3},{2,0},{3,1},{4,6},{5,7},{6,4},{7,5},{8,10},{9,11},{10,... | collective-permute-start | bytes 884744 | tf_op jit(solution)/shard_map/ppermute | solution.py:342
  37.2 13.6 %collective-permute-start.5 = (bf16[1152,128]{1,0:T(8,128)(2,1)S(1)}, bf16[1152,128]{1,0:T(8,128)(2,1)S(1)}, u32[]{:S(2)}, u32[]{:S(2)}) collective-permute-start(bf16[1152,128]{1,0:T(8,128)(2,1)S(1)} %get-tuple-element.58), channel_id=1, source_target_pairs={{0,1},{1,2},{2,3},{3,0},{4,5},{5,6},{6,7},{7,4},{8,9},{9,10},{10,1... | collective-permute-start | bytes 884744 | tf_op jit(solution)/shard_map/ppermute | solution.py:342
  40.0 10.8 %collective-permute-start.6 = (bf16[1152,128]{1,0:T(8,128)(2,1)S(1)}, bf16[1152,128]{1,0:T(8,128)(2,1)S(1)}, u32[]{:S(2)}, u32[]{:S(2)}) collective-permute-start(bf16[1152,128]{1,0:T(8,128)(2,1)S(1)} %get-tuple-element.59), channel_id=1, source_target_pairs={{0,3},{1,0},{2,1},{3,2},{4,7},{5,4},{6,5},{7,6},{8,11},{9,8},{10,9... | collective-permute-start | bytes 884744 | tf_op jit(solution)/shard_map/ppermute | solution.py:342
  52.5 26.3 %all-to-all-start.1 = ((f32[64,2,128]{2,1,0:T(2,128)}), f32[64,2,128]{2,1,0:T(2,128)S(1)}, u32[]{:S(2)}, u32[]{:S(2)}) async-start(f32[64,2,128]{2,1,0:T(2,128)} %get-tuple-element.62.refs_3_), calls=%async_computation.1 | async-start | bytes 131072 | tf_op jit(solution)/shard_map/all_to_all | solution.py:89
  63.1 23.9 %collective-permute-start.10 = (bf16[9,128,128]{2,1,0:T(8,128)(2,1)S(1)}, bf16[9,128,128]{2,1,0:T(8,128)(2,1)S(1)}, u32[]{:S(2)}, u32[]{:S(2)}) collective-permute-start(bf16[9,128,128]{2,1,0:T(8,128)(2,1)S(1)} %get-tuple-element.73), channel_id=1, source_target_pairs={{0,2},{1,3},{2,0},{3,1},{4,6},{5,7},{6,4},{7,5},{8,10},{9,11},{10,... | collective-permute-start | bytes 884744 | tf_op jit(solution)/shard_map/ppermute | solution.py:342
  65.0 21.9 %collective-permute-start.11 = (bf16[9,128,128]{2,1,0:T(8,128)(2,1)S(1)}, bf16[9,128,128]{2,1,0:T(8,128)(2,1)S(1)}, u32[]{:S(2)}, u32[]{:S(2)}) collective-permute-start(bf16[9,128,128]{2,1,0:T(8,128)(2,1)S(1)} %get-tuple-element.74), channel_id=1, source_target_pairs={{0,3},{1,0},{2,1},{3,2},{4,7},{5,4},{6,5},{7,6},{8,11},{9,8},{10,9... | collective-permute-start | bytes 884744 | tf_op jit(solution)/shard_map/ppermute | solution.py:342
  66.8 20.1 %collective-permute-start.9 = (bf16[9,128,128]{2,1,0:T(8,128)(2,1)S(1)}, bf16[9,128,128]{2,1,0:T(8,128)(2,1)S(1)}, u32[]{:S(2)}, u32[]{:S(2)}) collective-permute-start(bf16[9,128,128]{2,1,0:T(8,128)(2,1)S(1)} %get-tuple-element.72), channel_id=1, source_target_pairs={{0,1},{1,2},{2,3},{3,0},{4,5},{5,6},{6,7},{7,4},{8,9},{9,10},{10,1... | collective-permute-start | bytes 884744 | tf_op jit(solution)/shard_map/ppermute | solution.py:342
  66.8 7.1 %collective-permute-start.7 = (bf16[144,128]{1,0:T(8,128)(2,1)S(1)}, bf16[144,128]{1,0:T(8,128)(2,1)S(1)}, u32[]{:S(2)}, u32[]{:S(2)}) collective-permute-start(bf16[144,128]{1,0:T(8,128)(2,1)S(1)} %get-tuple-element.64), channel_id=1, source_target_pairs={{0,16},{16,32},{32,48},{48,64},{64,80},{80,96},{96,112},{112,128},... | collective-permute-start | bytes 110600 | tf_op jit(solution)/shard_map/ppermute | solution.py:139
  72.0 6.8 %collective-permute-start.8 = (bf16[144,128]{1,0:T(8,128)(2,1)S(1)}, bf16[144,128]{1,0:T(8,128)(2,1)S(1)}, u32[]{:S(2)}, u32[]{:S(2)}) collective-permute-start(bf16[144,128]{1,0:T(8,128)(2,1)S(1)} %get-tuple-element.65), channel_id=1, source_target_pairs={{16,0},{32,16},{48,32},{64,48},{80,64},{96,80},{112,96},{128,112},... | collective-permute-start | bytes 110600 | tf_op jit(solution)/shard_map/ppermute | solution.py:140
  83.3 9.8 %collective-permute-start.12 = (bf16[1088,128]{1,0:T(8,128)(2,1)S(1)}, bf16[1088,128]{1,0:T(8,128)(2,1)S(1)}, u32[]{:S(2)}, u32[]{:S(2)}) collective-permute-start(bf16[1088,128]{1,0:T(8,128)(2,1)S(1)} %get-tuple-element.76), channel_id=1, source_target_pairs={{0,2},{1,3},{2,0},{3,1},{4,6},{5,7},{6,4},{7,5},{8,10},{9,11},{10,... | collective-permute-start | bytes 835592 | tf_op jit(solution)/shard_map/ppermute | solution.py:342
  84.8 11.3 %collective-permute-start.13 = (bf16[1088,128]{1,0:T(8,128)(2,1)S(1)}, bf16[1088,128]{1,0:T(8,128)(2,1)S(1)}, u32[]{:S(2)}, u32[]{:S(2)}) collective-permute-start(bf16[1088,128]{1,0:T(8,128)(2,1)S(1)} %get-tuple-element.77), channel_id=1, source_target_pairs={{0,1},{1,2},{2,3},{3,0},{4,5},{5,6},{6,7},{7,4},{8,9},{9,10},{10,1... | collective-permute-start | bytes 835592 | tf_op jit(solution)/shard_map/ppermute | solution.py:342
  89.5 7.4 %collective-permute-start.14 = (bf16[1088,128]{1,0:T(8,128)(2,1)S(1)}, bf16[1088,128]{1,0:T(8,128)(2,1)S(1)}, u32[]{:S(2)}, u32[]{:S(2)}) collective-permute-start(bf16[1088,128]{1,0:T(8,128)(2,1)S(1)} %get-tuple-element.78), channel_id=1, source_target_pairs={{0,3},{1,0},{2,1},{3,2},{4,7},{5,4},{6,5},{7,6},{8,11},{9,8},{10,9... | collective-permute-start | bytes 835592 | tf_op jit(solution)/shard_map/ppermute | solution.py:342
  97.6 15.5 %collective-permute-start.17 = (bf16[4,272,128]{2,1,0:T(8,128)(2,1)S(1)}, bf16[4,272,128]{2,1,0:T(8,128)(2,1)S(1)}, u32[]{:S(2)}, u32[]{:S(2)}) collective-permute-start(bf16[4,272,128]{2,1,0:T(8,128)(2,1)S(1)} %get-tuple-element.81.refs_0_), channel_id=1, source_target_pairs={{0,2},{1,3},{2,0},{3,1},{4,6},{5,7},{6,4},{7,5},{8,10},{9,11},{10,... | collective-permute-start | bytes 835592 | tf_op jit(solution)/shard_map/ppermute | solution.py:342
  99.1 18.2 %collective-permute-start.22 = (bf16[4,272,128]{2,1,0:T(8,128)(2,1)S(1)}, bf16[4,272,128]{2,1,0:T(8,128)(2,1)S(1)}, u32[]{:S(2)}, u32[]{:S(2)}) collective-permute-start(bf16[4,272,128]{2,1,0:T(8,128)(2,1)S(1)} %get-tuple-element.81.refs_0_), channel_id=1, source_target_pairs={{0,3},{1,0},{2,1},{3,2},{4,7},{5,4},{6,5},{7,6},{8,11},{9,8},{10,9... | collective-permute-start | bytes 835592 | tf_op jit(solution)/shard_map/ppermute | solution.py:342
  100.9 17.0 %collective-permute-start.21 = (bf16[4,272,128]{2,1,0:T(8,128)(2,1)S(1)}, bf16[4,272,128]{2,1,0:T(8,128)(2,1)S(1)}, u32[]{:S(2)}, u32[]{:S(2)}) collective-permute-start(bf16[4,272,128]{2,1,0:T(8,128)(2,1)S(1)} %get-tuple-element.81.refs_0_), channel_id=1, source_target_pairs={{0,1},{1,2},{2,3},{3,0},{4,5},{5,6},{6,7},{7,4},{8,9},{9,10},{10,1... | collective-permute-start | bytes 835592 | tf_op jit(solution)/shard_map/ppermute | solution.py:342
  100.9 7.3 %collective-permute-start.15 = (bf16[4,40,128]{2,1,0:T(8,128)(2,1)S(1)}, bf16[4,40,128]{2,1,0:T(8,128)(2,1)S(1)}, u32[]{:S(2)}, u32[]{:S(2)}) collective-permute-start(bf16[4,40,128]{2,1,0:T(8,128)(2,1)S(1)} %get-tuple-element.79), channel_id=1, source_target_pairs={{0,16},{16,32},{32,48},{48,64},{64,80},{80,96},{96,112},{112,128},... | collective-permute-start | bytes 122888 | tf_op jit(solution)/shard_map/ppermute | solution.py:139
  106.3 6.8 %collective-permute-start.16 = (bf16[4,40,128]{2,1,0:T(8,128)(2,1)S(1)}, bf16[4,40,128]{2,1,0:T(8,128)(2,1)S(1)}, u32[]{:S(2)}, u32[]{:S(2)}) collective-permute-start(bf16[4,40,128]{2,1,0:T(8,128)(2,1)S(1)} %get-tuple-element.80), channel_id=1, source_target_pairs={{16,0},{32,16},{48,32},{64,48},{80,64},{96,80},{112,96},{128,112},... | collective-permute-start | bytes 122888 | tf_op jit(solution)/shard_map/ppermute | solution.py:140
  113.1 5.5 %collective-permute-start.18 = (bf16[4,80,128]{2,1,0:T(8,128)(2,1)S(1)}, bf16[4,80,128]{2,1,0:T(8,128)(2,1)S(1)}, u32[]{:S(2)}, u32[]{:S(2)}) collective-permute-start(bf16[4,80,128]{2,1,0:T(8,128)(2,1)S(1)} %pack.1.refs_0_), channel_id=1, source_target_pairs={{0,1},{1,2},{2,3},{3,0},{4,5},{5,6},{6,7},{7,4},{8,9},{9,10},{10,1... | collective-permute-start | bytes 245768 | tf_op jit(solution)/shard_map/ppermute | solution.py:342
  114.2 5.9 %collective-permute-start.19 = (bf16[4,80,128]{2,1,0:T(8,128)(2,1)S(1)}, bf16[4,80,128]{2,1,0:T(8,128)(2,1)S(1)}, u32[]{:S(2)}, u32[]{:S(2)}) collective-permute-start(bf16[4,80,128]{2,1,0:T(8,128)(2,1)S(1)} %pack.1.refs_0_), channel_id=1, source_target_pairs={{0,2},{1,3},{2,0},{3,1},{4,6},{5,7},{6,4},{7,5},{8,10},{9,11},{10,... | collective-permute-start | bytes 245768 | tf_op jit(solution)/shard_map/ppermute | solution.py:342
  (2 other events, 13.2 us)
